TPU v7x, 32 devices: a whole 2x2x4 slice. The times are simulated.
32 devices in a mesh: dp: 4 (over y, x), fsdp: 8 (over z, core).
Axes of the slice: x: 2, y: 2, z: 4, core: 2. Of those that a mesh axis runs over, the one named last changes fastest.
Arguments:
- tokens: bfloat16 [32, 1024, 1024], P(('dp', 'fsdp')), may hold values from -6 to 6
- cotangent: bfloat16 [32, 1024, 1024], P(('dp', 'fsdp')), may hold values from -6 to 6
- segment_ids: int32 [32, 1024], P(('dp', 'fsdp')), may hold values from 0 to 3, never falling along the last dimension, each value on 1 to 512 neighbouring positions
- padding_mask: int32 [32, 1024], P(('dp', 'fsdp')), may hold values from 0 to 1, as said below
- w_qkv: bfloat16 [1024, 3072], P(('dp', 'fsdp')), may hold values from -0.1875 to 0.1875
- bias_qv: bfloat16 [2048], P(('dp', 'fsdp')), may hold values from -4 to 4
- w_out: bfloat16 [1024, 1024], P(('dp', 'fsdp')), may hold values from -0.75 to 0.75
- bias_out: bfloat16 [1024], P(('dp', 'fsdp')), may hold values from -4 to 4
- gain_attn: bfloat16 [1024], P(('dp', 'fsdp')), may hold values from 0.25 to 1.75
- gain_mlp: bfloat16 [1024], P(('dp', 'fsdp')), may hold values from 0.25 to 1.75
- w_up: bfloat16 [1024, 4096], P(('dp', 'fsdp')), may hold values from -0.1875 to 0.1875
- bias_up: bfloat16 [4096], P(('dp', 'fsdp')), may hold values from -6 to 6
- w_down: bfloat16 [4096, 1024], P(('dp', 'fsdp')), may hold values from -0.09375 to 0.09375
- bias_down: bfloat16 [1024], P(('dp', 'fsdp')), may hold values from -4 to 4
Outputs:
- output: bfloat16 [32, 1024, 1024], P(('dp', 'fsdp'))
- input_grad: bfloat16 [32, 1024, 1024], P(('dp', 'fsdp'))
- grad_w_qkv: float32 [1024, 3072], P(('dp', 'fsdp'))
- grad_bias_qv: float32 [2048], P(('dp', 'fsdp'))
- grad_w_out: float32 [1024, 1024], P(('dp', 'fsdp'))
- grad_bias_out: float32 [1024], P(('dp', 'fsdp'))
- grad_gain_attn: float32 [1024], P(('dp', 'fsdp'))
- grad_gain_mlp: float32 [1024], P(('dp', 'fsdp'))
- grad_w_up: float32 [1024, 4096], P(('dp', 'fsdp'))
- grad_bias_up: float32 [4096], P(('dp', 'fsdp'))
- grad_w_down: float32 [4096, 1024], P(('dp', 'fsdp'))
- grad_bias_down: float32 [1024], P(('dp', 'fsdp'))
- stats: float32 [5], replicated
- real_frames: float32 [1], replicated
Inputs may be any that keep to these rules, and one draw needn't show every extreme that they name: `segment_ids`: along each packed row the ids never fall; an item covers at most 512 frames. `padding_mask`: the first frame of every row is real.
All inputs are finite; a program needn't handle non-finite values.
Results may differ from a plain program's by a relative error of at most 0.012.
Values may be sent and summed in bfloat16 or wider, within the bound.
No kernel may reach another device: no remote copies, remote signals or barrier semaphores. Data moves between devices by JAX's collectives and lax.ppermute only.
A program may use at most 256 MiB of HBM per device.

v0:
```python
import jax
import jax.numpy as jnp
from jax import lax
from jax.sharding import PartitionSpec as P

HD = 64


def rms_norm(values, gain):
    return values * lax.rsqrt(jnp.mean(values * values, -1, keepdims=True) + 1e-05) * gain


def gelu_tanh(values):
    return (
        0.5
        * values
        * (1.0 + jnp.tanh(0.7978845608028654 * (values + 0.044715 * values * values * values)))
    )


def contract_rows(left, right):
    return lax.dot_general(
        left, right, (((0,), (0,)), ((), ())), preferred_element_type=jnp.float32
    )


def times_transposed(left, weight):
    return lax.dot_general(
        left, weight, (((1,), (1,)), ((), ())), preferred_element_type=jnp.float32
    )


def block_allowed(segment_ids, padding_mask, first_row, block_rows, key_count):
    query_pos = first_row + jnp.arange(block_rows)
    key_pos = jnp.arange(key_count)
    same_item = (
        segment_ids[:, first_row : first_row + block_rows, None] == segment_ids[:, None, :key_count]
    )
    causal = key_pos[None, None, :] <= query_pos[None, :, None]
    itself = key_pos[None, None, :] == query_pos[None, :, None]
    usable = (padding_mask[:, None, :key_count] == 1) | itself
    return (same_item & causal & usable)[:, None]


def block_scores(queries, keys_all, segment_ids, padding_mask, first_row, block_rows):
    key_count = first_row + block_rows
    scale = queries.shape[-1] ** (-0.5)
    scores = (
        jnp.einsum(
            "rqhd,rkhd->rhqk",
            queries[:, first_row:key_count],
            keys_all[:, :key_count],
            preferred_element_type=jnp.float32,
        )
        * scale
    )
    allowed = block_allowed(segment_ids, padding_mask, first_row, block_rows, key_count)
    return jnp.where(allowed, scores, -1e30)


def attend_forward(queries, keys_all, values_all, segment_ids, padding_mask, block_rows):
    outputs = []
    log_parts = []
    for block_index in range(queries.shape[1] // block_rows):
        first_row = block_index * block_rows
        key_count = first_row + block_rows
        scores = block_scores(queries, keys_all, segment_ids, padding_mask, first_row, block_rows)
        highest_score = jnp.max(scores, -1, keepdims=True)
        log_total = highest_score + jnp.log(
            jnp.sum(jnp.exp(scores - highest_score), -1, keepdims=True)
        )
        probs = jnp.exp(scores - log_total)
        mixed = jnp.einsum(
            "rhqk,rkhd->rqhd",
            probs.astype(jnp.bfloat16),
            values_all[:, :key_count],
            preferred_element_type=jnp.float32,
        )
        outputs.append(mixed.astype(jnp.bfloat16))
        log_parts.append(log_total)
    return (jnp.concatenate(outputs, 1), jnp.concatenate(log_parts, 2))


def attend_backward(
    queries, keys_all, values_all, log_sums, grad_mixed, segment_ids, padding_mask, block_rows
):
    scale = queries.shape[-1] ** (-0.5)
    grad_keys = jnp.zeros(keys_all.shape, jnp.float32)
    grad_values = jnp.zeros(values_all.shape, jnp.float32)
    query_parts = []
    for block_index in range(queries.shape[1] // block_rows):
        first_row = block_index * block_rows
        key_count = first_row + block_rows
        scores = block_scores(queries, keys_all, segment_ids, padding_mask, first_row, block_rows)
        probs = jnp.exp(scores - log_sums[:, :, first_row:key_count])
        grad_block = grad_mixed[:, first_row:key_count]
        query_block = queries[:, first_row:key_count]
        grad_probs = jnp.einsum(
            "rqhd,rkhd->rhqk",
            grad_block,
            values_all[:, :key_count],
            preferred_element_type=jnp.float32,
        )
        inner = jnp.sum(probs * grad_probs, -1, keepdims=True)
        grad_scores = (probs * (grad_probs - inner)).astype(jnp.bfloat16)
        query_grad = (
            jnp.einsum(
                "rhqk,rkhd->rqhd",
                grad_scores,
                keys_all[:, :key_count],
                preferred_element_type=jnp.float32,
            )
            * scale
        )
        query_parts.append(query_grad.astype(jnp.bfloat16))
        key_part = (
            jnp.einsum(
                "rhqk,rqhd->rkhd", grad_scores, query_block, preferred_element_type=jnp.float32
            )
            * scale
        )
        value_part = jnp.einsum(
            "rhqk,rqhd->rkhd",
            probs.astype(jnp.bfloat16),
            grad_block,
            preferred_element_type=jnp.float32,
        )
        grad_keys = grad_keys.at[:, :key_count].add(key_part)
        grad_values = grad_values.at[:, :key_count].add(value_part)
    return (
        jnp.concatenate(query_parts, 1),
        grad_keys.astype(jnp.bfloat16),
        grad_values.astype(jnp.bfloat16),
    )


def masked_squares(values, valid):
    return jnp.sum(valid * jnp.sum(values * values, -1))


def local(
    tokens,
    cotangent,
    segment_ids,
    padding_mask,
    w_qkv,
    bias_qv,
    w_out,
    bias_out,
    gain_attn,
    gain_mlp,
    w_up,
    bias_up,
    w_down,
    bias_down,
):
    gathered = (
        lax.all_gather(w_qkv, ("dp", "fsdp"), axis=0, tiled=True),
        lax.all_gather(bias_qv, ("dp", "fsdp"), axis=0, tiled=True),
        lax.all_gather(w_out, ("dp", "fsdp"), axis=0, tiled=True),
        lax.all_gather(bias_out, ("dp", "fsdp"), axis=0, tiled=True),
        lax.all_gather(gain_attn, ("dp", "fsdp"), axis=0, tiled=True),
        lax.all_gather(gain_mlp, ("dp", "fsdp"), axis=0, tiled=True),
        lax.all_gather(w_up, ("dp", "fsdp"), axis=0, tiled=True),
        lax.all_gather(bias_up, ("dp", "fsdp"), axis=0, tiled=True),
        lax.all_gather(w_down, ("dp", "fsdp"), axis=0, tiled=True),
        lax.all_gather(bias_down, ("dp", "fsdp"), axis=0, tiled=True),
    )
    qkv_w, qv_bias, out_w, out_bias, attn_gain, mlp_gain, up_w, up_bias, down_w, down_bias = (
        gathered
    )
    rows_local, length, width = tokens.shape
    heads = width // HD
    block_rows = min(512, length)
    frame_count = rows_local * length
    frames = tokens.reshape(frame_count, width).astype(jnp.float32)
    attn_scale = attn_gain.astype(jnp.float32)
    mlp_scale = mlp_gain.astype(jnp.float32)
    normed_in = rms_norm(frames, attn_scale).astype(jnp.bfloat16)
    projected = jnp.dot(normed_in, qkv_w, preferred_element_type=jnp.float32)
    qv_float = qv_bias.astype(jnp.float32)
    queries = (
        (projected[:, :width] + qv_float[:width])
        .astype(jnp.bfloat16)
        .reshape(rows_local, length, heads, HD)
    )
    keys_all = (
        projected[:, width : 2 * width].astype(jnp.bfloat16).reshape(rows_local, length, heads, HD)
    )
    values_all = (
        (projected[:, 2 * width :] + qv_float[width:])
        .astype(jnp.bfloat16)
        .reshape(rows_local, length, heads, HD)
    )
    mixed, log_sums = attend_forward(
        queries, keys_all, values_all, segment_ids, padding_mask, block_rows
    )
    mixed_flat = mixed.reshape(frame_count, width)
    attn_branch = jnp.dot(mixed_flat, out_w, preferred_element_type=jnp.float32) + out_bias.astype(
        jnp.float32
    )
    middle = frames + attn_branch
    normed_mid = rms_norm(middle, mlp_scale).astype(jnp.bfloat16)
    pre_act = jnp.dot(normed_mid, up_w, preferred_element_type=jnp.float32) + up_bias.astype(
        jnp.float32
    )
    activated = gelu_tanh(pre_act).astype(jnp.bfloat16)
    mlp_branch = jnp.dot(activated, down_w, preferred_element_type=jnp.float32) + down_bias.astype(
        jnp.float32
    )
    final = middle + mlp_branch
    output = final.astype(jnp.bfloat16).reshape(tokens.shape)
    valid = padding_mask.reshape(frame_count).astype(jnp.float32)
    totals = lax.psum(
        (
            masked_squares(frames, valid),
            masked_squares(middle, valid),
            masked_squares(final, valid),
            masked_squares(attn_branch, valid),
            masked_squares(mlp_branch, valid),
            jnp.sum(valid),
        ),
        ("dp", "fsdp"),
    )
    count_all = totals[5]
    stats = jnp.stack([jnp.sqrt(member / (count_all * width)) for member in totals[:5]])
    real_frames = jnp.reshape(count_all, (1,))
    weights_back = (
        lax.all_gather(w_qkv, ("dp", "fsdp"), axis=0, tiled=True),
        lax.all_gather(bias_qv, ("dp", "fsdp"), axis=0, tiled=True),
        lax.all_gather(w_out, ("dp", "fsdp"), axis=0, tiled=True),
        lax.all_gather(bias_out, ("dp", "fsdp"), axis=0, tiled=True),
        lax.all_gather(gain_attn, ("dp", "fsdp"), axis=0, tiled=True),
        lax.all_gather(gain_mlp, ("dp", "fsdp"), axis=0, tiled=True),
        lax.all_gather(w_up, ("dp", "fsdp"), axis=0, tiled=True),
        lax.all_gather(bias_up, ("dp", "fsdp"), axis=0, tiled=True),
        lax.all_gather(w_down, ("dp", "fsdp"), axis=0, tiled=True),
        lax.all_gather(bias_down, ("dp", "fsdp"), axis=0, tiled=True),
    )
    qkv_w, qv_bias, out_w, out_bias, attn_gain, mlp_gain, up_w, up_bias, down_w, down_bias = (
        weights_back
    )
    grad_out = cotangent.reshape(frame_count, width)
    grad_float = grad_out.astype(jnp.float32)
    grad_down_w = contract_rows(activated, grad_out)
    grad_down_bias = jnp.sum(grad_float, 0)
    grad_act = times_transposed(grad_out, down_w)
    _, gelu_pull = jax.vjp(gelu_tanh, pre_act)
    grad_pre = gelu_pull(grad_act)[0].astype(jnp.bfloat16)
    grad_up_w = contract_rows(normed_mid, grad_pre)
    grad_up_bias = jnp.sum(grad_pre.astype(jnp.float32), 0)
    grad_normed_mid = times_transposed(grad_pre, up_w)
    _, mid_pull = jax.vjp(rms_norm, middle, mlp_scale)
    grad_middle_norm, grad_mlp_gain = mid_pull(grad_normed_mid)
    grad_middle = grad_float + grad_middle_norm
    grad_branch = grad_middle.astype(jnp.bfloat16)
    grad_out_w = contract_rows(mixed_flat, grad_branch)
    grad_out_bias = jnp.sum(grad_branch.astype(jnp.float32), 0)
    grad_mixed = (
        times_transposed(grad_branch, out_w)
        .astype(jnp.bfloat16)
        .reshape(rows_local, length, heads, HD)
    )
    grad_queries, grad_keys, grad_values = attend_backward(
        queries, keys_all, values_all, log_sums, grad_mixed, segment_ids, padding_mask, block_rows
    )
    query_flat = grad_queries.reshape(frame_count, width)
    value_flat = grad_values.reshape(frame_count, width)
    grad_projected = jnp.concatenate(
        [query_flat, grad_keys.reshape(frame_count, width), value_flat], 1
    )
    grad_qkv_w = contract_rows(normed_in, grad_projected)
    grad_qv_bias = jnp.concatenate(
        [jnp.sum(query_flat.astype(jnp.float32), 0), jnp.sum(value_flat.astype(jnp.float32), 0)]
    )
    grad_normed_in = times_transposed(grad_projected, qkv_w)
    _, first_pull = jax.vjp(rms_norm, frames, attn_scale)
    grad_input_norm, grad_attn_gain = first_pull(grad_normed_in)
    input_grad = (grad_middle + grad_input_norm).astype(jnp.bfloat16).reshape(tokens.shape)
    owned = (
        lax.psum_scatter(grad_qkv_w, ("dp", "fsdp"), scatter_dimension=0, tiled=True),
        lax.psum_scatter(grad_qv_bias, ("dp", "fsdp"), scatter_dimension=0, tiled=True),
        lax.psum_scatter(grad_out_w, ("dp", "fsdp"), scatter_dimension=0, tiled=True),
        lax.psum_scatter(grad_out_bias, ("dp", "fsdp"), scatter_dimension=0, tiled=True),
        lax.psum_scatter(grad_attn_gain, ("dp", "fsdp"), scatter_dimension=0, tiled=True),
        lax.psum_scatter(grad_mlp_gain, ("dp", "fsdp"), scatter_dimension=0, tiled=True),
        lax.psum_scatter(grad_up_w, ("dp", "fsdp"), scatter_dimension=0, tiled=True),
        lax.psum_scatter(grad_up_bias, ("dp", "fsdp"), scatter_dimension=0, tiled=True),
        lax.psum_scatter(grad_down_w, ("dp", "fsdp"), scatter_dimension=0, tiled=True),
        lax.psum_scatter(grad_down_bias, ("dp", "fsdp"), scatter_dimension=0, tiled=True),
    )
    return (
        output,
        input_grad,
        owned[0],
        owned[1],
        owned[2],
        owned[3],
        owned[4],
        owned[5],
        owned[6],
        owned[7],
        owned[8],
        owned[9],
        stats,
        real_frames,
    )


def solution(mesh):
    return jax.shard_map(
        local,
        mesh=mesh,
        in_specs=(
            P(("dp", "fsdp"), None, None),
            P(("dp", "fsdp"), None, None),
            P(("dp", "fsdp"), None),
            P(("dp", "fsdp"), None),
            P(("dp", "fsdp"), None),
            P(("dp", "fsdp")),
            P(("dp", "fsdp"), None),
            P(("dp", "fsdp")),
            P(("dp", "fsdp")),
            P(("dp", "fsdp")),
            P(("dp", "fsdp"), None),
            P(("dp", "fsdp")),
            P(("dp", "fsdp"), None),
            P(("dp", "fsdp")),
        ),
        out_specs=(
            P(("dp", "fsdp"), None, None),
            P(("dp", "fsdp"), None, None),
            P(("dp", "fsdp"), None),
            P(("dp", "fsdp")),
            P(("dp", "fsdp"), None),
            P(("dp", "fsdp")),
            P(("dp", "fsdp")),
            P(("dp", "fsdp")),
            P(("dp", "fsdp"), None),
            P(("dp", "fsdp")),
            P(("dp", "fsdp"), None),
            P(("dp", "fsdp")),
            P(),
            P(),
        ),
        check_vma=False,
    )
```

profile of v0, /device:TPU:0, one launch (start us, length us, event | category | flops | bytes accessed | tf_op | source)
XLA Modules:
  0.0 1098.0 jit_solution(8145300168299504931)
XLA Ops:
  14.9 42.5 %all-reduce.14 = (bf16[2048]{0:T(1024)(128)(2,1)S(1)}, bf16[1024]{0:T(1024)(128)(2,1)S(1)}, bf16[1024]{0:T(1024)(128)(2,1)S(1)}, bf16[1024]{0:T(1024)(128)(2,1)S(1)}, bf16[1024]{0:T(1024)(128)(2,1)S(1)}) all-reduce(bf16[2048]{0:T(1024)(128)(2,1)S(1)} %dynamic-update-slice.11, ...), channel_id=1, replica_groups=mesh['dp'=4,'fsdp'=8] {'dp','fsdp'}, use_global_device_ids=true, to_apply=%add.3 | all-reduce | flops 6144 | bytes 24576
  58.1 40.2 %all-gather = bf16[32,1,128]{2,1,0:T(2,128)(2,1)S(1)} all-gather(bf16[1,1,128]{2,1,0:T(2,128)(2,1)} %bitcast.177), channel_id=1, replica_groups=mesh['dp'=4,'fsdp'=8] {'dp','fsdp'}, dimensions={0}, use_global_device_ids=true | all-gather | bytes 8448 | tf_op jit(solution)/shard_map/all_gather | solution.py:165
  98.3 2.9 copy.65
  101.2 4.6 copy.72
  107.8 9.2 fusion.46
  117.1 4.6 copy-done.11
  123.3 2.9 copy.68
  126.1 7.6 fusion.18
  133.7 3.9 copy.67
  137.7 3.9 copy.66
  141.6 8.6 fusion.8
  150.3 9.4 exponential_reduce_fusion.1
  159.7 15.8 %fusion = (f32[16,512]{1,0:T(8,128)S(1)}, f32[16,512,1024]{2,1,0:T(8,128)}) fusion(pred[512,1024]{1,0:T(8,128)(4,1)S(1)} %fusion.32, bf16[1024,16,64]{0,2,1:T(8,128)(2,1)} %bitcast.150, bf16[1,1024,16,64]{1,3,2,0:T(8,128)(2,1)} %bitcast.154), kind=kOutput, calls=%fused_computation.5 | convolution fusion | flops 1098899456 | bytes 37257216 | tf_op jit(solution)/shard_map/rqhd,rkhd->rhqk/dot_general | solution.py:49
  175.6 15.9 %exponential_reduce_fusion = f32[16,512]{1,0:T(8,128)S(1)} fusion(f32[16,512,1024]{2,1,0:T(8,128)} %get-tuple-element.165, f32[16,512]{1,0:T(8,128)S(1)} %get-tuple-element.164, pred[512,1024]{1,0:T(8,128)(4,1)S(1)} %fusion.32), kind=kLoop, calls=%fused_computation.3 | loop fusion | flops 33546240 | bytes 34144256 | tf_op jit(solution)/shard_map/reduce_sum | solution.py:70
  191.6 4.8 fusion.35
  196.4 16.5 %fusion.37 = bf16[1,512,16,64]{1,3,2,0:T(8,128)(2,1)} fusion(bf16[1024,16,64]{0,2,1:T(8,128)(2,1)} %bitcast.157, f32[16,512,1024]{2,1,0:T(8,128)} %get-tuple-element.165, f32[16,512]{1,0:T(8,128)S(1)} %log_add_fusion, pred[512,1024]{1,0:T(8,128)(4,1)S(1)} %fusion.32), kind=kOutput, calls=%fused_computation.89 | convolution fusion | flops 1107820544 | bytes 37257216 | tf_op jit(solution)/shard_map/rhqk,rkhd->rqhd/dot_general | solution.py:73
  212.9 3.3 pad_maximum_fusion.3
  216.2 8.0 multiply_reduce_fusion.7
  224.2 22.0 %multiply_convert_fusion.2 = (bf16[1024,4096]{1,0:T(8,128)(2,1)}, f32[1024,4096]{1,0:T(8,128)}) fusion(f32[4096]{0:T(1024)S(1)} %bitcast.174, bf16[1024,4096]{1,0:T(8,128)(2,1)} %all-gather.10.cloned.1.call-done, f32[1024,1024]{0,1:T(8,128)} %get-tuple-element.153, f32[1024]{0:T(1024)S(1)} %convert_element_type.160, f32[1024]{0:T(1024)S(1)} %fusion.53), kind=kOutput, calls=%fused_computation.20 | convolution fusion | flops 8635023360 | bytes 37773312 | tf_op jit(solution)/shard_map/dot_general | solution.py:204
  246.2 53.4 %all-gather.12.cloned.1.call-done = bf16[4096,1024]{1,0:T(8,128)(2,1)} async-done(((bf16[128,1024]{1,0:T(8,128)(2,1)}), bf16[4096,1024]{1,0:T(8,128)(2,1)}) %all-gather.12.cloned.1.call-update) | async-done | bytes 8388624 | tf_op jit(solution)/shard_map/all_gather | solution.py:166
  299.6 27.5 %convert_reduce_fusion = (f32[4096]{0:T(1024)}, bf16[1024,4096]{1,0:T(8,128)(2,1)}) fusion(bf16[4096,1024]{1,0:T(8,128)(2,1)} %all-gather.12.cloned.1.call-done, bf16[1,1024,1024]{2,1,0:T(8,128)(2,1)S(1)} %copy-done.15, f32[1024,4096]{1,0:T(8,128)} %get-tuple-element.169, f32[4096]{0:T(1024)S(1)} %bitcast.175), kind=kOutput, calls=%fused_computation.17 | convolution fusion | flops 8703176704 | bytes 35684352 | tf_op jit(solution)/shard_map/dot_general | solution.py:28
  327.1 12.8 %fusion.71 = f32[1024,1024]{0,1:T(8,128)} fusion(bf16[1024,4096]{1,0:T(8,128)(2,1)} %get-tuple-element.178, bf16[1024,4096]{1,0:T(8,128)(2,1)S(1)} %copy-done.36), kind=kOutput, calls=%fused_computation.141 | convolution fusion | flops 8589934592 | bytes 20971520 | tf_op jit(solution)/shard_map/dot_general | solution.py:28
  339.9 18.8 %multiply_reduce_fusion.2 = (f32[1024]{0:T(1024)}, f32[1024]{0:T(1024)}, f32[1024]{0:T(1024)S(1)}, f32[1024]{0:T(1024)}, bf16[1,1024,1024]{1,2,0:T(8,128)(2,1)}) fusion(f32[1024]{0:T(1024)S(1)} %copy-done.34, f32[1024,1024]{0,1:T(8,128)} %get-tuple-element.153, f32[1024,1024]{0,1:T(8,128)} %fusion.71, f32[1024]{0:T(1024)S(1)} %convert_element_type.160, ...), kind=kOutput, calls=%fused_computation.53 | convolution fusion | flops 8603561984 | bytes 27291648 | tf_op jit(solution)/shard_map/dot_general | solution.py:208
  358.7 5.7 convert_reduce_fusion.2
  366.4 4.4 fusion.56
  370.8 4.7 convolution_convert_fusion
  375.5 12.9 %multiply_reduce_fusion.1 = (f32[16,512]{1,0:T(8,128)S(1)}, f32[16,512,512]{1,2,0:T(8,128)}) fusion(f32[16,512,512]{1,2,0:T(8,128)} %get-tuple-element.167, f32[16,512]{1,0:T(8,128)S(1)} %log_add_fusion.1, pred[512,512]{0,1:T(8,128)(4,1)S(1)} %fusion.39, bf16[1,1024,16,64]{1,3,2,0:T(8,128)(2,1)S(1)} %bitcast.159, bf16[1,1024,16,64]{1,3,2,0:T(8,128)(2,1)S(1)} %bitcast.163), kind=kOutput, calls=%fused_computation.19 | convolution fusion | flops 557834240 | bytes 35979264 | tf_op jit(solution)/shard_map/rqhd,rkhd->rhqk/dot_general | solution.py:98
  388.4 25.5 %multiply_reduce_fusion = (f32[16,512]{1,0:T(8,128)S(1)}, f32[16,512,1024]{2,1,0:T(8,128)}) fusion(f32[16,512,1024]{2,1,0:T(8,128)} %get-tuple-element.165, f32[16,512]{1,0:T(8,128)S(1)} %log_add_fusion, pred[512,1024]{1,0:T(8,128)(4,1)S(1)} %fusion.32, bf16[1024,16,64]{0,2,1:T(8,128)(2,1)S(1)} %bitcast.160, bf16[1,1024,16,64]{1,3,2,0:T(8,128)(2,1)S(1)} %bitcast.164), kind=kOutput, calls=%fused_computation.1 | convolution fusion | flops 1115676672 | bytes 70844416 | tf_op jit(solution)/shard_map/rqhd,rkhd->rhqk/dot_general | solution.py:98
  413.9 16.0 %multiply_convert_fusion.1 = bf16[16,512,512]{1,2,0:T(8,128)(2,1)} fusion(f32[16,512,512]{1,2,0:T(8,128)} %get-tuple-element.171, f32[16,512,512]{1,2,0:T(8,128)} %get-tuple-element.167, f32[16,512]{1,0:T(8,128)S(1)} %get-tuple-element.170, f32[16,512]{1,0:T(8,128)S(1)} %log_add_fusion.1, pred[512,512]{0,1:T(8,128)(4,1)S(1)} %fusion.39), kind=kLoop, calls=%fused_computation.18 | loop fusion | flops 25165824 | bytes 42270720 | tf_op jit(solution)/shard_map/convert_element_type | solution.py:105
  430.0 28.3 %multiply_convert_fusion = bf16[16,512,1024]{2,1,0:T(8,128)(2,1)} fusion(f32[16,512,1024]{2,1,0:T(8,128)} %get-tuple-element.173, f32[16,512,1024]{2,1,0:T(8,128)} %get-tuple-element.165, f32[16,512]{1,0:T(8,128)S(1)} %get-tuple-element.172, f32[16,512]{1,0:T(8,128)S(1)} %log_add_fusion, pred[512,1024]{1,0:T(8,128)(4,1)S(1)} %fusion.32), kind=kLoop, calls=%fused_computation | loop fusion | flops 50331648 | bytes 84475904 | tf_op jit(solution)/shard_map/convert_element_type | solution.py:105
  458.3 5.9 fusion.34
  464.1 12.0 %fusion.36 = bf16[1,512,16,64]{1,3,2,0:T(8,128)(2,1)} fusion(bf16[1024,16,64]{0,2,1:T(8,128)(2,1)S(1)} %bitcast.152, bf16[16,512,1024]{2,1,0:T(8,128)(2,1)} %multiply_convert_fusion), kind=kOutput, calls=%fused_computation.88 | convolution fusion | flops 1074790400 | bytes 19922944 | tf_op jit(solution)/shard_map/rhqk,rkhd->rqhd/dot_general | solution.py:107
  476.1 3.3 pad_maximum_fusion.4
  479.5 6.1 multiply_bitcast_fusion
  485.5 10.5 fusion.21
  496.0 9.5 convolution_bitcast_fusion
  505.5 17.0 %convert_reduce_fusion.3 = (f32[16,64]{1,0:T(8,128)S(1)}, bf16[1,1024,16,64]{1,3,2,0:T(8,128)(2,1)}) fusion(f32[16,512,1024]{2,1,0:T(8,128)} %get-tuple-element.165, f32[16,512]{1,0:T(8,128)S(1)} %log_add_fusion, pred[512,1024]{1,0:T(8,128)(4,1)S(1)} %fusion.32, bf16[1,1024,16,64]{1,3,2,0:T(8,128)(2,1)} %bitcast.165, ...), kind=kOutput, calls=%fused_computation.58 | convolution fusion | flops 1111489536 | bytes 39358464 | tf_op jit(solution)/shard_map/rhqk,rqhd->rkhd/dot_general | solution.py:122
  522.5 14.1 %fusion.22 = f32[1024,3072]{1,0:T(8,128)} fusion(bf16[1024,1024]{0,1:T(8,128)(2,1)} %bitcast.178, bf16[1024,1024]{0,1:T(8,128)(2,1)} %bitcast.161, bf16[1024,1024]{0,1:T(8,128)(2,1)} %bitcast.167, bf16[1,1024,1024]{1,2,0:T(8,128)(2,1)S(1)} %copy-done.7, f32[1024]{0:T(1024)S(1)} %copy-done.24, f32[1024]{0:T(1024)S(1)} %copy-done.26), kind=kOutput, calls=%fused_computation.64 | convolution fusion | flops 6465519616 | bytes 20979712 | tf_op jit(solution)/shard_map/dot_general | solution.py:22
  536.6 15.9 %fusion.67 = f32[1024,4096]{1,0:T(8,128)} fusion(bf16[1024,4096]{1,0:T(8,128)(2,1)} %get-tuple-element.178, f32[1024,1024]{0,1:T(8,128)} %get-tuple-element.153, f32[1024]{0:T(1024)S(1)} %convert_element_type.160, f32[1024]{0:T(1024)S(1)} %fusion.53), kind=kOutput, calls=%fused_computation.137 | convolution fusion | flops 8593080320 | bytes 29368320 | tf_op jit(solution)/shard_map/dot_general | solution.py:22
  552.6 16.6 %fusion.25 = f32[4096,1024]{1,0:T(8,128)} fusion(bf16[1024,4096]{1,0:T(8,128)(2,1)} %get-tuple-element.168, bf16[1,1024,1024]{2,1,0:T(8,128)(2,1)} %param.27), kind=kOutput, calls=%fused_computation.69 | convolution fusion | flops 8589934592 | bytes 27262976 | tf_op jit(solution)/shard_map/dot_general | solution.py:22
  570.5 4.0 copy.80
  576.3 11.9 %fusion.13 = (f32[1024]{0:T(1024)S(1)}, f32[1024]{0:T(1024)S(1)}, f32[1024,1024]{0,1:T(8,128)S(1)}) fusion(bf16[1,1024,1024]{1,2,0:T(8,128)(2,1)S(1)} %copy-done.7, f32[1024]{0:T(1024)S(1)} %copy-done.26, f32[1024]{0:T(1024)S(1)} %copy-done.24, bf16[1024,3072]{1,0:T(8,128)(2,1)} %all-gather.6.cloned.1.call-done, bf16[1024,1024]{0,1:T(8,128)(2,1)} %bitcast.179, ...), kind=kOutput, calls=%fused_computation.39 | convolution fusion | flops 6468663296 | bytes 18890752 | tf_op jit(solution)/shard_map/dot_general | solution.py:28
  588.9 2.4 fusion.24
  591.3 4.1 copy.81
  595.4 41.6 %all-reduce.13 = (f32[2048]{0:T(1024)S(1)}, f32[1024]{0:T(1024)S(1)}, f32[1024]{0:T(1024)S(1)}, f32[1024]{0:T(1024)S(1)}, f32[4096]{0:T(1024)S(1)}, /*index=5*/f...) all-reduce(f32[2048]{0:T(1024)S(1)} %pad_maximum_fusion.5, ...), channel_id=3, replica_groups=mesh['dp'=4,'fsdp'=8] {'dp','fsdp'}, use_global_device_ids=true, to_apply=%region_13.14.clone | all-reduce | flops 10246 | bytes 81968
  645.3 69.4 %reduce-scatter.5.cloned.1.call-done = f32[32,3072]{1,0:T(8,128)} async-done(((f32[1024,3072]{1,0:T(8,128)}), f32[32,3072]{1,0:T(8,128)}) %reduce-scatter.5.cloned.1.call-update) | async-done | bytes 393232 | tf_op jit(solution)/shard_map/reduce_scatter | solution.py:281
  714.6 188.7 %reduce-scatter.9.cloned.1.call-done = f32[32,4096]{1,0:T(8,128)} async-done(((f32[1024,4096]{1,0:T(8,128)}), f32[32,4096]{1,0:T(8,128)}) %reduce-scatter.9.cloned.1.call-update) | async-done | bytes 524304 | tf_op jit(solution)/shard_map/reduce_scatter | solution.py:287
  903.4 187.3 %reduce-scatter.11.cloned.1.call-done = f32[128,1024]{1,0:T(8,128)} async-done(((f32[4096,1024]{1,0:T(8,128)}), f32[128,1024]{1,0:T(8,128)}) %reduce-scatter.11.cloned.1.call-update) | async-done | bytes 524304 | tf_op jit(solution)/shard_map/reduce_scatter | solution.py:289
  (147 shorter events, 22.1 us)
Async XLA Ops:
  7.2 100.6 %all-gather.6.cloned.1.call-start = ((), (), s32[]{:S(2)}) async-start(), calls=%async_computation.4 | async-start | bytes 6488064 | tf_op jit(solution)/shard_map/all_gather | solution.py:158
  7.9 208.2 %all-gather.8.cloned.1.call-start = ((), (), s32[]{:S(2)}) async-start(), calls=%async_computation.5 | async-start | bytes 2162688 | tf_op jit(solution)/shard_map/all_gather | solution.py:160
  8.7 215.5 %all-gather.10.cloned.1.call-start = ((), (), s32[]{:S(2)}) async-start(), calls=%async_computation.6 | async-start | bytes 8650752 | tf_op jit(solution)/shard_map/all_gather | solution.py:164
  9.4 290.2 %all-gather.12.cloned.1.call-start = ((), (), s32[]{:S(2)}) async-start(), calls=%async_computation.7 | async-start | bytes 8650752 | tf_op jit(solution)/shard_map/all_gather | solution.py:166
  10.0 635.3 %reduce-scatter.7.cloned.1.call-start = ((), (), s32[]{:S(2)}) async-start(), calls=%async_computation.9 | async-start | bytes 4325376 | tf_op jit(solution)/shard_map/reduce_scatter | solution.py:283
  57.5 50.3 %copy-start.23 = (f32[1024]{0:T(1024)}, f32[1024]{0:T(1024)S(1)}, u32[]{:S(2)}) copy-start(f32[1024]{0:T(1024)S(1)} %convert_element_type.146) | copy-start | bytes 12292
  98.3 7.5 copy-start.17
  98.3 7.5 copy-start.27
  101.2 15.8 %copy-start.5 = (bf16[1,1024,1024]{1,2,0:T(8,128)(2,1)}, bf16[1,1024,1024]{1,2,0:T(8,128)(2,1)S(1)}, u32[]{:S(2)}) copy-start(bf16[1,1024,1024]{1,2,0:T(8,128)(2,1)S(1)} %copy.65) | copy-start | bytes 6291460
  106.4 10.7 copy-start.25
  117.1 4.6 copy-start.11
  126.1 15.5 %copy-start = (bf16[1024,1024]{0,1:T(8,128)(2,1)}, bf16[1024,1024]{0,1:T(8,128)(2,1)S(1)}, u32[]{:S(2)}) copy-start(bf16[1024,1024]{0,1:T(8,128)(2,1)S(1)} %copy.68) | copy-start | bytes 6291460
  159.7 31.8 %slice-start = ((s8[16777216]{0:T(1024)(128)(4,1)}), s8[4194304]{0:T(1024)(128)(4,1)S(1)}, s32[]{:S(2)}) async-start(s8[16777216]{0:T(1024)(128)(4,1)} %bitcast.147), calls=%async_computation.12 | async-start | bytes 8388608
  159.7 31.8 %slice-start.1 = ((s8[16777216]{0:T(1024)(128)(4,1)}), s8[4194304]{0:T(1024)(128)(4,1)S(1)}, s32[]{:S(2)}) async-start(s8[16777216]{0:T(1024)(128)(4,1)} %bitcast.147), calls=%async_computation.13 | async-start | bytes 8388608
  159.7 31.8 %slice-start.2 = ((s8[16777216]{0:T(1024)(128)(4,1)}), s8[4194304]{0:T(1024)(128)(4,1)S(1)}, s32[]{:S(2)}) async-start(s8[16777216]{0:T(1024)(128)(4,1)} %bitcast.147), calls=%async_computation.14 | async-start | bytes 8388608
  175.6 15.9 %slice-start.3 = ((s8[16777216]{0:T(1024)(128)(4,1)}), s8[4194304]{0:T(1024)(128)(4,1)S(1)}, s32[]{:S(2)}) async-start(s8[16777216]{0:T(1024)(128)(4,1)} %bitcast.147), calls=%async_computation.15 | async-start | bytes 8388608
  175.6 16.0 %copy-start.3 = (bf16[1024,1024]{0,1:T(8,128)(2,1)S(1)}, bf16[1024,1024]{0,1:T(8,128)(2,1)}, u32[]{:S(2)}) copy-start(bf16[1024,1024]{0,1:T(8,128)(2,1)} %copy.66) | copy-start | bytes 6291460
  212.9 3.3 copy-start.6
  224.2 134.5 %copy-start.21 = (f32[1024]{0:T(1024)}, f32[1024]{0:T(1024)S(1)}, u32[]{:S(2)}) copy-start(f32[1024]{0:T(1024)S(1)} %get-tuple-element.152) | copy-start | bytes 12292
  224.2 75.4 %copy-start.15 = (bf16[1,1024,1024]{2,1,0:T(8,128)(2,1)S(1)}, bf16[1,1024,1024]{2,1,0:T(8,128)(2,1)}, u32[]{:S(2)}) copy-start(bf16[1,1024,1024]{2,1,0:T(8,128)(2,1)} %param.27) | copy-start | bytes 6291460
  299.6 27.5 %copy-start.36 = (bf16[1024,4096]{1,0:T(8,128)(2,1)S(1)}, bf16[1024,4096]{1,0:T(8,128)(2,1)}, u32[]{:S(2)}) copy-start(bf16[1024,4096]{1,0:T(8,128)(2,1)} %all-gather.10.cloned.1.call-done) | copy-start | bytes 25165828
  327.1 12.8 %copy-start.34 = (f32[1024]{0:T(1024)S(1)}, f32[1024]{0:T(1024)}, u32[]{:S(2)}) copy-start(f32[1024]{0:T(1024)} %convert_element_type.164) | copy-start | bytes 12292
  339.9 18.8 %copy-start.12 = (bf16[1,1024,1024]{1,2,0:T(8,128)(2,1)S(1)}, bf16[1,1024,1024]{1,2,0:T(8,128)(2,1)}, u32[]{:S(2)}) copy-start(bf16[1,1024,1024]{1,2,0:T(8,128)(2,1)} %copy.72) | copy-start | bytes 6291460
  358.7 7.8 copy-start.16
  364.4 2.0 copy-start.8
  366.4 4.4 copy-start.37
  370.8 4.7 copy-start.4
  375.5 12.9 %copy-start.13 = (bf16[1024,1024]{0,1:T(8,128)(2,1)}, bf16[1024,1024]{0,1:T(8,128)(2,1)S(1)}, u32[]{:S(2)}) copy-start(bf16[1024,1024]{0,1:T(8,128)(2,1)S(1)} %convolution_convert_fusion) | copy-start | bytes 6291460
  413.9 300.8 %reduce-scatter.5.cloned.1.call-start = ((), (), s32[]{:S(2)}) async-start(), calls=%async_computation.8 | async-start | bytes 12976128 | tf_op jit(solution)/shard_map/reduce_scatter | solution.py:281
  430.0 28.3 %copy-start.1 = (bf16[1024,1024]{0,1:T(8,128)(2,1)S(1)}, bf16[1024,1024]{0,1:T(8,128)(2,1)}, u32[]{:S(2)}) copy-start(bf16[1024,1024]{0,1:T(8,128)(2,1)} %copy-done) | copy-start | bytes 6291460
  476.1 3.3 copy-start.2
  485.5 10.5 copy-start.14
  505.5 17.0 %copy-start.7 = (bf16[1,1024,1024]{1,2,0:T(8,128)(2,1)S(1)}, bf16[1,1024,1024]{1,2,0:T(8,128)(2,1)}, u32[]{:S(2)}) copy-start(bf16[1,1024,1024]{1,2,0:T(8,128)(2,1)} %copy-done.5) | copy-start | bytes 6291460
  505.5 17.0 %copy-start.24 = (f32[1024]{0:T(1024)S(1)}, f32[1024]{0:T(1024)}, u32[]{:S(2)}) copy-start(f32[1024]{0:T(1024)} %copy-done.23) | copy-start | bytes 12292
  505.5 17.0 %copy-start.26 = (f32[1024]{0:T(1024)S(1)}, f32[1024]{0:T(1024)}, u32[]{:S(2)}) copy-start(f32[1024]{0:T(1024)} %copy-done.25) | copy-start | bytes 12292
  536.6 366.8 %reduce-scatter.9.cloned.1.call-start = ((), (), s32[]{:S(2)}) async-start(), calls=%async_computation.10 | async-start | bytes 17301504 | tf_op jit(solution)/shard_map/reduce_scatter | solution.py:287
  552.5 538.2 %reduce-scatter.11.cloned.1.call-start = ((), (), s32[]{:S(2)}) async-start(), calls=%async_computation.11 | async-start | bytes 17301504 | tf_op jit(solution)/shard_map/reduce_scatter | solution.py:289
  569.1 5.4 copy-start.10
  576.2 11.9 %copy-start.20 = (f32[1024]{0:T(1024)S(1)}, f32[1024]{0:T(1024)}, u32[]{:S(2)}) copy-start(f32[1024]{0:T(1024)} %copy-done.19) | copy-start | bytes 12292
  576.2 11.9 %copy-start.22 = (f32[1024]{0:T(1024)S(1)}, f32[1024]{0:T(1024)}, u32[]{:S(2)}) copy-start(f32[1024]{0:T(1024)} %copy-done.21) | copy-start | bytes 12292
  576.2 12.0 %copy-start.31 = (f32[1024]{0:T(1024)S(1)}, f32[1024]{0:T(1024)}, u32[]{:S(2)}) copy-start(f32[1024]{0:T(1024)} %get-tuple-element.157) | copy-start | bytes 12292
  576.3 12.0 %copy-start.32 = (f32[1024]{0:T(1024)S(1)}, f32[1024]{0:T(1024)}, u32[]{:S(2)}) copy-start(f32[1024]{0:T(1024)} %get-tuple-element.124) | copy-start | bytes 12292
  576.3 12.0 %copy-start.33 = (f32[1024]{0:T(1024)S(1)}, f32[1024]{0:T(1024)}, u32[]{:S(2)}) copy-start(f32[1024]{0:T(1024)} %get-tuple-element.125) | copy-start | bytes 12292
  576.3 12.6 %copy-start.9 = (f32[1024,1024]{0,1:T(8,128)S(1)}, f32[1024,1024]{0,1:T(8,128)}, u32[]{:S(2)}) copy-start(f32[1024,1024]{0,1:T(8,128)} %copy-done.8) | copy-start | bytes 12582916
  591.3 4.1 copy-start.28
  591.3 4.1 copy-start.29
  591.3 4.1 copy-start.30
  591.3 4.1 copy-start.35
  (2 other events, 1.3 us)
Sparse Core Ops, SparseCore 0:
  11.0 72.4 all-gather.5
  86.5 54.9 all-gather.7
  144.6 76.1 all-gather.9
  223.5 76.0 all-gather.11
  414.0 141.4 reduce-scatter.6
  562.0 152.6 reduce-scatter.4
  717.6 185.6 reduce-scatter.8
  906.3 184.3 reduce-scatter.10
where the time goes:
time: 1110 us; the launch traced here: 1100 us
  waiting for transfers between devices  502 us (45%)
  matrix products  311 us (28%)
  blocking collectives  124 us (11%)
  other arithmetic  97.8 us (9%)
  local copies, waits for them, and re-layouts  44.1 us (4%)
  between operations  19.2 us (2%)
    reduce_scatter x1, waiting for transfers between devices, local(): lax.psum_scatter(grad_up_w, ('dp', 'fsdp'), scatter_dimension=0, tiled=True)  189 us
    reduce_scatter x1, waiting for transfers between devices, local(): lax.psum_scatter(grad_down_w, ('dp', 'fsdp'), scatter_dimension=0, tiled=...  187 us
    unnamed x2, blocking collectives  84.2 us
    reduce_scatter x1, waiting for transfers between devices, local(): lax.psum_scatter(grad_qkv_w, ('dp', 'fsdp'), scatter_dimension=0, tiled=T...  69.4 us
    dot_general x4, matrix products, times_transposed(): lax.dot_general(left, weight, (((1,), (1,)), ((), ())), preferred_element...  56.8 us
    all_gather x1, waiting for transfers between devices, local(): lax.all_gather(w_down, ('dp', 'fsdp'), axis=0, tiled=True)  53.4 us
    dot_general x4, matrix products, contract_rows(): lax.dot_general(left, right, (((0,), (0,)), ((), ())), preferred_element_...  50.8 us
    convert_element_type x2, other arithmetic, attend_backward(): grad_scores = (probs * (grad_probs - inner)).astype(jnp.bfloat16)  44.3 us
  transfers between devices with their start and end apart: 8, of which 4 were waited for; matrix products, arithmetic and copies ran while one was open for 30% of the time, Pallas kernels for 0%

commit v1 on v0

v1 whole, which is shorter than its diff:
```python
import functools

import jax
import jax.numpy as jnp
import numpy as np
from jax import lax
from jax.experimental import pallas as pl
from jax.experimental.pallas import tpu as pltpu
from jax.sharding import PartitionSpec as P

AXES = ("dp", "fsdp")
HD = 64
QB = 128
SPAN = 512
F32 = jnp.float32
BF16 = jnp.bfloat16

CORE = 1


def ladder_hops(mesh):
    if dict(mesh.shape) != {"dp": 4, "fsdp": 8}:
        return None
    return ((4, 2, 8, 16), (4, 2, 16, 8))


def slot_keys(hops):
    def own(bits):
        keys = [0]
        for bit in bits:
            keys = keys + [key ^ bit for key in keys]
        return keys

    first, second = own(hops[0]), own(hops[1])
    return np.array(
        [first + [key ^ CORE for key in second], second + [key ^ CORE for key in first]], np.int32
    )


def hop(value, bits, count):
    pairs = [(device, device ^ bits[device & CORE]) for device in range(count)]
    return lax.ppermute(value, AXES, pairs)


class Ladder:
    def __init__(self, mesh):
        self.hops = ladder_hops(mesh)
        self.count = int(np.prod(list(mesh.shape.values())))
        self.native = self.hops is None
        if not self.native:
            self.keys = slot_keys(self.hops)
            self.places = np.argsort(self.keys, 1).astype(np.int32)

    def tables(self):
        every = jnp.arange(self.count, dtype=jnp.int32)
        if self.native:
            return every, every
        me = lax.axis_index(AXES)
        odd = (me & CORE) == 1
        shard_of = me ^ jnp.where(odd, self.keys[1], self.keys[0])
        place = jnp.where(odd, self.places[1], self.places[0])
        return shard_of, place[every ^ me]

    def step(self, value, level):
        return hop(value, [self.hops[0][level], self.hops[1][level]], self.count)

    def across(self, value):
        return hop(value, [CORE, CORE], self.count)

    def gather(self, shard):
        if self.native:
            return [lax.all_gather(shard, AXES, axis=0, tiled=False)]
        held = shard[None]
        for level in range(3):
            held = jnp.concatenate([held, self.step(held, level)], 0)
        far = self.step(held, 3)
        return [held, far, self.across(held), self.across(far)]

    def scatter(self, keep, send, wire):
        parts = [keep, self.across(send)]
        for level in (3, 2, 1, 0):
            half = parts[0].shape[0] // 2
            total = sum(part[half:].astype(F32) for part in parts).astype(wire)
            parts = [part[:half] for part in parts] + [self.step(total, level)]
        return sum(part.astype(F32) for part in parts)[0]

    def reduce_blocks(self, blocks, shard_of, wire):
        if self.native:
            flat = blocks.reshape((blocks.shape[0] * blocks.shape[1],) + blocks.shape[2:])
            return lax.psum_scatter(flat.astype(F32), AXES, scatter_dimension=0, tiled=True)
        half = self.count // 2
        ordered = jnp.take(blocks.astype(wire), shard_of, axis=0)
        return self.scatter(ordered[:half], ordered[half:], wire)

def nt(a, b):
    return lax.dot_general(a, b, (((1,), (1,)), ((), ())), preferred_element_type=F32)


def nn(a, b):
    return lax.dot_general(a, b, (((1,), (0,)), ((), ())), preferred_element_type=F32)


def fill_bias(lo_ref, segc_ref, padc_ref, segr_ref, bias_ref, nblocks, most):
    def one(qb, _):
        lo = lo_ref[qb]
        q0 = pl.multiple_of(qb * QB, QB)
        segq = segr_ref[pl.ds(qb, 1), :]
        qpos = q0 + lax.broadcasted_iota(jnp.int32, (QB, QB), 1)

        def part(j, _):
            k0 = pl.multiple_of((lo + j) * QB, QB)
            kpos = k0 + lax.broadcasted_iota(jnp.int32, (QB, QB), 0)
            segk = segc_ref[pl.ds(k0, QB), :]
            padk = padc_ref[pl.ds(k0, QB), :]
            ok = (segk == segq) & (kpos <= qpos) & ((padk == 1) | (kpos == qpos))
            bias_ref[qb, pl.ds(pl.multiple_of(j * QB, QB), QB), :] = jnp.where(ok, 0.0, -1e30)
            return 0

        lax.fori_loop(0, qb - lo + 1, part, 0)
        return 0

    lax.fori_loop(0, nblocks, one, 0)


def head_pair(x, scale):
    lane = lax.broadcasted_iota(jnp.int32, x.shape, 1)
    first = jnp.where(lane < HD, scale, 0.0).astype(x.dtype)
    second = jnp.where(lane < HD, 0.0, scale).astype(x.dtype)
    return jnp.concatenate([x * first, x * second], 0)


def attn_fwd_kernel(nblocks, most, lo_ref, segc_ref, padc_ref, segr_ref, q_ref, k_ref, v_ref, o_ref, lse_ref, bias_ref, vt_ref):
    @pl.when(pl.program_id(0) == 0)
    def _():
        fill_bias(lo_ref, segc_ref, padc_ref, segr_ref, bias_ref, nblocks, most)

    vt_ref[...] = v_ref[...].astype(F32).T.astype(BF16)

    def block(qb, _):
        lo = lo_ref[qb]
        q0 = pl.multiple_of(qb * QB, QB)
        q2 = head_pair(q_ref[pl.ds(q0, QB), :], HD ** -0.5)
        k0 = pl.multiple_of(lo * QB, QB)
        for n in range(1, most + 1):
            @pl.when(qb - lo + 1 == n)
            def _(n=n):
                w = n * QB
                s = nt(k_ref[pl.ds(k0, w), :], q2)
                bias = bias_ref[qb, 0:w, :]
                s = s + jnp.concatenate([bias, bias], 1)
                m = jnp.max(s, 0, keepdims=True)
                p = jnp.exp(s - m)
                total = jnp.sum(p, 0, keepdims=True)
                p = p * (1.0 / total)
                o = nn(vt_ref[:, pl.ds(k0, w)], p.astype(BF16))
                o = jnp.concatenate([o[:HD, :QB], o[HD:, QB:]], 0)
                o_ref[pl.ds(q0, QB), :] = o.T.astype(BF16)
                lse_ref[pl.ds(qb, 1), :] = m + jnp.log(total)
        return 0

    lax.fori_loop(0, nblocks, block, 0)


def attn_bwd_kernel(nblocks, most, lo_ref, segc_ref, padc_ref, segr_ref, q_ref, k_ref, v_ref, do_ref, lse_ref,
                    dq_ref, dk_ref, dv_ref, sums_ref, bias_ref, kt_ref, dk_acc, dv_acc):
    @pl.when(pl.program_id(0) == 0)
    def _():
        fill_bias(lo_ref, segc_ref, padc_ref, segr_ref, bias_ref, nblocks, most)

    kt_ref[...] = k_ref[...].astype(F32).T.astype(BF16)
    dk_acc[...] = jnp.zeros_like(dk_acc)
    dv_acc[...] = jnp.zeros_like(dv_acc)
    sums_ref[...] = jnp.zeros_like(sums_ref)

    def block(qb, _):
        lo = lo_ref[qb]
        q0 = pl.multiple_of(qb * QB, QB)
        q2 = head_pair(q_ref[pl.ds(q0, QB), :], HD ** -0.5)
        do2 = head_pair(do_ref[pl.ds(q0, QB), :], 1.0)
        k0 = pl.multiple_of(lo * QB, QB)
        lse = lse_ref[pl.ds(qb, 1), :]
        for n in range(1, most + 1):
            @pl.when(qb - lo + 1 == n)
            def _(n=n):
                w = n * QB
                s = nt(k_ref[pl.ds(k0, w), :], q2)
                bias = bias_ref[qb, 0:w, :]
                p = jnp.exp(s + jnp.concatenate([bias, bias], 1) - lse)
                dp = nt(v_ref[pl.ds(k0, w), :], do2)
                inner = jnp.sum(p * dp, 0, keepdims=True)
                ds = (p * (dp - inner)).astype(BF16)
                dv_acc[pl.ds(k0, w), :] += nn(p.astype(BF16), do2)
                dk_acc[pl.ds(k0, w), :] += nn(ds, q2)
                dq = nn(kt_ref[:, pl.ds(k0, w)], ds)
                dq = jnp.concatenate([dq[:HD, :QB], dq[HD:, QB:]], 0) * (HD ** -0.5)
                dq = dq.T.astype(BF16)
                dq_ref[pl.ds(q0, QB), :] = dq
                sums_ref[0:1, :] += jnp.sum(dq.astype(F32), 0, keepdims=True)
        return 0

    lax.fori_loop(0, nblocks, block, 0)
    dk_ref[...] = dk_acc[...].astype(BF16)
    dv = dv_acc[...].astype(BF16)
    dv_ref[...] = dv
    sums_ref[1:2, :] = jnp.sum(dv.astype(F32), 0, keepdims=True)


def mask_inputs(segment_ids, padding_mask):
    length = segment_ids.shape[0]
    nblocks = length // QB
    first = segment_ids.reshape(nblocks, QB)[:, 0]
    start = jnp.sum((segment_ids[None, :] < first[:, None]).astype(jnp.int32), 1)
    lo = start // QB
    segc = jnp.broadcast_to(segment_ids[:, None], (length, QB))
    padc = jnp.broadcast_to(padding_mask[:, None], (length, QB))
    return lo.astype(jnp.int32), segc, padc, segment_ids.reshape(nblocks, QB)


def attn_forward(q, k, v, masks, first=0, pairs=None):
    length, width = q[0].shape[0], 128
    nblocks = length // QB
    most = min(nblocks, SPAN // QB + 1)
    pairs = pairs or 8
    lo, segc, padc, segr = masks
    (qa, qo), (ka, ko), (va, vo) = q, k, v
    whole = lambda p, lo: (0, 0)
    col = lambda off: pl.BlockSpec((length, width), lambda p, lo: (0, off + first + p))
    return pl.pallas_call(
        functools.partial(attn_fwd_kernel, nblocks, most),
        grid_spec=pltpu.PrefetchScalarGridSpec(
            num_scalar_prefetch=1, grid=(pairs,),
            in_specs=[pl.BlockSpec((length, QB), whole), pl.BlockSpec((length, QB), whole), pl.BlockSpec((nblocks, QB), whole),
                      col(qo), col(ko), col(vo)],
            out_specs=[pl.BlockSpec((length, width), lambda p, lo: (0, p)),
                       pl.BlockSpec((None, nblocks, 2 * QB), lambda p, lo: (p, 0, 0))],
            scratch_shapes=[pltpu.VMEM((nblocks, most * QB, QB), F32), pltpu.VMEM((width, length), BF16)]),
        out_shape=[jax.ShapeDtypeStruct((length, pairs * width), BF16), jax.ShapeDtypeStruct((pairs, nblocks, 2 * QB), F32)],
        compiler_params=pltpu.CompilerParams(vmem_limit_bytes=48 << 20),
        name="attn_forward",
    )(lo, segc, padc, segr, qa, ka, va)


def attn_backward(q, k, v, do, lse, masks, first=0, pairs=None):
    length, width = q[0].shape[0], 128
    nblocks = length // QB
    most = min(nblocks, SPAN // QB + 1)
    pairs = pairs or 8
    lo, segc, padc, segr = masks
    (qa, qo), (ka, ko), (va, vo) = q, k, v
    whole = lambda p, lo: (0, 0)
    col = lambda off: pl.BlockSpec((length, width), lambda p, lo: (0, off + first + p))
    out = pl.BlockSpec((length, width), lambda p, lo: (0, p))
    return pl.pallas_call(
        functools.partial(attn_bwd_kernel, nblocks, most),
        grid_spec=pltpu.PrefetchScalarGridSpec(
            num_scalar_prefetch=1, grid=(pairs,),
            in_specs=[pl.BlockSpec((length, QB), whole), pl.BlockSpec((length, QB), whole), pl.BlockSpec((nblocks, QB), whole),
                      col(qo), col(ko), col(vo), col(0),
                      pl.BlockSpec((None, nblocks, 2 * QB), lambda p, lo: (first + p, 0, 0))],
            out_specs=[out, out, out, pl.BlockSpec((8, width), lambda p, lo: (0, p))],
            scratch_shapes=[pltpu.VMEM((nblocks, most * QB, QB), F32), pltpu.VMEM((width, length), BF16),
                            pltpu.VMEM((length, width), F32), pltpu.VMEM((length, width), F32)]),
        out_shape=[jax.ShapeDtypeStruct((length, pairs * width), BF16)] * 3 + [jax.ShapeDtypeStruct((8, pairs * width), F32)],
        compiler_params=pltpu.CompilerParams(vmem_limit_bytes=48 << 20),
        name="attn_backward",
    )(lo, segc, padc, segr, qa, ka, va, do, lse)


def rms_norm(values, gain):
    return values * lax.rsqrt(jnp.mean(values * values, -1, keepdims=True) + 1e-05) * gain


def gelu_tanh(values):
    return (
        0.5
        * values
        * (1.0 + jnp.tanh(0.7978845608028654 * (values + 0.044715 * values * values * values)))
    )


def contract_rows(left, right):
    return lax.dot_general(left, right, (((0,), (0,)), ((), ())), preferred_element_type=F32)


def row_squares(values, valid):
    return jnp.sum(valid * jnp.sum(values * values, -1))


def local(ladder, tokens, cotangent, segment_ids, padding_mask, w_qkv, bias_qv, w_out, bias_out, gain_attn, gain_mlp,
          w_up, bias_up, w_down, bias_down):
    length, width = tokens.shape[1], tokens.shape[2]
    count = ladder.count
    shard_of, place = ladder.tables()

    def whole(pieces):
        full = pieces[0] if len(pieces) == 1 else jnp.take(jnp.concatenate(pieces, 0), place, axis=0)
        return full.reshape((full.shape[0] * full.shape[1],) + full.shape[2:])

    smalls = [bias_qv, bias_out, gain_attn, gain_mlp, bias_up, bias_down]
    sizes = [s.shape[0] for s in smalls]
    total = sum(sizes)
    rows = w_qkv.shape[0]
    extra = -(-total // (rows * 128)) * 128
    packed = jnp.pad(jnp.concatenate(smalls), (0, rows * extra - total)).reshape(rows, extra)
    qkv_packed = whole(ladder.gather(jnp.concatenate([w_qkv, packed], 1)))
    qkv_w = qkv_packed[:, : 3 * width]
    vectors = qkv_packed[:, 3 * width :].reshape(count, rows * extra).astype(F32)
    ends = np.cumsum([0] + sizes)
    qv_bias, out_bias, attn_gain, mlp_gain, up_bias, down_bias = [
        vectors[:, ends[i] : ends[i + 1]].reshape(-1) for i in range(6)
    ]
    out_w = whole(ladder.gather(w_out))
    up_w = whole(ladder.gather(w_up))
    down_w = whole(ladder.gather(w_down))

    masks = mask_inputs(segment_ids[0], padding_mask[0])
    valid = padding_mask[0].astype(F32)
    frames = tokens[0].astype(F32)
    normed_in = rms_norm(frames, attn_gain).astype(BF16)
    projected = jnp.dot(normed_in, qkv_w, preferred_element_type=F32)
    offset = jnp.concatenate([qv_bias[:width], jnp.zeros((width,), F32), qv_bias[width:]])
    projected = (projected + offset).astype(BF16)
    per = width // 128
    triple = ((projected, 0), (projected, per), (projected, 2 * per))
    mixed, lse = attn_forward(*triple, masks)
    attn_branch = jnp.dot(mixed, out_w, preferred_element_type=F32) + out_bias
    middle = frames + attn_branch
    normed_mid = rms_norm(middle, mlp_gain).astype(BF16)
    pre_act = jnp.dot(normed_mid, up_w, preferred_element_type=F32) + up_bias
    activated = gelu_tanh(pre_act).astype(BF16)
    mlp_branch = jnp.dot(activated, down_w, preferred_element_type=F32) + down_bias
    final = middle + mlp_branch
    output = final.astype(BF16)[None]

    grad_out = cotangent[0]
    grad_float = grad_out.astype(F32)
    blocks = lambda g: g.reshape((count, g.shape[0] // count) + g.shape[1:])
    own = lambda g: ladder.reduce_blocks(blocks(g), shard_of, BF16)
    own_down = own(contract_rows(activated, grad_out))
    grad_act = nt(grad_out, down_w)
    _, gelu_pull = jax.vjp(gelu_tanh, pre_act)
    grad_pre = gelu_pull(grad_act)[0].astype(BF16)
    own_up = own(contract_rows(normed_mid, grad_pre))
    grad_normed_mid = nt(grad_pre, up_w)
    _, mid_pull = jax.vjp(rms_norm, middle, mlp_gain)
    grad_middle_norm, grad_mlp_gain = mid_pull(grad_normed_mid)
    grad_middle = grad_float + grad_middle_norm
    grad_branch = grad_middle.astype(BF16)
    own_out = own(contract_rows(mixed, grad_branch))
    grad_mixed = nt(grad_branch, out_w).astype(BF16)
    dq, dk, dv, sums = attn_backward(*triple, grad_mixed, lse, masks)
    grad_projected = jnp.concatenate([dq, dk, dv], 1)
    own_qkv = own(contract_rows(normed_in, grad_projected))
    grad_normed_in = nt(grad_projected, qkv_w)
    _, first_pull = jax.vjp(rms_norm, frames, attn_gain)
    grad_input_norm, grad_attn_gain = first_pull(grad_normed_in)
    input_grad = (grad_middle + grad_input_norm).astype(BF16)[None]

    members = jnp.stack([row_squares(frames, valid), row_squares(middle, valid), row_squares(final, valid),
                         row_squares(attn_branch, valid), row_squares(mlp_branch, valid), jnp.sum(valid)])
    small_grads = [jnp.concatenate([sums[0], sums[1]]), jnp.sum(grad_branch.astype(F32), 0), grad_attn_gain, grad_mlp_gain,
                   jnp.sum(grad_pre.astype(F32), 0), jnp.sum(grad_float, 0)]
    table = jnp.concatenate([g.reshape(count, -1) for g in small_grads] + [jnp.broadcast_to(members, (count, 6))], 1)
    size = -(-table.shape[1] // 128) * 128
    table = jnp.pad(table, ((0, 0), (0, size - table.shape[1])))
    own_small = ladder.reduce_blocks(table[:, None], shard_of, F32).reshape(-1)
    owned = [own_small[ends[i] : ends[i + 1]] for i in range(6)]
    totals = own_small[total : total + 6]
    stats = jnp.sqrt(totals[:5] / (totals[5] * width))
    return (output, input_grad, own_qkv, owned[0], own_out, owned[1], owned[2], owned[3], own_up, owned[4], own_down,
            owned[5], stats, totals[5:6])


def solution(mesh):
    rows, wide, flat = P(AXES, None, None), P(AXES, None), P(AXES)
    return jax.shard_map(
        functools.partial(local, Ladder(mesh)),
        mesh=mesh,
        in_specs=(rows, rows, wide, wide, wide, flat, wide, flat, flat, flat, wide, flat, wide, flat),
        out_specs=(rows, rows, wide, flat, wide, flat, flat, flat, wide, flat, wide, flat, P(), P()),
        check_vma=False,
    )
```

time: 1110 us -> 752 us (0.68)
  waiting for transfers between devices: 502 us -> 173 us
  matrix products: 311 us -> 159 us
  blocking collectives: 124 us -> 0 us
  local copies, waits for them, and re-layouts: 44.1 us -> 158 us
  Pallas kernels: 0 us -> 91.9 us
  starting transfers between devices: 0.32 us -> 50.3 us
  between operations: 19.2 us -> 2.69 us
    reduce_scatter x4 -> x0, waiting for transfers between devices: 445 us -> none  [the longest x1 189 us: local(): lax.psum_scatter(grad_up_w, ('dp', 'fsdp'), scatter_dimension=0, tiled=True)]
    ppermute x0 -> x49, waiting for transfers between devices: none -> 173 us  [hop(): return lax.ppermute(value, AXES, pairs)]
    dot_general x20 -> x8, matrix products: 260 us -> 121 us  [the longest x4 58.6 us: nt(): lax.dot_general(a, b, (((1,), (1,)), ((), ())), preferred_element_type=F32)]
    pallas_call x0 -> x2, Pallas kernels: none -> 91.9 us  [the longest x1 48 us: attn_backward(): pl.pallas_call(functools.partial(attn_bwd_kernel, nblocks, most), grid_sp...]
    unnamed x2 -> x0, blocking collectives: 84.2 us -> none
    gather x0 -> x10, local copies, waits for them, and re-layouts: none -> 55 us  [the longest x4 27.5 us: whole(): jnp.take(jnp.concatenate(pieces, 0), place, axis=0)]
    all_gather x4 -> x0, waiting for transfers between devices: 53.5 us -> none  [the longest x1 53.4 us: local(): lax.all_gather(w_down, ('dp', 'fsdp'), axis=0, tiled=True)]
    ppermute x0 -> x49, starting transfers between devices: none -> 50.3 us  [hop(): return lax.ppermute(value, AXES, pairs)]
  transfers between devices with their start and end apart: 8 -> 49, of which waited for: 4 -> 18; matrix products, arithmetic and copies ran while one was open for 30% -> 37% of each run, Pallas kernels for 0% -> 12%
where the time goes in v1:
time: 752 us; the launch traced here: 741 us
  waiting for transfers between devices  173 us (23%)
  matrix products  159 us (21%)
  local copies, waits for them, and re-layouts  158 us (21%)
  other arithmetic  105 us (14%)
  Pallas kernels  91.9 us (12%)
  starting transfers between devices  50.3 us (7%)
    ppermute x49, waiting for transfers between devices, hop(): return lax.ppermute(value, AXES, pairs)  173 us
    dot_general x4, matrix products, nt(): lax.dot_general(a, b, (((1,), (1,)), ((), ())), preferred_element_type=F32)  58.6 us
    unnamed x143, local copies, waits for them, and re-layouts  54.1 us
    ppermute x49, starting transfers between devices, hop(): return lax.ppermute(value, AXES, pairs)  50.3 us
    pallas_call x1, Pallas kernels, attn_backward(): pl.pallas_call(functools.partial(attn_bwd_kernel, nblocks, most), grid_sp...  48 us
    pallas_call x1, Pallas kernels, attn_forward(): pl.pallas_call(functools.partial(attn_fwd_kernel, nblocks, most), grid_sp...  43.8 us
    dot_general x4, matrix products, contract_rows(): lax.dot_general(left, right, (((0,), (0,)), ((), ())), preferred_element_...  38.5 us
    gather x4, local copies, waits for them, and re-layouts, whole(): jnp.take(jnp.concatenate(pieces, 0), place, axis=0)  27.5 us
  transfers between devices with their start and end apart: 49, of which 18 were waited for; matrix products, arithmetic and copies ran while one was open for 37% of the time, Pallas kernels for 12%

profile of v1, /device:TPU:0, one launch (start us, length us, event | category | flops | bytes accessed | tf_op | source)
XLA Modules:
  0.0 740.9 jit_solution(16247949950365789426)
XLA Ops:
  0.6 4.1 collective-permute-start.6
  4.7 4.1 concatenate.83
  31.5 4.0 copy.53
  36.1 11.0 %collective-permute-done.7 = bf16[2,32,1024]{2,1,0:T(8,128)(2,1)} collective-permute-done((bf16[2,32,1024]{2,1,0:T(8,128)(2,1)}, bf16[2,32,1024]{2,1,0:T(8,128)(2,1)}, u32[]{:S(2)}, u32[]{:S(2)}) %collective-permute-start.7) | collective-permute-done | bytes 131104 | tf_op jit(solution)/shard_map/ppermute | solution.py:42
  67.0 8.8 %collective-permute-done.13 = bf16[2,32,4096]{2,1,0:T(8,128)(2,1)S(1)} collective-permute-done((bf16[2,32,4096]{2,1,0:T(8,128)(2,1)S(1)}, bf16[2,32,4096]{2,1,0:T(8,128)(2,1)S(1)}, u32[]{:S(2)}, u32[]{:S(2)}) %collective-permute-start.13) | collective-permute-done | bytes 524320 | tf_op jit(solution)/shard_map/ppermute | solution.py:42
  76.5 9.3 %collective-permute-done.19 = bf16[2,128,1024]{2,1,0:T(8,128)(2,1)S(1)} collective-permute-done((bf16[2,128,1024]{2,1,0:T(8,128)(2,1)S(1)}, bf16[2,128,1024]{2,1,0:T(8,128)(2,1)S(1)}, u32[]{:S(2)}, u32[]{:S(2)}) %collective-permute-start.19) | collective-permute-done | bytes 524320 | tf_op jit(solution)/shard_map/ppermute | solution.py:42
  97.8 9.6 %collective-permute-done.20 = bf16[4,128,1024]{2,1,0:T(8,128)(2,1)S(1)} collective-permute-done((bf16[4,128,1024]{2,1,0:T(8,128)(2,1)S(1)}, bf16[4,128,1024]{2,1,0:T(8,128)(2,1)S(1)}, u32[]{:S(2)}, u32[]{:S(2)}) %collective-permute-start.20) | collective-permute-done | bytes 1048608 | tf_op jit(solution)/shard_map/ppermute | solution.py:42
  128.3 11.5 %collective-permute-done.15 = bf16[8,32,4096]{2,1,0:T(8,128)(2,1)} collective-permute-done((bf16[8,32,4096]{2,1,0:T(8,128)(2,1)}, bf16[8,32,4096]{2,1,0:T(8,128)(2,1)}, u32[]{:S(2)}, u32[]{:S(2)}) %collective-permute-start.15) | collective-permute-done | bytes 2097184 | tf_op jit(solution)/shard_map/ppermute | solution.py:42
  142.3 20.0 %collective-permute-done.21 = bf16[8,128,1024]{2,1,0:T(8,128)(2,1)} collective-permute-done((bf16[8,128,1024]{2,1,0:T(8,128)(2,1)}, bf16[8,128,1024]{2,1,0:T(8,128)(2,1)}, u32[]{:S(2)}, u32[]{:S(2)}) %collective-permute-start.21) | collective-permute-done | bytes 2097184 | tf_op jit(solution)/shard_map/ppermute | solution.py:42
  175.1 7.0 gather_fusion.1
  189.5 12.6 %add_convert_fusion.q_ref.k_ref.v_ref = bf16[1024,3072]{1,0:T(8,128)(2,1)} fusion(f32[3072]{0:T(1024)S(1)} %pad_maximum_fusion.13, bf16[1024,1024]{0,1:T(8,128)(2,1)S(1)} %fusion.25, bf16[1024,3200]{1,0:T(8,128)(2,1)} %copy-done.19), kind=kOutput, calls=%fused_computation.34 | convolution fusion | flops 6448742400 | bytes 14692352 | tf_op jit(solution)/shard_map/dot_general | solution.py:320
  202.7 43.8 %attn_forward.1 = (bf16[1024,1024]{1,0:T(8,128)(2,1)S(1)}, f32[8,8,256]{2,1,0:T(8,128)S(1)}) custom-call(s32[8]{0:T(128)S(1)} %and_select_fusion.lo_ref, s32[1024,128]{1,0:T(8,128)S(1)} %broadcast_in_dim.112.segc_ref, s32[1024,128]{1,0:T(8,128)S(1)} %broadcast_in_dim.114.padc_ref, s32[8,128]{1,0:T(8,128)S(1)} %bitcast.133, ...), custom_call_target="tpu_custom_call" | custom-call | tf_op jit(solution)/shard_map/attn_forward/pallas_call | solution.py:228
  246.6 5.6 multiply_reduce_fusion.5
  256.1 8.4 %gather_fusion.5 = bf16[32,32,4096]{2,1,0:T(8,128)(2,1)} fusion(bf16[32,32,4096]{2,1,0:T(8,128)(2,1)} %constant_dynamic-update-slice_fusion.14, s32[1024]{0:T(1024)S(1)} %pad_clamp_fusion.1), kind=kCustom, calls=%fused_computation.1.clone | custom fusion | bytes 16777344 | tf_op jit(solution)/shard_map/jit(_take)/gather | solution.py:296
  264.6 7.5 %broadcast_select_fusion.3 = bf16[32,32,4096]{2,1,0:T(8,128)(2,1)} fusion(bf16[32,32,4096]{2,1,0:T(8,128)(2,1)} %gather_fusion.5, pred[32]{0:T(512)(128)(4,1)S(1)} %compare_and_fusion.1), kind=kLoop, calls=%fused_computation.43 | loop fusion | flops 4194304 | bytes 16777248 | tf_op jit(solution)/shard_map/jit(_take)/select_n | solution.py:296
  275.2 8.4 %gather_fusion.6 = bf16[32,128,1024]{2,1,0:T(8,128)(2,1)} fusion(bf16[32,128,1024]{2,1,0:T(8,128)(2,1)} %constant_dynamic-update-slice_fusion.21, s32[1024]{0:T(1024)S(1)} %pad_clamp_fusion.1), kind=kCustom, calls=%fused_computation.2.clone | custom fusion | bytes 16777344 | tf_op jit(solution)/shard_map/jit(_take)/gather | solution.py:296
  283.7 7.5 %broadcast_select_fusion.2 = bf16[32,128,1024]{2,1,0:T(8,128)(2,1)} fusion(bf16[32,128,1024]{2,1,0:T(8,128)(2,1)} %gather_fusion.6, pred[32]{0:T(512)(128)(4,1)S(1)} %compare_and_fusion.1), kind=kLoop, calls=%fused_computation.42 | loop fusion | flops 4194304 | bytes 16777248 | tf_op jit(solution)/shard_map/jit(_take)/select_n | solution.py:296
  291.2 21.8 %fusion.10 = (bf16[4096,1024]{0,1:T(8,128)(2,1)}, f32[1024,4096]{1,0:T(8,128)}) fusion(f32[4096]{0:T(1024)S(1)} %slice_bitcast_fusion, bf16[1024,4096]{1,0:T(8,128)(2,1)} %bitcast.138, f32[1024,1024]{0,1:T(8,128)} %get-tuple-element.92, f32[1024]{0:T(1024)S(1)} %mul.239, f32[1024]{0:T(1024)S(1)} %fusion.35), kind=kOutput, calls=%fused_computation.25 | convolution fusion | flops 8635023360 | bytes 37773312 | tf_op jit(solution)/shard_map/dot_general | solution.py:329
  313.0 28.6 %convert_reduce_fusion = (f32[4096]{0:T(1024)}, bf16[1024,4096]{1,0:T(8,128)(2,1)}) fusion(bf16[4096,1024]{1,0:T(8,128)(2,1)} %bitcast.136, bf16[1,1024,1024]{2,1,0:T(8,128)(2,1)S(1)} %copy-done.33, f32[1024,4096]{1,0:T(8,128)} %get-tuple-element.111, f32[4096]{0:T(1024)S(1)} %slice_bitcast_fusion), kind=kOutput, calls=%fused_computation.32 | convolution fusion | flops 8703176704 | bytes 35684352 | tf_op jit(solution)/shard_map/dot_general | solution.py:96
  341.6 15.4 %fusion.51 = f32[1024,1024]{0,1:T(8,128)} fusion(bf16[1024,4096]{1,0:T(8,128)(2,1)} %get-tuple-element.109, bf16[1024,4096]{1,0:T(8,128)(2,1)} %bitcast.139), kind=kOutput, calls=%fused_computation.222 | convolution fusion | flops 8589934592 | bytes 20971520 | tf_op jit(solution)/shard_map/dot_general | solution.py:96
  357.0 11.5 %convolution_convert_fusion = bf16[1024,4096]{1,0:T(8,128)(2,1)} fusion(bf16[1024,4096]{1,0:T(8,128)(2,1)S(1)} %copy-done.56, f32[1024,1024]{0,1:T(8,128)S(1)} %copy-done.20, f32[1024]{0:T(1024)S(1)} %mul.239, f32[1024]{0:T(1024)S(1)} %fusion.35), kind=kOutput, calls=%fused_computation.45 | convolution fusion | flops 8597274624 | bytes 20979712 | tf_op jit(solution)/shard_map/dot_general | solution.py:282
  368.5 11.9 %copy.65 = bf16[4096,1024]{1,0:T(8,128)(2,1)} copy(bf16[4096,1024]{0,1:T(8,128)(2,1)} %get-tuple-element.110) | data formatting | bytes 16777216 | tf_op jit(solution)/shard_map/dot_general | solution.py:282
  380.4 14.6 %convolution_convert_fusion.1 = bf16[32,128,1024]{2,1,0:T(8,128)(2,1)} fusion(bf16[32,128,1024]{2,1,0:T(8,128)(2,1)} %bitcast.140, bf16[1,1024,1024]{2,1,0:T(8,128)(2,1)S(1)} %copy-done.33), kind=kOutput, calls=%fused_computation.46 | convolution fusion | flops 8594128896 | bytes 18874368 | tf_op jit(solution)/shard_map/dot_general | solution.py:282
  395.0 8.8 %gather_fusion.9 = bf16[32,128,1024]{2,1,0:T(8,128)(2,1)} fusion(bf16[32,128,1024]{2,1,0:T(8,128)(2,1)} %convolution_convert_fusion.1, s32[1024]{0:T(1024)S(1)} %copy-done.52), kind=kCustom, calls=%fused_computation.5.clone | custom fusion | bytes 16777344 | tf_op jit(solution)/shard_map/jit(_take)/gather | solution.py:92
  403.9 7.5 %broadcast_select_fusion = bf16[32,128,1024]{2,1,0:T(8,128)(2,1)} fusion(bf16[32,128,1024]{2,1,0:T(8,128)(2,1)} %gather_fusion.9, pred[32]{0:T(512)(128)(4,1)S(1)} %copy-done.48), kind=kLoop, calls=%fused_computation.40 | loop fusion | flops 4194304 | bytes 16777248 | tf_op jit(solution)/shard_map/jit(_take)/select_n | solution.py:92
  411.4 4.9 slice.790
  417.1 22.2 %multiply_reduce_fusion = (f32[1024]{0:T(1024)S(1)}, f32[1024]{0:T(1024)S(1)}, f32[1024]{0:T(1024)S(1)}, f32[1024]{0:T(1024)S(1)}, bf16[1,1024,1024]{1,2,0:T(8,128)(2,1)}) fusion(f32[1024]{0:T(1024)S(1)} %copy-done.54, f32[1024,1024]{0,1:T(8,128)S(1)} %copy-done.21, f32[1024,1024]{0,1:T(8,128)} %fusion.51, f32[1024]{0:T(1024)S(1)} %mul.239, ...), kind=kOutput, calls=%fused_computation.69 | convolution fusion | flops 8645505024 | bytes 35696640 | tf_op jit(solution)/shard_map/dot_general | solution.py:331
  439.3 4.0 convert_reduce_fusion.2
  447.1 48.0 %attn_backward.1 = (bf16[1024,1024]{1,0:T(8,128)(2,1)S(1)}, bf16[1024,1024]{1,0:T(8,128)(2,1)S(1)}, bf16[1024,1024]{1,0:T(8,128)(2,1)}, f32[8,1024]{1,0:T(8,128)S(1)}) custom-call(s32[8]{0:T(128)S(1)} %copy-done.8, s32[1024,128]{1,0:T(8,128)S(1)} %copy-done.3, s32[1024,128]{1,0:T(8,128)S(1)} %copy-done.1, s32[8,128]{1,0:T(8,128)S(1)} %bitcast.134, ...), custom_call_target="tpu_custom_call" | custom-call | tf_op jit(solution)/shard_map/attn_backward/pallas_call | solution.py:253
  500.5 10.8 %fusion.26 = (f32[1024]{0:T(1024)S(1)}, f32[1024]{0:T(1024)S(1)}, f32[1024,1024]{0,1:T(8,128)}) fusion(bf16[1,1024,1024]{1,2,0:T(8,128)(2,1)S(1)} %copy-done.12, f32[1024]{0:T(1024)S(1)} %copy-done.43, f32[1024]{0:T(1024)S(1)} %copy-done.41, bf16[1024,3072]{1,0:T(8,128)(2,1)S(1)} %constant_dynamic-update-slice_fusion.28, bf16[1024,3200]{1,0:T(8,128)(2,1)} %copy-done.19), kind=kOutput, calls=%fused_computation.62 | convolution fusion | flops 6449788928 | bytes 18890752 | tf_op jit(solution)/shard_map/dot_general | solution.py:96
  511.3 8.7 %fusion.17 = bf16[32,32,3072]{2,1,0:T(8,128)(2,1)} fusion(bf16[32,32,1024]{2,1,0:T(8,128)(2,1)S(1)} %bitcast.151, bf16[1024,3072]{1,0:T(8,128)(2,1)S(1)} %constant_dynamic-update-slice_fusion.28), kind=kOutput, calls=%fused_computation.53 | convolution fusion | flops 6445596672 | bytes 14680064 | tf_op jit(solution)/shard_map/dot_general | solution.py:282
  520.0 6.5 gather_fusion.2
  527.2 4.0 stack.27
  533.1 6.1 broadcast_select_fusion.4
  539.2 8.7 %gather_fusion.8 = bf16[32,32,4096]{2,1,0:T(8,128)(2,1)} fusion(bf16[32,32,4096]{2,1,0:T(8,128)(2,1)} %bitcast.135, s32[1024]{0:T(1024)S(1)} %copy-done.52), kind=kCustom, calls=%fused_computation.4.clone | custom fusion | bytes 16777344 | tf_op jit(solution)/shard_map/jit(_take)/gather | solution.py:92
  551.8 7.6 %broadcast_select_fusion.1 = bf16[32,32,4096]{2,1,0:T(8,128)(2,1)} fusion(bf16[32,32,4096]{2,1,0:T(8,128)(2,1)} %gather_fusion.8, pred[32]{0:T(512)(128)(4,1)S(1)} %copy-done.48), kind=kLoop, calls=%fused_computation.41 | loop fusion | flops 4194304 | bytes 16777248 | tf_op jit(solution)/shard_map/jit(_take)/select_n | solution.py:92
  559.4 4.9 slice.769
  579.8 3.9 copy.60
  593.6 4.6 collective-permute-done.35
  609.2 8.7 %collective-permute-done.25 = bf16[8,32,3072]{2,1,0:T(8,128)(2,1)S(1)} collective-permute-done((bf16[8,32,3072]{2,1,0:T(8,128)(2,1)S(1)}, bf16[8,32,3072]{2,1,0:T(8,128)(2,1)S(1)}, u32[]{:S(2)}, u32[]{:S(2)}) %collective-permute-start.25) | collective-permute-done | bytes 1572896 | tf_op jit(solution)/shard_map/ppermute | solution.py:42
  624.9 3.9 collective-permute-done.37
  631.4 8.8 %collective-permute-done.26 = bf16[4,32,3072]{2,1,0:T(8,128)(2,1)S(1)} collective-permute-done((bf16[4,32,3072]{2,1,0:T(8,128)(2,1)S(1)}, bf16[4,32,3072]{2,1,0:T(8,128)(2,1)S(1)}, u32[]{:S(2)}, u32[]{:S(2)}) %collective-permute-start.26) | collective-permute-done | bytes 786464 | tf_op jit(solution)/shard_map/ppermute | solution.py:42
  643.1 5.7 collective-permute-done.45
  652.4 30.1 %collective-permute-done.40 = bf16[8,32,4096]{2,1,0:T(8,128)(2,1)S(1)} collective-permute-done((bf16[8,32,4096]{2,1,0:T(8,128)(2,1)S(1)}, bf16[8,32,4096]{2,1,0:T(8,128)(2,1)S(1)}, u32[]{:S(2)}, u32[]{:S(2)}) %collective-permute-start.40) | collective-permute-done | bytes 2097184 | tf_op jit(solution)/shard_map/ppermute | solution.py:42
  693.4 6.0 collective-permute-done.41
  704.4 4.7 collective-permute-done.47
  710.4 14.2 %collective-permute-done.42 = bf16[2,32,4096]{2,1,0:T(8,128)(2,1)S(1)} collective-permute-done((bf16[2,32,4096]{2,1,0:T(8,128)(2,1)S(1)}, bf16[2,32,4096]{2,1,0:T(8,128)(2,1)S(1)}, u32[]{:S(2)}, u32[]{:S(2)}) %collective-permute-start.42) | collective-permute-done | bytes 524320 | tf_op jit(solution)/shard_map/ppermute | solution.py:42
  728.0 10.5 %collective-permute-done.43 = bf16[1,32,4096]{2,1,0:T(8,128)(2,1)S(1)} collective-permute-done((bf16[1,32,4096]{2,1,0:T(8,128)(2,1)S(1)}, bf16[1,32,4096]{2,1,0:T(8,128)(2,1)S(1)}, u32[]{:S(2)}, u32[]{:S(2)}) %collective-permute-start.43) | collective-permute-done | bytes 262176 | tf_op jit(solution)/shard_map/ppermute | solution.py:42
  (331 shorter events, 197.4 us)
Async XLA Ops:
  0.6 27.0 %collective-permute-start.6 = (bf16[1,32,1024]{2,1,0:T(8,128)(2,1)}, bf16[1,32,1024]{2,1,0:T(8,128)(2,1)S(1)}, u32[]{:S(2)}, u32[]{:S(2)}) collective-permute-start(bf16[1,32,1024]{2,1,0:T(8,128)(2,1)} %bitcast.153), channel_id=1, source_target_pairs={{0,4},{1,5},{2,6},{3,7},{4,0},{5,1},{6,2},{7,3},{8,12},{9,13},{10,... | collective-permute-start | bytes 196616 | tf_op jit(solution)/shard_map/ppermute | solution.py:42
  9.8 41.3 %collective-permute-start = (bf16[1,32,3200]{2,1,0:T(8,128)(2,1)S(1)}, bf16[1,32,3200]{2,1,0:T(8,128)(2,1)}, u32[]{:S(2)}, u32[]{:S(2)}) collective-permute-start(bf16[1,32,3200]{2,1,0:T(8,128)(2,1)S(1)} %maximum_bitcast_fusion), channel_id=1, source_target_pairs={{0,4},{1,5},{2,6},{3,7},{4,0},{5,1},{6,2},{7,3},{8,12},{9,13},{10,... | collective-permute-start | bytes 614408 | tf_op jit(solution)/shard_map/ppermute | solution.py:42
  9.9 44.0 %collective-permute-start.12 = (bf16[1,32,4096]{2,1,0:T(8,128)(2,1)}, bf16[1,32,4096]{2,1,0:T(8,128)(2,1)S(1)}, u32[]{:S(2)}, u32[]{:S(2)}) collective-permute-start(bf16[1,32,4096]{2,1,0:T(8,128)(2,1)} %bitcast.141), channel_id=1, source_target_pairs={{0,4},{1,5},{2,6},{3,7},{4,0},{5,1},{6,2},{7,3},{8,12},{9,13},{10,... | collective-permute-start | bytes 786440 | tf_op jit(solution)/shard_map/ppermute | solution.py:42
  12.8 43.2 %collective-permute-start.18 = (bf16[1,128,1024]{2,1,0:T(8,128)(2,1)}, bf16[1,128,1024]{2,1,0:T(8,128)(2,1)S(1)}, u32[]{:S(2)}, u32[]{:S(2)}) collective-permute-start(bf16[1,128,1024]{2,1,0:T(8,128)(2,1)} %bitcast.145), channel_id=1, source_target_pairs={{0,4},{1,5},{2,6},{3,7},{4,0},{5,1},{6,2},{7,3},{8,12},{9,13},{10,... | collective-permute-start | bytes 786440 | tf_op jit(solution)/shard_map/ppermute | solution.py:42
  28.3 18.8 %collective-permute-start.7 = (bf16[2,32,1024]{2,1,0:T(8,128)(2,1)}, bf16[2,32,1024]{2,1,0:T(8,128)(2,1)}, u32[]{:S(2)}, u32[]{:S(2)}) collective-permute-start(bf16[2,32,1024]{2,1,0:T(8,128)(2,1)} %pad_maximum_fusion.11), channel_id=1, source_target_pairs={{0,2},{1,3},{2,0},{3,1},{4,6},{5,7},{6,4},{7,5},{8,10},{9,11},{10,... | collective-permute-start | bytes 393224 | tf_op jit(solution)/shard_map/ppermute | solution.py:42
  48.0 9.6 %collective-permute-start.8 = (bf16[4,32,1024]{2,1,0:T(8,128)(2,1)S(1)}, bf16[4,32,1024]{2,1,0:T(8,128)(2,1)S(1)}, u32[]{:S(2)}, u32[]{:S(2)}) collective-permute-start(bf16[4,32,1024]{2,1,0:T(8,128)(2,1)S(1)} %pad_maximum_fusion.10), channel_id=1, source_target_pairs={{0,8},{1,17},{2,10},{3,19},{4,12},{5,21},{6,14},{7,23},{8,0},{9,25... | collective-permute-start | bytes 786440 | tf_op jit(solution)/shard_map/ppermute | solution.py:42
  52.1 12.4 %collective-permute-start.1 = (bf16[2,32,3200]{2,1,0:T(8,128)(2,1)S(1)}, bf16[2,32,3200]{2,1,0:T(8,128)(2,1)S(1)}, u32[]{:S(2)}, u32[]{:S(2)}) collective-permute-start(bf16[2,32,3200]{2,1,0:T(8,128)(2,1)S(1)} %pad_maximum_fusion.9), channel_id=1, source_target_pairs={{0,2},{1,3},{2,0},{3,1},{4,6},{5,7},{6,4},{7,5},{8,10},{9,11},{10,... | collective-permute-start | bytes 1228808 | tf_op jit(solution)/shard_map/ppermute | solution.py:42
  53.9 21.9 %collective-permute-start.13 = (bf16[2,32,4096]{2,1,0:T(8,128)(2,1)S(1)}, bf16[2,32,4096]{2,1,0:T(8,128)(2,1)S(1)}, u32[]{:S(2)}, u32[]{:S(2)}) collective-permute-start(bf16[2,32,4096]{2,1,0:T(8,128)(2,1)S(1)} %pad_maximum_fusion.7), channel_id=1, source_target_pairs={{0,2},{1,3},{2,0},{3,1},{4,6},{5,7},{6,4},{7,5},{8,10},{9,11},{10,... | collective-permute-start | bytes 1572872 | tf_op jit(solution)/shard_map/ppermute | solution.py:42
  56.1 29.7 %collective-permute-start.19 = (bf16[2,128,1024]{2,1,0:T(8,128)(2,1)S(1)}, bf16[2,128,1024]{2,1,0:T(8,128)(2,1)S(1)}, u32[]{:S(2)}, u32[]{:S(2)}) collective-permute-start(bf16[2,128,1024]{2,1,0:T(8,128)(2,1)S(1)} %pad_maximum_fusion.8), channel_id=1, source_target_pairs={{0,2},{1,3},{2,0},{3,1},{4,6},{5,7},{6,4},{7,5},{8,10},{9,11},{10,... | collective-permute-start | bytes 1572872 | tf_op jit(solution)/shard_map/ppermute | solution.py:42
  58.6 35.2 %collective-permute-start.10 = (bf16[8,32,1024]{2,1,0:T(8,128)(2,1)S(1)}, bf16[8,32,1024]{2,1,0:T(8,128)(2,1)S(1)}, u32[]{:S(2)}, u32[]{:S(2)}) collective-permute-start(bf16[8,32,1024]{2,1,0:T(8,128)(2,1)S(1)} %pad_maximum_fusion.6), channel_id=1, source_target_pairs={{0,1},{1,0},{2,3},{3,2},{4,5},{5,4},{6,7},{7,6},{8,9},{9,8},{10,11... | collective-permute-start | bytes 1572872 | tf_op jit(solution)/shard_map/ppermute | solution.py:42
  58.6 31.5 %collective-permute-start.9 = (bf16[8,32,1024]{2,1,0:T(8,128)(2,1)S(1)}, bf16[8,32,1024]{2,1,0:T(8,128)(2,1)S(1)}, u32[]{:S(2)}, u32[]{:S(2)}) collective-permute-start(bf16[8,32,1024]{2,1,0:T(8,128)(2,1)S(1)} %pad_maximum_fusion.6), channel_id=1, source_target_pairs={{0,16},{1,9},{2,18},{3,11},{4,20},{5,13},{6,22},{7,15},{8,24},{9,1... | collective-permute-start | bytes 1572872 | tf_op jit(solution)/shard_map/ppermute | solution.py:42
  65.6 25.3 %collective-permute-start.2 = (bf16[4,32,3200]{2,1,0:T(8,128)(2,1)S(1)}, bf16[4,32,3200]{2,1,0:T(8,128)(2,1)S(1)}, u32[]{:S(2)}, u32[]{:S(2)}) collective-permute-start(bf16[4,32,3200]{2,1,0:T(8,128)(2,1)S(1)} %pad_maximum_fusion.5), channel_id=1, source_target_pairs={{0,8},{1,17},{2,10},{3,19},{4,12},{5,21},{6,14},{7,23},{8,0},{9,25... | collective-permute-start | bytes 2457608 | tf_op jit(solution)/shard_map/ppermute | solution.py:42
  75.9 19.0 %collective-permute-start.14 = (bf16[4,32,4096]{2,1,0:T(8,128)(2,1)S(1)}, bf16[4,32,4096]{2,1,0:T(8,128)(2,1)S(1)}, u32[]{:S(2)}, u32[]{:S(2)}) collective-permute-start(bf16[4,32,4096]{2,1,0:T(8,128)(2,1)S(1)} %pad_maximum_fusion.3), channel_id=1, source_target_pairs={{0,8},{1,17},{2,10},{3,19},{4,12},{5,21},{6,14},{7,23},{8,0},{9,25... | collective-permute-start | bytes 3145736 | tf_op jit(solution)/shard_map/ppermute | solution.py:42
  86.9 20.5 %collective-permute-start.20 = (bf16[4,128,1024]{2,1,0:T(8,128)(2,1)S(1)}, bf16[4,128,1024]{2,1,0:T(8,128)(2,1)S(1)}, u32[]{:S(2)}, u32[]{:S(2)}) collective-permute-start(bf16[4,128,1024]{2,1,0:T(8,128)(2,1)S(1)} %pad_maximum_fusion.4), channel_id=1, source_target_pairs={{0,8},{1,17},{2,10},{3,19},{4,12},{5,21},{6,14},{7,23},{8,0},{9,25... | collective-permute-start | bytes 3145736 | tf_op jit(solution)/shard_map/ppermute | solution.py:42
  90.1 22.5 %collective-permute-start.11 = (bf16[8,32,1024]{2,1,0:T(8,128)(2,1)S(1)}, bf16[8,32,1024]{2,1,0:T(8,128)(2,1)S(1)}, u32[]{:S(2)}, u32[]{:S(2)}) collective-permute-start(bf16[8,32,1024]{2,1,0:T(8,128)(2,1)S(1)} %collective-permute-done.9), channel_id=1, source_target_pairs={{0,1},{1,0},{2,3},{3,2},{4,5},{5,4},{6,7},{7,6},{8,9},{9,8},{10,11... | collective-permute-start | bytes 1572872 | tf_op jit(solution)/shard_map/ppermute | solution.py:42
  93.3 26.9 %collective-permute-start.3 = (bf16[8,32,3200]{2,1,0:T(8,128)(2,1)}, bf16[8,32,3200]{2,1,0:T(8,128)(2,1)}, u32[]{:S(2)}, u32[]{:S(2)}) collective-permute-start(bf16[8,32,3200]{2,1,0:T(8,128)(2,1)} %pad_maximum_fusion.2), channel_id=1, source_target_pairs={{0,16},{1,9},{2,18},{3,11},{4,20},{5,13},{6,22},{7,15},{8,24},{9,1... | collective-permute-start | bytes 4915208 | tf_op jit(solution)/shard_map/ppermute | solution.py:42
  94.6 30.8 %collective-permute-start.4 = (bf16[8,32,3200]{2,1,0:T(8,128)(2,1)}, bf16[8,32,3200]{2,1,0:T(8,128)(2,1)}, u32[]{:S(2)}, u32[]{:S(2)}) collective-permute-start(bf16[8,32,3200]{2,1,0:T(8,128)(2,1)} %pad_maximum_fusion.2), channel_id=1, source_target_pairs={{0,1},{1,0},{2,3},{3,2},{4,5},{5,4},{6,7},{7,6},{8,9},{9,8},{10,11... | collective-permute-start | bytes 4915208 | tf_op jit(solution)/shard_map/ppermute | solution.py:42
  96.5 43.3 %collective-permute-start.15 = (bf16[8,32,4096]{2,1,0:T(8,128)(2,1)}, bf16[8,32,4096]{2,1,0:T(8,128)(2,1)}, u32[]{:S(2)}, u32[]{:S(2)}) collective-permute-start(bf16[8,32,4096]{2,1,0:T(8,128)(2,1)} %pad_maximum_fusion), channel_id=1, source_target_pairs={{0,16},{1,9},{2,18},{3,11},{4,20},{5,13},{6,22},{7,15},{8,24},{9,1... | collective-permute-start | bytes 6291464 | tf_op jit(solution)/shard_map/ppermute | solution.py:42
  109.0 53.2 %collective-permute-start.21 = (bf16[8,128,1024]{2,1,0:T(8,128)(2,1)}, bf16[8,128,1024]{2,1,0:T(8,128)(2,1)}, u32[]{:S(2)}, u32[]{:S(2)}) collective-permute-start(bf16[8,128,1024]{2,1,0:T(8,128)(2,1)} %pad_maximum_fusion.1), channel_id=1, source_target_pairs={{0,16},{1,9},{2,18},{3,11},{4,20},{5,13},{6,22},{7,15},{8,24},{9,1... | collective-permute-start | bytes 6291464 | tf_op jit(solution)/shard_map/ppermute | solution.py:42
  117.0 50.6 %collective-permute-start.22 = (bf16[8,128,1024]{2,1,0:T(8,128)(2,1)}, bf16[8,128,1024]{2,1,0:T(8,128)(2,1)S(1)}, u32[]{:S(2)}, u32[]{:S(2)}) collective-permute-start(bf16[8,128,1024]{2,1,0:T(8,128)(2,1)} %pad_maximum_fusion.1), channel_id=1, source_target_pairs={{0,1},{1,0},{2,3},{3,2},{4,5},{5,4},{6,7},{7,6},{8,9},{9,8},{10,11... | collective-permute-start | bytes 6291464 | tf_op jit(solution)/shard_map/ppermute | solution.py:42
  120.2 52.2 %collective-permute-start.16 = (bf16[8,32,4096]{2,1,0:T(8,128)(2,1)}, bf16[8,32,4096]{2,1,0:T(8,128)(2,1)S(1)}, u32[]{:S(2)}, u32[]{:S(2)}) collective-permute-start(bf16[8,32,4096]{2,1,0:T(8,128)(2,1)} %pad_maximum_fusion), channel_id=1, source_target_pairs={{0,1},{1,0},{2,3},{3,2},{4,5},{5,4},{6,7},{7,6},{8,9},{9,8},{10,11... | collective-permute-start | bytes 6291464 | tf_op jit(solution)/shard_map/ppermute | solution.py:42
  125.5 48.4 %collective-permute-start.5 = (bf16[8,32,3200]{2,1,0:T(8,128)(2,1)}, bf16[8,32,3200]{2,1,0:T(8,128)(2,1)S(1)}, u32[]{:S(2)}, u32[]{:S(2)}) collective-permute-start(bf16[8,32,3200]{2,1,0:T(8,128)(2,1)} %collective-permute-done.3), channel_id=1, source_target_pairs={{0,1},{1,0},{2,3},{3,2},{4,5},{5,4},{6,7},{7,6},{8,9},{9,8},{10,11... | collective-permute-start | bytes 4915208 | tf_op jit(solution)/shard_map/ppermute | solution.py:42
  139.8 113.2 %collective-permute-start.17 = (bf16[8,32,4096]{2,1,0:T(8,128)(2,1)}, bf16[8,32,4096]{2,1,0:T(8,128)(2,1)}, u32[]{:S(2)}, u32[]{:S(2)}) collective-permute-start(bf16[8,32,4096]{2,1,0:T(8,128)(2,1)} %collective-permute-done.15), channel_id=1, source_target_pairs={{0,1},{1,0},{2,3},{3,2},{4,5},{5,4},{6,7},{7,6},{8,9},{9,8},{10,11... | collective-permute-start | bytes 6291464 | tf_op jit(solution)/shard_map/ppermute | solution.py:42
  162.2 109.8 %collective-permute-start.23 = (bf16[8,128,1024]{2,1,0:T(8,128)(2,1)}, bf16[8,128,1024]{2,1,0:T(8,128)(2,1)}, u32[]{:S(2)}, u32[]{:S(2)}) collective-permute-start(bf16[8,128,1024]{2,1,0:T(8,128)(2,1)} %collective-permute-done.21), channel_id=1, source_target_pairs={{0,1},{1,0},{2,3},{3,2},{4,5},{5,4},{6,7},{7,6},{8,9},{9,8},{10,11... | collective-permute-start | bytes 6291464 | tf_op jit(solution)/shard_map/ppermute | solution.py:42
  416.3 184.5 %collective-permute-start.44 = (bf16[16,128,1024]{2,1,0:T(8,128)(2,1)}, bf16[16,128,1024]{2,1,0:T(8,128)(2,1)}, u32[]{:S(2)}, u32[]{:S(2)}) collective-permute-start(bf16[16,128,1024]{2,1,0:T(8,128)(2,1)} %slice.790), channel_id=1, source_target_pairs={{0,1},{1,0},{2,3},{3,2},{4,5},{5,4},{6,7},{7,6},{8,9},{9,8},{10,11... | collective-permute-start | bytes 12582920 | tf_op jit(solution)/shard_map/ppermute | solution.py:42
  531.9 19.8 %collective-permute-start.29 = (f32[16,1,384]{2,0,1:T(8,128)S(1)}, f32[16,1,384]{2,0,1:T(8,128)S(1)}, u32[]{:S(2)}, u32[]{:S(2)}) collective-permute-start(f32[16,1,384]{2,0,1:T(8,128)S(1)} %slice.725), channel_id=1, source_target_pairs={{0,1},{1,0},{2,3},{3,2},{4,5},{5,4},{6,7},{7,6},{8,9},{9,8},{10,11... | collective-permute-start | bytes 73736 | tf_op jit(solution)/shard_map/ppermute | solution.py:42
  551.7 38.5 %collective-permute-start.24 = (bf16[16,32,3072]{2,1,0:T(8,128)(2,1)}, bf16[16,32,3072]{2,1,0:T(8,128)(2,1)}, u32[]{:S(2)}, u32[]{:S(2)}) collective-permute-start(bf16[16,32,3072]{2,1,0:T(8,128)(2,1)} %slice.705), channel_id=1, source_target_pairs={{0,1},{1,0},{2,3},{3,2},{4,5},{5,4},{6,7},{7,6},{8,9},{9,8},{10,11... | collective-permute-start | bytes 9437192 | tf_op jit(solution)/shard_map/ppermute | solution.py:42
  551.7 13.0 %collective-permute-start.30 = (f32[8,1,384]{2,0,1:T(8,128)S(1)}, f32[8,1,384]{2,0,1:T(8,128)S(1)}, u32[]{:S(2)}, u32[]{:S(2)}) collective-permute-start(f32[8,1,384]{2,0,1:T(8,128)S(1)} %slice_add_fusion), channel_id=1, source_target_pairs={{0,16},{1,9},{2,18},{3,11},{4,20},{5,13},{6,22},{7,15},{8,24},{9,1... | collective-permute-start | bytes 36872 | tf_op jit(solution)/shard_map/ppermute | solution.py:42
  564.3 40.6 %collective-permute-start.39 = (bf16[16,32,4096]{2,1,0:T(8,128)(2,1)}, bf16[16,32,4096]{2,1,0:T(8,128)(2,1)}, u32[]{:S(2)}, u32[]{:S(2)}) collective-permute-start(bf16[16,32,4096]{2,1,0:T(8,128)(2,1)} %slice.769), channel_id=1, source_target_pairs={{0,1},{1,0},{2,3},{3,2},{4,5},{5,4},{6,7},{7,6},{8,9},{9,8},{10,11... | collective-permute-start | bytes 12582920 | tf_op jit(solution)/shard_map/ppermute | solution.py:42
  564.7 7.9 %collective-permute-start.31 = (f32[4,1,384]{2,0,1:T(4,128)S(1)}, f32[4,1,384]{2,0,1:T(4,128)S(1)}, u32[]{:S(2)}, u32[]{:S(2)}) collective-permute-start(f32[4,1,384]{2,0,1:T(4,128)S(1)} %slice_add_fusion.1), channel_id=1, source_target_pairs={{0,8},{1,17},{2,10},{3,19},{4,12},{5,21},{6,14},{7,23},{8,0},{9,25... | collective-permute-start | bytes 18440 | tf_op jit(solution)/shard_map/ppermute | solution.py:42
  574.1 13.7 %collective-permute-start.34 = (bf16[16,32,1024]{2,1,0:T(8,128)(2,1)}, bf16[16,32,1024]{2,1,0:T(8,128)(2,1)S(1)}, u32[]{:S(2)}, u32[]{:S(2)}) collective-permute-start(bf16[16,32,1024]{2,1,0:T(8,128)(2,1)} %slice.746), channel_id=1, source_target_pairs={{0,1},{1,0},{2,3},{3,2},{4,5},{5,4},{6,7},{7,6},{8,9},{9,8},{10,11... | collective-permute-start | bytes 3145736 | tf_op jit(solution)/shard_map/ppermute | solution.py:42
  576.3 10.2 %collective-permute-start.33 = (f32[1,1,384]{2,0,1:T(1,128)S(1)}, f32[1,1,384]{2,0,1:T(1,128)S(1)}, u32[]{:S(2)}, u32[]{:S(2)}) collective-permute-start(f32[1,1,384]{2,0,1:T(1,128)S(1)} %slice_add_fusion.6), channel_id=1, source_target_pairs={{0,4},{1,5},{2,6},{3,7},{4,0},{5,1},{6,2},{7,3},{8,12},{9,13},{10,... | collective-permute-start | bytes 4616 | tf_op jit(solution)/shard_map/ppermute | solution.py:42
  589.0 9.2 %collective-permute-start.35 = (bf16[8,32,1024]{2,1,0:T(8,128)(2,1)S(1)}, bf16[8,32,1024]{2,1,0:T(8,128)(2,1)S(1)}, u32[]{:S(2)}, u32[]{:S(2)}) collective-permute-start(bf16[8,32,1024]{2,1,0:T(8,128)(2,1)S(1)} %add_convert_fusion.9), channel_id=1, source_target_pairs={{0,16},{1,9},{2,18},{3,11},{4,20},{5,13},{6,22},{7,15},{8,24},{9,1... | collective-permute-start | bytes 1572872 | tf_op jit(solution)/shard_map/ppermute | solution.py:42
  592.7 25.2 %collective-permute-start.25 = (bf16[8,32,3072]{2,1,0:T(8,128)(2,1)S(1)}, bf16[8,32,3072]{2,1,0:T(8,128)(2,1)S(1)}, u32[]{:S(2)}, u32[]{:S(2)}) collective-permute-start(bf16[8,32,3072]{2,1,0:T(8,128)(2,1)S(1)} %add_convert_fusion.3), channel_id=1, source_target_pairs={{0,16},{1,9},{2,18},{3,11},{4,20},{5,13},{6,22},{7,15},{8,24},{9,1... | collective-permute-start | bytes 4718600 | tf_op jit(solution)/shard_map/ppermute | solution.py:42
  599.3 23.5 %collective-permute-start.36 = (bf16[4,32,1024]{2,1,0:T(8,128)(2,1)S(1)}, bf16[4,32,1024]{2,1,0:T(8,128)(2,1)S(1)}, u32[]{:S(2)}, u32[]{:S(2)}) collective-permute-start(bf16[4,32,1024]{2,1,0:T(8,128)(2,1)S(1)} %add_convert_fusion.13), channel_id=1, source_target_pairs={{0,8},{1,17},{2,10},{3,19},{4,12},{5,21},{6,14},{7,23},{8,0},{9,25... | collective-permute-start | bytes 786440 | tf_op jit(solution)/shard_map/ppermute | solution.py:42
  604.0 44.8 %collective-permute-start.45 = (bf16[8,128,1024]{2,1,0:T(8,128)(2,1)S(1)}, bf16[8,128,1024]{2,1,0:T(8,128)(2,1)S(1)}, u32[]{:S(2)}, u32[]{:S(2)}) collective-permute-start(bf16[8,128,1024]{2,1,0:T(8,128)(2,1)S(1)} %add_convert_fusion.1), channel_id=1, source_target_pairs={{0,16},{1,9},{2,18},{3,11},{4,20},{5,13},{6,22},{7,15},{8,24},{9,1... | collective-permute-start | bytes 6291464 | tf_op jit(solution)/shard_map/ppermute | solution.py:42
  607.9 74.6 %collective-permute-start.40 = (bf16[8,32,4096]{2,1,0:T(8,128)(2,1)S(1)}, bf16[8,32,4096]{2,1,0:T(8,128)(2,1)S(1)}, u32[]{:S(2)}, u32[]{:S(2)}) collective-permute-start(bf16[8,32,4096]{2,1,0:T(8,128)(2,1)S(1)} %add_convert_fusion.2), channel_id=1, source_target_pairs={{0,16},{1,9},{2,18},{3,11},{4,20},{5,13},{6,22},{7,15},{8,24},{9,1... | collective-permute-start | bytes 6291464 | tf_op jit(solution)/shard_map/ppermute | solution.py:42
  619.6 20.5 %collective-permute-start.26 = (bf16[4,32,3072]{2,1,0:T(8,128)(2,1)S(1)}, bf16[4,32,3072]{2,1,0:T(8,128)(2,1)S(1)}, u32[]{:S(2)}, u32[]{:S(2)}) collective-permute-start(bf16[4,32,3072]{2,1,0:T(8,128)(2,1)S(1)} %add_convert_fusion.6), channel_id=1, source_target_pairs={{0,8},{1,17},{2,10},{3,19},{4,12},{5,21},{6,14},{7,23},{8,0},{9,25... | collective-permute-start | bytes 2359304 | tf_op jit(solution)/shard_map/ppermute | solution.py:42
  623.8 5.0 collective-permute-start.37
  629.7 56.2 %collective-permute-start.38 = (bf16[1,32,1024]{2,1,0:T(8,128)(2,1)S(1)}, bf16[1,32,1024]{2,1,0:T(8,128)(2,1)S(1)}, u32[]{:S(2)}, u32[]{:S(2)}) collective-permute-start(bf16[1,32,1024]{2,1,0:T(8,128)(2,1)S(1)} %add_convert_fusion.16), channel_id=1, source_target_pairs={{0,4},{1,5},{2,6},{3,7},{4,0},{5,1},{6,2},{7,3},{8,12},{9,13},{10,... | collective-permute-start | bytes 196616 | tf_op jit(solution)/shard_map/ppermute | solution.py:42
  641.5 46.0 %collective-permute-start.27 = (bf16[2,32,3072]{2,1,0:T(8,128)(2,1)S(1)}, bf16[2,32,3072]{2,1,0:T(8,128)(2,1)S(1)}, u32[]{:S(2)}, u32[]{:S(2)}) collective-permute-start(bf16[2,32,3072]{2,1,0:T(8,128)(2,1)S(1)} %add_convert_fusion.10), channel_id=1, source_target_pairs={{0,2},{1,3},{2,0},{3,1},{4,6},{5,7},{6,4},{7,5},{8,10},{9,11},{10,... | collective-permute-start | bytes 1179656 | tf_op jit(solution)/shard_map/ppermute | solution.py:42
  650.9 39.4 %collective-permute-start.46 = (bf16[4,128,1024]{2,1,0:T(8,128)(2,1)S(1)}, bf16[4,128,1024]{2,1,0:T(8,128)(2,1)S(1)}, u32[]{:S(2)}, u32[]{:S(2)}) collective-permute-start(bf16[4,128,1024]{2,1,0:T(8,128)(2,1)S(1)} %add_convert_fusion.4), channel_id=1, source_target_pairs={{0,8},{1,17},{2,10},{3,19},{4,12},{5,21},{6,14},{7,23},{8,0},{9,25... | collective-permute-start | bytes 3145736 | tf_op jit(solution)/shard_map/ppermute | solution.py:42
  684.5 14.9 %collective-permute-start.41 = (bf16[4,32,4096]{2,1,0:T(8,128)(2,1)S(1)}, bf16[4,32,4096]{2,1,0:T(8,128)(2,1)S(1)}, u32[]{:S(2)}, u32[]{:S(2)}) collective-permute-start(bf16[4,32,4096]{2,1,0:T(8,128)(2,1)S(1)} %add_convert_fusion.5), channel_id=1, source_target_pairs={{0,8},{1,17},{2,10},{3,19},{4,12},{5,21},{6,14},{7,23},{8,0},{9,25... | collective-permute-start | bytes 3145736 | tf_op jit(solution)/shard_map/ppermute | solution.py:42
  688.7 13.8 %collective-permute-start.28 = (bf16[1,32,3072]{2,1,0:T(8,128)(2,1)S(1)}, bf16[1,32,3072]{2,1,0:T(8,128)(2,1)S(1)}, u32[]{:S(2)}, u32[]{:S(2)}) collective-permute-start(bf16[1,32,3072]{2,1,0:T(8,128)(2,1)S(1)} %add_convert_fusion.14), channel_id=1, source_target_pairs={{0,4},{1,5},{2,6},{3,7},{4,0},{5,1},{6,2},{7,3},{8,12},{9,13},{10,... | collective-permute-start | bytes 589832 | tf_op jit(solution)/shard_map/ppermute | solution.py:42
  691.9 17.2 %collective-permute-start.47 = (bf16[2,128,1024]{2,1,0:T(8,128)(2,1)S(1)}, bf16[2,128,1024]{2,1,0:T(8,128)(2,1)S(1)}, u32[]{:S(2)}, u32[]{:S(2)}) collective-permute-start(bf16[2,128,1024]{2,1,0:T(8,128)(2,1)S(1)} %add_convert_fusion.7), channel_id=1, source_target_pairs={{0,2},{1,3},{2,0},{3,1},{4,6},{5,7},{6,4},{7,5},{8,10},{9,11},{10,... | collective-permute-start | bytes 1572872 | tf_op jit(solution)/shard_map/ppermute | solution.py:42
  700.8 23.8 %collective-permute-start.42 = (bf16[2,32,4096]{2,1,0:T(8,128)(2,1)S(1)}, bf16[2,32,4096]{2,1,0:T(8,128)(2,1)S(1)}, u32[]{:S(2)}, u32[]{:S(2)}) collective-permute-start(bf16[2,32,4096]{2,1,0:T(8,128)(2,1)S(1)} %add_convert_fusion.8), channel_id=1, source_target_pairs={{0,2},{1,3},{2,0},{3,1},{4,6},{5,7},{6,4},{7,5},{8,10},{9,11},{10,... | collective-permute-start | bytes 1572872 | tf_op jit(solution)/shard_map/ppermute | solution.py:42
  710.3 15.6 %collective-permute-start.48 = (bf16[1,128,1024]{2,1,0:T(8,128)(2,1)S(1)}, bf16[1,128,1024]{2,1,0:T(8,128)(2,1)S(1)}, u32[]{:S(2)}, u32[]{:S(2)}) collective-permute-start(bf16[1,128,1024]{2,1,0:T(8,128)(2,1)S(1)} %add_convert_fusion.11), channel_id=1, source_target_pairs={{0,4},{1,5},{2,6},{3,7},{4,0},{5,1},{6,2},{7,3},{8,12},{9,13},{10,... | collective-permute-start | bytes 786440 | tf_op jit(solution)/shard_map/ppermute | solution.py:42
  725.8 12.6 %collective-permute-start.43 = (bf16[1,32,4096]{2,1,0:T(8,128)(2,1)S(1)}, bf16[1,32,4096]{2,1,0:T(8,128)(2,1)S(1)}, u32[]{:S(2)}, u32[]{:S(2)}) collective-permute-start(bf16[1,32,4096]{2,1,0:T(8,128)(2,1)S(1)} %add_convert_fusion.12), channel_id=1, source_target_pairs={{0,4},{1,5},{2,6},{3,7},{4,0},{5,1},{6,2},{7,3},{8,12},{9,13},{10,... | collective-permute-start | bytes 786440 | tf_op jit(solution)/shard_map/ppermute | solution.py:42
  (58 other events, 1286.9 us)

commit v2 on v1

v2 whole, which is shorter than its diff:
```python
import functools

import jax
import jax.numpy as jnp
import numpy as np
from jax import lax
from jax.experimental import pallas as pl
from jax.experimental.pallas import tpu as pltpu
from jax.sharding import PartitionSpec as P

HD = 64
QB = 128
SPAN = 512
MANY = 4
WEIGH = 3
F32 = jnp.float32
BF16 = jnp.bfloat16

CORE = 1
Z_HOPS = (2, 4, 6)
MIX = ((0, 1, 2, 3), (0, 2, 1, 3))
FLIP = (0, 2, 1, 3)
HOPS = ((4, 2, 8, 16), (4, 2, 16, 8))


def tie(value, *others):
    return lax.optimization_barrier((value,) + others)[0]


def add_up(*terms):
    return sum(term.astype(F32) for term in terms)


def cost(microseconds):
    return pl.CostEstimate(flops=int(WEIGH * microseconds * 1.15e9), transcendentals=0, bytes_accessed=0)


class Ladder:
    def __init__(self, mesh):
        self.count = int(np.prod(list(mesh.shape.values())))
        self.native = dict(mesh.shape) != {"dp": 4, "fsdp": 8}
        self.axes = ("dp", "fsdp")
        if not self.native:
            keys = []
            for core in (0, 1):
                both = []
                for which, extra in ((core, 0), (1 - core, CORE)):
                    own = [extra]
                    for bit in HOPS[which]:
                        own = own + [key ^ bit for key in own]
                    both += own
                keys.append(both)
            self.keys = np.array(keys, np.int32)
            self.places = np.argsort(self.keys, 1).astype(np.int32)

    def place(self):
        if self.native:
            self.meta = jnp.array([0, 1, 2, 3, 0, 0], jnp.int32)
            self.order = jnp.arange(4)
            return
        me = lax.axis_index(self.axes)
        odd = (me & CORE) == 1
        mix = jnp.where(odd, jnp.array(MIX[1], jnp.int32), jnp.array(MIX[0], jnp.int32))
        self.meta = jnp.concatenate([(me >> 3) ^ mix, (me & CORE)[None], ((me >> 1) & 3)[None]])
        self.order = mix[jnp.arange(4) ^ (me >> 3)]
        every = jnp.arange(self.count, dtype=jnp.int32)
        self.shard_of = me ^ jnp.where(odd, self.keys[1], self.keys[0])
        self.slot_of = jnp.where(odd, self.places[1], self.places[0])[every ^ me]

    def flip(self, value, even, odd):
        bits = (even, odd)
        return lax.ppermute(value, self.axes, [(i, i ^ bits[i & CORE]) for i in range(self.count)])

    def step(self, value, level):
        return self.flip(value, HOPS[0][level], HOPS[1][level])

    def across(self, value):
        return self.flip(value, CORE, CORE)

    def gather_small(self, vector):
        if self.native:
            return lax.all_gather(vector, self.axes, axis=0, tiled=False)
        held = vector[None]
        for level in range(4):
            held = jnp.concatenate([held, self.step(held, level)], 0)
        return jnp.take(jnp.concatenate([held, self.across(held)], 0), self.slot_of, axis=0)

    def scatter_small(self, table):
        if self.native:
            return lax.psum_scatter(table, self.axes, scatter_dimension=0, tiled=True).reshape(-1)
        half = self.count // 2
        table = jnp.take(table, self.shard_of, axis=0)
        total = table[:half] + self.across(table[half:])
        for level in (3, 2, 1, 0):
            half = half // 2
            total = total[:half] + self.step(total[half:], level)
        return total[0]


def place_kernel(meta, *refs):
    pieces, out_ref = refs[:4], refs[4]
    for k in range(4):
        out_ref[meta[5] ^ k] = pieces[k][...]


def place_group(meta, pieces):
    rows, columns = pieces[0].shape
    tile = columns // 2
    return pl.pallas_call(
        place_kernel,
        grid_spec=pltpu.PrefetchScalarGridSpec(
            num_scalar_prefetch=1, grid=(2,), in_specs=[pl.BlockSpec((rows, tile), lambda n, meta: (0, n))] * 4,
            out_specs=pl.BlockSpec((4, rows, tile), lambda n, meta: (0, 0, n))),
        out_shape=jax.ShapeDtypeStruct((4, rows, columns), pieces[0].dtype),
        cost_estimate=cost(2),
        name="place_group",
    )(meta, *pieces)


def spread_kernel(meta, *refs):
    parts, outs = refs[:16], refs[16:]
    for k in range(4):
        total = sum(part[...].astype(F32) for part in parts[4 * k : 4 * k + 4])
        outs[k][...] = total.astype(outs[k].dtype)


def spread_sums(meta, keep, near, third, second):
    _, rows, columns = second.shape
    tile = columns // 2 if columns > 1024 else columns
    if rows > 32:
        tile = columns // 4
    specs, operands = [], []
    for k in range(4):
        group = pl.BlockSpec((None, rows, tile), lambda n, meta, k=k: (meta[5] ^ k, 0, n))
        pair = pl.BlockSpec((None, None, rows, tile), lambda n, meta, k=k: (0, meta[5] ^ k, 0, n))
        specs += [pair, pair, pair, group]
        operands += [keep, near, third, second]
    out = pl.BlockSpec((rows, tile), lambda n, meta: (0, n))
    return pl.pallas_call(
        spread_kernel,
        grid_spec=pltpu.PrefetchScalarGridSpec(num_scalar_prefetch=1, grid=(columns // tile,), in_specs=specs, out_specs=[out] * 4),
        out_shape=[jax.ShapeDtypeStruct((rows, columns), F32)] + [jax.ShapeDtypeStruct((rows, columns), BF16)] * 3,
        cost_estimate=cost(3),
        name="spread_sums",
    )(meta, *operands)


class Gather:
    def __init__(self, ladder, shard, direct):
        self.ladder, self.shard, self.native, self.direct = ladder, shard, ladder.native, direct
        self.sent = ()

    def start(self, *after):
        if not self.native:
            self.shard = tie(self.shard, *after)
            self.sent = (self.shard,)
            bits = Z_HOPS if self.direct else Z_HOPS[1:2]
            self.others = [self.ladder.flip(self.shard, bit, bit) for bit in bits]

    def low(self, *after):
        if not self.native:
            one, two = tie(self.others[0], *after), self.shard
            high = (self.ladder.meta[5] >> 1) == 1
            self.pair = jnp.where(high, jnp.stack([one, two]), jnp.stack([two, one]))
            self.sent = (self.pair,)
            self.others = [self.ladder.flip(self.pair, Z_HOPS[0], Z_HOPS[0])]

    def plane(self, *after):
        if not self.native:
            others = [tie(other, *after) for other in self.others]
            if self.direct:
                self.own = place_group(self.ladder.meta, [self.shard] + others)
            else:
                one, two = others[0], self.pair
                low = (self.ladder.meta[5] & 1) == 1
                own = jnp.where(low, jnp.stack([one, two], 1), jnp.stack([two, one], 1))
                self.own = own.reshape((4,) + self.shard.shape)
            self.sent = (self.own,)
            self.second = self.ladder.step(self.own, 2)
            self.third = self.ladder.step(self.own, 3)
            self.far = [self.ladder.across(self.own)]

    def corner(self, *after):
        if not self.native:
            self.second, self.third = tie(self.second, *after), tie(self.third, *after)
            self.sent = (self.second, self.third)
            self.fourth = self.ladder.step(self.second, 3)
            self.far += [self.ladder.across(self.third), self.ladder.across(self.second)]

    def finish(self, *after):
        if self.native:
            self.groups = [lax.all_gather(self.shard, self.ladder.axes, axis=0, tiled=True)]
        else:
            self.fourth = tie(self.fourth, *after)
            self.sent = (self.fourth,)
            self.far += [self.ladder.across(self.fourth)]
            self.groups = [self.own, self.second, self.third, self.fourth] + self.far
        return self.groups


class Scatter:
    def __init__(self, ladder, parts):
        self.ladder, self.native, self.parts = ladder, ladder.native, parts
        self.sent = ()
        if not self.native:
            self.keep = parts[0]
            self.near = ladder.across(parts[1])

    def corner(self, *after):
        if not self.native:
            self.near = tie(self.near, *after)
            total = add_up(self.keep[2:], self.near[2:]).astype(BF16)
            self.sent = (total,)
            self.third = self.ladder.step(total, 3)

    def plane(self, *after):
        if not self.native:
            self.third = tie(self.third, *after)
            total = add_up(self.keep[1], self.near[1], self.third[1]).astype(BF16)
            self.sent = (total,)
            self.second = self.ladder.step(total, 2)

    def spread(self, *after):
        if not self.native:
            second = tie(self.second, *after)
            self.mine, *away = spread_sums(self.ladder.meta, self.keep, self.near, self.third, second)
            self.sent = tuple(away)
            self.last = [self.ladder.flip(part, bit, bit) for part, bit in zip(away, Z_HOPS)]

    def finish(self, *after):
        if self.native:
            return lax.psum_scatter(self.parts[0].astype(F32), self.ladder.axes, scatter_dimension=0, tiled=True)
        total = add_up(self.mine, *[tie(part, *after) for part in self.last])
        self.sent = (total,)
        return total


def nt(a, b):
    return lax.dot_general(a, b, (((1,), (1,)), ((), ())), preferred_element_type=F32)


def nn(a, b):
    return lax.dot_general(a, b, (((1,), (0,)), ((), ())), preferred_element_type=F32)


def fill_bias(lo_ref, segc_ref, padc_ref, segr_ref, bias_ref, nblocks, most):
    def one(qb, _):
        lo = lo_ref[qb]
        q0 = pl.multiple_of(qb * QB, QB)
        segq = segr_ref[pl.ds(qb, 1), :]
        qpos = q0 + lax.broadcasted_iota(jnp.int32, (QB, QB), 1)

        def part(j, _):
            k0 = pl.multiple_of((lo + j) * QB, QB)
            kpos = k0 + lax.broadcasted_iota(jnp.int32, (QB, QB), 0)
            segk = segc_ref[pl.ds(k0, QB), :]
            padk = padc_ref[pl.ds(k0, QB), :]
            ok = (segk == segq) & (kpos <= qpos) & ((padk == 1) | (kpos == qpos))
            bias_ref[qb, pl.ds(pl.multiple_of(j * QB, QB), QB), :] = jnp.where(ok, 0.0, -1e30)
            return 0

        lax.fori_loop(0, qb - lo + 1, part, 0)
        return 0

    lax.fori_loop(0, nblocks, one, 0)


def head_pair(x, scale):
    lane = lax.broadcasted_iota(jnp.int32, x.shape, 1)
    first = jnp.where(lane < HD, scale, 0.0).astype(x.dtype)
    second = jnp.where(lane < HD, 0.0, scale).astype(x.dtype)
    return jnp.concatenate([x * first, x * second], 0)


def attn_fwd_kernel(nblocks, most, many, lo_ref, segc_ref, padc_ref, segr_ref, q_ref, k_ref, v_ref, o_ref, lse_ref, bias_ref, vt_ref):
    @pl.when(pl.program_id(0) == 0)
    def _():
        fill_bias(lo_ref, segc_ref, padc_ref, segr_ref, bias_ref, nblocks, most)

    vt_ref[...] = v_ref[...].T

    def block(qb, _):
        lo = lo_ref[qb]
        q0 = pl.multiple_of(qb * QB, QB)
        k0 = pl.multiple_of(lo * QB, QB)
        for n in range(1, most + 1):
            @pl.when(qb - lo + 1 == n)
            def _(n=n):
                w = n * QB
                bias = bias_ref[qb, 0:w, :]
                bias = jnp.concatenate([bias, bias], 1)
                cols = [slice(128 * i, 128 * (i + 1)) for i in range(many)]
                scores = [nt(k_ref[pl.ds(k0, w), c], head_pair(q_ref[pl.ds(q0, QB), c], HD ** -0.5)) + bias for c in cols]
                tops = [jnp.max(s, 0, keepdims=True) for s in scores]
                parts = [jnp.exp(s - m) for s, m in zip(scores, tops)]
                totals = [jnp.sum(p, 0, keepdims=True) for p in parts]
                outs = [nn(vt_ref[c, pl.ds(k0, w)], (p * (1.0 / t)).astype(BF16)) for c, p, t in zip(cols, parts, totals)]
                for i, (c, o, m, t) in enumerate(zip(cols, outs, tops, totals)):
                    o = jnp.concatenate([o[:HD, :QB], o[HD:, QB:]], 0)
                    o_ref[pl.ds(q0, QB), c] = o.T.astype(BF16)
                    lse_ref[i, pl.ds(qb, 1), :] = m + jnp.log(t)
        return 0

    lax.fori_loop(0, nblocks, block, 0)


def attn_bwd_kernel(nblocks, most, many, lo_ref, segc_ref, padc_ref, segr_ref, q_ref, k_ref, v_ref, do_ref, lse_ref,
                    out_ref, sums_ref, bias_ref, kt_ref, dk_acc, dv_acc):
    @pl.when(pl.program_id(0) == 0)
    def _():
        fill_bias(lo_ref, segc_ref, padc_ref, segr_ref, bias_ref, nblocks, most)

    kt_ref[...] = k_ref[...].T
    dk_acc[...] = jnp.zeros_like(dk_acc)
    dv_acc[...] = jnp.zeros_like(dv_acc)
    sums_ref[...] = jnp.zeros_like(sums_ref)

    def block(qb, _):
        lo = lo_ref[qb]
        q0 = pl.multiple_of(qb * QB, QB)
        k0 = pl.multiple_of(lo * QB, QB)
        for n in range(1, most + 1):
            @pl.when(qb - lo + 1 == n)
            def _(n=n):
                w = n * QB
                bias = bias_ref[qb, 0:w, :]
                bias = jnp.concatenate([bias, bias], 1)
                cols = [slice(128 * i, 128 * (i + 1)) for i in range(many)]
                rows, keys = pl.ds(q0, QB), pl.ds(k0, w)
                q2 = [head_pair(q_ref[rows, c], HD ** -0.5) for c in cols]
                do2 = [head_pair(do_ref[rows, c], 1.0) for c in cols]
                probs = [jnp.exp(nt(k_ref[keys, c], q) + bias - lse_ref[i, pl.ds(qb, 1), :]) for i, (c, q) in enumerate(zip(cols, q2))]
                dprobs = [nt(v_ref[keys, c], do) for c, do in zip(cols, do2)]
                inner = [jnp.sum(p * dp, 0, keepdims=True) for p, dp in zip(probs, dprobs)]
                ds = [(p * (dp - i)).astype(BF16) for p, dp, i in zip(probs, dprobs, inner)]
                for c, p, d, q, do in zip(cols, probs, ds, q2, do2):
                    dv_acc[keys, c] += nn(p.astype(BF16), do)
                    dk_acc[keys, c] += nn(d, q)
                    dq = nn(kt_ref[c, keys], d)
                    dq = jnp.concatenate([dq[:HD, :QB], dq[HD:, QB:]], 0) * (HD ** -0.5)
                    dq = dq.T.astype(BF16)
                    out_ref[0, rows, c] = dq
                    sums_ref[0:1, c] += jnp.sum(dq.astype(F32), 0, keepdims=True)
        return 0

    lax.fori_loop(0, nblocks, block, 0)
    out_ref[1] = dk_acc[...].astype(BF16)
    dv = dv_acc[...].astype(BF16)
    out_ref[2] = dv
    sums_ref[1:2, :] = jnp.sum(dv.astype(F32), 0, keepdims=True)


def mask_inputs(segment_ids, padding_mask):
    length = segment_ids.shape[0]
    nblocks = length // QB
    first = segment_ids.reshape(nblocks, QB)[:, 0]
    start = jnp.sum((segment_ids[None, :] < first[:, None]).astype(jnp.int32), 1)
    lo = start // QB
    segc = jnp.broadcast_to(segment_ids[:, None], (length, QB))
    padc = jnp.broadcast_to(padding_mask[:, None], (length, QB))
    return lo.astype(jnp.int32), segc, padc, segment_ids.reshape(nblocks, QB)


def attn_forward(q, k, v, masks, first=0, pairs=None):
    length, many = q[0].shape[0], MANY
    width = 128 * many
    nblocks = length // QB
    most = min(nblocks, SPAN // QB + 1)
    pairs = pairs or 8
    lo, segc, padc, segr = masks
    (qa, qo), (ka, ko), (va, vo) = q, k, v
    whole = lambda p, lo: (0, 0)
    col = lambda off: pl.BlockSpec((length, width), lambda p, lo: (0, (off + first) // many + p))
    return pl.pallas_call(
        functools.partial(attn_fwd_kernel, nblocks, most, many),
        grid_spec=pltpu.PrefetchScalarGridSpec(
            num_scalar_prefetch=1, grid=(pairs // many,),
            in_specs=[pl.BlockSpec((length, QB), whole), pl.BlockSpec((length, QB), whole), pl.BlockSpec((nblocks, QB), whole),
                      col(qo), col(ko), col(vo)],
            out_specs=[pl.BlockSpec((length, width), lambda p, lo: (0, p)),
                       pl.BlockSpec((many, nblocks, 2 * QB), lambda p, lo: (p, 0, 0))],
            scratch_shapes=[pltpu.VMEM((nblocks, most * QB, QB), F32), pltpu.VMEM((width, length), BF16)]),
        out_shape=[jax.ShapeDtypeStruct((length, pairs * 128), BF16), jax.ShapeDtypeStruct((pairs, nblocks, 2 * QB), F32)],
        compiler_params=pltpu.CompilerParams(vmem_limit_bytes=48 << 20),
        cost_estimate=cost(11),
        name="attn_forward",
    )(lo, segc, padc, segr, qa, ka, va)


def attn_backward(q, k, v, do, lse, masks, first=0, pairs=None):
    length, many = q[0].shape[0], MANY
    width = 128 * many
    nblocks = length // QB
    most = min(nblocks, SPAN // QB + 1)
    pairs = pairs or 8
    lo, segc, padc, segr = masks
    (qa, qo), (ka, ko), (va, vo) = q, k, v
    whole = lambda p, lo: (0, 0)
    col = lambda off: pl.BlockSpec((length, width), lambda p, lo: (0, (off + first) // many + p))
    return pl.pallas_call(
        functools.partial(attn_bwd_kernel, nblocks, most, many),
        grid_spec=pltpu.PrefetchScalarGridSpec(
            num_scalar_prefetch=1, grid=(pairs // many,),
            in_specs=[pl.BlockSpec((length, QB), whole), pl.BlockSpec((length, QB), whole), pl.BlockSpec((nblocks, QB), whole),
                      col(qo), col(ko), col(vo), col(0),
                      pl.BlockSpec((many, nblocks, 2 * QB), lambda p, lo: (first // many + p, 0, 0))],
            out_specs=[pl.BlockSpec((3, length, width), lambda p, lo: (0, 0, p)), pl.BlockSpec((8, width), lambda p, lo: (0, p))],
            scratch_shapes=[pltpu.VMEM((nblocks, most * QB, QB), F32), pltpu.VMEM((width, length), BF16),
                            pltpu.VMEM((length, width), F32), pltpu.VMEM((length, width), F32)]),
        out_shape=[jax.ShapeDtypeStruct((3, length, pairs * 128), BF16), jax.ShapeDtypeStruct((8, pairs * 128), F32)],
        compiler_params=pltpu.CompilerParams(vmem_limit_bytes=48 << 20),
        cost_estimate=cost(16),
        name="attn_backward",
    )(lo, segc, padc, segr, qa, ka, va, do, lse)


ANY = pl.BlockSpec(memory_space=pl.ANY)
META = 1


def params(megabytes=56):
    return pltpu.CompilerParams(vmem_limit_bytes=megabytes << 20)


def tile_shape(native, rows, columns):
    return (1, 1, 1, rows, columns) if native else (4, 4, 2, rows // 32, columns)


def fetch_columns(native, meta, groups, target, start, columns, sem):
    cols = pl.ds(start, columns)
    if native:
        pltpu.make_async_copy(groups[0].at[:, cols], target.at[0, 0, 0], sem).start()
        return
    core = meta[4]
    for t in range(4):
        pltpu.make_async_copy(groups[t].at[:, :, cols], target.at[meta[t], :, core], sem).start()
        pltpu.make_async_copy(groups[4 + t].at[:, :, cols], target.at[meta[t], :, 1 - core], sem).start()


def quarter_shape(native, rows, columns):
    return (1, 1, rows // 4, columns) if native else (4, 2, rows // 32, columns)


def fetch_quarter(native, meta, groups, target, t, sem):
    if native:
        rows = target.shape[-2]
        pltpu.make_async_copy(groups[0].at[pl.ds(t * rows, rows), :], target.at[0, 0], sem).start()
        return
    core = meta[4]
    pltpu.make_async_copy(groups[t], target.at[:, core], sem).start()
    pltpu.make_async_copy(groups[4 + t], target.at[:, 1 - core], sem).start()


def arrive(target, sem):
    pltpu.make_async_copy(target, target, sem).wait()


def group_specs(groups):
    return [ANY] * len(groups)


def flat(value):
    return value.reshape(-1, value.shape[-1])


def out_blocks(native, rows, columns):
    if native:
        return [jax.ShapeDtypeStruct((rows, columns), BF16)]
    return [jax.ShapeDtypeStruct((4, 4, rows // 32, columns), BF16)] * 2


def push_columns(native, meta, stage, outs, start, columns, sem):
    cols = pl.ds(start, columns)
    if native:
        pltpu.make_async_copy(stage.at[0, 0, 0], outs[0].at[:, cols], sem).start()
        return
    core = meta[4]
    for t in range(4):
        pltpu.make_async_copy(stage.at[meta[t], :, core], outs[0].at[t, :, :, cols], sem).start()
        pltpu.make_async_copy(stage.at[meta[t], :, 1 - core], outs[1].at[FLIP[t], :, :, cols], sem).start()


def squares(values, valid):
    return jnp.sum(values * values * valid, 0, keepdims=True)


def scale_of(values):
    return lax.rsqrt(jnp.mean(values * values, -1, keepdims=True) + 1e-05)


def project_kernel(native, tile, meta, tok_ref, gain_ref, valid_ref, bias_ref, *rest):
    groups, (out_ref, normed_ref, sq_ref, weight, sems) = rest[:-5], rest[-5:]
    n, steps = pl.program_id(0), pl.num_programs(0)

    @pl.when(n == 0)
    def _():
        fetch_columns(native, meta, groups, weight.at[0], 0, tile, sems.at[0])

    @pl.when(n + 1 < steps)
    def _():
        slot = (n + 1) % 2
        fetch_columns(native, meta, groups, weight.at[slot], pl.multiple_of((n + 1) * tile, tile), tile, sems.at[slot])

    @pl.when(n == 0)
    def _():
        frames = tok_ref[...].astype(F32)
        sq_ref[...] = squares(frames, valid_ref[...])
        normed_ref[...] = (frames * scale_of(frames) * gain_ref[...]).astype(BF16)

    arrive(weight.at[n % 2], sems.at[n % 2])
    out_ref[...] = (nn(normed_ref[...], flat(weight[n % 2])) + bias_ref[...]).astype(BF16)


def project(ladder, tokens, gain, valid, bias, groups):
    length, width = tokens.shape
    columns, tile = bias.shape[1], 512
    whole = lambda n, meta: (0, 0)
    return pl.pallas_call(
        functools.partial(project_kernel, ladder.native, tile),
        grid_spec=pltpu.PrefetchScalarGridSpec(
            num_scalar_prefetch=1, grid=(columns // tile,),
            in_specs=[pl.BlockSpec((length, width), whole), pl.BlockSpec((1, width), whole), pl.BlockSpec((length, 1), whole),
                      pl.BlockSpec((1, tile), lambda n, meta: (0, n))] + group_specs(groups),
            out_specs=[pl.BlockSpec((length, tile), lambda n, meta: (0, n)), pl.BlockSpec((length, width), whole),
                       pl.BlockSpec((1, width), whole)],
            scratch_shapes=[pltpu.VMEM((2,) + tile_shape(ladder.native, width, tile), BF16), pltpu.SemaphoreType.DMA((2,))]),
        out_shape=[jax.ShapeDtypeStruct((length, columns), BF16), jax.ShapeDtypeStruct((length, width), BF16),
                   jax.ShapeDtypeStruct((1, width), F32)],
        compiler_params=params(),
        cost_estimate=cost(14),
        name="project",
    )(ladder.meta, tokens, gain, valid, bias, *groups)


def gelu_pair(u):
    c, d = 0.7978845608028654, 0.044715
    square = u * u
    bend = 0.5 * jnp.tanh(u * (c + c * d * square))
    half = 0.5 + bend
    slope = half * (1.0 + (0.5 - bend) * (u * (2.0 * c + 6.0 * c * d * square)))
    return (u * half).astype(BF16), slope.astype(BF16)


def expand_kernel(native, tile, count, meta, mixed_ref, tok_ref, bias_ref, gain_ref, valid_ref, up_bias_ref, *rest):
    groups, rest = rest[:count], rest[count:]
    middle_ref, normed_ref, sq_ref, act_ref, slope_ref, middle, out_weight, weight, sems = rest
    n, steps = pl.program_id(0), pl.num_programs(0)
    half = out_weight.shape[-1]
    first = 2 * half
    store = pltpu.make_async_copy(middle, middle_ref, sems.at[4])

    @pl.when(n == 0)
    def _():
        for side in range(2):
            fetch_columns(native, meta, groups, out_weight.at[side], side * half, half, sems.at[2 + side])
        fetch_columns(native, meta, groups, weight.at[0], first, tile, sems.at[0])

    @pl.when(n + 1 < steps)
    def _():
        slot = (n + 1) % 2
        fetch_columns(native, meta, groups, weight.at[slot], pl.multiple_of(first + (n + 1) * tile, tile), tile, sems.at[slot])

    @pl.when(n == 0)
    def _():
        for side in range(2):
            arrive(out_weight.at[side], sems.at[2 + side])
        sq_ref[...] = jnp.zeros_like(sq_ref)
        rows = 256

        def part(i, _):
            at = pl.ds(pl.multiple_of(i * rows, rows), rows)
            branch = jnp.concatenate([nn(mixed_ref[at, :], flat(out_weight[side])) for side in range(2)], 1) + bias_ref[...]
            total = tok_ref[at, :].astype(F32) + branch
            middle[at, :] = total
            normed_ref[at, :] = (total * scale_of(total) * gain_ref[...]).astype(BF16)
            sq_ref[0:1, :] += squares(branch, valid_ref[at, :])
            sq_ref[1:2, :] += squares(total, valid_ref[at, :])
            return 0

        lax.fori_loop(0, middle.shape[0] // rows, part, 0)
        store.start()

    arrive(weight.at[n % 2], sems.at[n % 2])
    act_ref[...], slope_ref[...] = gelu_pair(nn(normed_ref[...], flat(weight[n % 2])) + up_bias_ref[...])

    @pl.when(n == steps - 1)
    def _():
        store.wait()


def expand(ladder, mixed, tokens, bias, gain, valid, up_bias, groups):
    length, width = tokens.shape
    columns, tile = up_bias.shape[1], 512
    whole = lambda n, meta: (0, 0)
    column = lambda n, meta: (0, n)
    square, line = pl.BlockSpec((length, width), whole), pl.BlockSpec((1, width), whole)
    return pl.pallas_call(
        functools.partial(expand_kernel, ladder.native, tile, len(groups)),
        grid_spec=pltpu.PrefetchScalarGridSpec(
            num_scalar_prefetch=1, grid=(columns // tile,),
            in_specs=[square, square, line, line, pl.BlockSpec((length, 1), whole), pl.BlockSpec((1, tile), column)]
            + group_specs(groups),
            out_specs=[ANY, square, pl.BlockSpec((8, width), whole), pl.BlockSpec((length, tile), column),
                       pl.BlockSpec((length, tile), column)],
            scratch_shapes=[pltpu.VMEM((length, width), F32),
                            pltpu.VMEM((2,) + tile_shape(ladder.native, width, width // 2), BF16),
                            pltpu.VMEM((2,) + tile_shape(ladder.native, width, tile), BF16), pltpu.SemaphoreType.DMA((5,))]),
        out_shape=[jax.ShapeDtypeStruct((length, width), F32), jax.ShapeDtypeStruct((length, width), BF16),
                   jax.ShapeDtypeStruct((8, width), F32)] + [jax.ShapeDtypeStruct((length, columns), BF16)] * 2,
        compiler_params=params(),
        cost_estimate=cost(29),
        name="expand",
    )(ladder.meta, mixed, tokens, bias, gain, valid, up_bias, *groups)


def fetch_turn(native, meta, groups, weight, sems, t, first=0, last=3):
    for at in range(first, last + 1):
        @pl.when(t == max(at - 1, first))
        def _(at=at):
            fetch_quarter(native, meta, groups, weight.at[at % 2], at, sems.at[at % 2])

    arrive(weight.at[t % 2], sems.at[t % 2])


def tn(a, b):
    return lax.dot_general(a, b, (((0,), (0,)), ((), ())), preferred_element_type=F32)


def down_grad_kernel(native, count, meta, act_ref, cot_ref, *rest):
    outs, (sum_ref, stage, sems) = rest[:count], rest[count:]
    t = pl.program_id(0)
    slot = t % 2

    @pl.when(t >= 2)
    def _():
        arrive(stage.at[slot], sems.at[slot])

    stage[slot] = tn(act_ref[...], cot_ref[...]).astype(BF16).reshape(stage.shape[1:])
    if native:
        rows = stage.shape[-2]
        pltpu.make_async_copy(stage.at[slot, 0, 0], outs[0].at[pl.ds(t * rows, rows), :], sems.at[slot]).start()
    else:
        for k in range(4):
            @pl.when(t == k)
            def _(k=k):
                pltpu.make_async_copy(stage.at[slot, :, meta[4]], outs[0].at[k], sems.at[slot]).start()
                pltpu.make_async_copy(stage.at[slot, :, 1 - meta[4]], outs[1].at[FLIP[k]], sems.at[slot]).start()

    @pl.when(t == 0)
    def _():
        sum_ref[...] = jnp.sum(cot_ref[...].astype(F32), 0, keepdims=True)

    @pl.when(t == 3)
    def _():
        arrive(stage.at[1 - slot], sems.at[1 - slot])
        arrive(stage.at[slot], sems.at[slot])


def down_grad(ladder, act, cot):
    length, width = cot.shape
    hidden = act.shape[1]
    outs = out_blocks(ladder.native, hidden, width)
    whole = lambda t, meta: (0, 0)
    return pl.pallas_call(
        functools.partial(down_grad_kernel, ladder.native, len(outs)),
        grid_spec=pltpu.PrefetchScalarGridSpec(
            num_scalar_prefetch=1, grid=(4,),
            in_specs=[pl.BlockSpec((length, hidden // 4), lambda t, meta: (0, meta[t])), pl.BlockSpec((length, width), whole)],
            out_specs=[ANY] * len(outs) + [pl.BlockSpec((1, width), whole)],
            scratch_shapes=[pltpu.VMEM((2,) + quarter_shape(ladder.native, hidden, width), BF16), pltpu.SemaphoreType.DMA((2,))]),
        out_shape=outs + [jax.ShapeDtypeStruct((1, width), F32)],
        compiler_params=params(),
        cost_estimate=cost(14),
        name="down_grad",
    )(ladder.meta, act, cot)


def row_grad_kernel(native, tile, count, meta, left_ref, right_ref, *rest):
    outs, (stage, sems) = rest[:count], rest[count:]
    n, steps = pl.program_id(0), pl.num_programs(0)
    slot = n % 2

    @pl.when(n >= 2)
    def _():
        arrive(stage.at[slot], sems.at[slot])

    stage[slot] = tn(left_ref[...], right_ref[...]).astype(BF16).reshape(stage.shape[1:])
    push_columns(native, meta, stage.at[slot], outs, pl.multiple_of(n * tile, tile), tile, sems.at[slot])

    @pl.when(n == steps - 1)
    def _():
        arrive(stage.at[1 - slot], sems.at[1 - slot])
        arrive(stage.at[slot], sems.at[slot])


def row_grad(ladder, left, right, name):
    length, width = left.shape
    parts, _, each = right.shape
    tile = 512
    per = each // tile
    outs = out_blocks(ladder.native, width, parts * each)
    return pl.pallas_call(
        functools.partial(row_grad_kernel, ladder.native, tile, len(outs)),
        grid_spec=pltpu.PrefetchScalarGridSpec(
            num_scalar_prefetch=1, grid=(parts * per,),
            in_specs=[pl.BlockSpec((length, width), lambda n, meta: (0, 0)),
                      pl.BlockSpec((None, length, tile), lambda n, meta: (n // per, 0, n % per))],
            out_specs=[ANY] * len(outs),
            scratch_shapes=[pltpu.VMEM((2,) + tile_shape(ladder.native, width, tile), BF16), pltpu.SemaphoreType.DMA((2,))]),
        out_shape=outs,
        compiler_params=params(),
        cost_estimate=cost(8),
        name=name,
    )(ladder.meta, left, right)


def norm_grad(grad, source, gain):
    r = scale_of(source)
    hat = source * r
    gain_grad = jnp.sum(grad * hat, 0, keepdims=True)
    scaled = grad * gain
    return r * (scaled - hat * jnp.mean(scaled * hat, -1, keepdims=True)), gain_grad


def back_kernel(native, last, counts, meta, cot_ref, slope_ref, normed_ref, gain_ref, middle_ref, mixed_ref, *rest):
    down_groups, rest = rest[: counts[0]], rest[counts[0] :]
    groups, rest = rest[: counts[0]], rest[counts[0] :]
    if last:
        before, rest = rest[0], rest[1 + counts[1] :]
    pushed, rest = rest[: counts[1]], rest[counts[1] :]
    if last:
        out_ref, branch_ref, mixed_out_ref, sum_ref, up_sum_ref, rest = *rest[:5], rest[5:]
        acc, down_weight, weight, stage, sems, middle, out_weight, out_stage = rest
    else:
        after, up_sum_ref, acc, down_weight, weight, stage, sems = rest
    base = 2 if last else 0
    step = pl.program_id(0)
    t = step + base
    width, tile = normed_ref.shape[1], slope_ref.shape[1]
    slot = step

    def columns(at):
        return pl.multiple_of(width + meta[at] * tile, 512)

    @pl.when(step == 0)
    def _():
        for at in range(2):
            fetch_columns(native, meta, groups, weight.at[at], columns(base + at), tile, sems.at[2 + at])
        if last:
            pltpu.make_async_copy(before, acc, sems.at[6]).start()
            pltpu.make_async_copy(middle_ref, middle, sems.at[7]).start()
            fetch_columns(native, meta, groups, out_weight, 0, width, sems.at[8])

    fetch_turn(native, meta, down_groups, down_weight, sems, t, base, base + 1)
    grad = (nt(cot_ref[...], flat(down_weight[t % 2])) * slope_ref[...].astype(F32)).astype(BF16)
    up_sum_ref[...] = jnp.sum(grad.astype(F32), 0, keepdims=True)
    stage[slot] = tn(normed_ref[...], grad).astype(BF16).reshape(stage.shape[1:])
    push_columns(native, meta, stage.at[slot], pushed, columns(t), tile, sems.at[4 + slot])
    arrive(weight.at[slot], sems.at[2 + slot])
    product = nt(grad, flat(weight[slot]))

    @pl.when(step == 0)
    def _():
        if last:
            pltpu.make_async_copy(before, acc, sems.at[6]).wait()
            acc[...] += product
        else:
            acc[...] = product

    @pl.when(step == 1)
    def _():
        acc[...] += product
        if last:
            pltpu.make_async_copy(middle_ref, middle, sems.at[7]).wait()
            sum_ref[...] = jnp.zeros_like(sum_ref)
            rows = 256

            def part(i, _):
                at = pl.ds(pl.multiple_of(i * rows, rows), rows)
                back, gain_grad = norm_grad(acc[at, :], middle[at, :], gain_ref[...])
                total = cot_ref[at, :].astype(F32) + back
                acc[at, :] = total
                branch = total.astype(BF16)
                branch_ref[at, :] = branch
                sum_ref[0:1, :] += gain_grad
                sum_ref[1:2, :] += jnp.sum(branch.astype(F32), 0, keepdims=True)
                return 0

            lax.fori_loop(0, acc.shape[0] // rows, part, 0)
            pltpu.make_async_copy(acc, out_ref, sems.at[6]).start()
            out_stage[...] = tn(mixed_ref[...], branch_ref[...]).astype(BF16).reshape(out_stage.shape)
            push_columns(native, meta, out_stage, pushed, 0, width, sems.at[7])
            arrive(out_weight, sems.at[8])
            mixed_out_ref[...] = nt(branch_ref[...], flat(out_weight[...])).astype(BF16)
            arrive(out_stage, sems.at[7])
            pltpu.make_async_copy(acc, out_ref, sems.at[6]).wait()
        else:
            pltpu.make_async_copy(acc, after, sems.at[6]).start()
            pltpu.make_async_copy(acc, after, sems.at[6]).wait()
        for at in range(2):
            arrive(stage.at[at], sems.at[4 + at])


def back(ladder, cot, slope, normed, gain, middle, mixed, down_groups, groups, before=None):
    length, width = cot.shape
    hidden, tile = slope.shape[1], slope.shape[1] // 4
    last = before is not None
    base = 2 if last else 0
    whole = lambda t, meta: (0, 0)
    part = lambda t, meta: (0, meta[t + base])
    square = pl.BlockSpec((length, width), whole)
    once = pl.BlockSpec((length, width), whole, pipeline_mode=pl.Buffered(1))
    outs = out_blocks(ladder.native, width, hidden + width)
    counts = (len(groups), len(outs))
    full, wide = jax.ShapeDtypeStruct((length, width), F32), jax.ShapeDtypeStruct((length, width), BF16)
    sums = jax.ShapeDtypeStruct((1, hidden), F32)
    in_specs = [once, pl.BlockSpec((length, tile), part), once, pl.BlockSpec((1, width), whole), ANY, once if last else ANY]
    in_specs += [ANY] * (2 * counts[0])
    operands = [ladder.meta, cot, slope, normed, gain, middle, mixed, *down_groups, *groups]
    scratch = [pltpu.VMEM((length, width), F32), pltpu.VMEM((2,) + quarter_shape(ladder.native, hidden, width), BF16),
               pltpu.VMEM((2,) + tile_shape(ladder.native, width, tile), BF16),
               pltpu.VMEM((2,) + tile_shape(ladder.native, width, tile), BF16), pltpu.SemaphoreType.DMA((9,))]
    aliases = {}
    if last:
        aliases = {len(operands) + 1 + i: i for i in range(counts[1])}
        operands += list(before)
        in_specs += [ANY] * (1 + counts[1])
        out_specs = [ANY] * counts[1] + [ANY, square, square, pl.BlockSpec((8, width), whole)]
        out_shape = outs + [full, wide, wide, jax.ShapeDtypeStruct((8, width), F32)]
        scratch += [pltpu.VMEM((length, width), F32), pltpu.VMEM(tile_shape(ladder.native, width, width), BF16),
                    pltpu.VMEM(tile_shape(ladder.native, width, width), BF16)]
    else:
        out_specs, out_shape = [ANY] * counts[1] + [ANY], outs + [full]
    return pl.pallas_call(
        functools.partial(back_kernel, ladder.native, last, counts),
        grid_spec=pltpu.PrefetchScalarGridSpec(
            num_scalar_prefetch=1, grid=(2,), in_specs=in_specs, out_specs=out_specs + [pl.BlockSpec((1, tile), lambda t, meta: (0, t))],
            scratch_shapes=scratch),
        out_shape=out_shape + [jax.ShapeDtypeStruct((1, hidden // 2), F32)],
        input_output_aliases=aliases,
        compiler_params=params(),
        cost_estimate=cost(30 if last else 20),
        name="back",
    )(*operands)


def contract_kernel(native, meta, act_ref, bias_ref, valid_ref, middle_ref, *rest):
    groups, (out_ref, sq_ref, acc, middle, weight, sems) = rest[:-6], rest[-6:]
    t = pl.program_id(0)
    load = pltpu.make_async_copy(middle_ref, middle, sems.at[2])

    @pl.when(t == 0)
    def _():
        load.start()

    fetch_turn(native, meta, groups, weight, sems, t)
    product = nn(act_ref[...], flat(weight[t % 2]))

    @pl.when(t == 0)
    def _():
        acc[...] = product

    @pl.when(t > 0)
    def _():
        acc[...] += product

    @pl.when(t == 3)
    def _():
        load.wait()
        sq_ref[...] = jnp.zeros_like(sq_ref)
        rows = 256

        def part(i, _):
            at = pl.ds(pl.multiple_of(i * rows, rows), rows)
            branch = acc[at, :] + bias_ref[...]
            final = middle[at, :] + branch
            out_ref[at, :] = final.astype(BF16)
            sq_ref[0:1, :] += squares(branch, valid_ref[at, :])
            sq_ref[1:2, :] += squares(final, valid_ref[at, :])
            return 0

        lax.fori_loop(0, acc.shape[0] // rows, part, 0)


def contract(ladder, act, middle, bias, valid, groups):
    length, width = middle.shape
    hidden = act.shape[1]
    whole = lambda t, meta: (0, 0)
    return pl.pallas_call(
        functools.partial(contract_kernel, ladder.native),
        grid_spec=pltpu.PrefetchScalarGridSpec(
            num_scalar_prefetch=1, grid=(4,),
            in_specs=[pl.BlockSpec((length, hidden // 4), lambda t, meta: (0, meta[t])), pl.BlockSpec((1, width), whole),
                      pl.BlockSpec((length, 1), whole), ANY] + group_specs(groups),
            out_specs=[pl.BlockSpec((length, width), whole), pl.BlockSpec((8, width), whole)],
            scratch_shapes=[pltpu.VMEM((length, width), F32), pltpu.VMEM((length, width), F32),
                            pltpu.VMEM((2,) + quarter_shape(ladder.native, hidden, width), BF16), pltpu.SemaphoreType.DMA((3,))]),
        out_shape=[jax.ShapeDtypeStruct((length, width), BF16), jax.ShapeDtypeStruct((8, width), F32)],
        compiler_params=params(),
        cost_estimate=cost(16),
        name="contract",
    )(ladder.meta, act, bias, valid, middle, *groups)


def input_grad_kernel(native, calls, meta, *rest):
    grads, (tok_ref, middle_ref, gain_ref), rest = rest[:calls], rest[calls : calls + 3], rest[calls + 3 :]
    groups, (out_ref, sum_ref, acc, middle, weight, sems) = rest[:-6], rest[-6:]
    t = pl.program_id(0)
    load = pltpu.make_async_copy(middle_ref, middle, sems.at[2])

    @pl.when(t == 0)
    def _():
        load.start()

    fetch_turn(native, meta, groups, weight, sems, t)
    width = acc.shape[1]
    quarter = width // 4
    rows = flat(weight[t % 2])
    each = width // calls
    product = 0.0
    for part in range(3):
        for call in range(calls):
            first = part * width + call * each
            product += nt(grads[call][part], rows[:, first : first + each])
    acc[:, pl.ds(pl.multiple_of(meta[t] * quarter, quarter), quarter)] = product

    @pl.when(t == 3)
    def _():
        load.wait()
        sum_ref[...] = jnp.zeros_like(sum_ref)
        rows = 256

        def part(i, _):
            at = pl.ds(pl.multiple_of(i * rows, rows), rows)
            back, gain_grad = norm_grad(acc[at, :], tok_ref[at, :].astype(F32), gain_ref[...])
            out_ref[at, :] = (middle[at, :] + back).astype(BF16)
            sum_ref[0:1, :] += gain_grad
            return 0

        lax.fori_loop(0, acc.shape[0] // rows, part, 0)


def input_grad(ladder, grads, tokens, grad_middle, gain, groups):
    length, width = tokens.shape
    calls = len(grads)
    whole = lambda t, meta: (0, 0)
    square = pl.BlockSpec((length, width), whole)
    return pl.pallas_call(
        functools.partial(input_grad_kernel, ladder.native, calls),
        grid_spec=pltpu.PrefetchScalarGridSpec(
            num_scalar_prefetch=1, grid=(4,),
            in_specs=[pl.BlockSpec((3, length, width // calls), lambda t, meta: (0, 0, 0))] * calls + [square, ANY, pl.BlockSpec((1, width), whole)]
            + group_specs(groups),
            out_specs=[square, pl.BlockSpec((8, width), whole)],
            scratch_shapes=[pltpu.VMEM((length, width), F32), pltpu.VMEM((length, width), F32),
                            pltpu.VMEM((2,) + quarter_shape(ladder.native, width, 3 * width), BF16), pltpu.SemaphoreType.DMA((3,))]),
        out_shape=[jax.ShapeDtypeStruct((length, width), BF16), jax.ShapeDtypeStruct((8, width), F32)],
        compiler_params=params(),
        cost_estimate=cost(18),
        name="input_grad",
    )(ladder.meta, *grads, tokens, grad_middle, gain, *groups)


def local(ladder, tokens, cotangent, segment_ids, padding_mask, w_qkv, bias_qv, w_out, bias_out, gain_attn, gain_mlp,
          w_up, bias_up, w_down, bias_down):
    length, width = tokens.shape[1], tokens.shape[2]
    count = ladder.count
    ladder.place()
    tokens, cotangent = tokens[0], cotangent[0]

    def sent(*flows):
        return [value for flow in flows for value in flow.sent]

    out_up = jnp.concatenate([w_out, w_up], 1)
    qkv = Gather(ladder, w_qkv, True)
    rest, down = Gather(ladder, out_up, False), Gather(ladder, w_down, False)
    qkv.start()
    smalls = [bias_qv, bias_out, gain_attn, gain_mlp, bias_up, bias_down]
    sizes = [s.shape[0] for s in smalls]
    total = sum(sizes)
    ends = np.cumsum([0] + sizes)
    packed = jnp.pad(jnp.concatenate(smalls), (0, -total % 128))
    vectors = ladder.gather_small(packed).astype(F32)
    qv_bias, out_bias, attn_gain, mlp_gain, up_bias, down_bias = [
        vectors[:, ends[i] : ends[i + 1]].reshape(1, -1) for i in range(6)
    ]
    offset = jnp.concatenate([qv_bias[:, :width], jnp.zeros((1, width), F32), qv_bias[:, width:]], 1)
    masks = mask_inputs(segment_ids[0], padding_mask[0])
    valid = padding_mask[0].astype(F32)[:, None]
    qkv.plane(vectors)
    rest.start(*qkv.sent)
    qkv.corner()
    rest.low(*qkv.sent)
    qkv_groups = qkv.finish()
    rest.plane(*qkv.sent)
    projected, normed_in, sq_frames = project(ladder, tie(tokens, *sent(rest)), attn_gain, valid, offset, qkv_groups)
    down.start(projected)
    per = width // 128
    calls = 2
    each = per // calls

    def triple():
        return (projected, 0), (projected, per), (projected, 2 * per)

    mixed_parts, lse_parts = [], []
    for call in range(calls):
        mixed_part, lse_part = attn_forward(*triple(), masks, call * each, each)
        mixed_parts.append(mixed_part)
        lse_parts.append(lse_part)
        if call == 0:
            rest.corner(mixed_part)
            down.low(mixed_part)
            projected = tie(projected, mixed_part, *sent(rest, down))
    down.plane(mixed_parts[-1])
    rest_groups = rest.finish(mixed_parts[-1])
    mixed = jnp.concatenate(mixed_parts, 1)
    lse = jnp.concatenate(lse_parts, 0)
    middle, normed_mid, sq_middle, act, slope = expand(
        ladder, tie(mixed, *sent(down)), tokens, out_bias, mlp_gain, valid, up_bias, rest_groups)

    down.corner(act)
    *down_parts, sum_down = down_grad(ladder, tie(act, *sent(down)), cotangent)
    flow_down = Scatter(ladder, down_parts)
    down_groups = down.finish(sum_down)
    *first_parts, first_acc, first_sum = back(
        ladder, tie(cotangent, sum_down), slope, normed_mid, mlp_gain, middle, mixed, down_groups, rest_groups)
    flow_down.corner(first_acc)
    *rest_parts, grad_middle, grad_branch, grad_mixed, sum_middle, second_sum = back(
        ladder, tie(cotangent, *sent(flow_down)), slope, normed_mid, mlp_gain, middle, mixed, down_groups, rest_groups,
        [first_acc, *first_parts])
    sum_up = jnp.concatenate([first_sum, second_sum], 1).reshape(4, -1)[ladder.order].reshape(1, -1)
    flow_rest = Scatter(ladder, rest_parts)
    flow_down.plane(grad_mixed)
    grad_mixed = tie(grad_mixed, *sent(flow_down))
    grad_parts, sums, flow_qkv = [], [], []
    for call in range(calls):
        part, sum_part = attn_backward(*triple(), grad_mixed, lse, masks, call * each, each)
        if call == 0:
            flow_down.spread(part)
            flow_rest.corner(part)
            part = tie(part, *sent(flow_down, flow_rest))
        else:
            own_down = flow_down.finish(part)
            flow_rest.plane(part)
            flow_qkv[0].corner(part)
            part = tie(part, *sent(flow_down, flow_rest, flow_qkv[0]))
        grad_parts.append(part)
        sums.append(sum_part)
        flow_qkv.append(Scatter(ladder, row_grad(ladder, normed_in, part, "qkv_grad")))
        if call == 0:
            grad_mixed = tie(grad_mixed, *flow_qkv[0].parts)
    sum_qv = jnp.concatenate(sums, 1)
    tail = tie(tokens, *flow_qkv[1].parts)
    grad_tokens, sum_in = input_grad(ladder, grad_parts, tail, grad_middle, attn_gain, qkv_groups)
    flow_rest.spread(grad_tokens)
    flow_qkv[0].plane(grad_tokens)
    flow_qkv[1].corner(grad_tokens)
    act_last = tie(act, grad_tokens, *sent(flow_rest, *flow_qkv))
    output, sq_final = contract(ladder, act_last, middle, down_bias, valid, down_groups)
    own_rest = flow_rest.finish(output)
    flow_qkv[0].spread(output)
    flow_qkv[1].plane(output)
    members = [sq_frames[0], sq_middle[1], sq_final[1], sq_middle[0], sq_final[0]]
    members = jnp.stack([jnp.sum(member) for member in members] + [jnp.sum(valid)])
    small_grads = [sum_qv[:2].reshape(-1), sum_middle[1], sum_in[0], sum_middle[0], sum_up[0], sum_down[0]]
    table = jnp.concatenate([g.reshape(count, -1) for g in small_grads] + [jnp.broadcast_to(members, (count, 6))], 1)
    table = jnp.pad(table, ((0, 0), (0, -table.shape[1] % 128)))
    own_small = ladder.scatter_small(tie(table, *sent(*flow_qkv)))
    flow_qkv[1].spread()
    owns = [flow.finish().reshape(-1, 3, width // calls) for flow in flow_qkv]
    own_qkv = jnp.concatenate(owns, 2).reshape(-1, 3 * width)

    owned = [own_small[ends[i] : ends[i + 1]] for i in range(6)]
    totals = own_small[total : total + 6]
    stats = jnp.sqrt(totals[:5] / (totals[5] * width))
    own_out, own_up = own_rest[:, :width], own_rest[:, width:]
    return (output[None], grad_tokens[None], own_qkv, owned[0], own_out, owned[1], owned[2], owned[3], own_up, owned[4],
            own_down, owned[5], stats, totals[5:6])


def solution(mesh):
    rows, wide, flat = P(("dp", "fsdp"), None, None), P(("dp", "fsdp"), None), P(("dp", "fsdp"))
    return jax.shard_map(
        functools.partial(local, Ladder(mesh)),
        mesh=mesh,
        in_specs=(rows, rows, wide, wide, wide, flat, wide, flat, flat, flat, wide, flat, wide, flat),
        out_specs=(rows, rows, wide, flat, wide, flat, flat, flat, wide, flat, wide, flat, P(), P()),
        check_vma=False,
    )
```

time: 752 us -> 487 us (0.65)
  matrix products: 159 us -> 0 us
  Pallas kernels: 91.9 us -> 242 us
  local copies, waits for them, and re-layouts: 158 us -> 38 us
  waiting for transfers between devices: 173 us -> 90.1 us
  other arithmetic: 105 us -> 41.3 us
  starting transfers between devices: 50.3 us -> 63.8 us
    dot_general x12 -> x0, matrix products: 159 us -> none  [the longest x4 58.6 us: nt(): lax.dot_general(a, b, (((1,), (1,)), ((), ())), preferred_element_type=F32)]
    pallas_call x2 -> x18, Pallas kernels: 91.9 us -> 242 us  [the longest x2 59.2 us: back(): pl.pallas_call(functools.partial(back_kernel, ladder.native, last, counts...]
    ppermute x49 -> x62, waiting for transfers between devices: 173 us -> 90.1 us  [flip(): lax.ppermute(value, self.axes, [(i, i ^ bits[i & CORE]) for i in range(se...]
    gather x10 -> x5, local copies, waits for them, and re-layouts: 55 us -> 3.51 us  [the longest x1 0.86 us: scatter_small(): table = jnp.take(table, self.shard_of, axis=0)]
    unnamed x143 -> x117, local copies, waits for them, and re-layouts: 54.1 us -> 9.38 us
    select_n x13, other arithmetic: 44.1 us -> 5.6 us  [the longest x2 2.64 us: plane(): own = jnp.where(low, jnp.stack([one, two], 1), jnp.stack([two, one], 1))]
    ppermute x49 -> x62, starting transfers between devices: 50.3 us -> 63.8 us  [flip(): lax.ppermute(value, self.axes, [(i, i ^ bits[i & CORE]) for i in range(se...]
    dot_general x1 -> x0, local copies, waits for them, and re-layouts: 11.9 us -> none  [contract_rows(): lax.dot_general(left, right, (((0,), (0,)), ((), ())), preferred_element_...]
  transfers between devices with their start and end apart: 49 -> 62, of which waited for: 18 -> 18; matrix products, arithmetic and copies ran while one was open for 37% -> 13% of each run, Pallas kernels for 12% -> 49%
where the time goes in v2:
time: 487 us; the launch traced here: 478 us
  Pallas kernels  242 us (50%)
  waiting for transfers between devices  90.1 us (19%)
  starting transfers between devices  63.8 us (13%)
  other arithmetic  41.3 us (8%)
  local copies, waits for them, and re-layouts  38 us (8%)
    ppermute x62, waiting for transfers between devices, flip(): lax.ppermute(value, self.axes, [(i, i ^ bits[i & CORE]) for i in range(se...  90.1 us
    ppermute x62, starting transfers between devices, flip(): lax.ppermute(value, self.axes, [(i, i ^ bits[i & CORE]) for i in range(se...  63.8 us
    pallas_call x2, Pallas kernels, back(): pl.pallas_call(functools.partial(back_kernel, ladder.native, last, counts...  59.2 us
    pallas_call x2, Pallas kernels, attn_backward(): pl.pallas_call(functools.partial(attn_bwd_kernel, nblocks, most, many), g...  32.8 us
    pallas_call x1, Pallas kernels, expand(): pl.pallas_call(functools.partial(expand_kernel, ladder.native, tile, len(...  28.8 us
    pallas_call x2, Pallas kernels, attn_forward(): pl.pallas_call(functools.partial(attn_fwd_kernel, nblocks, most, many), g...  22.1 us
    pallas_call x1, Pallas kernels, contract(): pl.pallas_call(functools.partial(contract_kernel, ladder.native), grid_sp...  19.4 us
    pallas_call x1, Pallas kernels, input_grad(): pl.pallas_call(functools.partial(input_grad_kernel, ladder.native, calls)...  17.8 us
  transfers between devices with their start and end apart: 62, of which 18 were waited for; matrix products, arithmetic and copies ran while one was open for 13% of the time, Pallas kernels for 49%

profile of v2, /device:TPU:0, one launch (start us, length us, event | category | flops | bytes accessed | tf_op | source)
XLA Modules:
  0.0 477.8 jit_solution(317263921896656859)
XLA Ops:
  0.6 5.1 %collective-permute-start.7 = (bf16[32,3072]{1,0:T(8,128)(2,1)}, bf16[32,3072]{1,0:T(8,128)(2,1)S(1)}, u32[]{:S(2)}, u32[]{:S(2)}) collective-permute-start(bf16[32,3072]{1,0:T(8,128)(2,1)} %refs_0_), channel_id=1, source_target_pairs={{0,6},{1,7},{2,4},{3,5},{4,2},{5,3},{6,0},{7,1},{8,14},{9,15},{10,... | collective-permute-start | bytes 589832 | tf_op jit(solution)/shard_map/ppermute | solution.py:72
  6.4 4.1 concatenate.79
  10.5 2.3 collective-permute-start.1
  17.3 5.5 %collective-permute-done.1 = bf16[1,384]{1,0:T(2,128)(2,1)S(1)} collective-permute-done((bf16[1,384]{1,0:T(2,128)(2,1)S(1)}, bf16[1,384]{1,0:T(2,128)(2,1)S(1)}, u32[]{:S(2)}, u32[]{:S(2)}) %collective-permute-start.1) | collective-permute-done | bytes 800 | tf_op jit(solution)/shard_map/ppermute | solution.py:72
  23.7 2.7 collective-permute-done.2
  28.0 2.1 collective-permute-done.3
  31.7 2.1 collective-permute-done.4
  37.8 2.7 place_group.1.rest_0_.rest_5_
  45.2 15.6 %collective-permute-done.9.rest_1_.rest_6_ = bf16[4,32,3072]{2,1,0:T(8,128)(2,1)} collective-permute-done((bf16[4,32,3072]{2,1,0:T(8,128)(2,1)}, bf16[4,32,3072]{2,1,0:T(8,128)(2,1)}, u32[]{:S(2)}, u32[]{:S(2)}) %collective-permute-start.9) | collective-permute-done | bytes 786464 | tf_op jit(solution)/shard_map/ppermute | solution.py:72
  64.4 8.7 %collective-permute-done.12.rest_3_.rest_8_ = bf16[4,32,3072]{2,1,0:T(8,128)(2,1)} collective-permute-done((bf16[4,32,3072]{2,1,0:T(8,128)(2,1)}, bf16[4,32,3072]{2,1,0:T(8,128)(2,1)}, u32[]{:S(2)}, u32[]{:S(2)}) %collective-permute-start.12) | collective-permute-done | bytes 786464 | tf_op jit(solution)/shard_map/ppermute | solution.py:72
  73.2 5.7 %collective-permute-done.11 = bf16[2,32,5120]{2,1,0:T(8,128)(2,1)S(1)} collective-permute-done((bf16[2,32,5120]{2,1,0:T(8,128)(2,1)S(1)}, bf16[2,32,5120]{2,1,0:T(8,128)(2,1)S(1)}, u32[]{:S(2)}, u32[]{:S(2)}) %collective-permute-start.11) | collective-permute-done | bytes 655392 | tf_op jit(solution)/shard_map/ppermute | solution.py:72
  83.4 13.2 %project.1 = (bf16[1024,3072]{1,0:T(8,128)(2,1)}, bf16[1024,1024]{1,0:T(8,128)(2,1)}, f32[1,1024]{1,0:T(1,128)}) custom-call(s32[6]{0:T(128)} %pad_add_fusion.meta, bf16[1024,1024]{1,0:T(8,128)(2,1)} %bitcast.99, f32[1,1024]{1,0:T(1,128)} %reshape.306.gain_ref.rest_4_, f32[1024,1]{1,0:T(8,128)} %copy.39.valid_ref, f32[1,3072]{1,0:T(1,128)} %pad_maximum_fusion.2.bias_ref, ...), custom_call_target="tpu_custom_call" | custom-call | flops 48299999232 | tf_op jit(solution)/shard_map/project/pallas_call | solution.py:518
  98.5 10.9 %attn_forward.2 = (bf16[1024,512]{1,0:T(8,128)(2,1)S(1)}, f32[4,8,256]{2,1,0:T(8,128)S(1)}) custom-call(s32[8]{0:T(128)S(1)} %and_select_fusion.lo_ref, s32[1024,128]{1,0:T(8,128)S(1)} %broadcast_in_dim.61.segc_ref, s32[1024,128]{1,0:T(8,128)S(1)} %broadcast_in_dim.63.padc_ref, s32[8,128]{1,0:T(8,128)S(1)} %bitcast.72, ...), custom_call_target="tpu_custom_call" | custom-call | flops 37950001152 | tf_op jit(solution)/shard_map/attn_forward/pallas_call | solution.py:374
  113.6 11.2 %attn_forward.3 = (bf16[1024,512]{1,0:T(8,128)(2,1)S(1)}, f32[4,8,256]{2,1,0:T(8,128)S(1)}) custom-call(s32[8]{0:T(128)S(1)} %and_select_fusion.lo_ref, s32[1024,128]{1,0:T(8,128)S(1)} %broadcast_in_dim.61.segc_ref, s32[1024,128]{1,0:T(8,128)S(1)} %broadcast_in_dim.63.padc_ref, s32[8,128]{1,0:T(8,128)S(1)} %bitcast.73, ...), custom_call_target="tpu_custom_call" | custom-call | flops 37950001152 | tf_op jit(solution)/shard_map/attn_forward/pallas_call | solution.py:374
  124.8 5.2 %collective-permute-done.21.rest_3_.rest_11_ = bf16[4,32,5120]{2,1,0:T(8,128)(2,1)} collective-permute-done((bf16[4,32,5120]{2,1,0:T(8,128)(2,1)}, bf16[4,32,5120]{2,1,0:T(8,128)(2,1)}, u32[]{:S(2)}, u32[]{:S(2)}) %collective-permute-start.21) | collective-permute-done | bytes 1310752 | tf_op jit(solution)/shard_map/ppermute | solution.py:72
  134.6 10.1 %collective-permute-done.20 = bf16[2,128,1024]{2,1,0:T(8,128)(2,1)} collective-permute-done((bf16[2,128,1024]{2,1,0:T(8,128)(2,1)}, bf16[2,128,1024]{2,1,0:T(8,128)(2,1)}, u32[]{:S(2)}, u32[]{:S(2)}) %collective-permute-start.20) | collective-permute-done | bytes 524320 | tf_op jit(solution)/shard_map/ppermute | solution.py:72
  144.7 2.4 maximum_select_fusion.1
  149.0 28.8 %expand.1 = (f32[1024,1024]{1,0:T(8,128)}, bf16[1024,1024]{1,0:T(8,128)(2,1)}, f32[8,1024]{1,0:T(8,128)}, bf16[1024,4096]{1,0:T(8,128)(2,1)}, bf16[1024,4096]{1,0:T(8,128)(2,1)}) custom-call(s32[6]{0:T(128)} %pad_add_fusion.meta, bf16[1024,1024]{1,0:T(8,128)(2,1)} %copy-done.21, bf16[1024,1024]{1,0:T(8,128)(2,1)} %bitcast.100, f32[1,1024]{1,0:T(1,128)} %reshape.308.bias_ref, ...), custom_call_target="tpu_custom_call" | custom-call | flops 100050001920 | tf_op jit(solution)/shard_map/expand/pallas_call | solution.py:597
  179.6 14.9 %down_grad.1 = (bf16[4,4,128,1024]{3,2,1,0:T(8,128)(2,1)}, bf16[4,4,128,1024]{3,2,1,0:T(8,128)(2,1)}, f32[1,1024]{1,0:T(1,128)}) custom-call(s32[6]{0:T(128)} %pad_add_fusion.meta, bf16[1024,4096]{1,0:T(8,128)(2,1)} %get-tuple-element.184.act_ref, bf16[1024,1024]{1,0:T(8,128)(2,1)} %bitcast.96), custom_call_target="tpu_custom_call" | custom-call | flops 48299999232 | tf_op jit(solution)/shard_map/down_grad/pallas_call | solution.py:664
  203.5 24.5 %back.2 = (bf16[4,4,32,5120]{3,2,1,0:T(8,128)(2,1)}, bf16[4,4,32,5120]{3,2,1,0:T(8,128)(2,1)}, f32[1024,1024]{1,0:T(8,128)}, f32[1,2048]{1,0:T(1,128)}) custom-call(s32[6]{0:T(128)} %pad_add_fusion.meta, bf16[1024,1024]{1,0:T(8,128)(2,1)} %bitcast.97, bf16[1024,4096]{1,0:T(8,128)(2,1)} %get-tuple-element.138.slope_ref, ...), custom_call_target="tpu_custom_call" | custom-call | flops 69000003584 | tf_op jit(solution)/shard_map/back/pallas_call | solution.py:834
  228.0 4.0 add_convert_fusion.1
  232.8 34.7 %back.3 = (bf16[4,4,32,5120]{3,2,1,0:T(8,128)(2,1)}, bf16[4,4,32,5120]{3,2,1,0:T(8,128)(2,1)}, f32[1024,1024]{1,0:T(8,128)}, bf16[1024,1024]{1,0:T(8,128)(2,1)},...) custom-call(s32[6]{0:T(128)} %pad_add_fusion.meta, ...), custom_call_target="tpu_custom_call", output_to_operand_aliasing={{0}: (24, {}), {1}: (25, {})} | custom-call | flops 103499997184 | tf_op jit(solution)/shard_map/back/pallas_call | solution.py:834
  271.9 3.0 fusion.1
  276.3 16.3 %attn_backward.2 = (bf16[3,1024,512]{2,1,0:T(8,128)(2,1)}, f32[8,512]{1,0:T(8,128)S(1)}) custom-call(s32[8]{0:T(128)S(1)} %and_select_fusion.lo_ref, s32[1024,128]{1,0:T(8,128)S(1)} %copy-done.3, s32[1024,128]{1,0:T(8,128)S(1)} %copy-done.1, s32[8,128]{1,0:T(8,128)S(1)} %bitcast.74, bf16[1024,3072]{1,0:T(8,128)(2,1)} %get-tuple-element.125.q_ref.k_ref.v_ref, ...), custom_call_target="tpu_custom_call" | custom-call | flops 55199997952 | tf_op jit(solution)/shard_map/attn_backward/pallas_call | solution.py:400
  292.5 4.8 %spread_sums.4 = (f32[128,1024]{1,0:T(8,128)}, bf16[128,1024]{1,0:T(8,128)(2,1)}, bf16[128,1024]{1,0:T(8,128)(2,1)}, bf16[128,1024]{1,0:T(8,128)(2,1)}) custom-call(s32[6]{0:T(128)} %pad_add_fusion.meta, bf16[4,4,128,1024]{3,2,1,0:T(8,128)(2,1)} %get-tuple-element.134.refs_0_.refs_4_.refs_8_.refs_12_, ...), custom_call_target="tpu_custom_call" | custom-call | flops 10350000128 | tf_op jit(solution)/shard_map/spread_sums/pallas_call | solution.py:139
  297.5 3.0 collective-permute-start.38
  301.8 5.0 %add_convert_fusion = bf16[2,4,32,5120]{3,2,1,0:T(8,128)(2,1)} fusion(bf16[4,4,32,5120]{3,2,1,0:T(8,128)(2,1)} %collective-permute-done.36.refs_1_.refs_5_.refs_9_.refs_13_, bf16[4,4,32,5120]{3,2,1,0:T(8,128)(2,1)} %get-tuple-element.157.refs_0_.refs_4_.refs_8_.refs_12_), kind=kLoop, calls=%fused_computation.5 | loop fusion | flops 5242880 | bytes 7864320 | tf_op jit(solution)/shard_map/convert_element_type | solution.py:212
  307.5 7.9 %qkv_grad.2 = (bf16[4,4,32,1536]{3,2,1,0:T(8,128)(2,1)}, bf16[4,4,32,1536]{3,2,1,0:T(8,128)(2,1)}) custom-call(s32[6]{0:T(128)} %pad_add_fusion.meta, bf16[1024,1024]{1,0:T(8,128)(2,1)} %get-tuple-element.161.left_ref, bf16[3,1024,512]{2,1,0:T(8,128)(2,1)} %get-tuple-element.160.right_ref.rest_0_), custom_call_target="tpu_custom_call" | custom-call | flops 27599998976 | tf_op jit(solution)/shard_map/qkv_grad/pallas_call | solution.py:702
  315.4 16.5 %attn_backward.3 = (bf16[3,1024,512]{2,1,0:T(8,128)(2,1)}, f32[8,512]{1,0:T(8,128)S(1)}) custom-call(s32[8]{0:T(128)S(1)} %and_select_fusion.lo_ref, s32[1024,128]{1,0:T(8,128)S(1)} %copy-done.3, s32[1024,128]{1,0:T(8,128)S(1)} %copy-done.1, s32[8,128]{1,0:T(8,128)S(1)} %bitcast.75, bf16[1024,3072]{1,0:T(8,128)(2,1)} %get-tuple-element.125.q_ref.k_ref.v_ref, ...), custom_call_target="tpu_custom_call" | custom-call | flops 55199997952 | tf_op jit(solution)/shard_map/attn_backward/pallas_call | solution.py:400
  333.3 2.1 convert_add_fusion.1
  338.8 2.7 fusion
  341.6 7.8 %qkv_grad.3 = (bf16[4,4,32,1536]{3,2,1,0:T(8,128)(2,1)}, bf16[4,4,32,1536]{3,2,1,0:T(8,128)(2,1)}) custom-call(s32[6]{0:T(128)} %pad_add_fusion.meta, bf16[1024,1024]{1,0:T(8,128)(2,1)} %get-tuple-element.161.left_ref, bf16[3,1024,512]{2,1,0:T(8,128)(2,1)} %get-tuple-element.172.right_ref.rest_1_), custom_call_target="tpu_custom_call" | custom-call | flops 27599998976 | tf_op jit(solution)/shard_map/qkv_grad/pallas_call | solution.py:702
  349.5 17.8 %input_grad.1 = (bf16[1024,1024]{1,0:T(8,128)(2,1)}, f32[8,1024]{1,0:T(8,128)}) custom-call(s32[6]{0:T(128)} %pad_add_fusion.meta, bf16[3,1024,512]{2,1,0:T(8,128)(2,1)} %get-tuple-element.160.right_ref.rest_0_, bf16[3,1024,512]{2,1,0:T(8,128)(2,1)} %get-tuple-element.172.right_ref.rest_1_, bf16[1024,1024]{1,0:T(8,128)(2,1)} %bitcast.101, ...), custom_call_target="tpu_custom_call" | custom-call | flops 62100000768 | tf_op jit(solution)/shard_map/input_grad/pallas_call | solution.py:948
  370.4 2.1 collective-permute-start.45
  373.6 4.6 spread_sums.5
  380.4 19.4 %contract.1 = (bf16[1024,1024]{1,0:T(8,128)(2,1)}, f32[8,1024]{1,0:T(8,128)}) custom-call(s32[6]{0:T(128)} %pad_add_fusion.meta, bf16[1024,4096]{1,0:T(8,128)(2,1)} %get-tuple-element.184.act_ref, f32[1,1024]{1,0:T(1,128)} %reshape.311.bias_ref, f32[1024,1]{1,0:T(8,128)} %copy.39.valid_ref, f32[1024,1024]{1,0:T(8,128)} %get-tuple-element.140.middle_ref, ...), custom_call_target="tpu_custom_call" | custom-call | flops 55199997952 | tf_op jit(solution)/shard_map/contract/pallas_call | solution.py:889
  401.3 4.0 stack.117
  405.4 3.0 spread_sums.6
  411.2 2.6 collective-permute-start.60
  417.1 2.2 collective-permute-done.55
  420.0 15.8 %collective-permute-done.61 = bf16[32,5120]{1,0:T(8,128)(2,1)S(1)} collective-permute-done((bf16[32,5120]{1,0:T(8,128)(2,1)S(1)}, bf16[32,5120]{1,0:T(8,128)(2,1)S(1)}, u32[]{:S(2)}, u32[]{:S(2)}) %collective-permute-start.61) | collective-permute-done | bytes 327712 | tf_op jit(solution)/shard_map/ppermute | solution.py:72
  435.8 8.5 %collective-permute-start.47 = (bf16[32,1536]{1,0:T(8,128)(2,1)S(1)}, bf16[32,1536]{1,0:T(8,128)(2,1)S(1)}, u32[]{:S(2)}, u32[]{:S(2)}) collective-permute-start(bf16[32,1536]{1,0:T(8,128)(2,1)S(1)} %copy-done.55), channel_id=1, source_target_pairs={{0,4},{1,5},{2,6},{3,7},{4,0},{5,1},{6,2},{7,3},{8,12},{9,13},{10,... | collective-permute-start | bytes 294920 | tf_op jit(solution)/shard_map/ppermute | solution.py:72
  448.0 4.1 collective-permute-done.47
  452.1 2.2 collective-permute-start.58
  459.6 2.8 collective-permute-done.50.refs_3_.refs_7_.refs_11_.refs_15_
  463.1 3.0 spread_sums.7
  468.5 2.0 collective-permute-start.53
  471.5 3.8 collective-permute-done.52
  (320 shorter events, 91.5 us)
Async XLA Ops:
  0.6 35.8 %collective-permute-start.7 = (bf16[32,3072]{1,0:T(8,128)(2,1)}, bf16[32,3072]{1,0:T(8,128)(2,1)S(1)}, u32[]{:S(2)}, u32[]{:S(2)}) collective-permute-start(bf16[32,3072]{1,0:T(8,128)(2,1)} %refs_0_), channel_id=1, source_target_pairs={{0,6},{1,7},{2,4},{3,5},{4,2},{5,3},{6,0},{7,1},{8,14},{9,15},{10,... | collective-permute-start | bytes 589832 | tf_op jit(solution)/shard_map/ppermute | solution.py:72
  5.8 30.7 %collective-permute-start.6 = (bf16[32,3072]{1,0:T(8,128)(2,1)}, bf16[32,3072]{1,0:T(8,128)(2,1)S(1)}, u32[]{:S(2)}, u32[]{:S(2)}) collective-permute-start(bf16[32,3072]{1,0:T(8,128)(2,1)} %refs_0_), channel_id=1, source_target_pairs={{0,4},{1,5},{2,6},{3,7},{4,0},{5,1},{6,2},{7,3},{8,12},{9,13},{10,... | collective-permute-start | bytes 589832 | tf_op jit(solution)/shard_map/ppermute | solution.py:72
  5.8 30.7 %collective-permute-start = (bf16[32,3072]{1,0:T(8,128)(2,1)}, bf16[32,3072]{1,0:T(8,128)(2,1)S(1)}, u32[]{:S(2)}, u32[]{:S(2)}) collective-permute-start(bf16[32,3072]{1,0:T(8,128)(2,1)} %refs_0_), channel_id=1, source_target_pairs={{0,2},{1,3},{2,0},{3,1},{4,6},{5,7},{6,4},{7,5},{8,10},{9,11},{10,... | collective-permute-start | bytes 589832 | tf_op jit(solution)/shard_map/ppermute | solution.py:72
  10.5 12.2 %collective-permute-start.1 = (bf16[1,384]{1,0:T(2,128)(2,1)S(1)}, bf16[1,384]{1,0:T(2,128)(2,1)S(1)}, u32[]{:S(2)}, u32[]{:S(2)}) collective-permute-start(bf16[1,384]{1,0:T(2,128)(2,1)S(1)} %broadcast_in_dim.65), channel_id=1, source_target_pairs={{0,4},{1,5},{2,6},{3,7},{4,0},{5,1},{6,2},{7,3},{8,12},{9,13},{10,... | collective-permute-start | bytes 2312 | tf_op jit(solution)/shard_map/ppermute | solution.py:72
  40.5 21.8 %collective-permute-start.10 = (bf16[4,32,3072]{2,1,0:T(8,128)(2,1)}, bf16[4,32,3072]{2,1,0:T(8,128)(2,1)S(1)}, u32[]{:S(2)}, u32[]{:S(2)}) collective-permute-start(bf16[4,32,3072]{2,1,0:T(8,128)(2,1)} %place_group.1.rest_0_.rest_5_), channel_id=1, source_target_pairs={{0,16},{1,9},{2,18},{3,11},{4,20},{5,13},{6,22},{7,15},{8,24},{9,1... | collective-permute-start | bytes 2359304 | tf_op jit(solution)/shard_map/ppermute | solution.py:72
  42.1 18.7 %collective-permute-start.9 = (bf16[4,32,3072]{2,1,0:T(8,128)(2,1)}, bf16[4,32,3072]{2,1,0:T(8,128)(2,1)}, u32[]{:S(2)}, u32[]{:S(2)}) collective-permute-start(bf16[4,32,3072]{2,1,0:T(8,128)(2,1)} %place_group.1.rest_0_.rest_5_), channel_id=1, source_target_pairs={{0,8},{1,17},{2,10},{3,19},{4,12},{5,21},{6,14},{7,23},{8,0},{9,25... | collective-permute-start | bytes 2359304 | tf_op jit(solution)/shard_map/ppermute | solution.py:72
  43.6 18.8 %collective-permute-start.8 = (bf16[32,5120]{1,0:T(8,128)(2,1)S(1)}, bf16[32,5120]{1,0:T(8,128)(2,1)S(1)}, u32[]{:S(2)}, u32[]{:S(2)}) collective-permute-start(bf16[32,5120]{1,0:T(8,128)(2,1)S(1)} %pad_maximum_fusion.1), channel_id=1, source_target_pairs={{0,4},{1,5},{2,6},{3,7},{4,0},{5,1},{6,2},{7,3},{8,12},{9,13},{10,... | collective-permute-start | bytes 983048 | tf_op jit(solution)/shard_map/ppermute | solution.py:72
  60.8 12.3 %collective-permute-start.12 = (bf16[4,32,3072]{2,1,0:T(8,128)(2,1)}, bf16[4,32,3072]{2,1,0:T(8,128)(2,1)}, u32[]{:S(2)}, u32[]{:S(2)}) collective-permute-start(bf16[4,32,3072]{2,1,0:T(8,128)(2,1)} %collective-permute-done.9.rest_1_.rest_6_), channel_id=1, source_target_pairs={{0,16},{1,9},{2,18},{3,11},{4,20},{5,13},{6,22},{7,15},{8,24},{9,1... | collective-permute-start | bytes 2359304 | tf_op jit(solution)/shard_map/ppermute | solution.py:72
  62.4 16.5 %collective-permute-start.11 = (bf16[2,32,5120]{2,1,0:T(8,128)(2,1)S(1)}, bf16[2,32,5120]{2,1,0:T(8,128)(2,1)S(1)}, u32[]{:S(2)}, u32[]{:S(2)}) collective-permute-start(bf16[2,32,5120]{2,1,0:T(8,128)(2,1)S(1)} %maximum_select_fusion.2), channel_id=1, source_target_pairs={{0,2},{1,3},{2,0},{3,1},{4,6},{5,7},{6,4},{7,5},{8,10},{9,11},{10,... | collective-permute-start | bytes 1966088 | tf_op jit(solution)/shard_map/ppermute | solution.py:72
  63.9 15.4 %collective-permute-start.13 = (bf16[4,32,3072]{2,1,0:T(8,128)(2,1)}, bf16[4,32,3072]{2,1,0:T(8,128)(2,1)S(1)}, u32[]{:S(2)}, u32[]{:S(2)}) collective-permute-start(bf16[4,32,3072]{2,1,0:T(8,128)(2,1)} %place_group.1.rest_0_.rest_5_), channel_id=1, source_target_pairs={{0,1},{1,0},{2,3},{3,2},{4,5},{5,4},{6,7},{7,6},{8,9},{9,8},{10,11... | collective-permute-start | bytes 2359304 | tf_op jit(solution)/shard_map/ppermute | solution.py:72
  63.9 17.0 %collective-permute-start.14 = (bf16[4,32,3072]{2,1,0:T(8,128)(2,1)S(1)}, bf16[4,32,3072]{2,1,0:T(8,128)(2,1)S(1)}, u32[]{:S(2)}, u32[]{:S(2)}) collective-permute-start(bf16[4,32,3072]{2,1,0:T(8,128)(2,1)S(1)} %collective-permute-done.10.rest_2_.rest_7_), channel_id=1, source_target_pairs={{0,1},{1,0},{2,3},{3,2},{4,5},{5,4},{6,7},{7,6},{8,9},{9,8},{10,11... | collective-permute-start | bytes 2359304 | tf_op jit(solution)/shard_map/ppermute | solution.py:72
  64.4 17.2 %collective-permute-start.15 = (bf16[4,32,3072]{2,1,0:T(8,128)(2,1)}, bf16[4,32,3072]{2,1,0:T(8,128)(2,1)S(1)}, u32[]{:S(2)}, u32[]{:S(2)}) collective-permute-start(bf16[4,32,3072]{2,1,0:T(8,128)(2,1)} %collective-permute-done.9.rest_1_.rest_6_), channel_id=1, source_target_pairs={{0,1},{1,0},{2,3},{3,2},{4,5},{5,4},{6,7},{7,6},{8,9},{9,8},{10,11... | collective-permute-start | bytes 2359304 | tf_op jit(solution)/shard_map/ppermute | solution.py:72
  79.2 67.9 %collective-permute-start.22 = (bf16[4,32,5120]{2,1,0:T(8,128)(2,1)S(1)}, bf16[4,32,5120]{2,1,0:T(8,128)(2,1)}, u32[]{:S(2)}, u32[]{:S(2)}) collective-permute-start(bf16[4,32,5120]{2,1,0:T(8,128)(2,1)S(1)} %bitcast.79), channel_id=1, source_target_pairs={{0,1},{1,0},{2,3},{3,2},{4,5},{5,4},{6,7},{7,6},{8,9},{9,8},{10,11... | collective-permute-start | bytes 3932168 | tf_op jit(solution)/shard_map/ppermute | solution.py:72
  79.3 33.3 %collective-permute-start.18 = (bf16[4,32,5120]{2,1,0:T(8,128)(2,1)S(1)}, bf16[4,32,5120]{2,1,0:T(8,128)(2,1)}, u32[]{:S(2)}, u32[]{:S(2)}) collective-permute-start(bf16[4,32,5120]{2,1,0:T(8,128)(2,1)S(1)} %bitcast.80), channel_id=1, source_target_pairs={{0,16},{1,9},{2,18},{3,11},{4,20},{5,13},{6,22},{7,15},{8,24},{9,1... | collective-permute-start | bytes 3932168 | tf_op jit(solution)/shard_map/ppermute | solution.py:72
  80.9 31.2 %collective-permute-start.17 = (bf16[4,32,5120]{2,1,0:T(8,128)(2,1)S(1)}, bf16[4,32,5120]{2,1,0:T(8,128)(2,1)}, u32[]{:S(2)}, u32[]{:S(2)}) collective-permute-start(bf16[4,32,5120]{2,1,0:T(8,128)(2,1)S(1)} %bitcast.81), channel_id=1, source_target_pairs={{0,8},{1,17},{2,10},{3,19},{4,12},{5,21},{6,14},{7,23},{8,0},{9,25... | collective-permute-start | bytes 3932168 | tf_op jit(solution)/shard_map/ppermute | solution.py:72
  96.7 14.5 %collective-permute-start.19 = (bf16[128,1024]{1,0:T(8,128)(2,1)S(1)}, bf16[128,1024]{1,0:T(8,128)(2,1)S(1)}, u32[]{:S(2)}, u32[]{:S(2)}) collective-permute-start(bf16[128,1024]{1,0:T(8,128)(2,1)S(1)} %copy-done.15), channel_id=1, source_target_pairs={{0,4},{1,5},{2,6},{3,7},{4,0},{5,1},{6,2},{7,3},{8,12},{9,13},{10,... | collective-permute-start | bytes 786440 | tf_op jit(solution)/shard_map/ppermute | solution.py:72
  112.1 35.6 %collective-permute-start.24 = (bf16[4,32,5120]{2,1,0:T(8,128)(2,1)}, bf16[4,32,5120]{2,1,0:T(8,128)(2,1)}, u32[]{:S(2)}, u32[]{:S(2)}) collective-permute-start(bf16[4,32,5120]{2,1,0:T(8,128)(2,1)} %collective-permute-done.17.rest_1_.rest_9_), channel_id=1, source_target_pairs={{0,1},{1,0},{2,3},{3,2},{4,5},{5,4},{6,7},{7,6},{8,9},{9,8},{10,11... | collective-permute-start | bytes 3932168 | tf_op jit(solution)/shard_map/ppermute | solution.py:72
  112.1 17.9 %collective-permute-start.21 = (bf16[4,32,5120]{2,1,0:T(8,128)(2,1)}, bf16[4,32,5120]{2,1,0:T(8,128)(2,1)}, u32[]{:S(2)}, u32[]{:S(2)}) collective-permute-start(bf16[4,32,5120]{2,1,0:T(8,128)(2,1)} %collective-permute-done.17.rest_1_.rest_9_), channel_id=1, source_target_pairs={{0,16},{1,9},{2,18},{3,11},{4,20},{5,13},{6,22},{7,15},{8,24},{9,1... | collective-permute-start | bytes 3932168 | tf_op jit(solution)/shard_map/ppermute | solution.py:72
  112.6 36.4 %collective-permute-start.23 = (bf16[4,32,5120]{2,1,0:T(8,128)(2,1)}, bf16[4,32,5120]{2,1,0:T(8,128)(2,1)}, u32[]{:S(2)}, u32[]{:S(2)}) collective-permute-start(bf16[4,32,5120]{2,1,0:T(8,128)(2,1)} %collective-permute-done.18.rest_2_.rest_10_), channel_id=1, source_target_pairs={{0,1},{1,0},{2,3},{3,2},{4,5},{5,4},{6,7},{7,6},{8,9},{9,8},{10,11... | collective-permute-start | bytes 3932168 | tf_op jit(solution)/shard_map/ppermute | solution.py:72
  130.0 19.0 %collective-permute-start.25 = (bf16[4,32,5120]{2,1,0:T(8,128)(2,1)}, bf16[4,32,5120]{2,1,0:T(8,128)(2,1)}, u32[]{:S(2)}, u32[]{:S(2)}) collective-permute-start(bf16[4,32,5120]{2,1,0:T(8,128)(2,1)} %collective-permute-done.21.rest_3_.rest_11_), channel_id=1, source_target_pairs={{0,1},{1,0},{2,3},{3,2},{4,5},{5,4},{6,7},{7,6},{8,9},{9,8},{10,11... | collective-permute-start | bytes 3932168 | tf_op jit(solution)/shard_map/ppermute | solution.py:72
  130.0 14.7 %collective-permute-start.20 = (bf16[2,128,1024]{2,1,0:T(8,128)(2,1)}, bf16[2,128,1024]{2,1,0:T(8,128)(2,1)}, u32[]{:S(2)}, u32[]{:S(2)}) collective-permute-start(bf16[2,128,1024]{2,1,0:T(8,128)(2,1)} %maximum_select_fusion.4), channel_id=1, source_target_pairs={{0,2},{1,3},{2,0},{3,1},{4,6},{5,7},{6,4},{7,5},{8,10},{9,11},{10,... | collective-permute-start | bytes 1572872 | tf_op jit(solution)/shard_map/ppermute | solution.py:72
  147.1 56.3 %collective-permute-start.30 = (bf16[4,128,1024]{2,1,0:T(8,128)(2,1)}, bf16[4,128,1024]{2,1,0:T(8,128)(2,1)}, u32[]{:S(2)}, u32[]{:S(2)}) collective-permute-start(bf16[4,128,1024]{2,1,0:T(8,128)(2,1)} %bitcast.21.rest_0_), channel_id=1, source_target_pairs={{0,1},{1,0},{2,3},{3,2},{4,5},{5,4},{6,7},{7,6},{8,9},{9,8},{10,11... | collective-permute-start | bytes 3145736 | tf_op jit(solution)/shard_map/ppermute | solution.py:72
  147.1 32.4 %collective-permute-start.27 = (bf16[4,128,1024]{2,1,0:T(8,128)(2,1)}, bf16[4,128,1024]{2,1,0:T(8,128)(2,1)S(1)}, u32[]{:S(2)}, u32[]{:S(2)}) collective-permute-start(bf16[4,128,1024]{2,1,0:T(8,128)(2,1)} %bitcast.21.rest_0_), channel_id=1, source_target_pairs={{0,16},{1,9},{2,18},{3,11},{4,20},{5,13},{6,22},{7,15},{8,24},{9,1... | collective-permute-start | bytes 3145736 | tf_op jit(solution)/shard_map/ppermute | solution.py:72
  147.7 30.2 %collective-permute-start.26 = (bf16[4,128,1024]{2,1,0:T(8,128)(2,1)}, bf16[4,128,1024]{2,1,0:T(8,128)(2,1)S(1)}, u32[]{:S(2)}, u32[]{:S(2)}) collective-permute-start(bf16[4,128,1024]{2,1,0:T(8,128)(2,1)} %bitcast.21.rest_0_), channel_id=1, source_target_pairs={{0,8},{1,17},{2,10},{3,19},{4,12},{5,21},{6,14},{7,23},{8,0},{9,25... | collective-permute-start | bytes 3145736 | tf_op jit(solution)/shard_map/ppermute | solution.py:72
  177.9 25.5 %collective-permute-start.32 = (bf16[4,128,1024]{2,1,0:T(8,128)(2,1)S(1)}, bf16[4,128,1024]{2,1,0:T(8,128)(2,1)}, u32[]{:S(2)}, u32[]{:S(2)}) collective-permute-start(bf16[4,128,1024]{2,1,0:T(8,128)(2,1)S(1)} %collective-permute-done.26.rest_1_), channel_id=1, source_target_pairs={{0,1},{1,0},{2,3},{3,2},{4,5},{5,4},{6,7},{7,6},{8,9},{9,8},{10,11... | collective-permute-start | bytes 3145736 | tf_op jit(solution)/shard_map/ppermute | solution.py:72
  178.0 16.6 %collective-permute-start.29 = (bf16[4,128,1024]{2,1,0:T(8,128)(2,1)S(1)}, bf16[4,128,1024]{2,1,0:T(8,128)(2,1)}, u32[]{:S(2)}, u32[]{:S(2)}) collective-permute-start(bf16[4,128,1024]{2,1,0:T(8,128)(2,1)S(1)} %collective-permute-done.26.rest_1_), channel_id=1, source_target_pairs={{0,16},{1,9},{2,18},{3,11},{4,20},{5,13},{6,22},{7,15},{8,24},{9,1... | collective-permute-start | bytes 3145736 | tf_op jit(solution)/shard_map/ppermute | solution.py:72
  179.5 24.0 %collective-permute-start.31 = (bf16[4,128,1024]{2,1,0:T(8,128)(2,1)S(1)}, bf16[4,128,1024]{2,1,0:T(8,128)(2,1)}, u32[]{:S(2)}, u32[]{:S(2)}) collective-permute-start(bf16[4,128,1024]{2,1,0:T(8,128)(2,1)S(1)} %collective-permute-done.27.rest_2_), channel_id=1, source_target_pairs={{0,1},{1,0},{2,3},{3,2},{4,5},{5,4},{6,7},{7,6},{8,9},{9,8},{10,11... | collective-permute-start | bytes 3145736 | tf_op jit(solution)/shard_map/ppermute | solution.py:72
  194.6 8.9 %collective-permute-start.33 = (bf16[4,128,1024]{2,1,0:T(8,128)(2,1)}, bf16[4,128,1024]{2,1,0:T(8,128)(2,1)}, u32[]{:S(2)}, u32[]{:S(2)}) collective-permute-start(bf16[4,128,1024]{2,1,0:T(8,128)(2,1)} %collective-permute-done.29.rest_3_), channel_id=1, source_target_pairs={{0,1},{1,0},{2,3},{3,2},{4,5},{5,4},{6,7},{7,6},{8,9},{9,8},{10,11... | collective-permute-start | bytes 3145736 | tf_op jit(solution)/shard_map/ppermute | solution.py:72
  201.9 26.0 %collective-permute-start.28 = (bf16[4,4,128,1024]{3,2,1,0:T(8,128)(2,1)}, bf16[4,4,128,1024]{3,2,1,0:T(8,128)(2,1)}, u32[]{:S(2)}, u32[]{:S(2)}) collective-permute-start(bf16[4,4,128,1024]{3,2,1,0:T(8,128)(2,1)} %get-tuple-element.135), channel_id=1, source_target_pairs={{0,1},{1,0},{2,3},{3,2},{4,5},{5,4},{6,7},{7,6},{8,9},{9,8},{10,11... | collective-permute-start | bytes 12582920 | tf_op jit(solution)/shard_map/ppermute | solution.py:72
  232.0 39.9 %collective-permute-start.34 = (bf16[2,4,128,1024]{3,2,1,0:T(8,128)(2,1)}, bf16[2,4,128,1024]{3,2,1,0:T(8,128)(2,1)S(1)}, u32[]{:S(2)}, u32[]{:S(2)}) collective-permute-start(bf16[2,4,128,1024]{3,2,1,0:T(8,128)(2,1)} %add_convert_fusion.1), channel_id=1, source_target_pairs={{0,16},{1,9},{2,18},{3,11},{4,20},{5,13},{6,22},{7,15},{8,24},{9,1... | collective-permute-start | bytes 6291464 | tf_op jit(solution)/shard_map/ppermute | solution.py:72
  271.8 30.0 %collective-permute-start.36 = (bf16[4,4,32,5120]{3,2,1,0:T(8,128)(2,1)}, bf16[4,4,32,5120]{3,2,1,0:T(8,128)(2,1)}, u32[]{:S(2)}, u32[]{:S(2)}) collective-permute-start(bf16[4,4,32,5120]{3,2,1,0:T(8,128)(2,1)} %get-tuple-element.158), channel_id=1, source_target_pairs={{0,1},{1,0},{2,3},{3,2},{4,5},{5,4},{6,7},{7,6},{8,9},{9,8},{10,11... | collective-permute-start | bytes 15728648 | tf_op jit(solution)/shard_map/ppermute | solution.py:72
  274.9 17.7 %collective-permute-start.35 = (bf16[4,128,1024]{2,1,0:T(8,128)(2,1)S(1)}, bf16[4,128,1024]{2,1,0:T(8,128)(2,1)}, u32[]{:S(2)}, u32[]{:S(2)}) collective-permute-start(bf16[4,128,1024]{2,1,0:T(8,128)(2,1)S(1)} %fusion.1), channel_id=1, source_target_pairs={{0,8},{1,17},{2,10},{3,19},{4,12},{5,21},{6,14},{7,23},{8,0},{9,25... | collective-permute-start | bytes 3145736 | tf_op jit(solution)/shard_map/ppermute | solution.py:72
  297.4 34.6 %collective-permute-start.37 = (bf16[128,1024]{1,0:T(8,128)(2,1)}, bf16[128,1024]{1,0:T(8,128)(2,1)S(1)}, u32[]{:S(2)}, u32[]{:S(2)}) collective-permute-start(bf16[128,1024]{1,0:T(8,128)(2,1)} %get-tuple-element.154), channel_id=1, source_target_pairs={{0,2},{1,3},{2,0},{3,1},{4,6},{5,7},{6,4},{7,5},{8,10},{9,11},{10,... | collective-permute-start | bytes 786440 | tf_op jit(solution)/shard_map/ppermute | solution.py:72
  297.5 34.5 %collective-permute-start.38 = (bf16[128,1024]{1,0:T(8,128)(2,1)}, bf16[128,1024]{1,0:T(8,128)(2,1)S(1)}, u32[]{:S(2)}, u32[]{:S(2)}) collective-permute-start(bf16[128,1024]{1,0:T(8,128)(2,1)} %get-tuple-element.155), channel_id=1, source_target_pairs={{0,4},{1,5},{2,6},{3,7},{4,0},{5,1},{6,2},{7,3},{8,12},{9,13},{10,... | collective-permute-start | bytes 786440 | tf_op jit(solution)/shard_map/ppermute | solution.py:72
  300.5 31.4 %collective-permute-start.39 = (bf16[128,1024]{1,0:T(8,128)(2,1)}, bf16[128,1024]{1,0:T(8,128)(2,1)S(1)}, u32[]{:S(2)}, u32[]{:S(2)}) collective-permute-start(bf16[128,1024]{1,0:T(8,128)(2,1)} %get-tuple-element.156), channel_id=1, source_target_pairs={{0,6},{1,7},{2,4},{3,5},{4,2},{5,3},{6,0},{7,1},{8,14},{9,15},{10,... | collective-permute-start | bytes 786440 | tf_op jit(solution)/shard_map/ppermute | solution.py:72
  306.9 32.0 %collective-permute-start.40 = (bf16[2,4,32,5120]{3,2,1,0:T(8,128)(2,1)}, bf16[2,4,32,5120]{3,2,1,0:T(8,128)(2,1)}, u32[]{:S(2)}, u32[]{:S(2)}) collective-permute-start(bf16[2,4,32,5120]{3,2,1,0:T(8,128)(2,1)} %add_convert_fusion), channel_id=1, source_target_pairs={{0,16},{1,9},{2,18},{3,11},{4,20},{5,13},{6,22},{7,15},{8,24},{9,1... | collective-permute-start | bytes 7864328 | tf_op jit(solution)/shard_map/ppermute | solution.py:72
  315.4 20.0 %collective-permute-start.41 = (bf16[4,4,32,1536]{3,2,1,0:T(8,128)(2,1)}, bf16[4,4,32,1536]{3,2,1,0:T(8,128)(2,1)}, u32[]{:S(2)}, u32[]{:S(2)}) collective-permute-start(bf16[4,4,32,1536]{3,2,1,0:T(8,128)(2,1)} %get-tuple-element.163), channel_id=1, source_target_pairs={{0,1},{1,0},{2,3},{3,2},{4,5},{5,4},{6,7},{7,6},{8,9},{9,8},{10,11... | collective-permute-start | bytes 4718600 | tf_op jit(solution)/shard_map/ppermute | solution.py:72
  336.7 30.6 %collective-permute-start.43 = (bf16[2,4,32,1536]{3,2,1,0:T(8,128)(2,1)S(1)}, bf16[2,4,32,1536]{3,2,1,0:T(8,128)(2,1)S(1)}, u32[]{:S(2)}, u32[]{:S(2)}) collective-permute-start(bf16[2,4,32,1536]{3,2,1,0:T(8,128)(2,1)S(1)} %add_convert_fusion.5), channel_id=1, source_target_pairs={{0,16},{1,9},{2,18},{3,11},{4,20},{5,13},{6,22},{7,15},{8,24},{9,1... | collective-permute-start | bytes 2359304 | tf_op jit(solution)/shard_map/ppermute | solution.py:72
  341.5 31.0 %collective-permute-start.42 = (bf16[4,32,5120]{2,1,0:T(8,128)(2,1)S(1)}, bf16[4,32,5120]{2,1,0:T(8,128)(2,1)S(1)}, u32[]{:S(2)}, u32[]{:S(2)}) collective-permute-start(bf16[4,32,5120]{2,1,0:T(8,128)(2,1)S(1)} %fusion), channel_id=1, source_target_pairs={{0,8},{1,17},{2,10},{3,19},{4,12},{5,21},{6,14},{7,23},{8,0},{9,25... | collective-permute-start | bytes 3932168 | tf_op jit(solution)/shard_map/ppermute | solution.py:72
  349.4 28.8 %collective-permute-start.44 = (bf16[4,4,32,1536]{3,2,1,0:T(8,128)(2,1)}, bf16[4,4,32,1536]{3,2,1,0:T(8,128)(2,1)}, u32[]{:S(2)}, u32[]{:S(2)}) collective-permute-start(bf16[4,4,32,1536]{3,2,1,0:T(8,128)(2,1)} %get-tuple-element.174), channel_id=1, source_target_pairs={{0,1},{1,0},{2,3},{3,2},{4,5},{5,4},{6,7},{7,6},{8,9},{9,8},{10,11... | collective-permute-start | bytes 4718600 | tf_op jit(solution)/shard_map/ppermute | solution.py:72
  370.4 30.9 %collective-permute-start.45 = (bf16[4,32,1536]{2,1,0:T(8,128)(2,1)S(1)}, bf16[4,32,1536]{2,1,0:T(8,128)(2,1)S(1)}, u32[]{:S(2)}, u32[]{:S(2)}) collective-permute-start(bf16[4,32,1536]{2,1,0:T(8,128)(2,1)S(1)} %fusion.2), channel_id=1, source_target_pairs={{0,8},{1,17},{2,10},{3,19},{4,12},{5,21},{6,14},{7,23},{8,0},{9,25... | collective-permute-start | bytes 1179656 | tf_op jit(solution)/shard_map/ppermute | solution.py:72
  379.7 28.8 %collective-permute-start.49 = (bf16[2,4,32,1536]{3,2,1,0:T(8,128)(2,1)S(1)}, bf16[2,4,32,1536]{3,2,1,0:T(8,128)(2,1)}, u32[]{:S(2)}, u32[]{:S(2)}) collective-permute-start(bf16[2,4,32,1536]{3,2,1,0:T(8,128)(2,1)S(1)} %add_convert_fusion.4), channel_id=1, source_target_pairs={{0,16},{1,9},{2,18},{3,11},{4,20},{5,13},{6,22},{7,15},{8,24},{9,1... | collective-permute-start | bytes 2359304 | tf_op jit(solution)/shard_map/ppermute | solution.py:72
  411.1 35.2 %collective-permute-start.59 = (bf16[32,5120]{1,0:T(8,128)(2,1)S(1)}, bf16[32,5120]{1,0:T(8,128)(2,1)S(1)}, u32[]{:S(2)}, u32[]{:S(2)}) collective-permute-start(bf16[32,5120]{1,0:T(8,128)(2,1)S(1)} %copy-done.48), channel_id=1, source_target_pairs={{0,2},{1,3},{2,0},{3,1},{4,6},{5,7},{6,4},{7,5},{8,10},{9,11},{10,... | collective-permute-start | bytes 983048 | tf_op jit(solution)/shard_map/ppermute | solution.py:72
  411.2 33.2 %collective-permute-start.60 = (bf16[32,5120]{1,0:T(8,128)(2,1)S(1)}, bf16[32,5120]{1,0:T(8,128)(2,1)S(1)}, u32[]{:S(2)}, u32[]{:S(2)}) collective-permute-start(bf16[32,5120]{1,0:T(8,128)(2,1)S(1)} %copy-done.49), channel_id=1, source_target_pairs={{0,4},{1,5},{2,6},{3,7},{4,0},{5,1},{6,2},{7,3},{8,12},{9,13},{10,... | collective-permute-start | bytes 983048 | tf_op jit(solution)/shard_map/ppermute | solution.py:72
  413.7 22.1 %collective-permute-start.61 = (bf16[32,5120]{1,0:T(8,128)(2,1)S(1)}, bf16[32,5120]{1,0:T(8,128)(2,1)S(1)}, u32[]{:S(2)}, u32[]{:S(2)}) collective-permute-start(bf16[32,5120]{1,0:T(8,128)(2,1)S(1)} %copy-done.50), channel_id=1, source_target_pairs={{0,6},{1,7},{2,4},{3,5},{4,2},{5,3},{6,0},{7,1},{8,14},{9,15},{10,... | collective-permute-start | bytes 983048 | tf_op jit(solution)/shard_map/ppermute | solution.py:72
  419.3 26.9 %collective-permute-start.56 = (f32[4,384]{1,0:T(4,128)S(1)}, f32[4,384]{1,0:T(4,128)S(1)}, u32[]{:S(2)}, u32[]{:S(2)}) collective-permute-start(f32[4,384]{1,0:T(4,128)S(1)} %slice.285), channel_id=1, source_target_pairs={{0,8},{1,17},{2,10},{3,19},{4,12},{5,21},{6,14},{7,23},{8,0},{9,25... | collective-permute-start | bytes 18440 | tf_op jit(solution)/shard_map/ppermute | solution.py:72
  419.6 28.4 %collective-permute-start.46 = (bf16[32,1536]{1,0:T(8,128)(2,1)S(1)}, bf16[32,1536]{1,0:T(8,128)(2,1)S(1)}, u32[]{:S(2)}, u32[]{:S(2)}) collective-permute-start(bf16[32,1536]{1,0:T(8,128)(2,1)S(1)} %copy-done.56), channel_id=1, source_target_pairs={{0,2},{1,3},{2,0},{3,1},{4,6},{5,7},{6,4},{7,5},{8,10},{9,11},{10,... | collective-permute-start | bytes 294920 | tf_op jit(solution)/shard_map/ppermute | solution.py:72
  435.8 16.2 %collective-permute-start.47 = (bf16[32,1536]{1,0:T(8,128)(2,1)S(1)}, bf16[32,1536]{1,0:T(8,128)(2,1)S(1)}, u32[]{:S(2)}, u32[]{:S(2)}) collective-permute-start(bf16[32,1536]{1,0:T(8,128)(2,1)S(1)} %copy-done.55), channel_id=1, source_target_pairs={{0,4},{1,5},{2,6},{3,7},{4,0},{5,1},{6,2},{7,3},{8,12},{9,13},{10,... | collective-permute-start | bytes 294920 | tf_op jit(solution)/shard_map/ppermute | solution.py:72
  (71 other events, 771.4 us)

commit v3 on v2

--- a/solution.py
+++ b/solution.py
@@ -12,7 +12,7 @@
 QB = 128
 SPAN = 512
 MANY = 4
-WEIGH = 3
+WEIGH = 2
 F32 = jnp.float32
 BF16 = jnp.bfloat16
 
@@ -51,21 +51,20 @@
                     both += own
                 keys.append(both)
             self.keys = np.array(keys, np.int32)
-            self.places = np.argsort(self.keys, 1).astype(np.int32)
 
     def place(self):
         if self.native:
             self.meta = jnp.array([0, 1, 2, 3, 0, 0], jnp.int32)
             self.order = jnp.arange(4)
+            self.tables = ()
             return
         me = lax.axis_index(self.axes)
         odd = (me & CORE) == 1
         mix = jnp.where(odd, jnp.array(MIX[1], jnp.int32), jnp.array(MIX[0], jnp.int32))
         self.meta = jnp.concatenate([(me >> 3) ^ mix, (me & CORE)[None], ((me >> 1) & 3)[None]])
         self.order = mix[jnp.arange(4) ^ (me >> 3)]
-        every = jnp.arange(self.count, dtype=jnp.int32)
         self.shard_of = me ^ jnp.where(odd, self.keys[1], self.keys[0])
-        self.slot_of = jnp.where(odd, self.places[1], self.places[0])[every ^ me]
+        self.tables = (self.order, self.shard_of)
 
     def flip(self, value, even, odd):
         bits = (even, odd)
@@ -77,24 +76,17 @@
     def across(self, value):
         return self.flip(value, CORE, CORE)
 
-    def gather_small(self, vector):
-        if self.native:
-            return lax.all_gather(vector, self.axes, axis=0, tiled=False)
-        held = vector[None]
-        for level in range(4):
-            held = jnp.concatenate([held, self.step(held, level)], 0)
-        return jnp.take(jnp.concatenate([held, self.across(held)], 0), self.slot_of, axis=0)
-
     def scatter_small(self, table):
         if self.native:
-            return lax.psum_scatter(table, self.axes, scatter_dimension=0, tiled=True).reshape(-1)
+            own = lax.psum_scatter(table, self.axes, scatter_dimension=0, tiled=True).reshape(-1)
+            return own, own
         half = self.count // 2
         table = jnp.take(table, self.shard_of, axis=0)
         total = table[:half] + self.across(table[half:])
         for level in (3, 2, 1, 0):
-            half = half // 2
+            half, before = half // 2, total
             total = total[:half] + self.step(total[half:], level)
-        return total[0]
+        return total[0], before
 
 
 def place_kernel(meta, *refs):
@@ -105,11 +97,11 @@
 
 def place_group(meta, pieces):
     rows, columns = pieces[0].shape
-    tile = columns // 2
+    tile = columns
     return pl.pallas_call(
         place_kernel,
         grid_spec=pltpu.PrefetchScalarGridSpec(
-            num_scalar_prefetch=1, grid=(2,), in_specs=[pl.BlockSpec((rows, tile), lambda n, meta: (0, n))] * 4,
+            num_scalar_prefetch=1, grid=(1,), in_specs=[pl.BlockSpec((rows, tile), lambda n, meta: (0, n))] * 4,
             out_specs=pl.BlockSpec((4, rows, tile), lambda n, meta: (0, 0, n))),
         out_shape=jax.ShapeDtypeStruct((4, rows, columns), pieces[0].dtype),
         cost_estimate=cost(2),
@@ -148,7 +140,7 @@
 class Gather:
     def __init__(self, ladder, shard, direct):
         self.ladder, self.shard, self.native, self.direct = ladder, shard, ladder.native, direct
-        self.sent = ()
+        self.sent, self.others = (), []
 
     def start(self, *after):
         if not self.native:
@@ -361,57 +353,62 @@
     return lo.astype(jnp.int32), segc, padc, segment_ids.reshape(nblocks, QB)
 
 
-def attn_forward(q, k, v, masks, first=0, pairs=None):
-    length, many = q[0].shape[0], MANY
-    width = 128 * many
+def attn_call(kernel, name, each, operands, specs, shapes, out_specs, scratch, masks, first, pairs, before):
+    lo, segc, padc, segr = masks
+    length = segc.shape[0]
     nblocks = length // QB
     most = min(nblocks, SPAN // QB + 1)
-    pairs = pairs or 8
-    lo, segc, padc, segr = masks
+    whole = lambda p, lo: (0, 0)
+    in_specs = [pl.BlockSpec((length, QB), whole), pl.BlockSpec((length, QB), whole), pl.BlockSpec((nblocks, QB), whole)] + specs
+    arguments = [lo, segc, padc, segr] + operands
+    aliases = {}
+    if before is not None:
+        aliases = {len(arguments) + i: i for i in range(len(before))}
+        in_specs, arguments = in_specs + [pl.BlockSpec(memory_space=pl.ANY)] * len(before), arguments + list(before)
+
+    def body(*refs):
+        inputs, rest = refs[: len(arguments) - len(aliases)], refs[len(arguments) :]
+        kernel(nblocks, most, MANY, *inputs, *rest)
+
+    return pl.pallas_call(
+        body,
+        grid_spec=pltpu.PrefetchScalarGridSpec(
+            num_scalar_prefetch=1, grid=(pairs // MANY,), in_specs=in_specs, out_specs=out_specs,
+            scratch_shapes=[pltpu.VMEM((nblocks, most * QB, QB), F32)] + scratch),
+        out_shape=shapes,
+        input_output_aliases=aliases,
+        compiler_params=pltpu.CompilerParams(vmem_limit_bytes=48 << 20),
+        cost_estimate=cost(each * pairs),
+        name=name,
+    )(*arguments)
+
+
+def attn_forward(q, k, v, masks, first, pairs, before=None):
     (qa, qo), (ka, ko), (va, vo) = q, k, v
-    whole = lambda p, lo: (0, 0)
-    col = lambda off: pl.BlockSpec((length, width), lambda p, lo: (0, (off + first) // many + p))
-    return pl.pallas_call(
-        functools.partial(attn_fwd_kernel, nblocks, most, many),
-        grid_spec=pltpu.PrefetchScalarGridSpec(
-            num_scalar_prefetch=1, grid=(pairs // many,),
-            in_specs=[pl.BlockSpec((length, QB), whole), pl.BlockSpec((length, QB), whole), pl.BlockSpec((nblocks, QB), whole),
-                      col(qo), col(ko), col(vo)],
-            out_specs=[pl.BlockSpec((length, width), lambda p, lo: (0, p)),
-                       pl.BlockSpec((many, nblocks, 2 * QB), lambda p, lo: (p, 0, 0))],
-            scratch_shapes=[pltpu.VMEM((nblocks, most * QB, QB), F32), pltpu.VMEM((width, length), BF16)]),
-        out_shape=[jax.ShapeDtypeStruct((length, pairs * 128), BF16), jax.ShapeDtypeStruct((pairs, nblocks, 2 * QB), F32)],
-        compiler_params=pltpu.CompilerParams(vmem_limit_bytes=48 << 20),
-        cost_estimate=cost(11),
-        name="attn_forward",
-    )(lo, segc, padc, segr, qa, ka, va)
-
-
-def attn_backward(q, k, v, do, lse, masks, first=0, pairs=None):
-    length, many = q[0].shape[0], MANY
-    width = 128 * many
-    nblocks = length // QB
-    most = min(nblocks, SPAN // QB + 1)
-    pairs = pairs or 8
-    lo, segc, padc, segr = masks
+    length, width = qa.shape[0], 128 * MANY
+    at = first // MANY
+    col = lambda off: pl.BlockSpec((length, width), lambda p, lo: (0, off // MANY + at + p))
+    stat = pl.BlockSpec((MANY, length // QB, 2 * QB), lambda p, lo: (at + p, 0, 0))
+    total = ko - qo
+    return attn_call(
+        attn_fwd_kernel, "attn_forward", 2.7, [qa, ka, va], [col(qo), col(ko), col(vo)],
+        [jax.ShapeDtypeStruct((length, 128 * total), BF16), jax.ShapeDtypeStruct((total, length // QB, 2 * QB), F32)],
+        [col(0), stat], [pltpu.VMEM((width, length), BF16)], masks, first, pairs, before)
+
+
+def attn_backward(q, k, v, do, lse, masks, first, pairs, before=None):
     (qa, qo), (ka, ko), (va, vo) = q, k, v
-    whole = lambda p, lo: (0, 0)
-    col = lambda off: pl.BlockSpec((length, width), lambda p, lo: (0, (off + first) // many + p))
-    return pl.pallas_call(
-        functools.partial(attn_bwd_kernel, nblocks, most, many),
-        grid_spec=pltpu.PrefetchScalarGridSpec(
-            num_scalar_prefetch=1, grid=(pairs // many,),
-            in_specs=[pl.BlockSpec((length, QB), whole), pl.BlockSpec((length, QB), whole), pl.BlockSpec((nblocks, QB), whole),
-                      col(qo), col(ko), col(vo), col(0),
-                      pl.BlockSpec((many, nblocks, 2 * QB), lambda p, lo: (first // many + p, 0, 0))],
-            out_specs=[pl.BlockSpec((3, length, width), lambda p, lo: (0, 0, p)), pl.BlockSpec((8, width), lambda p, lo: (0, p))],
-            scratch_shapes=[pltpu.VMEM((nblocks, most * QB, QB), F32), pltpu.VMEM((width, length), BF16),
-                            pltpu.VMEM((length, width), F32), pltpu.VMEM((length, width), F32)]),
-        out_shape=[jax.ShapeDtypeStruct((3, length, pairs * 128), BF16), jax.ShapeDtypeStruct((8, pairs * 128), F32)],
-        compiler_params=pltpu.CompilerParams(vmem_limit_bytes=48 << 20),
-        cost_estimate=cost(16),
-        name="attn_backward",
-    )(lo, segc, padc, segr, qa, ka, va, do, lse)
+    length, width = qa.shape[0], 128 * MANY
+    at = first // MANY
+    col = lambda off: pl.BlockSpec((length, width), lambda p, lo: (0, off // MANY + at + p))
+    stat = pl.BlockSpec((MANY, length // QB, 2 * QB), lambda p, lo: (at + p, 0, 0))
+    total = ko - qo
+    return attn_call(
+        attn_bwd_kernel, "attn_backward", 3.4, [qa, ka, va, do, lse], [col(qo), col(ko), col(vo), col(0), stat],
+        [jax.ShapeDtypeStruct((3, length, 128 * total), BF16), jax.ShapeDtypeStruct((8, 128 * total), F32)],
+        [pl.BlockSpec((3, length, width), lambda p, lo: (0, 0, at + p)), pl.BlockSpec((8, width), lambda p, lo: (0, at + p))],
+        [pltpu.VMEM((width, length), BF16), pltpu.VMEM((length, width), F32), pltpu.VMEM((length, width), F32)],
+        masks, first, pairs, before)
 
 
 ANY = pl.BlockSpec(memory_space=pl.ANY)
@@ -442,13 +439,14 @@
 
 
 def fetch_quarter(native, meta, groups, target, t, sem):
+    cols = pl.ds(0, target.shape[-1])
     if native:
         rows = target.shape[-2]
-        pltpu.make_async_copy(groups[0].at[pl.ds(t * rows, rows), :], target.at[0, 0], sem).start()
+        pltpu.make_async_copy(groups[0].at[pl.ds(t * rows, rows), cols], target.at[0, 0], sem).start()
         return
     core = meta[4]
-    pltpu.make_async_copy(groups[t], target.at[:, core], sem).start()
-    pltpu.make_async_copy(groups[4 + t], target.at[:, 1 - core], sem).start()
+    pltpu.make_async_copy(groups[t].at[:, :, cols], target.at[:, core], sem).start()
+    pltpu.make_async_copy(groups[4 + t].at[:, :, cols], target.at[:, 1 - core], sem).start()
 
 
 def arrive(target, sem):
@@ -480,6 +478,14 @@
         pltpu.make_async_copy(stage.at[meta[t], :, 1 - core], outs[1].at[FLIP[t], :, :, cols], sem).start()
 
 
+def each_rows(total, rows, body):
+    def step(i, _):
+        body(i, pl.ds(pl.multiple_of(i * rows, rows), rows))
+        return 0
+
+    lax.fori_loop(0, total // rows, step, 0)
+
+
 def squares(values, valid):
     return jnp.sum(values * values * valid, 0, keepdims=True)
 
@@ -488,12 +494,51 @@
     return lax.rsqrt(jnp.mean(values * values, -1, keepdims=True) + 1e-05)
 
 
-def project_kernel(native, tile, meta, tok_ref, gain_ref, valid_ref, bias_ref, *rest):
-    groups, (out_ref, normed_ref, sq_ref, weight, sems) = rest[:-5], rest[-5:]
+SMALL = 16
+
+
+def pack_smalls(bias_up, bias_qv, bias_out, gain_attn, gain_mlp, bias_down, rows):
+    at = lax.broadcasted_iota(jnp.int32, (rows, 128), 0)
+    block = jnp.zeros((rows, 128), bias_up.dtype)
+    for row, part in enumerate((bias_up, bias_qv, bias_out, gain_attn, gain_mlp, bias_down)):
+        block = jnp.where(at == row, jnp.pad(part, (0, 128 - part.shape[0]))[None], block)
+    return block
+
+
+def unpack_smalls(held, up_ref, qkv_ref, lines_ref):
+    width = lines_ref.shape[1]
+    for shard in range(32):
+        up_ref[0:1, shard * 128 : (shard + 1) * 128] = held[shard, 0:1].astype(F32)
+    halves = held[...].astype(F32).reshape(16, 2, SMALL, 128)
+    halves = halves[:, 0] + pltpu.roll(halves[:, 1], 64, 2)
+    fours = held[...].astype(F32).reshape(8, 4, SMALL, 128)
+    fours = fours[:, 0] + sum(pltpu.roll(fours[:, i], 32 * i, 2) for i in range(1, 4))
+    qkv_ref[...] = jnp.zeros_like(qkv_ref)
+    for i in range(16):
+        first = i * 128 + (width if i >= 8 else 0)
+        qkv_ref[0:1, first : first + 128] = halves[i, 1:2]
+    for i in range(8):
+        lines_ref[0:4, i * 128 : (i + 1) * 128] = fours[i, 2:6]
+
+
+def project_kernel(native, tile, count, meta, tok_ref, valid_ref, *rest):
+    groups, rest = rest[:count], rest[count:]
+    if native:
+        up_in, qkv_in, lines_in, out_ref, normed_ref, sq_ref, weight, sems = rest
+    else:
+        out_ref, normed_ref, sq_ref, up_ref, lines_ref, weight, held, qkv_in, sems = rest
+        lines_in = lines_ref
     n, steps = pl.program_id(0), pl.num_programs(0)
+    columns = steps * tile
 
     @pl.when(n == 0)
     def _():
+        if not native:
+            last = pl.ds(columns, 128)
+            for t in range(4):
+                for first, side in ((0, meta[4]), (4, 1 - meta[4])):
+                    source = groups[first + t].at[:, pl.ds(0, SMALL), last]
+                    pltpu.make_async_copy(source, held.at[meta[t], :, side], sems.at[2]).start()
         fetch_columns(native, meta, groups, weight.at[0], 0, tile, sems.at[0])
 
     @pl.when(n + 1 < steps)
@@ -503,33 +548,52 @@
 
     @pl.when(n == 0)
     def _():
-        frames = tok_ref[...].astype(F32)
-        sq_ref[...] = squares(frames, valid_ref[...])
-        normed_ref[...] = (frames * scale_of(frames) * gain_ref[...]).astype(BF16)
+        if not native:
+            arrive(held, sems.at[2])
+            unpack_smalls(held[...].reshape(32, SMALL, 128), up_ref, qkv_in, lines_ref)
+        sq_ref[...] = jnp.zeros_like(sq_ref)
+
+        def norm(i, at):
+            frames = tok_ref[at, :].astype(F32)
+            sq_ref[...] += squares(frames, valid_ref[at, :])
+            normed_ref[at, :] = (frames * scale_of(frames) * lines_in[1:2, :]).astype(BF16)
+
+        each_rows(tok_ref.shape[0], 256, norm)
 
     arrive(weight.at[n % 2], sems.at[n % 2])
-    out_ref[...] = (nn(normed_ref[...], flat(weight[n % 2])) + bias_ref[...]).astype(BF16)
-
-
-def project(ladder, tokens, gain, valid, bias, groups):
+    bias = qkv_in[0:1, pl.ds(pl.multiple_of(n * tile, tile), tile)]
+    out_ref[...] = (nn(normed_ref[...], flat(weight[n % 2])) + bias).astype(BF16)
+
+
+def project(ladder, tokens, valid, groups, known=None):
     length, width = tokens.shape
-    columns, tile = bias.shape[1], 512
+    columns, tile, hidden = 3 * width, 512, 4 * width
+    native = ladder.native
     whole = lambda n, meta: (0, 0)
-    return pl.pallas_call(
-        functools.partial(project_kernel, ladder.native, tile),
+    up, lines = pl.BlockSpec((1, hidden), whole), pl.BlockSpec((4, width), whole)
+    out_specs = [pl.BlockSpec((length, tile), lambda n, meta: (0, n)), pl.BlockSpec((length, width), whole), pl.BlockSpec((1, width), whole)]
+    out_shape = [jax.ShapeDtypeStruct((length, columns), BF16), jax.ShapeDtypeStruct((length, width), BF16),
+                 jax.ShapeDtypeStruct((1, width), F32)]
+    scratch = [pltpu.VMEM((2,) + tile_shape(native, width, tile), BF16)]
+    vectors = [jax.ShapeDtypeStruct((1, hidden), F32), jax.ShapeDtypeStruct((4, width), F32)]
+    extra = []
+    if native:
+        extra = [up, pl.BlockSpec((1, columns), whole), lines]
+    else:
+        out_specs, out_shape = out_specs + [up, lines], out_shape + vectors
+        scratch += [pltpu.VMEM((4, 4, 2, SMALL, 128), BF16), pltpu.VMEM((1, columns), F32)]
+    results = pl.pallas_call(
+        functools.partial(project_kernel, native, tile, len(groups)),
         grid_spec=pltpu.PrefetchScalarGridSpec(
             num_scalar_prefetch=1, grid=(columns // tile,),
-            in_specs=[pl.BlockSpec((length, width), whole), pl.BlockSpec((1, width), whole), pl.BlockSpec((length, 1), whole),
-                      pl.BlockSpec((1, tile), lambda n, meta: (0, n))] + group_specs(groups),
-            out_specs=[pl.BlockSpec((length, tile), lambda n, meta: (0, n)), pl.BlockSpec((length, width), whole),
-                       pl.BlockSpec((1, width), whole)],
-            scratch_shapes=[pltpu.VMEM((2,) + tile_shape(ladder.native, width, tile), BF16), pltpu.SemaphoreType.DMA((2,))]),
-        out_shape=[jax.ShapeDtypeStruct((length, columns), BF16), jax.ShapeDtypeStruct((length, width), BF16),
-                   jax.ShapeDtypeStruct((1, width), F32)],
+            in_specs=[pl.BlockSpec((length, width), whole), pl.BlockSpec((length, 1), whole)] + group_specs(groups) + extra,
+            out_specs=out_specs, scratch_shapes=scratch + [pltpu.SemaphoreType.DMA((3,))]),
+        out_shape=out_shape,
         compiler_params=params(),
         cost_estimate=cost(14),
         name="project",
-    )(ladder.meta, tokens, gain, valid, bias, *groups)
+    )(ladder.meta, tokens, valid, *groups, *(known or ()))
+    return results if not native else list(results) + [known[0], known[2]]
 
 
 def gelu_pair(u):
@@ -541,7 +605,7 @@
     return (u * half).astype(BF16), slope.astype(BF16)
 
 
-def expand_kernel(native, tile, count, meta, mixed_ref, tok_ref, bias_ref, gain_ref, valid_ref, up_bias_ref, *rest):
+def expand_kernel(native, tile, count, meta, mixed_ref, tok_ref, lines_ref, valid_ref, up_bias_ref, *rest):
     groups, rest = rest[:count], rest[count:]
     middle_ref, normed_ref, sq_ref, act_ref, slope_ref, middle, out_weight, weight, sems = rest
     n, steps = pl.program_id(0), pl.num_programs(0)
@@ -565,19 +629,16 @@
         for side in range(2):
             arrive(out_weight.at[side], sems.at[2 + side])
         sq_ref[...] = jnp.zeros_like(sq_ref)
-        rows = 256
-
-        def part(i, _):
-            at = pl.ds(pl.multiple_of(i * rows, rows), rows)
-            branch = jnp.concatenate([nn(mixed_ref[at, :], flat(out_weight[side])) for side in range(2)], 1) + bias_ref[...]
+
+        def part(i, at):
+            branch = jnp.concatenate([nn(mixed_ref[at, :], flat(out_weight[side])) for side in range(2)], 1) + lines_ref[0:1, :]
             total = tok_ref[at, :].astype(F32) + branch
             middle[at, :] = total
-            normed_ref[at, :] = (total * scale_of(total) * gain_ref[...]).astype(BF16)
+            normed_ref[at, :] = (total * scale_of(total) * lines_ref[2:3, :]).astype(BF16)
             sq_ref[0:1, :] += squares(branch, valid_ref[at, :])
             sq_ref[1:2, :] += squares(total, valid_ref[at, :])
-            return 0
-
-        lax.fori_loop(0, middle.shape[0] // rows, part, 0)
+
+        each_rows(middle.shape[0], 256, part)
         store.start()
 
     arrive(weight.at[n % 2], sems.at[n % 2])
@@ -588,17 +649,17 @@
         store.wait()
 
 
-def expand(ladder, mixed, tokens, bias, gain, valid, up_bias, groups):
+def expand(ladder, mixed, tokens, lines, valid, up_bias, groups):
     length, width = tokens.shape
     columns, tile = up_bias.shape[1], 512
     whole = lambda n, meta: (0, 0)
     column = lambda n, meta: (0, n)
-    square, line = pl.BlockSpec((length, width), whole), pl.BlockSpec((1, width), whole)
+    square = pl.BlockSpec((length, width), whole)
     return pl.pallas_call(
         functools.partial(expand_kernel, ladder.native, tile, len(groups)),
         grid_spec=pltpu.PrefetchScalarGridSpec(
             num_scalar_prefetch=1, grid=(columns // tile,),
-            in_specs=[square, square, line, line, pl.BlockSpec((length, 1), whole), pl.BlockSpec((1, tile), column)]
+            in_specs=[square, square, pl.BlockSpec((4, width), whole), pl.BlockSpec((length, 1), whole), pl.BlockSpec((1, tile), column)]
             + group_specs(groups),
             out_specs=[ANY, square, pl.BlockSpec((8, width), whole), pl.BlockSpec((length, tile), column),
                        pl.BlockSpec((length, tile), column)],
@@ -610,7 +671,7 @@
         compiler_params=params(),
         cost_estimate=cost(29),
         name="expand",
-    )(ladder.meta, mixed, tokens, bias, gain, valid, up_bias, *groups)
+    )(ladder.meta, mixed, tokens, lines, valid, up_bias, *groups)
 
 
 def fetch_turn(native, meta, groups, weight, sems, t, first=0, last=3):
@@ -722,7 +783,7 @@
     return r * (scaled - hat * jnp.mean(scaled * hat, -1, keepdims=True)), gain_grad
 
 
-def back_kernel(native, last, counts, meta, cot_ref, slope_ref, normed_ref, gain_ref, middle_ref, mixed_ref, *rest):
+def back_kernel(native, last, counts, meta, cot_ref, slope_ref, normed_ref, lines_ref, middle_ref, mixed_ref, *rest):
     down_groups, rest = rest[: counts[0]], rest[counts[0] :]
     groups, rest = rest[: counts[0]], rest[counts[0] :]
     if last:
@@ -730,7 +791,7 @@
     pushed, rest = rest[: counts[1]], rest[counts[1] :]
     if last:
         out_ref, branch_ref, mixed_out_ref, sum_ref, up_sum_ref, rest = *rest[:5], rest[5:]
-        acc, down_weight, weight, stage, sems, middle, out_weight, out_stage = rest
+        acc, down_weight, weight, stage, sems, middle, out_weight = rest
     else:
         after, up_sum_ref, acc, down_weight, weight, stage, sems = rest
     base = 2 if last else 0
@@ -752,6 +813,7 @@
             fetch_columns(native, meta, groups, out_weight, 0, width, sems.at[8])
 
     fetch_turn(native, meta, down_groups, down_weight, sems, t, base, base + 1)
+    length = acc.shape[0]
     grad = (nt(cot_ref[...], flat(down_weight[t % 2])) * slope_ref[...].astype(F32)).astype(BF16)
     up_sum_ref[...] = jnp.sum(grad.astype(F32), 0, keepdims=True)
     stage[slot] = tn(normed_ref[...], grad).astype(BF16).reshape(stage.shape[1:])
@@ -773,26 +835,23 @@
         if last:
             pltpu.make_async_copy(middle_ref, middle, sems.at[7]).wait()
             sum_ref[...] = jnp.zeros_like(sum_ref)
-            rows = 256
-
-            def part(i, _):
-                at = pl.ds(pl.multiple_of(i * rows, rows), rows)
-                back, gain_grad = norm_grad(acc[at, :], middle[at, :], gain_ref[...])
+
+            def part(i, at):
+                back, gain_grad = norm_grad(acc[at, :], middle[at, :], lines_ref[2:3, :])
                 total = cot_ref[at, :].astype(F32) + back
                 acc[at, :] = total
                 branch = total.astype(BF16)
                 branch_ref[at, :] = branch
                 sum_ref[0:1, :] += gain_grad
                 sum_ref[1:2, :] += jnp.sum(branch.astype(F32), 0, keepdims=True)
-                return 0
-
-            lax.fori_loop(0, acc.shape[0] // rows, part, 0)
+
+            each_rows(length, 256, part)
             pltpu.make_async_copy(acc, out_ref, sems.at[6]).start()
-            out_stage[...] = tn(mixed_ref[...], branch_ref[...]).astype(BF16).reshape(out_stage.shape)
-            push_columns(native, meta, out_stage, pushed, 0, width, sems.at[7])
+            arrive(stage.at[0], sems.at[4])
+            stage[0] = tn(mixed_ref[...], branch_ref[...]).astype(BF16).reshape(stage.shape[1:])
+            push_columns(native, meta, stage.at[0], pushed, 0, width, sems.at[4])
             arrive(out_weight, sems.at[8])
             mixed_out_ref[...] = nt(branch_ref[...], flat(out_weight[...])).astype(BF16)
-            arrive(out_stage, sems.at[7])
             pltpu.make_async_copy(acc, out_ref, sems.at[6]).wait()
         else:
             pltpu.make_async_copy(acc, after, sems.at[6]).start()
@@ -801,7 +860,7 @@
             arrive(stage.at[at], sems.at[4 + at])
 
 
-def back(ladder, cot, slope, normed, gain, middle, mixed, down_groups, groups, before=None):
+def back(ladder, cot, slope, normed, lines, middle, mixed, down_groups, groups, before=None):
     length, width = cot.shape
     hidden, tile = slope.shape[1], slope.shape[1] // 4
     last = before is not None
@@ -814,9 +873,9 @@
     counts = (len(groups), len(outs))
     full, wide = jax.ShapeDtypeStruct((length, width), F32), jax.ShapeDtypeStruct((length, width), BF16)
     sums = jax.ShapeDtypeStruct((1, hidden), F32)
-    in_specs = [once, pl.BlockSpec((length, tile), part), once, pl.BlockSpec((1, width), whole), ANY, once if last else ANY]
+    in_specs = [once, pl.BlockSpec((length, tile), part), once, pl.BlockSpec((4, width), whole), ANY, once if last else ANY]
     in_specs += [ANY] * (2 * counts[0])
-    operands = [ladder.meta, cot, slope, normed, gain, middle, mixed, *down_groups, *groups]
+    operands = [ladder.meta, cot, slope, normed, lines, middle, mixed, *down_groups, *groups]
     scratch = [pltpu.VMEM((length, width), F32), pltpu.VMEM((2,) + quarter_shape(ladder.native, hidden, width), BF16),
                pltpu.VMEM((2,) + tile_shape(ladder.native, width, tile), BF16),
                pltpu.VMEM((2,) + tile_shape(ladder.native, width, tile), BF16), pltpu.SemaphoreType.DMA((9,))]
@@ -827,8 +886,7 @@
         in_specs += [ANY] * (1 + counts[1])
         out_specs = [ANY] * counts[1] + [ANY, square, square, pl.BlockSpec((8, width), whole)]
         out_shape = outs + [full, wide, wide, jax.ShapeDtypeStruct((8, width), F32)]
-        scratch += [pltpu.VMEM((length, width), F32), pltpu.VMEM(tile_shape(ladder.native, width, width), BF16),
-                    pltpu.VMEM(tile_shape(ladder.native, width, width), BF16)]
+        scratch += [pltpu.VMEM((length, width), F32), pltpu.VMEM(tile_shape(ladder.native, width, width), BF16)]
     else:
         out_specs, out_shape = [ANY] * counts[1] + [ANY], outs + [full]
     return pl.pallas_call(
@@ -844,10 +902,10 @@
     )(*operands)
 
 
-def contract_kernel(native, meta, act_ref, bias_ref, valid_ref, middle_ref, *rest):
+def contract_kernel(native, first, meta, act_ref, lines_ref, valid_ref, middle_ref, *rest):
     groups, (out_ref, sq_ref, acc, middle, weight, sems) = rest[:-6], rest[-6:]
     t = pl.program_id(0)
-    load = pltpu.make_async_copy(middle_ref, middle, sems.at[2])
+    load = pltpu.make_async_copy(middle_ref.at[pl.ds(first, acc.shape[0]), :], middle, sems.at[2])
 
     @pl.when(t == 0)
     def _():
@@ -872,7 +930,7 @@
 
         def part(i, _):
             at = pl.ds(pl.multiple_of(i * rows, rows), rows)
-            branch = acc[at, :] + bias_ref[...]
+            branch = acc[at, :] + lines_ref[3:4, :]
             final = middle[at, :] + branch
             out_ref[at, :] = final.astype(BF16)
             sq_ref[0:1, :] += squares(branch, valid_ref[at, :])
@@ -882,28 +940,29 @@
         lax.fori_loop(0, acc.shape[0] // rows, part, 0)
 
 
-def contract(ladder, act, middle, bias, valid, groups):
+def contract(ladder, act, middle, lines, valid, groups, part, parts):
     length, width = middle.shape
+    length //= parts
     hidden = act.shape[1]
     whole = lambda t, meta: (0, 0)
     return pl.pallas_call(
-        functools.partial(contract_kernel, ladder.native),
+        functools.partial(contract_kernel, ladder.native, part * length),
         grid_spec=pltpu.PrefetchScalarGridSpec(
             num_scalar_prefetch=1, grid=(4,),
-            in_specs=[pl.BlockSpec((length, hidden // 4), lambda t, meta: (0, meta[t])), pl.BlockSpec((1, width), whole),
-                      pl.BlockSpec((length, 1), whole), ANY] + group_specs(groups),
+            in_specs=[pl.BlockSpec((length, hidden // 4), lambda t, meta: (part, meta[t])), pl.BlockSpec((4, width), whole),
+                      pl.BlockSpec((length, 1), lambda t, meta: (part, 0)), ANY] + group_specs(groups),
             out_specs=[pl.BlockSpec((length, width), whole), pl.BlockSpec((8, width), whole)],
             scratch_shapes=[pltpu.VMEM((length, width), F32), pltpu.VMEM((length, width), F32),
                             pltpu.VMEM((2,) + quarter_shape(ladder.native, hidden, width), BF16), pltpu.SemaphoreType.DMA((3,))]),
         out_shape=[jax.ShapeDtypeStruct((length, width), BF16), jax.ShapeDtypeStruct((8, width), F32)],
         compiler_params=params(),
-        cost_estimate=cost(16),
+        cost_estimate=cost(16 // parts),
         name="contract",
-    )(ladder.meta, act, bias, valid, middle, *groups)
+    )(ladder.meta, act, lines, valid, middle, *groups)
 
 
 def input_grad_kernel(native, calls, meta, *rest):
-    grads, (tok_ref, middle_ref, gain_ref), rest = rest[:calls], rest[calls : calls + 3], rest[calls + 3 :]
+    grads, (tok_ref, middle_ref, lines_ref), rest = rest[:calls], rest[calls : calls + 3], rest[calls + 3 :]
     groups, (out_ref, sum_ref, acc, middle, weight, sems) = rest[:-6], rest[-6:]
     t = pl.program_id(0)
     load = pltpu.make_async_copy(middle_ref, middle, sems.at[2])
@@ -932,7 +991,7 @@
 
         def part(i, _):
             at = pl.ds(pl.multiple_of(i * rows, rows), rows)
-            back, gain_grad = norm_grad(acc[at, :], tok_ref[at, :].astype(F32), gain_ref[...])
+            back, gain_grad = norm_grad(acc[at, :], tok_ref[at, :].astype(F32), lines_ref[1:2, :])
             out_ref[at, :] = (middle[at, :] + back).astype(BF16)
             sum_ref[0:1, :] += gain_grad
             return 0
@@ -940,7 +999,7 @@
         lax.fori_loop(0, acc.shape[0] // rows, part, 0)
 
 
-def input_grad(ladder, grads, tokens, grad_middle, gain, groups):
+def input_grad(ladder, grads, tokens, grad_middle, lines, groups):
     length, width = tokens.shape
     calls = len(grads)
     whole = lambda t, meta: (0, 0)
@@ -949,7 +1008,7 @@
         functools.partial(input_grad_kernel, ladder.native, calls),
         grid_spec=pltpu.PrefetchScalarGridSpec(
             num_scalar_prefetch=1, grid=(4,),
-            in_specs=[pl.BlockSpec((3, length, width // calls), lambda t, meta: (0, 0, 0))] * calls + [square, ANY, pl.BlockSpec((1, width), whole)]
+            in_specs=[pl.BlockSpec((3, length, width // calls), lambda t, meta: (0, 0, 0))] * calls + [square, ANY, pl.BlockSpec((4, width), whole)]
             + group_specs(groups),
             out_specs=[square, pl.BlockSpec((8, width), whole)],
             scratch_shapes=[pltpu.VMEM((length, width), F32), pltpu.VMEM((length, width), F32),
@@ -958,7 +1017,7 @@
         compiler_params=params(),
         cost_estimate=cost(18),
         name="input_grad",
-    )(ladder.meta, *grads, tokens, grad_middle, gain, *groups)
+    )(ladder.meta, *grads, tokens, grad_middle, lines, *groups)
 
 
 def local(ladder, tokens, cotangent, segment_ids, padding_mask, w_qkv, bias_qv, w_out, bias_out, gain_attn, gain_mlp,
@@ -971,104 +1030,107 @@
     def sent(*flows):
         return [value for flow in flows for value in flow.sent]
 
-    out_up = jnp.concatenate([w_out, w_up], 1)
-    qkv = Gather(ladder, w_qkv, True)
-    rest, down = Gather(ladder, out_up, False), Gather(ladder, w_down, False)
-    qkv.start()
-    smalls = [bias_qv, bias_out, gain_attn, gain_mlp, bias_up, bias_down]
-    sizes = [s.shape[0] for s in smalls]
+    sizes = [part.shape[0] for part in (bias_qv, bias_out, gain_attn, gain_mlp, bias_up, bias_down)]
     total = sum(sizes)
     ends = np.cumsum([0] + sizes)
-    packed = jnp.pad(jnp.concatenate(smalls), (0, -total % 128))
-    vectors = ladder.gather_small(packed).astype(F32)
-    qv_bias, out_bias, attn_gain, mlp_gain, up_bias, down_bias = [
-        vectors[:, ends[i] : ends[i + 1]].reshape(1, -1) for i in range(6)
-    ]
-    offset = jnp.concatenate([qv_bias[:, :width], jnp.zeros((1, width), F32), qv_bias[:, width:]], 1)
+    known = None
+    first = w_qkv
+    if ladder.native:
+        every = lambda part: lax.all_gather(part, ladder.axes, axis=0, tiled=True).astype(F32)[None]
+        qv = every(bias_qv)
+        known = [every(bias_up), jnp.concatenate([qv[:, :width], jnp.zeros((1, width), F32), qv[:, width:]], 1),
+                 jnp.concatenate([every(bias_out), every(gain_attn), every(gain_mlp), every(bias_down)], 0)]
+    else:
+        first = jnp.concatenate([w_qkv, pack_smalls(bias_up, bias_qv, bias_out, gain_attn, gain_mlp, bias_down, w_qkv.shape[0])], 1)
+    qkv, down = Gather(ladder, first, True), Gather(ladder, w_down, False)
+    qkv.start()
+    rest = Gather(ladder, jnp.concatenate([w_out, w_up], 1), False)
     masks = mask_inputs(segment_ids[0], padding_mask[0])
     valid = padding_mask[0].astype(F32)[:, None]
-    qkv.plane(vectors)
+    qkv.plane()
     rest.start(*qkv.sent)
     qkv.corner()
-    rest.low(*qkv.sent)
+    rest.low()
     qkv_groups = qkv.finish()
-    rest.plane(*qkv.sent)
-    projected, normed_in, sq_frames = project(ladder, tie(tokens, *sent(rest)), attn_gain, valid, offset, qkv_groups)
-    down.start(projected)
+    rest.plane()
+    down.start(*rest.sent)
+    projected, normed_in, sq_frames, up_bias, lines = project(ladder, tie(tokens, *sent(rest), *masks, *ladder.tables), valid, qkv_groups, known)
     per = width // 128
     calls = 2
     each = per // calls
 
+    down.low(projected)
+    projected = tie(projected, *sent(down))
+    per = width // 128
+    calls = 2
+    each = per // calls
+
     def triple():
         return (projected, 0), (projected, per), (projected, 2 * per)
 
-    mixed_parts, lse_parts = [], []
+    heads = None
     for call in range(calls):
-        mixed_part, lse_part = attn_forward(*triple(), masks, call * each, each)
-        mixed_parts.append(mixed_part)
-        lse_parts.append(lse_part)
+        heads = attn_forward(*triple(), masks, call * each, each, heads)
         if call == 0:
-            rest.corner(mixed_part)
-            down.low(mixed_part)
-            projected = tie(projected, mixed_part, *sent(rest, down))
-    down.plane(mixed_parts[-1])
-    rest_groups = rest.finish(mixed_parts[-1])
-    mixed = jnp.concatenate(mixed_parts, 1)
-    lse = jnp.concatenate(lse_parts, 0)
+            rest.corner(heads[0])
+            projected = tie(projected, heads[0], *sent(rest), *down.others)
+    mixed, lse = heads
+    rest_groups = rest.finish(mixed)
+    down.plane(*rest.sent)
     middle, normed_mid, sq_middle, act, slope = expand(
-        ladder, tie(mixed, *sent(down)), tokens, out_bias, mlp_gain, valid, up_bias, rest_groups)
+        ladder, tie(mixed, *sent(down)), tokens, lines, valid, up_bias, rest_groups)
 
     down.corner(act)
     *down_parts, sum_down = down_grad(ladder, tie(act, *sent(down)), cotangent)
     flow_down = Scatter(ladder, down_parts)
     down_groups = down.finish(sum_down)
     *first_parts, first_acc, first_sum = back(
-        ladder, tie(cotangent, sum_down), slope, normed_mid, mlp_gain, middle, mixed, down_groups, rest_groups)
+        ladder, tie(cotangent, sum_down), slope, normed_mid, lines, middle, mixed, down_groups, rest_groups)
     flow_down.corner(first_acc)
     *rest_parts, grad_middle, grad_branch, grad_mixed, sum_middle, second_sum = back(
-        ladder, tie(cotangent, *sent(flow_down)), slope, normed_mid, mlp_gain, middle, mixed, down_groups, rest_groups,
+        ladder, tie(cotangent, *sent(flow_down)), slope, normed_mid, lines, middle, mixed, down_groups, rest_groups,
         [first_acc, *first_parts])
     sum_up = jnp.concatenate([first_sum, second_sum], 1).reshape(4, -1)[ladder.order].reshape(1, -1)
     flow_rest = Scatter(ladder, rest_parts)
     flow_down.plane(grad_mixed)
     grad_mixed = tie(grad_mixed, *sent(flow_down))
-    grad_parts, sums, flow_qkv = [], [], []
+    heads = None
     for call in range(calls):
-        part, sum_part = attn_backward(*triple(), grad_mixed, lse, masks, call * each, each)
+        heads = attn_backward(*triple(), grad_mixed, lse, masks, call * each, each, heads)
         if call == 0:
-            flow_down.spread(part)
-            flow_rest.corner(part)
-            part = tie(part, *sent(flow_down, flow_rest))
-        else:
-            own_down = flow_down.finish(part)
-            flow_rest.plane(part)
-            flow_qkv[0].corner(part)
-            part = tie(part, *sent(flow_down, flow_rest, flow_qkv[0]))
-        grad_parts.append(part)
-        sums.append(sum_part)
-        flow_qkv.append(Scatter(ladder, row_grad(ladder, normed_in, part, "qkv_grad")))
-        if call == 0:
-            grad_mixed = tie(grad_mixed, *flow_qkv[0].parts)
-    sum_qv = jnp.concatenate(sums, 1)
-    tail = tie(tokens, *flow_qkv[1].parts)
-    grad_tokens, sum_in = input_grad(ladder, grad_parts, tail, grad_middle, attn_gain, qkv_groups)
-    flow_rest.spread(grad_tokens)
-    flow_qkv[0].plane(grad_tokens)
-    flow_qkv[1].corner(grad_tokens)
-    act_last = tie(act, grad_tokens, *sent(flow_rest, *flow_qkv))
-    output, sq_final = contract(ladder, act_last, middle, down_bias, valid, down_groups)
-    own_rest = flow_rest.finish(output)
-    flow_qkv[0].spread(output)
-    flow_qkv[1].plane(output)
-    members = [sq_frames[0], sq_middle[1], sq_final[1], sq_middle[0], sq_final[0]]
-    members = jnp.stack([jnp.sum(member) for member in members] + [jnp.sum(valid)])
+            flow_down.spread(heads[0])
+            flow_rest.corner(heads[0])
+            grad_mixed = tie(grad_mixed, heads[0], *sent(flow_down, flow_rest))
+    grad_projected, sum_qv = heads
+    own_down = flow_down.finish(grad_projected)
+    flow_qkv = Scatter(ladder, row_grad(ladder, normed_in, tie(grad_projected, *sent(flow_down)), "qkv_grad"))
+    flow_rest.plane(*flow_qkv.parts)
+    finals = []
+
+    def finish_rows(part, *after):
+        out, squares_out = contract(ladder, tie(act, *after), middle, lines, valid, down_groups, part, 2)
+        finals.append(squares_out)
+        return out
+
+    outputs = [finish_rows(0, *flow_qkv.parts, *sent(flow_rest))]
+    flow_rest.spread(outputs[0])
+    flow_qkv.corner(outputs[0])
+    tail = tie(tokens, *sent(flow_rest, flow_qkv))
+    grad_tokens, sum_in = input_grad(ladder, [grad_projected], tail, grad_middle, lines, qkv_groups)
+    flow_qkv.plane(grad_tokens)
+    outputs.append(finish_rows(1, *sent(flow_qkv)))
+    own_rest = flow_rest.finish(outputs[1])
+    flow_qkv.spread(outputs[1], own_rest)
+    output = jnp.concatenate(outputs, 0)
+
+    sq_final = finals[0] + finals[1]
+    members = [sq_frames, sq_middle[1:2], sq_final[1:2], sq_middle[:1], sq_final[:1], valid.reshape(1, -1)]
+    members = jnp.sum(jnp.concatenate(members, 0), 1)
     small_grads = [sum_qv[:2].reshape(-1), sum_middle[1], sum_in[0], sum_middle[0], sum_up[0], sum_down[0]]
     table = jnp.concatenate([g.reshape(count, -1) for g in small_grads] + [jnp.broadcast_to(members, (count, 6))], 1)
     table = jnp.pad(table, ((0, 0), (0, -table.shape[1] % 128)))
-    own_small = ladder.scatter_small(tie(table, *sent(*flow_qkv)))
-    flow_qkv[1].spread()
-    owns = [flow.finish().reshape(-1, 3, width // calls) for flow in flow_qkv]
-    own_qkv = jnp.concatenate(owns, 2).reshape(-1, 3 * width)
+    own_small, nearly = ladder.scatter_small(tie(table, *sent(flow_qkv)))
+    own_qkv = flow_qkv.finish(nearly)
 
     owned = [own_small[ends[i] : ends[i + 1]] for i in range(6)]
     totals = own_small[total : total + 6]

time: 487 us -> 419 us (0.86); the launches traced: 478 us -> 415 us
  starting transfers between devices: 63.8 us -> 43.1 us
  waiting for transfers between devices: 90.1 us -> 70.3 us
  local copies, waits for them, and re-layouts: 38 us -> 23.6 us
  other arithmetic: 41.3 us -> 33.3 us
    ppermute x62 -> x51, starting transfers between devices: 63.8 us -> 43.1 us  [flip(): lax.ppermute(value, self.axes, [(i, i ^ bits[i & CORE]) for i in range(se...]
    ppermute x62 -> x51, waiting for transfers between devices: 90.1 us -> 70.3 us  [flip(): lax.ppermute(value, self.axes, [(i, i ^ bits[i & CORE]) for i in range(se...]
    pallas_call x6 -> x7, Pallas kernels: 87.5 us -> 93.6 us  [the longest x4 54.6 us: attn_call(): pl.pallas_call(body, grid_spec=pltpu.PrefetchScalarGridSpec(num_scalar_pr...]
    pallas_call x2 -> x1, Pallas kernels: 15.6 us -> 12.3 us  [row_grad(): pl.pallas_call(functools.partial(row_grad_kernel, ladder.native, tile, le...]
    pallas_call x4 -> x3, Pallas kernels: 15.4 us -> 13 us  [spread_sums(): pl.pallas_call(spread_kernel, grid_spec=pltpu.PrefetchScalarGridSpec(num_...]
    convert_element_type x4 -> x3, other arithmetic: 11.9 us -> 11.5 us  [corner(): total = add_up(self.keep[2:], self.near[2:]).astype(BF16)]
  transfers between devices with their start and end apart: 62 -> 51, of which waited for: 18 -> 16; matrix products, arithmetic and copies ran while one was open for 13% -> 10% of each run, Pallas kernels for 49% -> 57%
where the time goes in v3:
time: 419 us; the launch traced here: 415 us
  Pallas kernels  242 us (58%)
  waiting for transfers between devices  70.3 us (17%)
  starting transfers between devices  43.1 us (10%)
  other arithmetic  33.3 us (8%)
  local copies, waits for them, and re-layouts  23.6 us (6%)
    ppermute x51, waiting for transfers between devices, flip(): lax.ppermute(value, self.axes, [(i, i ^ bits[i & CORE]) for i in range(se...  70.3 us
    pallas_call x2, Pallas kernels, back(): pl.pallas_call(functools.partial(back_kernel, ladder.native, last, counts...  58.5 us
    pallas_call x4, Pallas kernels, attn_call(): pl.pallas_call(body, grid_spec=pltpu.PrefetchScalarGridSpec(num_scalar_pr...  54.6 us
    ppermute x51, starting transfers between devices, flip(): lax.ppermute(value, self.axes, [(i, i ^ bits[i & CORE]) for i in range(se...  43.1 us
    pallas_call x1, Pallas kernels, expand(): pl.pallas_call(functools.partial(expand_kernel, ladder.native, tile, len(...  29.2 us
    pallas_call x2, Pallas kernels, contract(): pl.pallas_call(functools.partial(contract_kernel, ladder.native, part * l...  24.7 us
    pallas_call x1, Pallas kernels, input_grad(): pl.pallas_call(functools.partial(input_grad_kernel, ladder.native, calls)...  17.8 us
    pallas_call x1, Pallas kernels, down_grad(): pl.pallas_call(functools.partial(down_grad_kernel, ladder.native, len(out...  14.8 us
  transfers between devices with their start and end apart: 51, of which 16 were waited for; matrix products, arithmetic and copies ran while one was open for 10% of the time, Pallas kernels for 57%

profile of v3, /device:TPU:0, one launch (start us, length us, event | category | flops | bytes accessed | tf_op | source)
XLA Modules:
  0.0 414.9 jit_solution(14314846174829903359)
XLA Ops:
  5.7 5.1 %collective-permute-start.2 = (bf16[32,3200]{1,0:T(8,128)(2,1)S(1)}, bf16[32,3200]{1,0:T(8,128)(2,1)S(1)}, u32[]{:S(2)}, u32[]{:S(2)}) collective-permute-start(bf16[32,3200]{1,0:T(8,128)(2,1)S(1)} %pad_maximum_fusion.1.refs_0_), channel_id=1, source_target_pairs={{0,6},{1,7},{2,4},{3,5},{4,2},{5,3},{6,0},{7,1},{8,14},{9,15},{10,... | collective-permute-start | bytes 614408 | tf_op jit(solution)/shard_map/ppermute | solution.py:71
  14.1 2.8 collective-permute-done.2.refs_3_
  16.9 11.3 %collective-permute-done.1.refs_2_ = bf16[32,3200]{1,0:T(8,128)(2,1)S(1)} collective-permute-done((bf16[32,3200]{1,0:T(8,128)(2,1)S(1)}, bf16[32,3200]{1,0:T(8,128)(2,1)S(1)}, u32[]{:S(2)}, u32[]{:S(2)}) %collective-permute-start.1) | collective-permute-done | bytes 204832 | tf_op jit(solution)/shard_map/ppermute | solution.py:71
  29.6 2.8 place_group.1.rest_0_.rest_4_
  32.4 1.5 collective-permute-start.5
  34.7 1.6 collective-permute-start.6
  36.3 17.2 %collective-permute-done.5.rest_1_.rest_5_ = bf16[4,32,3200]{2,1,0:T(8,128)(2,1)} collective-permute-done((bf16[4,32,3200]{2,1,0:T(8,128)(2,1)}, bf16[4,32,3200]{2,1,0:T(8,128)(2,1)}, u32[]{:S(2)}, u32[]{:S(2)}) %collective-permute-start.5) | collective-permute-done | bytes 819232 | tf_op jit(solution)/shard_map/ppermute | solution.py:71
  53.5 1.8 collective-permute-start.7
  58.2 7.9 %collective-permute-done.7.rest_3_.rest_7_ = bf16[4,32,3200]{2,1,0:T(8,128)(2,1)} collective-permute-done((bf16[4,32,3200]{2,1,0:T(8,128)(2,1)}, bf16[4,32,3200]{2,1,0:T(8,128)(2,1)}, u32[]{:S(2)}, u32[]{:S(2)}) %collective-permute-start.7) | collective-permute-done | bytes 819232 | tf_op jit(solution)/shard_map/ppermute | solution.py:71
  66.3 2.6 collective-permute-done.4
  72.1 14.3 %project.1 = (bf16[1024,3072]{1,0:T(8,128)(2,1)}, bf16[1024,1024]{1,0:T(8,128)(2,1)}, f32[1,1024]{1,0:T(1,128)}, f32[1,4096]{1,0:T(1,128)}, f32[4,1024]{1,0:T(4,128)}) custom-call(s32[6]{0:T(128)} %pad_add_fusion.meta, bf16[1024,1024]{1,0:T(8,128)(2,1)} %bitcast.86, f32[1024,1]{1,0:T(8,128)} %copy.42.valid_ref, ...), custom_call_target="tpu_custom_call" | custom-call | flops 32199999488 | tf_op jit(solution)/shard_map/project/pallas_call | solution.py:585
  86.5 2.1 collective-permute-start.15
  88.5 11.1 %attn_forward.2 = (bf16[1024,1024]{1,0:T(8,128)(2,1)S(1)}, f32[8,8,256]{2,1,0:T(8,128)S(1)}) custom-call(s32[8]{0:T(128)S(1)} %and_select_fusion.refs_0_, s32[1024,128]{1,0:T(8,128)S(1)} %broadcast_in_dim.86.refs_1_, s32[1024,128]{1,0:T(8,128)S(1)} %broadcast_in_dim.88.refs_2_, s32[8,128]{1,0:T(8,128)S(1)} %bitcast.55, ...), custom_call_target="tpu_custom_call" | custom-call | flops 24839999488 | tf_op jit(solution)/shard_map/attn_forward/pallas_call | solution.py:373
  101.8 11.1 %attn_forward.3 = (bf16[1024,1024]{1,0:T(8,128)(2,1)S(1)}, f32[8,8,256]{2,1,0:T(8,128)S(1)}) custom-call(s32[8]{0:T(128)S(1)} %and_select_fusion.refs_0_, s32[1024,128]{1,0:T(8,128)S(1)} %broadcast_in_dim.86.refs_1_, s32[1024,128]{1,0:T(8,128)S(1)} %broadcast_in_dim.88.refs_2_, s32[8,128]{1,0:T(8,128)S(1)} %bitcast.56, ...), custom_call_target="tpu_custom_call", output_to_operand_aliasing={{0}: (7, {}), {1}: (8, {})} | custom-call | flops 24839999488 | tf_op jit(solution)/shard_map/attn_forward/pallas_call | solution.py:373
  112.9 6.1 %collective-permute-done.16.rest_3_.rest_11_ = bf16[4,32,5120]{2,1,0:T(8,128)(2,1)S(1)} collective-permute-done((bf16[4,32,5120]{2,1,0:T(8,128)(2,1)}, bf16[4,32,5120]{2,1,0:T(8,128)(2,1)S(1)}, u32[]{:S(2)}, u32[]{:S(2)}) %collective-permute-start.16) | collective-permute-done | bytes 1310752 | tf_op jit(solution)/shard_map/ppermute | solution.py:71
  123.3 29.2 %expand.1 = (f32[1024,1024]{1,0:T(8,128)}, bf16[1024,1024]{1,0:T(8,128)(2,1)}, f32[8,1024]{1,0:T(8,128)}, bf16[1024,4096]{1,0:T(8,128)(2,1)}, bf16[1024,4096]{1,0:T(8,128)(2,1)}) custom-call(s32[6]{0:T(128)} %pad_add_fusion.meta, bf16[1024,1024]{1,0:T(8,128)(2,1)} %copy-done.7, bf16[1024,1024]{1,0:T(8,128)(2,1)} %bitcast.87, ...), custom_call_target="tpu_custom_call" | custom-call | flops 66700001280 | tf_op jit(solution)/shard_map/expand/pallas_call | solution.py:658
  154.1 14.8 %down_grad.1 = (bf16[4,4,128,1024]{3,2,1,0:T(8,128)(2,1)}, bf16[4,4,128,1024]{3,2,1,0:T(8,128)(2,1)}, f32[1,1024]{1,0:T(1,128)}) custom-call(s32[6]{0:T(128)} %pad_add_fusion.meta, bf16[1024,4096]{1,0:T(8,128)(2,1)} %get-tuple-element.176.act_ref, bf16[1024,1024]{1,0:T(8,128)(2,1)} %bitcast.83), custom_call_target="tpu_custom_call" | custom-call | flops 32199999488 | tf_op jit(solution)/shard_map/down_grad/pallas_call | solution.py:725
  169.6 2.9 collective-permute-done.28.rest_7_
  173.5 24.0 %back.2 = (bf16[4,4,32,5120]{3,2,1,0:T(8,128)(2,1)}, bf16[4,4,32,5120]{3,2,1,0:T(8,128)(2,1)}, f32[1024,1024]{1,0:T(8,128)}, f32[1,2048]{1,0:T(1,128)}) custom-call(s32[6]{0:T(128)} %pad_add_fusion.meta, bf16[1024,1024]{1,0:T(8,128)(2,1)} %bitcast.84, bf16[1024,4096]{1,0:T(8,128)(2,1)} %get-tuple-element.133.slope_ref, ...), custom_call_target="tpu_custom_call" | custom-call | flops 46000001024 | tf_op jit(solution)/shard_map/back/pallas_call | solution.py:892
  197.4 3.2 add_convert_fusion.1
  202.1 34.6 %back.3 = (bf16[4,4,32,5120]{3,2,1,0:T(8,128)(2,1)}, bf16[4,4,32,5120]{3,2,1,0:T(8,128)(2,1)}, f32[1024,1024]{1,0:T(8,128)}, bf16[1024,1024]{1,0:T(8,128)(2,1)},...) custom-call(s32[6]{0:T(128)} %pad_add_fusion.meta, ...), custom_call_target="tpu_custom_call", output_to_operand_aliasing={{0}: (24, {}), {1}: (25, {})} | custom-call | flops 69000003584 | tf_op jit(solution)/shard_map/back/pallas_call | solution.py:892
  237.5 3.0 fusion.1
  241.2 16.0 %attn_backward.2 = (bf16[3,1024,1024]{2,1,0:T(8,128)(2,1)}, f32[8,1024]{1,0:T(8,128)S(1)}) custom-call(s32[8]{0:T(128)S(1)} %copy-done.6, s32[1024,128]{1,0:T(8,128)S(1)} %broadcast_in_dim.86.refs_1_, s32[1024,128]{1,0:T(8,128)S(1)} %broadcast_in_dim.88.refs_2_, s32[8,128]{1,0:T(8,128)S(1)} %bitcast.57, ...), custom_call_target="tpu_custom_call" | custom-call | flops 31280001024 | tf_op jit(solution)/shard_map/attn_backward/pallas_call | solution.py:373
  258.2 4.8 %spread_sums.3 = (f32[128,1024]{1,0:T(8,128)}, bf16[128,1024]{1,0:T(8,128)(2,1)}, bf16[128,1024]{1,0:T(8,128)(2,1)}, bf16[128,1024]{1,0:T(8,128)(2,1)}) custom-call(s32[6]{0:T(128)} %pad_add_fusion.meta, bf16[4,4,128,1024]{3,2,1,0:T(8,128)(2,1)} %get-tuple-element.129.refs_0_.refs_4_.refs_8_.refs_12_, ...), custom_call_target="tpu_custom_call" | custom-call | flops 6899999744 | tf_op jit(solution)/shard_map/spread_sums/pallas_call | solution.py:131
  264.2 3.3 collective-permute-start.34
  267.5 5.1 %add_convert_fusion = bf16[2,4,32,5120]{3,2,1,0:T(8,128)(2,1)} fusion(bf16[4,4,32,5120]{3,2,1,0:T(8,128)(2,1)} %collective-permute-done.31.refs_1_.refs_5_.refs_9_.refs_13_, bf16[4,4,32,5120]{3,2,1,0:T(8,128)(2,1)} %get-tuple-element.151.refs_0_.refs_4_.refs_8_.refs_12_), kind=kLoop, calls=%fused_computation.3 | loop fusion | flops 5242880 | bytes 7864320 | tf_op jit(solution)/shard_map/convert_element_type | solution.py:204
  272.7 16.4 %attn_backward.3 = (bf16[3,1024,1024]{2,1,0:T(8,128)(2,1)}, f32[8,1024]{1,0:T(8,128)S(1)}) custom-call(s32[8]{0:T(128)S(1)} %copy-done.6, s32[1024,128]{1,0:T(8,128)S(1)} %copy-done.3, s32[1024,128]{1,0:T(8,128)S(1)} %copy-done.1, s32[8,128]{1,0:T(8,128)S(1)} %bitcast.58, ...), custom_call_target="tpu_custom_call", output_to_operand_aliasing={{0}: (9, {}), {1}: (10, {})} | custom-call | flops 31280001024 | tf_op jit(solution)/shard_map/attn_backward/pallas_call | solution.py:373
  290.1 12.3 %qkv_grad.1 = (bf16[4,4,32,3072]{3,2,1,0:T(8,128)(2,1)}, bf16[4,4,32,3072]{3,2,1,0:T(8,128)(2,1)}) custom-call(s32[6]{0:T(128)} %pad_add_fusion.meta, bf16[1024,1024]{1,0:T(8,128)(2,1)} %get-tuple-element.125.left_ref, bf16[3,1024,1024]{2,1,0:T(8,128)(2,1)} %get-tuple-element.161.right_ref.rest_0_), custom_call_target="tpu_custom_call" | custom-call | flops 18400000000 | tf_op jit(solution)/shard_map/qkv_grad/pallas_call | solution.py:763
  307.5 2.7 fusion
  310.3 12.5 %contract.2 = (bf16[512,1024]{1,0:T(8,128)(2,1)}, f32[8,1024]{1,0:T(8,128)}) custom-call(s32[6]{0:T(128)} %pad_add_fusion.meta, bf16[1024,4096]{1,0:T(8,128)(2,1)} %get-tuple-element.176.act_ref, f32[4,1024]{1,0:T(4,128)} %get-tuple-element.122.lines_ref.rest_3_, f32[1024,1]{1,0:T(8,128)} %copy.42.valid_ref, f32[1024,1024]{1,0:T(8,128)} %get-tuple-element.135.middle_ref, ...), custom_call_target="tpu_custom_call" | custom-call | flops 18400000000 | tf_op jit(solution)/shard_map/contract/pallas_call | solution.py:948
  322.8 3.1 add_convert_fusion.2
  328.0 4.5 %spread_sums.4 = (f32[32,5120]{1,0:T(8,128)}, bf16[32,5120]{1,0:T(8,128)(2,1)}, bf16[32,5120]{1,0:T(8,128)(2,1)}, bf16[32,5120]{1,0:T(8,128)(2,1)}) custom-call(s32[6]{0:T(128)} %pad_add_fusion.meta, bf16[4,4,32,5120]{3,2,1,0:T(8,128)(2,1)} %get-tuple-element.151.refs_0_.refs_4_.refs_8_.refs_12_, ...), custom_call_target="tpu_custom_call" | custom-call | flops 6899999744 | tf_op jit(solution)/shard_map/spread_sums/pallas_call | solution.py:131
  334.6 2.4 collective-permute-start.42
  337.0 17.8 %input_grad.1 = (bf16[1024,1024]{1,0:T(8,128)(2,1)}, f32[8,1024]{1,0:T(8,128)}) custom-call(s32[6]{0:T(128)} %pad_add_fusion.meta, bf16[3,1024,1024]{2,1,0:T(8,128)(2,1)} %get-tuple-element.161.right_ref.rest_0_, bf16[1024,1024]{1,0:T(8,128)(2,1)} %bitcast.88, f32[1024,1024]{1,0:T(8,128)} %get-tuple-element.173.rest_2_, ...), custom_call_target="tpu_custom_call" | custom-call | flops 41400000512 | tf_op jit(solution)/shard_map/input_grad/pallas_call | solution.py:1007
  356.9 2.6 fusion.2
  359.9 12.3 %contract.3 = (bf16[512,1024]{1,0:T(8,128)(2,1)}, f32[8,1024]{1,0:T(8,128)}) custom-call(s32[6]{0:T(128)} %pad_add_fusion.meta, bf16[1024,4096]{1,0:T(8,128)(2,1)} %get-tuple-element.176.act_ref, f32[4,1024]{1,0:T(4,128)} %get-tuple-element.122.lines_ref.rest_3_, f32[1024,1]{1,0:T(8,128)} %copy.42.valid_ref, f32[1024,1024]{1,0:T(8,128)} %get-tuple-element.135.middle_ref, ...), custom_call_target="tpu_custom_call" | custom-call | flops 18400000000 | tf_op jit(solution)/shard_map/contract/pallas_call | solution.py:948
  375.5 3.6 spread_sums.5
  381.2 1.6 collective-permute-start.45
  382.8 2.2 collective-permute-done.45
  385.0 1.8 collective-permute-start.46
  386.8 1.9 collective-permute-done.46
  389.4 2.9 collective-permute-done.47
  392.4 1.6 collective-permute-start.50
  393.9 2.7 maximum_bitcast_fusion
  398.1 2.0 collective-permute-start.43
  400.5 2.1 collective-permute-start.49
  406.1 1.8 collective-permute-done.43
  407.9 5.9 %collective-permute-done.48 = bf16[32,3072]{1,0:T(8,128)(2,1)S(1)} collective-permute-done((bf16[32,3072]{1,0:T(8,128)(2,1)S(1)}, bf16[32,3072]{1,0:T(8,128)(2,1)S(1)}, u32[]{:S(2)}, u32[]{:S(2)}) %collective-permute-start.48) | collective-permute-done | bytes 196640 | tf_op jit(solution)/shard_map/ppermute | solution.py:71
  (268 shorter events, 55.4 us)
Async XLA Ops:
  5.7 11.2 %collective-permute-start.2 = (bf16[32,3200]{1,0:T(8,128)(2,1)S(1)}, bf16[32,3200]{1,0:T(8,128)(2,1)S(1)}, u32[]{:S(2)}, u32[]{:S(2)}) collective-permute-start(bf16[32,3200]{1,0:T(8,128)(2,1)S(1)} %pad_maximum_fusion.1.refs_0_), channel_id=1, source_target_pairs={{0,6},{1,7},{2,4},{3,5},{4,2},{5,3},{6,0},{7,1},{8,14},{9,15},{10,... | collective-permute-start | bytes 614408 | tf_op jit(solution)/shard_map/ppermute | solution.py:71
  10.8 17.4 %collective-permute-start.1 = (bf16[32,3200]{1,0:T(8,128)(2,1)S(1)}, bf16[32,3200]{1,0:T(8,128)(2,1)S(1)}, u32[]{:S(2)}, u32[]{:S(2)}) collective-permute-start(bf16[32,3200]{1,0:T(8,128)(2,1)S(1)} %pad_maximum_fusion.1.refs_0_), channel_id=1, source_target_pairs={{0,4},{1,5},{2,6},{3,7},{4,0},{5,1},{6,2},{7,3},{8,12},{9,13},{10,... | collective-permute-start | bytes 614408 | tf_op jit(solution)/shard_map/ppermute | solution.py:71
  10.8 17.4 %collective-permute-start = (bf16[32,3200]{1,0:T(8,128)(2,1)S(1)}, bf16[32,3200]{1,0:T(8,128)(2,1)S(1)}, u32[]{:S(2)}, u32[]{:S(2)}) collective-permute-start(bf16[32,3200]{1,0:T(8,128)(2,1)S(1)} %pad_maximum_fusion.1.refs_0_), channel_id=1, source_target_pairs={{0,2},{1,3},{2,0},{3,1},{4,6},{5,7},{6,4},{7,5},{8,10},{9,11},{10,... | collective-permute-start | bytes 614408 | tf_op jit(solution)/shard_map/ppermute | solution.py:71
  32.4 21.1 %collective-permute-start.5 = (bf16[4,32,3200]{2,1,0:T(8,128)(2,1)}, bf16[4,32,3200]{2,1,0:T(8,128)(2,1)}, u32[]{:S(2)}, u32[]{:S(2)}) collective-permute-start(bf16[4,32,3200]{2,1,0:T(8,128)(2,1)} %place_group.1.rest_0_.rest_4_), channel_id=1, source_target_pairs={{0,8},{1,17},{2,10},{3,19},{4,12},{5,21},{6,14},{7,23},{8,0},{9,25... | collective-permute-start | bytes 2457608 | tf_op jit(solution)/shard_map/ppermute | solution.py:71
  34.7 23.5 %collective-permute-start.6 = (bf16[4,32,3200]{2,1,0:T(8,128)(2,1)}, bf16[4,32,3200]{2,1,0:T(8,128)(2,1)}, u32[]{:S(2)}, u32[]{:S(2)}) collective-permute-start(bf16[4,32,3200]{2,1,0:T(8,128)(2,1)} %place_group.1.rest_0_.rest_4_), channel_id=1, source_target_pairs={{0,16},{1,9},{2,18},{3,11},{4,20},{5,13},{6,22},{7,15},{8,24},{9,1... | collective-permute-start | bytes 2457608 | tf_op jit(solution)/shard_map/ppermute | solution.py:71
  36.3 20.1 %collective-permute-start.3 = (bf16[32,5120]{1,0:T(8,128)(2,1)S(1)}, bf16[32,5120]{1,0:T(8,128)(2,1)S(1)}, u32[]{:S(2)}, u32[]{:S(2)}) collective-permute-start(bf16[32,5120]{1,0:T(8,128)(2,1)S(1)} %pad_maximum_fusion), channel_id=1, source_target_pairs={{0,4},{1,5},{2,6},{3,7},{4,0},{5,1},{6,2},{7,3},{8,12},{9,13},{10,... | collective-permute-start | bytes 983048 | tf_op jit(solution)/shard_map/ppermute | solution.py:71
  53.5 12.7 %collective-permute-start.7 = (bf16[4,32,3200]{2,1,0:T(8,128)(2,1)}, bf16[4,32,3200]{2,1,0:T(8,128)(2,1)}, u32[]{:S(2)}, u32[]{:S(2)}) collective-permute-start(bf16[4,32,3200]{2,1,0:T(8,128)(2,1)} %collective-permute-done.5.rest_1_.rest_5_), channel_id=1, source_target_pairs={{0,16},{1,9},{2,18},{3,11},{4,20},{5,13},{6,22},{7,15},{8,24},{9,1... | collective-permute-start | bytes 2457608 | tf_op jit(solution)/shard_map/ppermute | solution.py:71
  56.5 12.4 %collective-permute-start.4 = (bf16[2,32,5120]{2,1,0:T(8,128)(2,1)S(1)}, bf16[2,32,5120]{2,1,0:T(8,128)(2,1)S(1)}, u32[]{:S(2)}, u32[]{:S(2)}) collective-permute-start(bf16[2,32,5120]{2,1,0:T(8,128)(2,1)S(1)} %maximum_select_fusion.2), channel_id=1, source_target_pairs={{0,2},{1,3},{2,0},{3,1},{4,6},{5,7},{6,4},{7,5},{8,10},{9,11},{10,... | collective-permute-start | bytes 1966088 | tf_op jit(solution)/shard_map/ppermute | solution.py:71
  57.7 11.9 %collective-permute-start.8 = (bf16[4,32,3200]{2,1,0:T(8,128)(2,1)}, bf16[4,32,3200]{2,1,0:T(8,128)(2,1)S(1)}, u32[]{:S(2)}, u32[]{:S(2)}) collective-permute-start(bf16[4,32,3200]{2,1,0:T(8,128)(2,1)} %place_group.1.rest_0_.rest_4_), channel_id=1, source_target_pairs={{0,1},{1,0},{2,3},{3,2},{4,5},{5,4},{6,7},{7,6},{8,9},{9,8},{10,11... | collective-permute-start | bytes 2457608 | tf_op jit(solution)/shard_map/ppermute | solution.py:71
  57.7 13.4 %collective-permute-start.10 = (bf16[4,32,3200]{2,1,0:T(8,128)(2,1)}, bf16[4,32,3200]{2,1,0:T(8,128)(2,1)}, u32[]{:S(2)}, u32[]{:S(2)}) collective-permute-start(bf16[4,32,3200]{2,1,0:T(8,128)(2,1)} %collective-permute-done.5.rest_1_.rest_5_), channel_id=1, source_target_pairs={{0,1},{1,0},{2,3},{3,2},{4,5},{5,4},{6,7},{7,6},{8,9},{9,8},{10,11... | collective-permute-start | bytes 2457608 | tf_op jit(solution)/shard_map/ppermute | solution.py:71
  58.2 12.0 %collective-permute-start.9 = (bf16[4,32,3200]{2,1,0:T(8,128)(2,1)}, bf16[4,32,3200]{2,1,0:T(8,128)(2,1)S(1)}, u32[]{:S(2)}, u32[]{:S(2)}) collective-permute-start(bf16[4,32,3200]{2,1,0:T(8,128)(2,1)} %collective-permute-done.6.rest_2_.rest_6_), channel_id=1, source_target_pairs={{0,1},{1,0},{2,3},{3,2},{4,5},{5,4},{6,7},{7,6},{8,9},{9,8},{10,11... | collective-permute-start | bytes 2457608 | tf_op jit(solution)/shard_map/ppermute | solution.py:71
  66.2 5.9 %collective-permute-start.11 = (bf16[4,32,3200]{2,1,0:T(8,128)(2,1)}, bf16[4,32,3200]{2,1,0:T(8,128)(2,1)}, u32[]{:S(2)}, u32[]{:S(2)}) collective-permute-start(bf16[4,32,3200]{2,1,0:T(8,128)(2,1)} %collective-permute-done.7.rest_3_.rest_7_), channel_id=1, source_target_pairs={{0,1},{1,0},{2,3},{3,2},{4,5},{5,4},{6,7},{7,6},{8,9},{9,8},{10,11... | collective-permute-start | bytes 2457608 | tf_op jit(solution)/shard_map/ppermute | solution.py:71
  69.1 50.7 %collective-permute-start.17 = (bf16[4,32,5120]{2,1,0:T(8,128)(2,1)S(1)}, bf16[4,32,5120]{2,1,0:T(8,128)(2,1)S(1)}, u32[]{:S(2)}, u32[]{:S(2)}) collective-permute-start(bf16[4,32,5120]{2,1,0:T(8,128)(2,1)S(1)} %bitcast.61), channel_id=1, source_target_pairs={{0,1},{1,0},{2,3},{3,2},{4,5},{5,4},{6,7},{7,6},{8,9},{9,8},{10,11... | collective-permute-start | bytes 3932168 | tf_op jit(solution)/shard_map/ppermute | solution.py:71
  69.6 32.0 %collective-permute-start.14 = (bf16[4,32,5120]{2,1,0:T(8,128)(2,1)S(1)}, bf16[4,32,5120]{2,1,0:T(8,128)(2,1)}, u32[]{:S(2)}, u32[]{:S(2)}) collective-permute-start(bf16[4,32,5120]{2,1,0:T(8,128)(2,1)S(1)} %bitcast.62), channel_id=1, source_target_pairs={{0,16},{1,9},{2,18},{3,11},{4,20},{5,13},{6,22},{7,15},{8,24},{9,1... | collective-permute-start | bytes 3932168 | tf_op jit(solution)/shard_map/ppermute | solution.py:71
  70.2 30.8 %collective-permute-start.13 = (bf16[4,32,5120]{2,1,0:T(8,128)(2,1)S(1)}, bf16[4,32,5120]{2,1,0:T(8,128)(2,1)}, u32[]{:S(2)}, u32[]{:S(2)}) collective-permute-start(bf16[4,32,5120]{2,1,0:T(8,128)(2,1)S(1)} %bitcast.63), channel_id=1, source_target_pairs={{0,8},{1,17},{2,10},{3,19},{4,12},{5,21},{6,14},{7,23},{8,0},{9,25... | collective-permute-start | bytes 3932168 | tf_op jit(solution)/shard_map/ppermute | solution.py:71
  71.1 15.2 %collective-permute-start.12 = (bf16[128,1024]{1,0:T(8,128)(2,1)S(1)}, bf16[128,1024]{1,0:T(8,128)(2,1)S(1)}, u32[]{:S(2)}, u32[]{:S(2)}) collective-permute-start(bf16[128,1024]{1,0:T(8,128)(2,1)S(1)} %copy-done.18), channel_id=1, source_target_pairs={{0,4},{1,5},{2,6},{3,7},{4,0},{5,1},{6,2},{7,3},{8,12},{9,13},{10,... | collective-permute-start | bytes 786440 | tf_op jit(solution)/shard_map/ppermute | solution.py:71
  86.5 15.3 %collective-permute-start.15 = (bf16[2,128,1024]{2,1,0:T(8,128)(2,1)S(1)}, bf16[2,128,1024]{2,1,0:T(8,128)(2,1)S(1)}, u32[]{:S(2)}, u32[]{:S(2)}) collective-permute-start(bf16[2,128,1024]{2,1,0:T(8,128)(2,1)S(1)} %maximum_select_fusion.4), channel_id=1, source_target_pairs={{0,2},{1,3},{2,0},{3,1},{4,6},{5,7},{6,4},{7,5},{8,10},{9,11},{10,... | collective-permute-start | bytes 1572872 | tf_op jit(solution)/shard_map/ppermute | solution.py:71
  101.0 19.3 %collective-permute-start.19 = (bf16[4,32,5120]{2,1,0:T(8,128)(2,1)}, bf16[4,32,5120]{2,1,0:T(8,128)(2,1)}, u32[]{:S(2)}, u32[]{:S(2)}) collective-permute-start(bf16[4,32,5120]{2,1,0:T(8,128)(2,1)} %collective-permute-done.13.rest_1_.rest_9_), channel_id=1, source_target_pairs={{0,1},{1,0},{2,3},{3,2},{4,5},{5,4},{6,7},{7,6},{8,9},{9,8},{10,11... | collective-permute-start | bytes 3932168 | tf_op jit(solution)/shard_map/ppermute | solution.py:71
  101.1 17.8 %collective-permute-start.16 = (bf16[4,32,5120]{2,1,0:T(8,128)(2,1)}, bf16[4,32,5120]{2,1,0:T(8,128)(2,1)S(1)}, u32[]{:S(2)}, u32[]{:S(2)}) collective-permute-start(bf16[4,32,5120]{2,1,0:T(8,128)(2,1)} %collective-permute-done.13.rest_1_.rest_9_), channel_id=1, source_target_pairs={{0,16},{1,9},{2,18},{3,11},{4,20},{5,13},{6,22},{7,15},{8,24},{9,1... | collective-permute-start | bytes 3932168 | tf_op jit(solution)/shard_map/ppermute | solution.py:71
  101.6 19.5 %collective-permute-start.18 = (bf16[4,32,5120]{2,1,0:T(8,128)(2,1)}, bf16[4,32,5120]{2,1,0:T(8,128)(2,1)S(1)}, u32[]{:S(2)}, u32[]{:S(2)}) collective-permute-start(bf16[4,32,5120]{2,1,0:T(8,128)(2,1)} %collective-permute-done.14.rest_2_.rest_10_), channel_id=1, source_target_pairs={{0,1},{1,0},{2,3},{3,2},{4,5},{5,4},{6,7},{7,6},{8,9},{9,8},{10,11... | collective-permute-start | bytes 3932168 | tf_op jit(solution)/shard_map/ppermute | solution.py:71
  119.2 50.3 %collective-permute-start.25 = (bf16[4,128,1024]{2,1,0:T(8,128)(2,1)S(1)}, bf16[4,128,1024]{2,1,0:T(8,128)(2,1)S(1)}, u32[]{:S(2)}, u32[]{:S(2)}) collective-permute-start(bf16[4,128,1024]{2,1,0:T(8,128)(2,1)S(1)} %bitcast.69), channel_id=1, source_target_pairs={{0,1},{1,0},{2,3},{3,2},{4,5},{5,4},{6,7},{7,6},{8,9},{9,8},{10,11... | collective-permute-start | bytes 3145736 | tf_op jit(solution)/shard_map/ppermute | solution.py:71
  119.8 34.3 %collective-permute-start.22 = (bf16[4,128,1024]{2,1,0:T(8,128)(2,1)S(1)}, bf16[4,128,1024]{2,1,0:T(8,128)(2,1)S(1)}, u32[]{:S(2)}, u32[]{:S(2)}) collective-permute-start(bf16[4,128,1024]{2,1,0:T(8,128)(2,1)S(1)} %bitcast.70), channel_id=1, source_target_pairs={{0,16},{1,9},{2,18},{3,11},{4,20},{5,13},{6,22},{7,15},{8,24},{9,1... | collective-permute-start | bytes 3145736 | tf_op jit(solution)/shard_map/ppermute | solution.py:71
  120.3 32.2 %collective-permute-start.21 = (bf16[4,128,1024]{2,1,0:T(8,128)(2,1)S(1)}, bf16[4,128,1024]{2,1,0:T(8,128)(2,1)}, u32[]{:S(2)}, u32[]{:S(2)}) collective-permute-start(bf16[4,128,1024]{2,1,0:T(8,128)(2,1)S(1)} %bitcast.71), channel_id=1, source_target_pairs={{0,8},{1,17},{2,10},{3,19},{4,12},{5,21},{6,14},{7,23},{8,0},{9,25... | collective-permute-start | bytes 3145736 | tf_op jit(solution)/shard_map/ppermute | solution.py:71
  152.5 17.0 %collective-permute-start.27 = (bf16[4,128,1024]{2,1,0:T(8,128)(2,1)}, bf16[4,128,1024]{2,1,0:T(8,128)(2,1)S(1)}, u32[]{:S(2)}, u32[]{:S(2)}) collective-permute-start(bf16[4,128,1024]{2,1,0:T(8,128)(2,1)} %collective-permute-done.21.rest_1_), channel_id=1, source_target_pairs={{0,1},{1,0},{2,3},{3,2},{4,5},{5,4},{6,7},{7,6},{8,9},{9,8},{10,11... | collective-permute-start | bytes 3145736 | tf_op jit(solution)/shard_map/ppermute | solution.py:71
  152.6 16.3 %collective-permute-start.24 = (bf16[4,128,1024]{2,1,0:T(8,128)(2,1)}, bf16[4,128,1024]{2,1,0:T(8,128)(2,1)S(1)}, u32[]{:S(2)}, u32[]{:S(2)}) collective-permute-start(bf16[4,128,1024]{2,1,0:T(8,128)(2,1)} %collective-permute-done.21.rest_1_), channel_id=1, source_target_pairs={{0,16},{1,9},{2,18},{3,11},{4,20},{5,13},{6,22},{7,15},{8,24},{9,1... | collective-permute-start | bytes 3145736 | tf_op jit(solution)/shard_map/ppermute | solution.py:71
  154.1 15.5 %collective-permute-start.26 = (bf16[4,128,1024]{2,1,0:T(8,128)(2,1)S(1)}, bf16[4,128,1024]{2,1,0:T(8,128)(2,1)S(1)}, u32[]{:S(2)}, u32[]{:S(2)}) collective-permute-start(bf16[4,128,1024]{2,1,0:T(8,128)(2,1)S(1)} %collective-permute-done.22.rest_2_), channel_id=1, source_target_pairs={{0,1},{1,0},{2,3},{3,2},{4,5},{5,4},{6,7},{7,6},{8,9},{9,8},{10,11... | collective-permute-start | bytes 3145736 | tf_op jit(solution)/shard_map/ppermute | solution.py:71
  169.5 28.0 %collective-permute-start.23 = (bf16[4,4,128,1024]{3,2,1,0:T(8,128)(2,1)}, bf16[4,4,128,1024]{3,2,1,0:T(8,128)(2,1)}, u32[]{:S(2)}, u32[]{:S(2)}) collective-permute-start(bf16[4,4,128,1024]{3,2,1,0:T(8,128)(2,1)} %get-tuple-element.130), channel_id=1, source_target_pairs={{0,1},{1,0},{2,3},{3,2},{4,5},{5,4},{6,7},{7,6},{8,9},{9,8},{10,11... | collective-permute-start | bytes 12582920 | tf_op jit(solution)/shard_map/ppermute | solution.py:71
  200.6 36.8 %collective-permute-start.29 = (bf16[2,4,128,1024]{3,2,1,0:T(8,128)(2,1)S(1)}, bf16[2,4,128,1024]{3,2,1,0:T(8,128)(2,1)S(1)}, u32[]{:S(2)}, u32[]{:S(2)}) collective-permute-start(bf16[2,4,128,1024]{3,2,1,0:T(8,128)(2,1)S(1)} %add_convert_fusion.1), channel_id=1, source_target_pairs={{0,16},{1,9},{2,18},{3,11},{4,20},{5,13},{6,22},{7,15},{8,24},{9,1... | collective-permute-start | bytes 6291464 | tf_op jit(solution)/shard_map/ppermute | solution.py:71
  236.7 30.9 %collective-permute-start.31 = (bf16[4,4,32,5120]{3,2,1,0:T(8,128)(2,1)}, bf16[4,4,32,5120]{3,2,1,0:T(8,128)(2,1)}, u32[]{:S(2)}, u32[]{:S(2)}) collective-permute-start(bf16[4,4,32,5120]{3,2,1,0:T(8,128)(2,1)} %get-tuple-element.152), channel_id=1, source_target_pairs={{0,1},{1,0},{2,3},{3,2},{4,5},{5,4},{6,7},{7,6},{8,9},{9,8},{10,11... | collective-permute-start | bytes 15728648 | tf_op jit(solution)/shard_map/ppermute | solution.py:71
  240.4 16.8 %collective-permute-start.30 = (bf16[4,128,1024]{2,1,0:T(8,128)(2,1)S(1)}, bf16[4,128,1024]{2,1,0:T(8,128)(2,1)S(1)}, u32[]{:S(2)}, u32[]{:S(2)}) collective-permute-start(bf16[4,128,1024]{2,1,0:T(8,128)(2,1)S(1)} %fusion.1), channel_id=1, source_target_pairs={{0,8},{1,17},{2,10},{3,19},{4,12},{5,21},{6,14},{7,23},{8,0},{9,25... | collective-permute-start | bytes 3145736 | tf_op jit(solution)/shard_map/ppermute | solution.py:71
  263.1 26.1 %collective-permute-start.32 = (bf16[128,1024]{1,0:T(8,128)(2,1)}, bf16[128,1024]{1,0:T(8,128)(2,1)S(1)}, u32[]{:S(2)}, u32[]{:S(2)}) collective-permute-start(bf16[128,1024]{1,0:T(8,128)(2,1)} %get-tuple-element.148), channel_id=1, source_target_pairs={{0,2},{1,3},{2,0},{3,1},{4,6},{5,7},{6,4},{7,5},{8,10},{9,11},{10,... | collective-permute-start | bytes 786440 | tf_op jit(solution)/shard_map/ppermute | solution.py:71
  263.2 25.9 %collective-permute-start.33 = (bf16[128,1024]{1,0:T(8,128)(2,1)}, bf16[128,1024]{1,0:T(8,128)(2,1)S(1)}, u32[]{:S(2)}, u32[]{:S(2)}) collective-permute-start(bf16[128,1024]{1,0:T(8,128)(2,1)} %get-tuple-element.149), channel_id=1, source_target_pairs={{0,4},{1,5},{2,6},{3,7},{4,0},{5,1},{6,2},{7,3},{8,12},{9,13},{10,... | collective-permute-start | bytes 786440 | tf_op jit(solution)/shard_map/ppermute | solution.py:71
  264.2 25.0 %collective-permute-start.34 = (bf16[128,1024]{1,0:T(8,128)(2,1)}, bf16[128,1024]{1,0:T(8,128)(2,1)S(1)}, u32[]{:S(2)}, u32[]{:S(2)}) collective-permute-start(bf16[128,1024]{1,0:T(8,128)(2,1)} %get-tuple-element.150), channel_id=1, source_target_pairs={{0,6},{1,7},{2,4},{3,5},{4,2},{5,3},{6,0},{7,1},{8,14},{9,15},{10,... | collective-permute-start | bytes 786440 | tf_op jit(solution)/shard_map/ppermute | solution.py:71
  272.7 34.9 %collective-permute-start.35 = (bf16[2,4,32,5120]{3,2,1,0:T(8,128)(2,1)}, bf16[2,4,32,5120]{3,2,1,0:T(8,128)(2,1)}, u32[]{:S(2)}, u32[]{:S(2)}) collective-permute-start(bf16[2,4,32,5120]{3,2,1,0:T(8,128)(2,1)} %add_convert_fusion), channel_id=1, source_target_pairs={{0,16},{1,9},{2,18},{3,11},{4,20},{5,13},{6,22},{7,15},{8,24},{9,1... | collective-permute-start | bytes 7864328 | tf_op jit(solution)/shard_map/ppermute | solution.py:71
  302.4 20.4 %collective-permute-start.36 = (bf16[4,4,32,3072]{3,2,1,0:T(8,128)(2,1)}, bf16[4,4,32,3072]{3,2,1,0:T(8,128)(2,1)}, u32[]{:S(2)}, u32[]{:S(2)}) collective-permute-start(bf16[4,4,32,3072]{3,2,1,0:T(8,128)(2,1)} %get-tuple-element.163), channel_id=1, source_target_pairs={{0,1},{1,0},{2,3},{3,2},{4,5},{5,4},{6,7},{7,6},{8,9},{9,8},{10,11... | collective-permute-start | bytes 9437192 | tf_op jit(solution)/shard_map/ppermute | solution.py:71
  310.2 17.8 %collective-permute-start.38 = (bf16[4,32,5120]{2,1,0:T(8,128)(2,1)S(1)}, bf16[4,32,5120]{2,1,0:T(8,128)(2,1)}, u32[]{:S(2)}, u32[]{:S(2)}) collective-permute-start(bf16[4,32,5120]{2,1,0:T(8,128)(2,1)S(1)} %fusion), channel_id=1, source_target_pairs={{0,8},{1,17},{2,10},{3,19},{4,12},{5,21},{6,14},{7,23},{8,0},{9,25... | collective-permute-start | bytes 3932168 | tf_op jit(solution)/shard_map/ppermute | solution.py:71
  325.9 31.0 %collective-permute-start.37 = (bf16[2,4,32,3072]{3,2,1,0:T(8,128)(2,1)}, bf16[2,4,32,3072]{3,2,1,0:T(8,128)(2,1)}, u32[]{:S(2)}, u32[]{:S(2)}) collective-permute-start(bf16[2,4,32,3072]{3,2,1,0:T(8,128)(2,1)} %add_convert_fusion.2), channel_id=1, source_target_pairs={{0,16},{1,9},{2,18},{3,11},{4,20},{5,13},{6,22},{7,15},{8,24},{9,1... | collective-permute-start | bytes 4718600 | tf_op jit(solution)/shard_map/ppermute | solution.py:71
  332.6 40.4 %collective-permute-start.40 = (bf16[32,5120]{1,0:T(8,128)(2,1)}, bf16[32,5120]{1,0:T(8,128)(2,1)S(1)}, u32[]{:S(2)}, u32[]{:S(2)}) collective-permute-start(bf16[32,5120]{1,0:T(8,128)(2,1)} %get-tuple-element.169), channel_id=1, source_target_pairs={{0,2},{1,3},{2,0},{3,1},{4,6},{5,7},{6,4},{7,5},{8,10},{9,11},{10,... | collective-permute-start | bytes 983048 | tf_op jit(solution)/shard_map/ppermute | solution.py:71
  333.7 38.5 %collective-permute-start.41 = (bf16[32,5120]{1,0:T(8,128)(2,1)}, bf16[32,5120]{1,0:T(8,128)(2,1)}, u32[]{:S(2)}, u32[]{:S(2)}) collective-permute-start(bf16[32,5120]{1,0:T(8,128)(2,1)} %get-tuple-element.170), channel_id=1, source_target_pairs={{0,4},{1,5},{2,6},{3,7},{4,0},{5,1},{6,2},{7,3},{8,12},{9,13},{10,... | collective-permute-start | bytes 983048 | tf_op jit(solution)/shard_map/ppermute | solution.py:71
  334.6 37.6 %collective-permute-start.42 = (bf16[32,5120]{1,0:T(8,128)(2,1)}, bf16[32,5120]{1,0:T(8,128)(2,1)}, u32[]{:S(2)}, u32[]{:S(2)}) collective-permute-start(bf16[32,5120]{1,0:T(8,128)(2,1)} %get-tuple-element.171), channel_id=1, source_target_pairs={{0,6},{1,7},{2,4},{3,5},{4,2},{5,3},{6,0},{7,1},{8,14},{9,15},{10,... | collective-permute-start | bytes 983048 | tf_op jit(solution)/shard_map/ppermute | solution.py:71
  359.6 15.0 %collective-permute-start.39 = (bf16[4,32,3072]{2,1,0:T(8,128)(2,1)}, bf16[4,32,3072]{2,1,0:T(8,128)(2,1)S(1)}, u32[]{:S(2)}, u32[]{:S(2)}) collective-permute-start(bf16[4,32,3072]{2,1,0:T(8,128)(2,1)} %fusion.2), channel_id=1, source_target_pairs={{0,8},{1,17},{2,10},{3,19},{4,12},{5,21},{6,14},{7,23},{8,0},{9,25... | collective-permute-start | bytes 2359304 | tf_op jit(solution)/shard_map/ppermute | solution.py:71
  381.2 3.8 collective-permute-start.45
  385.0 3.7 collective-permute-start.46
  388.7 3.7 collective-permute-start.47
  392.4 10.2 %collective-permute-start.50 = (f32[1,384]{1,0:T(1,128)S(1)}, f32[1,384]{1,0:T(1,128)S(1)}, u32[]{:S(2)}, u32[]{:S(2)}) collective-permute-start(f32[1,384]{1,0:T(1,128)S(1)} %slice.227), channel_id=1, source_target_pairs={{0,4},{1,5},{2,6},{3,7},{4,0},{5,1},{6,2},{7,3},{8,12},{9,13},{10,... | collective-permute-start | bytes 4616 | tf_op jit(solution)/shard_map/ppermute | solution.py:71
  398.1 9.8 %collective-permute-start.43 = (bf16[32,3072]{1,0:T(8,128)(2,1)S(1)}, bf16[32,3072]{1,0:T(8,128)(2,1)S(1)}, u32[]{:S(2)}, u32[]{:S(2)}) collective-permute-start(bf16[32,3072]{1,0:T(8,128)(2,1)S(1)} %copy-done.55), channel_id=1, source_target_pairs={{0,2},{1,3},{2,0},{3,1},{4,6},{5,7},{6,4},{7,5},{8,10},{9,11},{10,... | collective-permute-start | bytes 589832 | tf_op jit(solution)/shard_map/ppermute | solution.py:71
  400.2 13.7 %collective-permute-start.48 = (bf16[32,3072]{1,0:T(8,128)(2,1)S(1)}, bf16[32,3072]{1,0:T(8,128)(2,1)S(1)}, u32[]{:S(2)}, u32[]{:S(2)}) collective-permute-start(bf16[32,3072]{1,0:T(8,128)(2,1)S(1)} %copy-done.54), channel_id=1, source_target_pairs={{0,4},{1,5},{2,6},{3,7},{4,0},{5,1},{6,2},{7,3},{8,12},{9,13},{10,... | collective-permute-start | bytes 589832 | tf_op jit(solution)/shard_map/ppermute | solution.py:71
  400.5 13.4 %collective-permute-start.49 = (bf16[32,3072]{1,0:T(8,128)(2,1)S(1)}, bf16[32,3072]{1,0:T(8,128)(2,1)S(1)}, u32[]{:S(2)}, u32[]{:S(2)}) collective-permute-start(bf16[32,3072]{1,0:T(8,128)(2,1)S(1)} %copy-done.53), channel_id=1, source_target_pairs={{0,6},{1,7},{2,4},{3,5},{4,2},{5,3},{6,0},{7,1},{8,14},{9,15},{10,... | collective-permute-start | bytes 589832 | tf_op jit(solution)/shard_map/ppermute | solution.py:71
  (59 other events, 1083.8 us)

commit v4 on v3

--- a/solution.py
+++ b/solution.py
@@ -13,6 +13,7 @@
 SPAN = 512
 MANY = 4
 WEIGH = 2
+PARTS = 1
 F32 = jnp.float32
 BF16 = jnp.bfloat16
 
@@ -40,17 +41,6 @@
         self.count = int(np.prod(list(mesh.shape.values())))
         self.native = dict(mesh.shape) != {"dp": 4, "fsdp": 8}
         self.axes = ("dp", "fsdp")
-        if not self.native:
-            keys = []
-            for core in (0, 1):
-                both = []
-                for which, extra in ((core, 0), (1 - core, CORE)):
-                    own = [extra]
-                    for bit in HOPS[which]:
-                        own = own + [key ^ bit for key in own]
-                    both += own
-                keys.append(both)
-            self.keys = np.array(keys, np.int32)
 
     def place(self):
         if self.native:
@@ -63,8 +53,7 @@
         mix = jnp.where(odd, jnp.array(MIX[1], jnp.int32), jnp.array(MIX[0], jnp.int32))
         self.meta = jnp.concatenate([(me >> 3) ^ mix, (me & CORE)[None], ((me >> 1) & 3)[None]])
         self.order = mix[jnp.arange(4) ^ (me >> 3)]
-        self.shard_of = me ^ jnp.where(odd, self.keys[1], self.keys[0])
-        self.tables = (self.order, self.shard_of)
+        self.tables = (self.order,)
 
     def flip(self, value, even, odd):
         bits = (even, odd)
@@ -77,36 +66,32 @@
         return self.flip(value, CORE, CORE)
 
     def scatter_small(self, table):
-        if self.native:
-            own = lax.psum_scatter(table, self.axes, scatter_dimension=0, tiled=True).reshape(-1)
-            return own, own
-        half = self.count // 2
-        table = jnp.take(table, self.shard_of, axis=0)
-        total = table[:half] + self.across(table[half:])
-        for level in (3, 2, 1, 0):
-            half, before = half // 2, total
-            total = total[:half] + self.step(total[half:], level)
-        return total[0], before
+        return jnp.sum(lax.all_to_all(table, self.axes, 0, 0, tiled=True), 0)
 
 
 def place_kernel(meta, *refs):
-    pieces, out_ref = refs[:4], refs[4]
+    pieces, beside, out_ref = refs[:4], refs[4:-1], refs[-1]
+    columns = pieces[0].shape[1]
     for k in range(4):
-        out_ref[meta[5] ^ k] = pieces[k][...]
-
-
-def place_group(meta, pieces):
-    rows, columns = pieces[0].shape
-    tile = columns
+        out_ref[meta[5] ^ k, :, :columns] = pieces[k][...]
+        if beside:
+            out_ref[meta[5] ^ k, :, columns:] = beside[k][...]
+
+
+def place_group(meta, pieces, beside):
+    rows = pieces[0].shape[0]
+    operands = list(pieces) + list(beside)
+    columns = sum(part[0].shape[1] for part in (pieces, beside) if part)
+    whole = lambda n, meta: (0, 0)
     return pl.pallas_call(
         place_kernel,
         grid_spec=pltpu.PrefetchScalarGridSpec(
-            num_scalar_prefetch=1, grid=(1,), in_specs=[pl.BlockSpec((rows, tile), lambda n, meta: (0, n))] * 4,
-            out_specs=pl.BlockSpec((4, rows, tile), lambda n, meta: (0, 0, n))),
+            num_scalar_prefetch=1, grid=(1,), in_specs=[pl.BlockSpec(part.shape, whole) for part in operands],
+            out_specs=pl.BlockSpec((4, rows, columns), lambda n, meta: (0, 0, 0))),
         out_shape=jax.ShapeDtypeStruct((4, rows, columns), pieces[0].dtype),
         cost_estimate=cost(2),
         name="place_group",
-    )(meta, *pieces)
+    )(meta, *operands)
 
 
 def spread_kernel(meta, *refs):
@@ -118,9 +103,7 @@
 
 def spread_sums(meta, keep, near, third, second):
     _, rows, columns = second.shape
-    tile = columns // 2 if columns > 1024 else columns
-    if rows > 32:
-        tile = columns // 4
+    tile = columns // PARTS
     specs, operands = [], []
     for k in range(4):
         group = pl.BlockSpec((None, rows, tile), lambda n, meta, k=k: (meta[5] ^ k, 0, n))
@@ -138,7 +121,8 @@
 
 
 class Gather:
-    def __init__(self, ladder, shard, direct):
+    def __init__(self, ladder, shard, direct, beside=None):
+        self.beside = beside
         self.ladder, self.shard, self.native, self.direct = ladder, shard, ladder.native, direct
         self.sent, self.others = (), []
 
@@ -148,6 +132,10 @@
             self.sent = (self.shard,)
             bits = Z_HOPS if self.direct else Z_HOPS[1:2]
             self.others = [self.ladder.flip(self.shard, bit, bit) for bit in bits]
+            self.sides = []
+            if self.beside is not None:
+                beside = tie(self.beside, self.others[0])
+                self.sides = [beside] + [self.ladder.flip(beside, bit, bit) for bit in bits]
 
     def low(self, *after):
         if not self.native:
@@ -161,7 +149,7 @@
         if not self.native:
             others = [tie(other, *after) for other in self.others]
             if self.direct:
-                self.own = place_group(self.ladder.meta, [self.shard] + others)
+                self.own = place_group(self.ladder.meta, [self.shard] + others, self.sides)
             else:
                 one, two = others[0], self.pair
                 low = (self.ladder.meta[5] & 1) == 1
@@ -1034,15 +1022,15 @@
     total = sum(sizes)
     ends = np.cumsum([0] + sizes)
     known = None
-    first = w_qkv
+    block = None
     if ladder.native:
         every = lambda part: lax.all_gather(part, ladder.axes, axis=0, tiled=True).astype(F32)[None]
         qv = every(bias_qv)
         known = [every(bias_up), jnp.concatenate([qv[:, :width], jnp.zeros((1, width), F32), qv[:, width:]], 1),
                  jnp.concatenate([every(bias_out), every(gain_attn), every(gain_mlp), every(bias_down)], 0)]
     else:
-        first = jnp.concatenate([w_qkv, pack_smalls(bias_up, bias_qv, bias_out, gain_attn, gain_mlp, bias_down, w_qkv.shape[0])], 1)
-    qkv, down = Gather(ladder, first, True), Gather(ladder, w_down, False)
+        block = pack_smalls(bias_up, bias_qv, bias_out, gain_attn, gain_mlp, bias_down, w_qkv.shape[0])
+    qkv, down = Gather(ladder, w_qkv, True, block), Gather(ladder, w_down, False)
     qkv.start()
     rest = Gather(ladder, jnp.concatenate([w_out, w_up], 1), False)
     masks = mask_inputs(segment_ids[0], padding_mask[0])
@@ -1129,8 +1117,8 @@
     small_grads = [sum_qv[:2].reshape(-1), sum_middle[1], sum_in[0], sum_middle[0], sum_up[0], sum_down[0]]
     table = jnp.concatenate([g.reshape(count, -1) for g in small_grads] + [jnp.broadcast_to(members, (count, 6))], 1)
     table = jnp.pad(table, ((0, 0), (0, -table.shape[1] % 128)))
-    own_small, nearly = ladder.scatter_small(tie(table, *sent(flow_qkv)))
-    own_qkv = flow_qkv.finish(nearly)
+    own_small = ladder.scatter_small(tie(table, *sent(flow_qkv)))
+    own_qkv = flow_qkv.finish(own_small)
 
     owned = [own_small[ends[i] : ends[i + 1]] for i in range(6)]
     totals = own_small[total : total + 6]

time: 419 us -> 405 us (0.967)
  waiting for transfers between devices: 70.3 us -> 54.3 us
  starting transfers between devices: 43.1 us -> 51.2 us
  other arithmetic: 33.3 us -> 28.7 us
    ppermute x51 -> x49, waiting for transfers between devices: 70.3 us -> 52.9 us  [flip(): lax.ppermute(value, self.axes, [(i, i ^ bits[i & CORE]) for i in range(se...]
    ppermute x51 -> x49, starting transfers between devices: 43.1 us -> 48.6 us  [flip(): lax.ppermute(value, self.axes, [(i, i ^ bits[i & CORE]) for i in range(se...]
  transfers between devices with their start and end apart: 51 -> 50, of which waited for: 16 -> 15; matrix products, arithmetic and copies ran while one was open for 10% -> 10% of each run, Pallas kernels for 57% -> 59%
where the time goes in v4:
time: 405 us; the launch traced here: 401 us
  Pallas kernels  241 us (60%)
  waiting for transfers between devices  54.3 us (13%)
  starting transfers between devices  51.2 us (13%)
  other arithmetic  28.7 us (7%)
  local copies, waits for them, and re-layouts  23.3 us (6%)
    pallas_call x2, Pallas kernels, back(): pl.pallas_call(functools.partial(back_kernel, ladder.native, last, counts...  58.4 us
    pallas_call x4, Pallas kernels, attn_call(): pl.pallas_call(body, grid_spec=pltpu.PrefetchScalarGridSpec(num_scalar_pr...  54.7 us
    ppermute x49, waiting for transfers between devices, flip(): lax.ppermute(value, self.axes, [(i, i ^ bits[i & CORE]) for i in range(se...  52.9 us
    ppermute x49, starting transfers between devices, flip(): lax.ppermute(value, self.axes, [(i, i ^ bits[i & CORE]) for i in range(se...  48.6 us
    pallas_call x1, Pallas kernels, expand(): pl.pallas_call(functools.partial(expand_kernel, ladder.native, tile, len(...  29.1 us
    pallas_call x2, Pallas kernels, contract(): pl.pallas_call(functools.partial(contract_kernel, ladder.native, part * l...  24.7 us
    pallas_call x1, Pallas kernels, input_grad(): pl.pallas_call(functools.partial(input_grad_kernel, ladder.native, calls)...  17.8 us
    pallas_call x1, Pallas kernels, down_grad(): pl.pallas_call(functools.partial(down_grad_kernel, ladder.native, len(out...  14.8 us
  transfers between devices with their start and end apart: 50, of which 15 were waited for; matrix products, arithmetic and copies ran while one was open for 10% of the time, Pallas kernels for 59%

profile of v4, /device:TPU:0, one launch (start us, length us, event | category | flops | bytes accessed | tf_op | source)
XLA Modules:
  0.0 401.1 jit_solution(12169898169770299610)
XLA Ops:
  0.6 5.1 %collective-permute-start.2 = (bf16[32,3072]{1,0:T(8,128)(2,1)}, bf16[32,3072]{1,0:T(8,128)(2,1)S(1)}, u32[]{:S(2)}, u32[]{:S(2)}) collective-permute-start(bf16[32,3072]{1,0:T(8,128)(2,1)} %refs_0_), channel_id=1, source_target_pairs={{0,6},{1,7},{2,4},{3,5},{4,2},{5,3},{6,0},{7,1},{8,14},{9,15},{10,... | collective-permute-start | bytes 589832 | tf_op jit(solution)/shard_map/ppermute | solution.py:60
  11.3 7.4 %collective-permute-done.refs_1_ = bf16[32,3072]{1,0:T(8,128)(2,1)S(1)} collective-permute-done((bf16[32,3072]{1,0:T(8,128)(2,1)}, bf16[32,3072]{1,0:T(8,128)(2,1)S(1)}, u32[]{:S(2)}, u32[]{:S(2)}) %collective-permute-start) | collective-permute-done | bytes 196640 | tf_op jit(solution)/shard_map/ppermute | solution.py:60
  19.0 3.5 collective-permute-start.4
  24.4 1.9 collective-permute-done.3.refs_5_
  26.9 2.8 place_group.1.rest_0_.rest_4_
  29.7 1.5 collective-permute-start.8
  32.0 1.6 collective-permute-start.9
  35.1 16.1 %collective-permute-done.8.rest_1_.rest_5_ = bf16[4,32,3200]{2,1,0:T(8,128)(2,1)} collective-permute-done((bf16[4,32,3200]{2,1,0:T(8,128)(2,1)}, bf16[4,32,3200]{2,1,0:T(8,128)(2,1)}, u32[]{:S(2)}, u32[]{:S(2)}) %collective-permute-start.8) | collective-permute-done | bytes 819232 | tf_op jit(solution)/shard_map/ppermute | solution.py:60
  51.2 1.6 collective-permute-start.10
  56.2 7.7 %collective-permute-done.10.rest_3_.rest_7_ = bf16[4,32,3200]{2,1,0:T(8,128)(2,1)} collective-permute-done((bf16[4,32,3200]{2,1,0:T(8,128)(2,1)}, bf16[4,32,3200]{2,1,0:T(8,128)(2,1)}, u32[]{:S(2)}, u32[]{:S(2)}) %collective-permute-start.10) | collective-permute-done | bytes 819232 | tf_op jit(solution)/shard_map/ppermute | solution.py:60
  65.3 1.5 collective-permute-start.17
  66.8 1.5 collective-permute-start.16
  68.3 1.5 collective-permute-start.15
  69.9 14.3 %project.1 = (bf16[1024,3072]{1,0:T(8,128)(2,1)}, bf16[1024,1024]{1,0:T(8,128)(2,1)}, f32[1,1024]{1,0:T(1,128)}, f32[1,4096]{1,0:T(1,128)}, f32[4,1024]{1,0:T(4,128)}) custom-call(s32[6]{0:T(128)} %pad_add_fusion.meta, bf16[1024,1024]{1,0:T(8,128)(2,1)} %bitcast.71, f32[1024,1]{1,0:T(8,128)} %copy.44.valid_ref, ...), custom_call_target="tpu_custom_call" | custom-call | flops 32199999488 | tf_op jit(solution)/shard_map/project/pallas_call | solution.py:573
  84.9 11.1 %attn_forward.2 = (bf16[1024,1024]{1,0:T(8,128)(2,1)S(1)}, f32[8,8,256]{2,1,0:T(8,128)S(1)}) custom-call(s32[8]{0:T(128)S(1)} %and_select_fusion.refs_0_, s32[1024,128]{1,0:T(8,128)S(1)} %broadcast_in_dim.74.refs_1_, s32[1024,128]{1,0:T(8,128)S(1)} %broadcast_in_dim.76.refs_2_, s32[8,128]{1,0:T(8,128)S(1)} %bitcast.40, ...), custom_call_target="tpu_custom_call" | custom-call | flops 24839999488 | tf_op jit(solution)/shard_map/attn_forward/pallas_call | solution.py:361
  98.6 11.1 %attn_forward.3 = (bf16[1024,1024]{1,0:T(8,128)(2,1)S(1)}, f32[8,8,256]{2,1,0:T(8,128)S(1)}) custom-call(s32[8]{0:T(128)S(1)} %and_select_fusion.refs_0_, s32[1024,128]{1,0:T(8,128)S(1)} %broadcast_in_dim.74.refs_1_, s32[1024,128]{1,0:T(8,128)S(1)} %broadcast_in_dim.76.refs_2_, s32[8,128]{1,0:T(8,128)S(1)} %bitcast.41, ...), custom_call_target="tpu_custom_call", output_to_operand_aliasing={{0}: (7, {}), {1}: (8, {})} | custom-call | flops 24839999488 | tf_op jit(solution)/shard_map/attn_forward/pallas_call | solution.py:361
  109.7 5.2 %collective-permute-done.19.rest_3_.rest_11_ = bf16[4,32,5120]{2,1,0:T(8,128)(2,1)S(1)} collective-permute-done((bf16[4,32,5120]{2,1,0:T(8,128)(2,1)}, bf16[4,32,5120]{2,1,0:T(8,128)(2,1)S(1)}, u32[]{:S(2)}, u32[]{:S(2)}) %collective-permute-start.19) | collective-permute-done | bytes 1310752 | tf_op jit(solution)/shard_map/ppermute | solution.py:60
  119.9 29.1 %expand.1 = (f32[1024,1024]{1,0:T(8,128)}, bf16[1024,1024]{1,0:T(8,128)(2,1)}, f32[8,1024]{1,0:T(8,128)}, bf16[1024,4096]{1,0:T(8,128)(2,1)}, bf16[1024,4096]{1,0:T(8,128)(2,1)}) custom-call(s32[6]{0:T(128)} %pad_add_fusion.meta, bf16[1024,1024]{1,0:T(8,128)(2,1)} %copy-done.7, bf16[1024,1024]{1,0:T(8,128)(2,1)} %bitcast.72, ...), custom_call_target="tpu_custom_call" | custom-call | flops 66700001280 | tf_op jit(solution)/shard_map/expand/pallas_call | solution.py:646
  150.9 14.8 %down_grad.1 = (bf16[4,4,128,1024]{3,2,1,0:T(8,128)(2,1)}, bf16[4,4,128,1024]{3,2,1,0:T(8,128)(2,1)}, f32[1,1024]{1,0:T(1,128)}) custom-call(s32[6]{0:T(128)} %pad_add_fusion.meta, bf16[1024,4096]{1,0:T(8,128)(2,1)} %get-tuple-element.178.act_ref, bf16[1024,1024]{1,0:T(8,128)(2,1)} %bitcast.68), custom_call_target="tpu_custom_call" | custom-call | flops 32199999488 | tf_op jit(solution)/shard_map/down_grad/pallas_call | solution.py:713
  166.3 2.8 collective-permute-done.31.rest_7_
  170.1 24.0 %back.2 = (bf16[4,4,32,5120]{3,2,1,0:T(8,128)(2,1)}, bf16[4,4,32,5120]{3,2,1,0:T(8,128)(2,1)}, f32[1024,1024]{1,0:T(8,128)}, f32[1,2048]{1,0:T(1,128)}) custom-call(s32[6]{0:T(128)} %pad_add_fusion.meta, bf16[1024,1024]{1,0:T(8,128)(2,1)} %bitcast.69, bf16[1024,4096]{1,0:T(8,128)(2,1)} %get-tuple-element.135.slope_ref, ...), custom_call_target="tpu_custom_call" | custom-call | flops 46000001024 | tf_op jit(solution)/shard_map/back/pallas_call | solution.py:880
  194.1 3.2 add_convert_fusion.1
  197.4 34.5 %back.3 = (bf16[4,4,32,5120]{3,2,1,0:T(8,128)(2,1)}, bf16[4,4,32,5120]{3,2,1,0:T(8,128)(2,1)}, f32[1024,1024]{1,0:T(8,128)}, bf16[1024,1024]{1,0:T(8,128)(2,1)},...) custom-call(s32[6]{0:T(128)} %pad_add_fusion.meta, ...), custom_call_target="tpu_custom_call", output_to_operand_aliasing={{0}: (24, {}), {1}: (25, {})} | custom-call | flops 69000003584 | tf_op jit(solution)/shard_map/back/pallas_call | solution.py:880
  232.2 3.0 fusion.1
  235.2 2.0 collective-permute-start.33
  237.2 16.1 %attn_backward.2 = (bf16[3,1024,1024]{2,1,0:T(8,128)(2,1)}, f32[8,1024]{1,0:T(8,128)S(1)}) custom-call(s32[8]{0:T(128)S(1)} %copy-done.6, s32[1024,128]{1,0:T(8,128)S(1)} %broadcast_in_dim.74.refs_1_, s32[1024,128]{1,0:T(8,128)S(1)} %broadcast_in_dim.76.refs_2_, s32[8,128]{1,0:T(8,128)S(1)} %bitcast.42, ...), custom_call_target="tpu_custom_call" | custom-call | flops 31280001024 | tf_op jit(solution)/shard_map/attn_backward/pallas_call | solution.py:361
  254.3 4.0 spread_sums.3
  259.8 2.8 collective-permute-start.37
  262.7 5.1 %add_convert_fusion = bf16[2,4,32,5120]{3,2,1,0:T(8,128)(2,1)} fusion(bf16[4,4,32,5120]{3,2,1,0:T(8,128)(2,1)} %collective-permute-done.34.refs_1_.refs_5_.refs_9_.refs_13_, bf16[4,4,32,5120]{3,2,1,0:T(8,128)(2,1)} %get-tuple-element.153.refs_0_.refs_4_.refs_8_.refs_12_), kind=kLoop, calls=%fused_computation.2 | loop fusion | flops 5242880 | bytes 7864320 | tf_op jit(solution)/shard_map/convert_element_type | solution.py:192
  268.0 16.4 %attn_backward.3 = (bf16[3,1024,1024]{2,1,0:T(8,128)(2,1)}, f32[8,1024]{1,0:T(8,128)S(1)}) custom-call(s32[8]{0:T(128)S(1)} %copy-done.6, s32[1024,128]{1,0:T(8,128)S(1)} %copy-done.3, s32[1024,128]{1,0:T(8,128)S(1)} %copy-done.1, s32[8,128]{1,0:T(8,128)S(1)} %bitcast.43, ...), custom_call_target="tpu_custom_call", output_to_operand_aliasing={{0}: (9, {}), {1}: (10, {})} | custom-call | flops 31280001024 | tf_op jit(solution)/shard_map/attn_backward/pallas_call | solution.py:361
  285.4 12.4 %qkv_grad.1 = (bf16[4,4,32,3072]{3,2,1,0:T(8,128)(2,1)}, bf16[4,4,32,3072]{3,2,1,0:T(8,128)(2,1)}) custom-call(s32[6]{0:T(128)} %pad_add_fusion.meta, bf16[1024,1024]{1,0:T(8,128)(2,1)} %get-tuple-element.127.left_ref, bf16[3,1024,1024]{2,1,0:T(8,128)(2,1)} %get-tuple-element.163.right_ref.rest_0_), custom_call_target="tpu_custom_call" | custom-call | flops 18400000000 | tf_op jit(solution)/shard_map/qkv_grad/pallas_call | solution.py:751
  302.9 2.7 fusion
  305.7 12.5 %contract.2 = (bf16[512,1024]{1,0:T(8,128)(2,1)}, f32[8,1024]{1,0:T(8,128)}) custom-call(s32[6]{0:T(128)} %pad_add_fusion.meta, bf16[1024,4096]{1,0:T(8,128)(2,1)} %get-tuple-element.178.act_ref, f32[4,1024]{1,0:T(4,128)} %get-tuple-element.124.lines_ref.rest_3_, f32[1024,1]{1,0:T(8,128)} %copy.44.valid_ref, f32[1024,1024]{1,0:T(8,128)} %get-tuple-element.137.middle_ref, ...), custom_call_target="tpu_custom_call" | custom-call | flops 18400000000 | tf_op jit(solution)/shard_map/contract/pallas_call | solution.py:936
  318.2 3.1 add_convert_fusion.2
  321.4 1.8 collective-permute-start.40
  323.4 4.5 %spread_sums.4 = (f32[32,5120]{1,0:T(8,128)}, bf16[32,5120]{1,0:T(8,128)(2,1)}, bf16[32,5120]{1,0:T(8,128)(2,1)}, bf16[32,5120]{1,0:T(8,128)(2,1)}) custom-call(s32[6]{0:T(128)} %pad_add_fusion.meta, bf16[4,4,32,5120]{3,2,1,0:T(8,128)(2,1)} %get-tuple-element.153.refs_0_.refs_4_.refs_8_.refs_12_, ...), custom_call_target="tpu_custom_call" | custom-call | flops 6899999744 | tf_op jit(solution)/shard_map/spread_sums/pallas_call | solution.py:114
  329.6 2.7 collective-permute-start.45
  332.3 17.8 %input_grad.1 = (bf16[1024,1024]{1,0:T(8,128)(2,1)}, f32[8,1024]{1,0:T(8,128)}) custom-call(s32[6]{0:T(128)} %pad_add_fusion.meta, bf16[3,1024,1024]{2,1,0:T(8,128)(2,1)} %get-tuple-element.163.right_ref.rest_0_, bf16[1024,1024]{1,0:T(8,128)(2,1)} %bitcast.73, f32[1024,1024]{1,0:T(8,128)} %get-tuple-element.175.rest_2_, ...), custom_call_target="tpu_custom_call" | custom-call | flops 41400000512 | tf_op jit(solution)/shard_map/input_grad/pallas_call | solution.py:995
  352.2 2.6 fusion.2
  354.8 1.6 collective-permute-start.42
  356.4 12.3 %contract.3 = (bf16[512,1024]{1,0:T(8,128)(2,1)}, f32[8,1024]{1,0:T(8,128)}) custom-call(s32[6]{0:T(128)} %pad_add_fusion.meta, bf16[1024,4096]{1,0:T(8,128)(2,1)} %get-tuple-element.178.act_ref, f32[4,1024]{1,0:T(4,128)} %get-tuple-element.124.lines_ref.rest_3_, f32[1024,1]{1,0:T(8,128)} %copy.44.valid_ref, f32[1024,1024]{1,0:T(8,128)} %get-tuple-element.137.middle_ref, ...), custom_call_target="tpu_custom_call" | custom-call | flops 18400000000 | tf_op jit(solution)/shard_map/contract/pallas_call | solution.py:936
  372.8 3.7 spread_sums.5
  377.1 2.6 all-to-all-start
  379.7 1.5 maximum_bitcast_fusion
  381.2 1.7 collective-permute-start.46
  382.9 2.5 collective-permute-start.47
  390.6 1.8 collective-permute-done.46
  392.4 7.6 %collective-permute-done.47 = bf16[32,3072]{1,0:T(8,128)(2,1)S(1)} collective-permute-done((bf16[32,3072]{1,0:T(8,128)(2,1)S(1)}, bf16[32,3072]{1,0:T(8,128)(2,1)S(1)}, u32[]{:S(2)}, u32[]{:S(2)}) %collective-permute-start.47) | collective-permute-done | bytes 196640 | tf_op jit(solution)/shard_map/ppermute | solution.py:60
  (256 shorter events, 50.1 us)
Async XLA Ops:
  0.6 23.1 %collective-permute-start.2 = (bf16[32,3072]{1,0:T(8,128)(2,1)}, bf16[32,3072]{1,0:T(8,128)(2,1)S(1)}, u32[]{:S(2)}, u32[]{:S(2)}) collective-permute-start(bf16[32,3072]{1,0:T(8,128)(2,1)} %refs_0_), channel_id=1, source_target_pairs={{0,6},{1,7},{2,4},{3,5},{4,2},{5,3},{6,0},{7,1},{8,14},{9,15},{10,... | collective-permute-start | bytes 589832 | tf_op jit(solution)/shard_map/ppermute | solution.py:60
  5.8 18.0 %collective-permute-start.1 = (bf16[32,3072]{1,0:T(8,128)(2,1)}, bf16[32,3072]{1,0:T(8,128)(2,1)S(1)}, u32[]{:S(2)}, u32[]{:S(2)}) collective-permute-start(bf16[32,3072]{1,0:T(8,128)(2,1)} %refs_0_), channel_id=1, source_target_pairs={{0,4},{1,5},{2,6},{3,7},{4,0},{5,1},{6,2},{7,3},{8,12},{9,13},{10,... | collective-permute-start | bytes 589832 | tf_op jit(solution)/shard_map/ppermute | solution.py:60
  5.8 13.0 %collective-permute-start = (bf16[32,3072]{1,0:T(8,128)(2,1)}, bf16[32,3072]{1,0:T(8,128)(2,1)S(1)}, u32[]{:S(2)}, u32[]{:S(2)}) collective-permute-start(bf16[32,3072]{1,0:T(8,128)(2,1)} %refs_0_), channel_id=1, source_target_pairs={{0,2},{1,3},{2,0},{3,1},{4,6},{5,7},{6,4},{7,5},{8,10},{9,11},{10,... | collective-permute-start | bytes 589832 | tf_op jit(solution)/shard_map/ppermute | solution.py:60
  18.8 5.5 %collective-permute-start.5 = (bf16[32,128]{1,0:T(8,128)(2,1)S(1)}, bf16[32,128]{1,0:T(8,128)(2,1)S(1)}, u32[]{:S(2)}, u32[]{:S(2)}) collective-permute-start(bf16[32,128]{1,0:T(8,128)(2,1)S(1)} %select_select_fusion.refs_4_), channel_id=1, source_target_pairs={{0,6},{1,7},{2,4},{3,5},{4,2},{5,3},{6,0},{7,1},{8,14},{9,15},{10,... | collective-permute-start | bytes 24584 | tf_op jit(solution)/shard_map/ppermute | solution.py:60
  19.0 5.3 %collective-permute-start.4 = (bf16[32,128]{1,0:T(8,128)(2,1)S(1)}, bf16[32,128]{1,0:T(8,128)(2,1)S(1)}, u32[]{:S(2)}, u32[]{:S(2)}) collective-permute-start(bf16[32,128]{1,0:T(8,128)(2,1)S(1)} %select_select_fusion.refs_4_), channel_id=1, source_target_pairs={{0,4},{1,5},{2,6},{3,7},{4,0},{5,1},{6,2},{7,3},{8,12},{9,13},{10,... | collective-permute-start | bytes 24584 | tf_op jit(solution)/shard_map/ppermute | solution.py:60
  22.6 3.7 collective-permute-start.3
  29.7 21.5 %collective-permute-start.8 = (bf16[4,32,3200]{2,1,0:T(8,128)(2,1)}, bf16[4,32,3200]{2,1,0:T(8,128)(2,1)}, u32[]{:S(2)}, u32[]{:S(2)}) collective-permute-start(bf16[4,32,3200]{2,1,0:T(8,128)(2,1)} %place_group.1.rest_0_.rest_4_), channel_id=1, source_target_pairs={{0,8},{1,17},{2,10},{3,19},{4,12},{5,21},{6,14},{7,23},{8,0},{9,25... | collective-permute-start | bytes 2457608 | tf_op jit(solution)/shard_map/ppermute | solution.py:60
  32.0 24.1 %collective-permute-start.9 = (bf16[4,32,3200]{2,1,0:T(8,128)(2,1)}, bf16[4,32,3200]{2,1,0:T(8,128)(2,1)}, u32[]{:S(2)}, u32[]{:S(2)}) collective-permute-start(bf16[4,32,3200]{2,1,0:T(8,128)(2,1)} %place_group.1.rest_0_.rest_4_), channel_id=1, source_target_pairs={{0,16},{1,9},{2,18},{3,11},{4,20},{5,13},{6,22},{7,15},{8,24},{9,1... | collective-permute-start | bytes 2457608 | tf_op jit(solution)/shard_map/ppermute | solution.py:60
  33.6 20.2 %collective-permute-start.6 = (bf16[32,5120]{1,0:T(8,128)(2,1)S(1)}, bf16[32,5120]{1,0:T(8,128)(2,1)S(1)}, u32[]{:S(2)}, u32[]{:S(2)}) collective-permute-start(bf16[32,5120]{1,0:T(8,128)(2,1)S(1)} %pad_maximum_fusion), channel_id=1, source_target_pairs={{0,4},{1,5},{2,6},{3,7},{4,0},{5,1},{6,2},{7,3},{8,12},{9,13},{10,... | collective-permute-start | bytes 983048 | tf_op jit(solution)/shard_map/ppermute | solution.py:60
  51.2 12.7 %collective-permute-start.10 = (bf16[4,32,3200]{2,1,0:T(8,128)(2,1)}, bf16[4,32,3200]{2,1,0:T(8,128)(2,1)}, u32[]{:S(2)}, u32[]{:S(2)}) collective-permute-start(bf16[4,32,3200]{2,1,0:T(8,128)(2,1)} %collective-permute-done.8.rest_1_.rest_5_), channel_id=1, source_target_pairs={{0,16},{1,9},{2,18},{3,11},{4,20},{5,13},{6,22},{7,15},{8,24},{9,1... | collective-permute-start | bytes 2457608 | tf_op jit(solution)/shard_map/ppermute | solution.py:60
  53.9 10.7 %collective-permute-start.7 = (bf16[2,32,5120]{2,1,0:T(8,128)(2,1)S(1)}, bf16[2,32,5120]{2,1,0:T(8,128)(2,1)S(1)}, u32[]{:S(2)}, u32[]{:S(2)}) collective-permute-start(bf16[2,32,5120]{2,1,0:T(8,128)(2,1)S(1)} %maximum_select_fusion.2), channel_id=1, source_target_pairs={{0,2},{1,3},{2,0},{3,1},{4,6},{5,7},{6,4},{7,5},{8,10},{9,11},{10,... | collective-permute-start | bytes 1966088 | tf_op jit(solution)/shard_map/ppermute | solution.py:60
  55.7 9.6 %collective-permute-start.11 = (bf16[4,32,3200]{2,1,0:T(8,128)(2,1)}, bf16[4,32,3200]{2,1,0:T(8,128)(2,1)S(1)}, u32[]{:S(2)}, u32[]{:S(2)}) collective-permute-start(bf16[4,32,3200]{2,1,0:T(8,128)(2,1)} %place_group.1.rest_0_.rest_4_), channel_id=1, source_target_pairs={{0,1},{1,0},{2,3},{3,2},{4,5},{5,4},{6,7},{7,6},{8,9},{9,8},{10,11... | collective-permute-start | bytes 2457608 | tf_op jit(solution)/shard_map/ppermute | solution.py:60
  55.7 12.7 %collective-permute-start.13 = (bf16[4,32,3200]{2,1,0:T(8,128)(2,1)}, bf16[4,32,3200]{2,1,0:T(8,128)(2,1)}, u32[]{:S(2)}, u32[]{:S(2)}) collective-permute-start(bf16[4,32,3200]{2,1,0:T(8,128)(2,1)} %collective-permute-done.8.rest_1_.rest_5_), channel_id=1, source_target_pairs={{0,1},{1,0},{2,3},{3,2},{4,5},{5,4},{6,7},{7,6},{8,9},{9,8},{10,11... | collective-permute-start | bytes 2457608 | tf_op jit(solution)/shard_map/ppermute | solution.py:60
  56.2 10.6 %collective-permute-start.12 = (bf16[4,32,3200]{2,1,0:T(8,128)(2,1)}, bf16[4,32,3200]{2,1,0:T(8,128)(2,1)S(1)}, u32[]{:S(2)}, u32[]{:S(2)}) collective-permute-start(bf16[4,32,3200]{2,1,0:T(8,128)(2,1)} %collective-permute-done.9.rest_2_.rest_6_), channel_id=1, source_target_pairs={{0,1},{1,0},{2,3},{3,2},{4,5},{5,4},{6,7},{7,6},{8,9},{9,8},{10,11... | collective-permute-start | bytes 2457608 | tf_op jit(solution)/shard_map/ppermute | solution.py:60
  63.8 6.0 %collective-permute-start.14 = (bf16[4,32,3200]{2,1,0:T(8,128)(2,1)}, bf16[4,32,3200]{2,1,0:T(8,128)(2,1)}, u32[]{:S(2)}, u32[]{:S(2)}) collective-permute-start(bf16[4,32,3200]{2,1,0:T(8,128)(2,1)} %collective-permute-done.10.rest_3_.rest_7_), channel_id=1, source_target_pairs={{0,1},{1,0},{2,3},{3,2},{4,5},{5,4},{6,7},{7,6},{8,9},{9,8},{10,11... | collective-permute-start | bytes 2457608 | tf_op jit(solution)/shard_map/ppermute | solution.py:60
  64.8 51.0 %collective-permute-start.20 = (bf16[4,32,5120]{2,1,0:T(8,128)(2,1)S(1)}, bf16[4,32,5120]{2,1,0:T(8,128)(2,1)S(1)}, u32[]{:S(2)}, u32[]{:S(2)}) collective-permute-start(bf16[4,32,5120]{2,1,0:T(8,128)(2,1)S(1)} %bitcast.46), channel_id=1, source_target_pairs={{0,1},{1,0},{2,3},{3,2},{4,5},{5,4},{6,7},{7,6},{8,9},{9,8},{10,11... | collective-permute-start | bytes 3932168 | tf_op jit(solution)/shard_map/ppermute | solution.py:60
  65.3 33.3 %collective-permute-start.17 = (bf16[4,32,5120]{2,1,0:T(8,128)(2,1)S(1)}, bf16[4,32,5120]{2,1,0:T(8,128)(2,1)}, u32[]{:S(2)}, u32[]{:S(2)}) collective-permute-start(bf16[4,32,5120]{2,1,0:T(8,128)(2,1)S(1)} %bitcast.47), channel_id=1, source_target_pairs={{0,16},{1,9},{2,18},{3,11},{4,20},{5,13},{6,22},{7,15},{8,24},{9,1... | collective-permute-start | bytes 3932168 | tf_op jit(solution)/shard_map/ppermute | solution.py:60
  66.8 29.8 %collective-permute-start.16 = (bf16[4,32,5120]{2,1,0:T(8,128)(2,1)S(1)}, bf16[4,32,5120]{2,1,0:T(8,128)(2,1)}, u32[]{:S(2)}, u32[]{:S(2)}) collective-permute-start(bf16[4,32,5120]{2,1,0:T(8,128)(2,1)S(1)} %bitcast.48), channel_id=1, source_target_pairs={{0,8},{1,17},{2,10},{3,19},{4,12},{5,21},{6,14},{7,23},{8,0},{9,25... | collective-permute-start | bytes 3932168 | tf_op jit(solution)/shard_map/ppermute | solution.py:60
  68.3 15.8 %collective-permute-start.15 = (bf16[128,1024]{1,0:T(8,128)(2,1)S(1)}, bf16[128,1024]{1,0:T(8,128)(2,1)S(1)}, u32[]{:S(2)}, u32[]{:S(2)}) collective-permute-start(bf16[128,1024]{1,0:T(8,128)(2,1)S(1)} %copy-done.19), channel_id=1, source_target_pairs={{0,4},{1,5},{2,6},{3,7},{4,0},{5,1},{6,2},{7,3},{8,12},{9,13},{10,... | collective-permute-start | bytes 786440 | tf_op jit(solution)/shard_map/ppermute | solution.py:60
  84.3 14.3 %collective-permute-start.18 = (bf16[2,128,1024]{2,1,0:T(8,128)(2,1)S(1)}, bf16[2,128,1024]{2,1,0:T(8,128)(2,1)S(1)}, u32[]{:S(2)}, u32[]{:S(2)}) collective-permute-start(bf16[2,128,1024]{2,1,0:T(8,128)(2,1)S(1)} %maximum_select_fusion.4), channel_id=1, source_target_pairs={{0,2},{1,3},{2,0},{3,1},{4,6},{5,7},{6,4},{7,5},{8,10},{9,11},{10,... | collective-permute-start | bytes 1572872 | tf_op jit(solution)/shard_map/ppermute | solution.py:60
  96.6 20.6 %collective-permute-start.22 = (bf16[4,32,5120]{2,1,0:T(8,128)(2,1)}, bf16[4,32,5120]{2,1,0:T(8,128)(2,1)}, u32[]{:S(2)}, u32[]{:S(2)}) collective-permute-start(bf16[4,32,5120]{2,1,0:T(8,128)(2,1)} %collective-permute-done.16.rest_1_.rest_9_), channel_id=1, source_target_pairs={{0,1},{1,0},{2,3},{3,2},{4,5},{5,4},{6,7},{7,6},{8,9},{9,8},{10,11... | collective-permute-start | bytes 3932168 | tf_op jit(solution)/shard_map/ppermute | solution.py:60
  97.1 17.8 %collective-permute-start.19 = (bf16[4,32,5120]{2,1,0:T(8,128)(2,1)}, bf16[4,32,5120]{2,1,0:T(8,128)(2,1)S(1)}, u32[]{:S(2)}, u32[]{:S(2)}) collective-permute-start(bf16[4,32,5120]{2,1,0:T(8,128)(2,1)} %collective-permute-done.16.rest_1_.rest_9_), channel_id=1, source_target_pairs={{0,16},{1,9},{2,18},{3,11},{4,20},{5,13},{6,22},{7,15},{8,24},{9,1... | collective-permute-start | bytes 3932168 | tf_op jit(solution)/shard_map/ppermute | solution.py:60
  98.6 19.2 %collective-permute-start.21 = (bf16[4,32,5120]{2,1,0:T(8,128)(2,1)}, bf16[4,32,5120]{2,1,0:T(8,128)(2,1)S(1)}, u32[]{:S(2)}, u32[]{:S(2)}) collective-permute-start(bf16[4,32,5120]{2,1,0:T(8,128)(2,1)} %collective-permute-done.17.rest_2_.rest_10_), channel_id=1, source_target_pairs={{0,1},{1,0},{2,3},{3,2},{4,5},{5,4},{6,7},{7,6},{8,9},{9,8},{10,11... | collective-permute-start | bytes 3932168 | tf_op jit(solution)/shard_map/ppermute | solution.py:60
  115.2 51.1 %collective-permute-start.28 = (bf16[4,128,1024]{2,1,0:T(8,128)(2,1)S(1)}, bf16[4,128,1024]{2,1,0:T(8,128)(2,1)S(1)}, u32[]{:S(2)}, u32[]{:S(2)}) collective-permute-start(bf16[4,128,1024]{2,1,0:T(8,128)(2,1)S(1)} %bitcast.54), channel_id=1, source_target_pairs={{0,1},{1,0},{2,3},{3,2},{4,5},{5,4},{6,7},{7,6},{8,9},{9,8},{10,11... | collective-permute-start | bytes 3145736 | tf_op jit(solution)/shard_map/ppermute | solution.py:60
  115.8 34.6 %collective-permute-start.25 = (bf16[4,128,1024]{2,1,0:T(8,128)(2,1)S(1)}, bf16[4,128,1024]{2,1,0:T(8,128)(2,1)S(1)}, u32[]{:S(2)}, u32[]{:S(2)}) collective-permute-start(bf16[4,128,1024]{2,1,0:T(8,128)(2,1)S(1)} %bitcast.55), channel_id=1, source_target_pairs={{0,16},{1,9},{2,18},{3,11},{4,20},{5,13},{6,22},{7,15},{8,24},{9,1... | collective-permute-start | bytes 3145736 | tf_op jit(solution)/shard_map/ppermute | solution.py:60
  117.2 31.8 %collective-permute-start.24 = (bf16[4,128,1024]{2,1,0:T(8,128)(2,1)S(1)}, bf16[4,128,1024]{2,1,0:T(8,128)(2,1)}, u32[]{:S(2)}, u32[]{:S(2)}) collective-permute-start(bf16[4,128,1024]{2,1,0:T(8,128)(2,1)S(1)} %bitcast.56), channel_id=1, source_target_pairs={{0,8},{1,17},{2,10},{3,19},{4,12},{5,21},{6,14},{7,23},{8,0},{9,25... | collective-permute-start | bytes 3145736 | tf_op jit(solution)/shard_map/ppermute | solution.py:60
  149.1 17.2 %collective-permute-start.30 = (bf16[4,128,1024]{2,1,0:T(8,128)(2,1)}, bf16[4,128,1024]{2,1,0:T(8,128)(2,1)S(1)}, u32[]{:S(2)}, u32[]{:S(2)}) collective-permute-start(bf16[4,128,1024]{2,1,0:T(8,128)(2,1)} %collective-permute-done.24.rest_1_), channel_id=1, source_target_pairs={{0,1},{1,0},{2,3},{3,2},{4,5},{5,4},{6,7},{7,6},{8,9},{9,8},{10,11... | collective-permute-start | bytes 3145736 | tf_op jit(solution)/shard_map/ppermute | solution.py:60
  149.2 16.5 %collective-permute-start.27 = (bf16[4,128,1024]{2,1,0:T(8,128)(2,1)}, bf16[4,128,1024]{2,1,0:T(8,128)(2,1)S(1)}, u32[]{:S(2)}, u32[]{:S(2)}) collective-permute-start(bf16[4,128,1024]{2,1,0:T(8,128)(2,1)} %collective-permute-done.24.rest_1_), channel_id=1, source_target_pairs={{0,16},{1,9},{2,18},{3,11},{4,20},{5,13},{6,22},{7,15},{8,24},{9,1... | collective-permute-start | bytes 3145736 | tf_op jit(solution)/shard_map/ppermute | solution.py:60
  150.4 15.9 %collective-permute-start.29 = (bf16[4,128,1024]{2,1,0:T(8,128)(2,1)S(1)}, bf16[4,128,1024]{2,1,0:T(8,128)(2,1)S(1)}, u32[]{:S(2)}, u32[]{:S(2)}) collective-permute-start(bf16[4,128,1024]{2,1,0:T(8,128)(2,1)S(1)} %collective-permute-done.25.rest_2_), channel_id=1, source_target_pairs={{0,1},{1,0},{2,3},{3,2},{4,5},{5,4},{6,7},{7,6},{8,9},{9,8},{10,11... | collective-permute-start | bytes 3145736 | tf_op jit(solution)/shard_map/ppermute | solution.py:60
  165.8 28.3 %collective-permute-start.26 = (bf16[4,4,128,1024]{3,2,1,0:T(8,128)(2,1)}, bf16[4,4,128,1024]{3,2,1,0:T(8,128)(2,1)}, u32[]{:S(2)}, u32[]{:S(2)}) collective-permute-start(bf16[4,4,128,1024]{3,2,1,0:T(8,128)(2,1)} %get-tuple-element.132), channel_id=1, source_target_pairs={{0,1},{1,0},{2,3},{3,2},{4,5},{5,4},{6,7},{7,6},{8,9},{9,8},{10,11... | collective-permute-start | bytes 12582920 | tf_op jit(solution)/shard_map/ppermute | solution.py:60
  197.4 34.8 %collective-permute-start.32 = (bf16[2,4,128,1024]{3,2,1,0:T(8,128)(2,1)S(1)}, bf16[2,4,128,1024]{3,2,1,0:T(8,128)(2,1)S(1)}, u32[]{:S(2)}, u32[]{:S(2)}) collective-permute-start(bf16[2,4,128,1024]{3,2,1,0:T(8,128)(2,1)S(1)} %add_convert_fusion.1), channel_id=1, source_target_pairs={{0,16},{1,9},{2,18},{3,11},{4,20},{5,13},{6,22},{7,15},{8,24},{9,1... | collective-permute-start | bytes 6291464 | tf_op jit(solution)/shard_map/ppermute | solution.py:60
  231.9 30.7 %collective-permute-start.34 = (bf16[4,4,32,5120]{3,2,1,0:T(8,128)(2,1)}, bf16[4,4,32,5120]{3,2,1,0:T(8,128)(2,1)}, u32[]{:S(2)}, u32[]{:S(2)}) collective-permute-start(bf16[4,4,32,5120]{3,2,1,0:T(8,128)(2,1)} %get-tuple-element.154), channel_id=1, source_target_pairs={{0,1},{1,0},{2,3},{3,2},{4,5},{5,4},{6,7},{7,6},{8,9},{9,8},{10,11... | collective-permute-start | bytes 15728648 | tf_op jit(solution)/shard_map/ppermute | solution.py:60
  235.2 18.1 %collective-permute-start.33 = (bf16[4,128,1024]{2,1,0:T(8,128)(2,1)S(1)}, bf16[4,128,1024]{2,1,0:T(8,128)(2,1)S(1)}, u32[]{:S(2)}, u32[]{:S(2)}) collective-permute-start(bf16[4,128,1024]{2,1,0:T(8,128)(2,1)S(1)} %fusion.1), channel_id=1, source_target_pairs={{0,8},{1,17},{2,10},{3,19},{4,12},{5,21},{6,14},{7,23},{8,0},{9,25... | collective-permute-start | bytes 3145736 | tf_op jit(solution)/shard_map/ppermute | solution.py:60
  258.3 26.2 %collective-permute-start.35 = (bf16[128,1024]{1,0:T(8,128)(2,1)}, bf16[128,1024]{1,0:T(8,128)(2,1)S(1)}, u32[]{:S(2)}, u32[]{:S(2)}) collective-permute-start(bf16[128,1024]{1,0:T(8,128)(2,1)} %get-tuple-element.150), channel_id=1, source_target_pairs={{0,2},{1,3},{2,0},{3,1},{4,6},{5,7},{6,4},{7,5},{8,10},{9,11},{10,... | collective-permute-start | bytes 786440 | tf_op jit(solution)/shard_map/ppermute | solution.py:60
  258.8 25.7 %collective-permute-start.36 = (bf16[128,1024]{1,0:T(8,128)(2,1)}, bf16[128,1024]{1,0:T(8,128)(2,1)S(1)}, u32[]{:S(2)}, u32[]{:S(2)}) collective-permute-start(bf16[128,1024]{1,0:T(8,128)(2,1)} %get-tuple-element.151), channel_id=1, source_target_pairs={{0,4},{1,5},{2,6},{3,7},{4,0},{5,1},{6,2},{7,3},{8,12},{9,13},{10,... | collective-permute-start | bytes 786440 | tf_op jit(solution)/shard_map/ppermute | solution.py:60
  259.8 24.7 %collective-permute-start.37 = (bf16[128,1024]{1,0:T(8,128)(2,1)}, bf16[128,1024]{1,0:T(8,128)(2,1)S(1)}, u32[]{:S(2)}, u32[]{:S(2)}) collective-permute-start(bf16[128,1024]{1,0:T(8,128)(2,1)} %get-tuple-element.152), channel_id=1, source_target_pairs={{0,6},{1,7},{2,4},{3,5},{4,2},{5,3},{6,0},{7,1},{8,14},{9,15},{10,... | collective-permute-start | bytes 786440 | tf_op jit(solution)/shard_map/ppermute | solution.py:60
  267.8 35.1 %collective-permute-start.38 = (bf16[2,4,32,5120]{3,2,1,0:T(8,128)(2,1)}, bf16[2,4,32,5120]{3,2,1,0:T(8,128)(2,1)}, u32[]{:S(2)}, u32[]{:S(2)}) collective-permute-start(bf16[2,4,32,5120]{3,2,1,0:T(8,128)(2,1)} %add_convert_fusion), channel_id=1, source_target_pairs={{0,16},{1,9},{2,18},{3,11},{4,20},{5,13},{6,22},{7,15},{8,24},{9,1... | collective-permute-start | bytes 7864328 | tf_op jit(solution)/shard_map/ppermute | solution.py:60
  297.8 20.4 %collective-permute-start.39 = (bf16[4,4,32,3072]{3,2,1,0:T(8,128)(2,1)}, bf16[4,4,32,3072]{3,2,1,0:T(8,128)(2,1)}, u32[]{:S(2)}, u32[]{:S(2)}) collective-permute-start(bf16[4,4,32,3072]{3,2,1,0:T(8,128)(2,1)} %get-tuple-element.165), channel_id=1, source_target_pairs={{0,1},{1,0},{2,3},{3,2},{4,5},{5,4},{6,7},{7,6},{8,9},{9,8},{10,11... | collective-permute-start | bytes 9437192 | tf_op jit(solution)/shard_map/ppermute | solution.py:60
  305.6 17.8 %collective-permute-start.41 = (bf16[4,32,5120]{2,1,0:T(8,128)(2,1)S(1)}, bf16[4,32,5120]{2,1,0:T(8,128)(2,1)}, u32[]{:S(2)}, u32[]{:S(2)}) collective-permute-start(bf16[4,32,5120]{2,1,0:T(8,128)(2,1)S(1)} %fusion), channel_id=1, source_target_pairs={{0,8},{1,17},{2,10},{3,19},{4,12},{5,21},{6,14},{7,23},{8,0},{9,25... | collective-permute-start | bytes 3932168 | tf_op jit(solution)/shard_map/ppermute | solution.py:60
  321.4 30.8 %collective-permute-start.40 = (bf16[2,4,32,3072]{3,2,1,0:T(8,128)(2,1)}, bf16[2,4,32,3072]{3,2,1,0:T(8,128)(2,1)}, u32[]{:S(2)}, u32[]{:S(2)}) collective-permute-start(bf16[2,4,32,3072]{3,2,1,0:T(8,128)(2,1)} %add_convert_fusion.2), channel_id=1, source_target_pairs={{0,16},{1,9},{2,18},{3,11},{4,20},{5,13},{6,22},{7,15},{8,24},{9,1... | collective-permute-start | bytes 4718600 | tf_op jit(solution)/shard_map/ppermute | solution.py:60
  327.9 40.8 %collective-permute-start.43 = (bf16[32,5120]{1,0:T(8,128)(2,1)}, bf16[32,5120]{1,0:T(8,128)(2,1)S(1)}, u32[]{:S(2)}, u32[]{:S(2)}) collective-permute-start(bf16[32,5120]{1,0:T(8,128)(2,1)} %get-tuple-element.171), channel_id=1, source_target_pairs={{0,2},{1,3},{2,0},{3,1},{4,6},{5,7},{6,4},{7,5},{8,10},{9,11},{10,... | collective-permute-start | bytes 983048 | tf_op jit(solution)/shard_map/ppermute | solution.py:60
  328.9 39.8 %collective-permute-start.44 = (bf16[32,5120]{1,0:T(8,128)(2,1)}, bf16[32,5120]{1,0:T(8,128)(2,1)}, u32[]{:S(2)}, u32[]{:S(2)}) collective-permute-start(bf16[32,5120]{1,0:T(8,128)(2,1)} %get-tuple-element.172), channel_id=1, source_target_pairs={{0,4},{1,5},{2,6},{3,7},{4,0},{5,1},{6,2},{7,3},{8,12},{9,13},{10,... | collective-permute-start | bytes 983048 | tf_op jit(solution)/shard_map/ppermute | solution.py:60
  329.6 39.2 %collective-permute-start.45 = (bf16[32,5120]{1,0:T(8,128)(2,1)}, bf16[32,5120]{1,0:T(8,128)(2,1)}, u32[]{:S(2)}, u32[]{:S(2)}) collective-permute-start(bf16[32,5120]{1,0:T(8,128)(2,1)} %get-tuple-element.173), channel_id=1, source_target_pairs={{0,6},{1,7},{2,4},{3,5},{4,2},{5,3},{6,0},{7,1},{8,14},{9,15},{10,... | collective-permute-start | bytes 983048 | tf_op jit(solution)/shard_map/ppermute | solution.py:60
  354.8 17.0 %collective-permute-start.42 = (bf16[4,32,3072]{2,1,0:T(8,128)(2,1)}, bf16[4,32,3072]{2,1,0:T(8,128)(2,1)S(1)}, u32[]{:S(2)}, u32[]{:S(2)}) collective-permute-start(bf16[4,32,3072]{2,1,0:T(8,128)(2,1)} %fusion.2), channel_id=1, source_target_pairs={{0,8},{1,17},{2,10},{3,19},{4,12},{5,21},{6,14},{7,23},{8,0},{9,25... | collective-permute-start | bytes 2359304 | tf_op jit(solution)/shard_map/ppermute | solution.py:60
  377.1 9.9 %all-to-all-start = ((f32[32,1,384]{2,1,0:T(1,128)}), f32[32,1,384]{2,1,0:T(1,128)S(1)}, u32[]{:S(2)}, u32[]{:S(2)}) async-start(f32[32,1,384]{2,1,0:T(1,128)} %all_to_all.6), calls=%async_computation | async-start | bytes 98304 | tf_op jit(solution)/shard_map/all_to_all | solution.py:69
  381.2 11.2 %collective-permute-start.46 = (bf16[32,3072]{1,0:T(8,128)(2,1)}, bf16[32,3072]{1,0:T(8,128)(2,1)S(1)}, u32[]{:S(2)}, u32[]{:S(2)}) collective-permute-start(bf16[32,3072]{1,0:T(8,128)(2,1)} %get-tuple-element.186), channel_id=1, source_target_pairs={{0,2},{1,3},{2,0},{3,1},{4,6},{5,7},{6,4},{7,5},{8,10},{9,11},{10,... | collective-permute-start | bytes 589832 | tf_op jit(solution)/shard_map/ppermute | solution.py:60
  382.9 17.1 %collective-permute-start.47 = (bf16[32,3072]{1,0:T(8,128)(2,1)S(1)}, bf16[32,3072]{1,0:T(8,128)(2,1)S(1)}, u32[]{:S(2)}, u32[]{:S(2)}) collective-permute-start(bf16[32,3072]{1,0:T(8,128)(2,1)S(1)} %copy-done.54), channel_id=1, source_target_pairs={{0,4},{1,5},{2,6},{3,7},{4,0},{5,1},{6,2},{7,3},{8,12},{9,13},{10,... | collective-permute-start | bytes 589832 | tf_op jit(solution)/shard_map/ppermute | solution.py:60
  385.4 14.6 %collective-permute-start.48 = (bf16[32,3072]{1,0:T(8,128)(2,1)S(1)}, bf16[32,3072]{1,0:T(8,128)(2,1)S(1)}, u32[]{:S(2)}, u32[]{:S(2)}) collective-permute-start(bf16[32,3072]{1,0:T(8,128)(2,1)S(1)} %copy-done.53), channel_id=1, source_target_pairs={{0,6},{1,7},{2,4},{3,5},{4,2},{5,3},{6,0},{7,1},{8,14},{9,15},{10,... | collective-permute-start | bytes 589832 | tf_op jit(solution)/shard_map/ppermute | solution.py:60
  (60 other events, 921.5 us)

commit v5 on v4

--- a/solution.py
+++ b/solution.py
@@ -45,15 +45,11 @@
     def place(self):
         if self.native:
             self.meta = jnp.array([0, 1, 2, 3, 0, 0], jnp.int32)
-            self.order = jnp.arange(4)
-            self.tables = ()
             return
         me = lax.axis_index(self.axes)
         odd = (me & CORE) == 1
         mix = jnp.where(odd, jnp.array(MIX[1], jnp.int32), jnp.array(MIX[0], jnp.int32))
         self.meta = jnp.concatenate([(me >> 3) ^ mix, (me & CORE)[None], ((me >> 1) & 3)[None]])
-        self.order = mix[jnp.arange(4) ^ (me >> 3)]
-        self.tables = (self.order,)
 
     def flip(self, value, even, odd):
         bits = (even, odd)
@@ -775,36 +771,55 @@
     down_groups, rest = rest[: counts[0]], rest[counts[0] :]
     groups, rest = rest[: counts[0]], rest[counts[0] :]
     if last:
-        before, rest = rest[0], rest[1 + counts[1] :]
+        before, rest = rest[0], rest[2 + counts[1] :]
     pushed, rest = rest[: counts[1]], rest[counts[1] :]
     if last:
         out_ref, branch_ref, mixed_out_ref, sum_ref, up_sum_ref, rest = *rest[:5], rest[5:]
-        acc, down_weight, weight, stage, sems, middle, out_weight = rest
+        acc, down_weight, weight, stage, slope, normed, sems, middle, out_weight, mixed = rest
     else:
-        after, up_sum_ref, acc, down_weight, weight, stage, sems = rest
+        after, up_sum_ref, acc, down_weight, weight, stage, slope, normed, sems = rest
     base = 2 if last else 0
     step = pl.program_id(0)
     t = step + base
-    width, tile = normed_ref.shape[1], slope_ref.shape[1]
+    width, tile = normed.shape[1], slope.shape[2]
     slot = step
 
     def columns(at):
         return pl.multiple_of(width + meta[at] * tile, 512)
 
+    loads = [pltpu.make_async_copy(slope_ref.at[:, pl.ds(pl.multiple_of(meta[base + at] * tile, 512), tile)], slope.at[at], sems.at[9 + at])
+             for at in range(2)]
+    loads.append(pltpu.make_async_copy(normed_ref, normed, sems.at[11]))
+    if last:
+        loads.append(pltpu.make_async_copy(mixed_ref, mixed, sems.at[12]))
+
     @pl.when(step == 0)
     def _():
+        fetch_quarter(native, meta, down_groups, down_weight.at[0], base, sems.at[0])
+        loads[0].start()
+        loads[2].start()
+        fetch_quarter(native, meta, down_groups, down_weight.at[1], base + 1, sems.at[1])
+        loads[1].start()
         for at in range(2):
             fetch_columns(native, meta, groups, weight.at[at], columns(base + at), tile, sems.at[2 + at])
         if last:
             pltpu.make_async_copy(before, acc, sems.at[6]).start()
             pltpu.make_async_copy(middle_ref, middle, sems.at[7]).start()
             fetch_columns(native, meta, groups, out_weight, 0, width, sems.at[8])
-
-    fetch_turn(native, meta, down_groups, down_weight, sems, t, base, base + 1)
+            loads[3].start()
+
+    arrive(down_weight.at[slot], sems.at[slot])
     length = acc.shape[0]
-    grad = (nt(cot_ref[...], flat(down_weight[t % 2])) * slope_ref[...].astype(F32)).astype(BF16)
+    product = nt(cot_ref[...], flat(down_weight[slot]))
+    arrive(slope.at[slot], sems.at[9 + slot])
+    grad = (product * slope[slot].astype(F32)).astype(BF16)
     up_sum_ref[...] = jnp.sum(grad.astype(F32), 0, keepdims=True)
-    stage[slot] = tn(normed_ref[...], grad).astype(BF16).reshape(stage.shape[1:])
+
+    @pl.when(step == 0)
+    def _():
+        loads[2].wait()
+
+    stage[slot] = tn(normed[...], grad).astype(BF16).reshape(stage.shape[1:])
     push_columns(native, meta, stage.at[slot], pushed, columns(t), tile, sems.at[4 + slot])
     arrive(weight.at[slot], sems.at[2 + slot])
     product = nt(grad, flat(weight[slot]))
@@ -836,7 +851,8 @@
             each_rows(length, 256, part)
             pltpu.make_async_copy(acc, out_ref, sems.at[6]).start()
             arrive(stage.at[0], sems.at[4])
-            stage[0] = tn(mixed_ref[...], branch_ref[...]).astype(BF16).reshape(stage.shape[1:])
+            loads[3].wait()
+            stage[0] = tn(mixed[...], branch_ref[...]).astype(BF16).reshape(stage.shape[1:])
             push_columns(native, meta, stage.at[0], pushed, 0, width, sems.at[4])
             arrive(out_weight, sems.at[8])
             mixed_out_ref[...] = nt(branch_ref[...], flat(out_weight[...])).astype(BF16)
@@ -861,28 +877,31 @@
     counts = (len(groups), len(outs))
     full, wide = jax.ShapeDtypeStruct((length, width), F32), jax.ShapeDtypeStruct((length, width), BF16)
     sums = jax.ShapeDtypeStruct((1, hidden), F32)
-    in_specs = [once, pl.BlockSpec((length, tile), part), once, pl.BlockSpec((4, width), whole), ANY, once if last else ANY]
+    in_specs = [once, ANY, ANY, pl.BlockSpec((4, width), whole), ANY, ANY]
     in_specs += [ANY] * (2 * counts[0])
     operands = [ladder.meta, cot, slope, normed, lines, middle, mixed, *down_groups, *groups]
     scratch = [pltpu.VMEM((length, width), F32), pltpu.VMEM((2,) + quarter_shape(ladder.native, hidden, width), BF16),
                pltpu.VMEM((2,) + tile_shape(ladder.native, width, tile), BF16),
-               pltpu.VMEM((2,) + tile_shape(ladder.native, width, tile), BF16), pltpu.SemaphoreType.DMA((9,))]
+               pltpu.VMEM((2,) + tile_shape(ladder.native, width, tile), BF16), pltpu.VMEM((2, length, tile), BF16),
+               pltpu.VMEM((length, width), BF16), pltpu.SemaphoreType.DMA((13,))]
     aliases = {}
     if last:
         aliases = {len(operands) + 1 + i: i for i in range(counts[1])}
+        aliases[len(operands) + 1 + counts[1]] = counts[1] + 4
         operands += list(before)
-        in_specs += [ANY] * (1 + counts[1])
+        in_specs += [ANY] * (2 + counts[1])
         out_specs = [ANY] * counts[1] + [ANY, square, square, pl.BlockSpec((8, width), whole)]
         out_shape = outs + [full, wide, wide, jax.ShapeDtypeStruct((8, width), F32)]
-        scratch += [pltpu.VMEM((length, width), F32), pltpu.VMEM(tile_shape(ladder.native, width, width), BF16)]
+        scratch += [pltpu.VMEM((length, width), F32), pltpu.VMEM(tile_shape(ladder.native, width, width), BF16),
+                    pltpu.VMEM((length, width), BF16)]
     else:
         out_specs, out_shape = [ANY] * counts[1] + [ANY], outs + [full]
     return pl.pallas_call(
         functools.partial(back_kernel, ladder.native, last, counts),
         grid_spec=pltpu.PrefetchScalarGridSpec(
-            num_scalar_prefetch=1, grid=(2,), in_specs=in_specs, out_specs=out_specs + [pl.BlockSpec((1, tile), lambda t, meta: (0, t))],
+            num_scalar_prefetch=1, grid=(2,), in_specs=in_specs, out_specs=out_specs + [pl.BlockSpec((1, tile), part)],
             scratch_shapes=scratch),
-        out_shape=out_shape + [jax.ShapeDtypeStruct((1, hidden // 2), F32)],
+        out_shape=out_shape + [jax.ShapeDtypeStruct((1, hidden), F32)],
         input_output_aliases=aliases,
         compiler_params=params(),
         cost_estimate=cost(30 if last else 20),
@@ -1042,7 +1061,7 @@
     qkv_groups = qkv.finish()
     rest.plane()
     down.start(*rest.sent)
-    projected, normed_in, sq_frames, up_bias, lines = project(ladder, tie(tokens, *sent(rest), *masks, *ladder.tables), valid, qkv_groups, known)
+    projected, normed_in, sq_frames, up_bias, lines = project(ladder, tie(tokens, *sent(rest), *masks), valid, qkv_groups, known)
     per = width // 128
     calls = 2
     each = per // calls
@@ -1075,10 +1094,9 @@
     *first_parts, first_acc, first_sum = back(
         ladder, tie(cotangent, sum_down), slope, normed_mid, lines, middle, mixed, down_groups, rest_groups)
     flow_down.corner(first_acc)
-    *rest_parts, grad_middle, grad_branch, grad_mixed, sum_middle, second_sum = back(
+    *rest_parts, grad_middle, grad_branch, grad_mixed, sum_middle, sum_up = back(
         ladder, tie(cotangent, *sent(flow_down)), slope, normed_mid, lines, middle, mixed, down_groups, rest_groups,
-        [first_acc, *first_parts])
-    sum_up = jnp.concatenate([first_sum, second_sum], 1).reshape(4, -1)[ladder.order].reshape(1, -1)
+        [first_acc, *first_parts, first_sum])
     flow_rest = Scatter(ladder, rest_parts)
     flow_down.plane(grad_mixed)
     grad_mixed = tie(grad_mixed, *sent(flow_down))
@@ -1108,13 +1126,13 @@
     flow_qkv.plane(grad_tokens)
     outputs.append(finish_rows(1, *sent(flow_qkv)))
     own_rest = flow_rest.finish(outputs[1])
-    flow_qkv.spread(outputs[1], own_rest)
+    flow_qkv.spread(outputs[1], *([] if ladder.native else flow_rest.last))
     output = jnp.concatenate(outputs, 0)
 
     sq_final = finals[0] + finals[1]
     members = [sq_frames, sq_middle[1:2], sq_final[1:2], sq_middle[:1], sq_final[:1], valid.reshape(1, -1)]
     members = jnp.sum(jnp.concatenate(members, 0), 1)
-    small_grads = [sum_qv[:2].reshape(-1), sum_middle[1], sum_in[0], sum_middle[0], sum_up[0], sum_down[0]]
+    small_grads = [sum_qv[:2], sum_middle[1:2], sum_in[:1], sum_middle[:1], sum_up, sum_down]
     table = jnp.concatenate([g.reshape(count, -1) for g in small_grads] + [jnp.broadcast_to(members, (count, 6))], 1)
     table = jnp.pad(table, ((0, 0), (0, -table.shape[1] % 128)))
     own_small = ladder.scatter_small(tie(table, *sent(flow_qkv)))

time: 405 us -> 401 us (level)
  Pallas kernels: 241 us -> 231 us
  starting transfers between devices: 51.2 us -> 56.2 us
    pallas_call x4, Pallas kernels: 54.7 us -> 48.7 us  [attn_call(): pl.pallas_call(body, grid_spec=pltpu.PrefetchScalarGridSpec(num_scalar_pr...]
    ppermute x49, starting transfers between devices: 48.6 us -> 52.9 us  [flip(): lax.ppermute(value, self.axes, [(i, i ^ bits[i & CORE]) for i in range(se...]
  transfers between devices with their start and end apart: 50 -> 50, of which waited for: 15 -> 13; matrix products, arithmetic and copies ran while one was open for 10% -> 10% of each run, Pallas kernels for 59% -> 57%
where the time goes in v5:
time: 401 us; the launch traced here: 396 us
  Pallas kernels  231 us (58%)
  waiting for transfers between devices  57 us (14%)
  starting transfers between devices  56.2 us (14%)
  other arithmetic  28.6 us (7%)
  local copies, waits for them, and re-layouts  20.3 us (5%)
    ppermute x49, waiting for transfers between devices, flip(): lax.ppermute(value, self.axes, [(i, i ^ bits[i & CORE]) for i in range(se...  55.6 us
    pallas_call x2, Pallas kernels, back(): pl.pallas_call(functools.partial(back_kernel, ladder.native, last, counts...  54.9 us
    ppermute x49, starting transfers between devices, flip(): lax.ppermute(value, self.axes, [(i, i ^ bits[i & CORE]) for i in range(se...  52.9 us
    pallas_call x4, Pallas kernels, attn_call(): pl.pallas_call(body, grid_spec=pltpu.PrefetchScalarGridSpec(num_scalar_pr...  48.7 us
    pallas_call x1, Pallas kernels, expand(): pl.pallas_call(functools.partial(expand_kernel, ladder.native, tile, len(...  29.1 us
    pallas_call x2, Pallas kernels, contract(): pl.pallas_call(functools.partial(contract_kernel, ladder.native, part * l...  24.6 us
    pallas_call x1, Pallas kernels, input_grad(): pl.pallas_call(functools.partial(input_grad_kernel, ladder.native, calls)...  17.8 us
    pallas_call x1, Pallas kernels, down_grad(): pl.pallas_call(functools.partial(down_grad_kernel, ladder.native, len(out...  14.8 us
  transfers between devices with their start and end apart: 50, of which 13 were waited for; matrix products, arithmetic and copies ran while one was open for 10% of the time, Pallas kernels for 57%

profile of v5, /device:TPU:0, one launch (start us, length us, event | category | flops | bytes accessed | tf_op | source)
XLA Modules:
  0.0 396.0 jit_solution(10676639932633417207)
XLA Ops:
  0.6 5.1 %collective-permute-start.2 = (bf16[32,3072]{1,0:T(8,128)(2,1)}, bf16[32,3072]{1,0:T(8,128)(2,1)S(1)}, u32[]{:S(2)}, u32[]{:S(2)}) collective-permute-start(bf16[32,3072]{1,0:T(8,128)(2,1)} %refs_0_), channel_id=1, source_target_pairs={{0,6},{1,7},{2,4},{3,5},{4,2},{5,3},{6,0},{7,1},{8,14},{9,15},{10,... | collective-permute-start | bytes 589832 | tf_op jit(solution)/shard_map/ppermute | solution.py:56
  10.5 8.2 %collective-permute-done.refs_1_ = bf16[32,3072]{1,0:T(8,128)(2,1)S(1)} collective-permute-done((bf16[32,3072]{1,0:T(8,128)(2,1)}, bf16[32,3072]{1,0:T(8,128)(2,1)S(1)}, u32[]{:S(2)}, u32[]{:S(2)}) %collective-permute-start) | collective-permute-done | bytes 196640 | tf_op jit(solution)/shard_map/ppermute | solution.py:56
  19.0 3.5 collective-permute-start.4
  24.4 1.9 collective-permute-done.3.refs_5_
  26.9 2.9 place_group.1.rest_0_.rest_4_
  31.4 1.5 collective-permute-start.6
  33.5 1.5 collective-permute-start.9
  35.0 16.1 %collective-permute-done.8.rest_1_.rest_5_ = bf16[4,32,3200]{2,1,0:T(8,128)(2,1)} collective-permute-done((bf16[4,32,3200]{2,1,0:T(8,128)(2,1)}, bf16[4,32,3200]{2,1,0:T(8,128)(2,1)}, u32[]{:S(2)}, u32[]{:S(2)}) %collective-permute-start.8) | collective-permute-done | bytes 819232 | tf_op jit(solution)/shard_map/ppermute | solution.py:56
  51.2 1.5 collective-permute-start.10
  55.1 8.7 %collective-permute-done.10.rest_3_.rest_7_ = bf16[4,32,3200]{2,1,0:T(8,128)(2,1)} collective-permute-done((bf16[4,32,3200]{2,1,0:T(8,128)(2,1)}, bf16[4,32,3200]{2,1,0:T(8,128)(2,1)}, u32[]{:S(2)}, u32[]{:S(2)}) %collective-permute-start.10) | collective-permute-done | bytes 819232 | tf_op jit(solution)/shard_map/ppermute | solution.py:56
  65.2 1.6 collective-permute-start.17
  68.3 1.5 collective-permute-start.15
  69.8 14.3 %project.1 = (bf16[1024,3072]{1,0:T(8,128)(2,1)}, bf16[1024,1024]{1,0:T(8,128)(2,1)}, f32[1,1024]{1,0:T(1,128)}, f32[1,4096]{1,0:T(1,128)}, f32[4,1024]{1,0:T(4,128)}) custom-call(s32[6]{0:T(128)} %pad_add_fusion.meta, bf16[1024,1024]{1,0:T(8,128)(2,1)} %bitcast.67, f32[1024,1]{1,0:T(8,128)} %copy.45.valid_ref, ...), custom_call_target="tpu_custom_call" | custom-call | flops 32199999488 | tf_op jit(solution)/shard_map/project/pallas_call | solution.py:569
  84.9 10.0 %attn_forward.2 = (bf16[1024,1024]{1,0:T(8,128)(2,1)S(1)}, f32[8,8,256]{2,1,0:T(8,128)S(1)}) custom-call(s32[8]{0:T(128)S(1)} %and_select_fusion.refs_0_, s32[1024,128]{1,0:T(8,128)S(1)} %broadcast_in_dim.72.refs_1_, s32[1024,128]{1,0:T(8,128)S(1)} %broadcast_in_dim.74.refs_2_, s32[8,128]{1,0:T(8,128)S(1)} %bitcast.35, ...), custom_call_target="tpu_custom_call" | custom-call | flops 24839999488 | tf_op jit(solution)/shard_map/attn_forward/pallas_call | solution.py:357
  98.5 10.0 %attn_forward.3 = (bf16[1024,1024]{1,0:T(8,128)(2,1)S(1)}, f32[8,8,256]{2,1,0:T(8,128)S(1)}) custom-call(s32[8]{0:T(128)S(1)} %and_select_fusion.refs_0_, s32[1024,128]{1,0:T(8,128)S(1)} %broadcast_in_dim.72.refs_1_, s32[1024,128]{1,0:T(8,128)S(1)} %broadcast_in_dim.74.refs_2_, s32[8,128]{1,0:T(8,128)S(1)} %bitcast.36, ...), custom_call_target="tpu_custom_call", output_to_operand_aliasing={{0}: (7, {}), {1}: (8, {})} | custom-call | flops 24839999488 | tf_op jit(solution)/shard_map/attn_forward/pallas_call | solution.py:357
  108.5 6.3 %collective-permute-done.19.rest_3_.rest_11_ = bf16[4,32,5120]{2,1,0:T(8,128)(2,1)S(1)} collective-permute-done((bf16[4,32,5120]{2,1,0:T(8,128)(2,1)}, bf16[4,32,5120]{2,1,0:T(8,128)(2,1)S(1)}, u32[]{:S(2)}, u32[]{:S(2)}) %collective-permute-start.19) | collective-permute-done | bytes 1310752 | tf_op jit(solution)/shard_map/ppermute | solution.py:56
  119.9 29.1 %expand.1 = (f32[1024,1024]{1,0:T(8,128)}, bf16[1024,1024]{1,0:T(8,128)(2,1)}, f32[8,1024]{1,0:T(8,128)}, bf16[1024,4096]{1,0:T(8,128)(2,1)}, bf16[1024,4096]{1,0:T(8,128)(2,1)}) custom-call(s32[6]{0:T(128)} %pad_add_fusion.meta, bf16[1024,1024]{1,0:T(8,128)(2,1)} %copy-done.7, bf16[1024,1024]{1,0:T(8,128)(2,1)} %bitcast.68, ...), custom_call_target="tpu_custom_call" | custom-call | flops 66700001280 | tf_op jit(solution)/shard_map/expand/pallas_call | solution.py:642
  150.8 14.8 %down_grad.1 = (bf16[4,4,128,1024]{3,2,1,0:T(8,128)(2,1)}, bf16[4,4,128,1024]{3,2,1,0:T(8,128)(2,1)}, f32[1,1024]{1,0:T(1,128)}) custom-call(s32[6]{0:T(128)} %pad_add_fusion.meta, bf16[1024,4096]{1,0:T(8,128)(2,1)} %get-tuple-element.179.act_ref, bf16[1024,1024]{1,0:T(8,128)(2,1)} %bitcast.64), custom_call_target="tpu_custom_call" | custom-call | flops 32199999488 | tf_op jit(solution)/shard_map/down_grad/pallas_call | solution.py:709
  166.3 2.8 collective-permute-done.31.rest_7_
  170.1 23.8 %back.2 = (bf16[4,4,32,5120]{3,2,1,0:T(8,128)(2,1)}, bf16[4,4,32,5120]{3,2,1,0:T(8,128)(2,1)}, f32[1024,1024]{1,0:T(8,128)}, f32[1,4096]{1,0:T(1,128)}) custom-call(s32[6]{0:T(128)} %pad_add_fusion.meta, bf16[1024,1024]{1,0:T(8,128)(2,1)} %bitcast.65, bf16[1024,4096]{1,0:T(8,128)(2,1)} %get-tuple-element.135.slope_ref, ...), custom_call_target="tpu_custom_call" | custom-call | flops 46000001024 | tf_op jit(solution)/shard_map/back/pallas_call | solution.py:899
  193.9 3.2 add_convert_fusion.1
  197.4 31.0 %back.3 = (bf16[4,4,32,5120]{3,2,1,0:T(8,128)(2,1)}, bf16[4,4,32,5120]{3,2,1,0:T(8,128)(2,1)}, f32[1024,1024]{1,0:T(8,128)}, bf16[1024,1024]{1,0:T(8,128)(2,1)},...) custom-call(s32[6]{0:T(128)} %pad_add_fusion.meta, ...), custom_call_target="tpu_custom_call", output_to_operand_aliasing={{0}: (24, {}), {1}: (25, {}), {6}: (26, {})} | custom-call | flops 69000003584 | tf_op jit(solution)/shard_map/back/pallas_call | solution.py:899
  228.6 3.0 fusion.1
  231.6 1.9 collective-permute-start.33
  233.4 14.2 %attn_backward.2 = (bf16[3,1024,1024]{2,1,0:T(8,128)(2,1)}, f32[8,1024]{1,0:T(8,128)S(1)}) custom-call(s32[8]{0:T(128)S(1)} %copy-done.6, s32[1024,128]{1,0:T(8,128)S(1)} %broadcast_in_dim.72.refs_1_, s32[1024,128]{1,0:T(8,128)S(1)} %broadcast_in_dim.74.refs_2_, s32[8,128]{1,0:T(8,128)S(1)} %bitcast.37, ...), custom_call_target="tpu_custom_call" | custom-call | flops 31280001024 | tf_op jit(solution)/shard_map/attn_backward/pallas_call | solution.py:357
  248.6 4.0 %spread_sums.3 = (f32[128,1024]{1,0:T(8,128)}, bf16[128,1024]{1,0:T(8,128)(2,1)}, bf16[128,1024]{1,0:T(8,128)(2,1)}, bf16[128,1024]{1,0:T(8,128)(2,1)}) custom-call(s32[6]{0:T(128)} %pad_add_fusion.meta, bf16[4,4,128,1024]{3,2,1,0:T(8,128)(2,1)} %get-tuple-element.131.refs_0_.refs_4_.refs_8_.refs_12_, ...), custom_call_target="tpu_custom_call" | custom-call | flops 6899999744 | tf_op jit(solution)/shard_map/spread_sums/pallas_call | solution.py:110
  252.6 2.4 collective-permute-start.35
  255.7 1.7 collective-permute-start.37
  257.5 5.1 %add_convert_fusion = bf16[2,4,32,5120]{3,2,1,0:T(8,128)(2,1)} fusion(bf16[4,4,32,5120]{3,2,1,0:T(8,128)(2,1)} %collective-permute-done.34.refs_1_.refs_5_.refs_9_.refs_13_, bf16[4,4,32,5120]{3,2,1,0:T(8,128)(2,1)} %get-tuple-element.154.refs_0_.refs_4_.refs_8_.refs_12_), kind=kLoop, calls=%fused_computation | loop fusion | flops 5242880 | bytes 7864320 | tf_op jit(solution)/shard_map/convert_element_type | solution.py:188
  262.6 1.9 collective-permute-start.38
  264.5 14.6 %attn_backward.3 = (bf16[3,1024,1024]{2,1,0:T(8,128)(2,1)}, f32[8,1024]{1,0:T(8,128)S(1)}) custom-call(s32[8]{0:T(128)S(1)} %copy-done.6, s32[1024,128]{1,0:T(8,128)S(1)} %copy-done.3, s32[1024,128]{1,0:T(8,128)S(1)} %copy-done.1, s32[8,128]{1,0:T(8,128)S(1)} %bitcast.38, ...), custom_call_target="tpu_custom_call", output_to_operand_aliasing={{0}: (9, {}), {1}: (10, {})} | custom-call | flops 31280001024 | tf_op jit(solution)/shard_map/attn_backward/pallas_call | solution.py:357
  280.0 12.3 %qkv_grad.1 = (bf16[4,4,32,3072]{3,2,1,0:T(8,128)(2,1)}, bf16[4,4,32,3072]{3,2,1,0:T(8,128)(2,1)}) custom-call(s32[6]{0:T(128)} %pad_add_fusion.meta, bf16[1024,1024]{1,0:T(8,128)(2,1)} %get-tuple-element.127.left_ref, bf16[3,1024,1024]{2,1,0:T(8,128)(2,1)} %get-tuple-element.164.right_ref.rest_0_), custom_call_target="tpu_custom_call" | custom-call | flops 18400000000 | tf_op jit(solution)/shard_map/qkv_grad/pallas_call | solution.py:747
  296.2 2.7 fusion
  298.9 1.7 collective-permute-start.41
  300.6 12.3 %contract.2 = (bf16[512,1024]{1,0:T(8,128)(2,1)}, f32[8,1024]{1,0:T(8,128)}) custom-call(s32[6]{0:T(128)} %pad_add_fusion.meta, bf16[1024,4096]{1,0:T(8,128)(2,1)} %get-tuple-element.179.act_ref, f32[4,1024]{1,0:T(4,128)} %get-tuple-element.124.lines_ref.rest_3_, f32[1024,1]{1,0:T(8,128)} %copy.45.valid_ref, f32[1024,1024]{1,0:T(8,128)} %get-tuple-element.137.middle_ref, ...), custom_call_target="tpu_custom_call" | custom-call | flops 18400000000 | tf_op jit(solution)/shard_map/contract/pallas_call | solution.py:955
  313.0 3.1 add_convert_fusion.2
  317.4 4.5 %spread_sums.4 = (f32[32,5120]{1,0:T(8,128)}, bf16[32,5120]{1,0:T(8,128)(2,1)}, bf16[32,5120]{1,0:T(8,128)(2,1)}, bf16[32,5120]{1,0:T(8,128)(2,1)}) custom-call(s32[6]{0:T(128)} %pad_add_fusion.meta, bf16[4,4,32,5120]{3,2,1,0:T(8,128)(2,1)} %get-tuple-element.154.refs_0_.refs_4_.refs_8_.refs_12_, ...), custom_call_target="tpu_custom_call" | custom-call | flops 6899999744 | tf_op jit(solution)/shard_map/spread_sums/pallas_call | solution.py:110
  321.9 1.6 collective-permute-start.43
  326.3 17.8 %input_grad.1 = (bf16[1024,1024]{1,0:T(8,128)(2,1)}, f32[8,1024]{1,0:T(8,128)}) custom-call(s32[6]{0:T(128)} %pad_add_fusion.meta, bf16[3,1024,1024]{2,1,0:T(8,128)(2,1)} %get-tuple-element.164.right_ref.rest_0_, bf16[1024,1024]{1,0:T(8,128)(2,1)} %bitcast.69, f32[1024,1024]{1,0:T(8,128)} %get-tuple-element.176.rest_2_, ...), custom_call_target="tpu_custom_call" | custom-call | flops 41400000512 | tf_op jit(solution)/shard_map/input_grad/pallas_call | solution.py:1014
  346.2 2.6 fusion.2
  348.9 1.5 collective-permute-start.42
  350.4 12.3 %contract.3 = (bf16[512,1024]{1,0:T(8,128)(2,1)}, f32[8,1024]{1,0:T(8,128)}) custom-call(s32[6]{0:T(128)} %pad_add_fusion.meta, bf16[1024,4096]{1,0:T(8,128)(2,1)} %get-tuple-element.179.act_ref, f32[4,1024]{1,0:T(4,128)} %get-tuple-element.124.lines_ref.rest_3_, f32[1024,1]{1,0:T(8,128)} %copy.45.valid_ref, f32[1024,1024]{1,0:T(8,128)} %get-tuple-element.137.middle_ref, ...), custom_call_target="tpu_custom_call" | custom-call | flops 18400000000 | tf_op jit(solution)/shard_map/contract/pallas_call | solution.py:955
  366.8 3.7 spread_sums.5
  371.1 3.4 all-to-all-start
  376.1 1.8 collective-permute-start.46
  377.8 2.4 collective-permute-start.47
  385.4 1.9 collective-permute-done.46
  387.3 7.7 %collective-permute-done.47 = bf16[32,3072]{1,0:T(8,128)(2,1)S(1)} collective-permute-done((bf16[32,3072]{1,0:T(8,128)(2,1)S(1)}, bf16[32,3072]{1,0:T(8,128)(2,1)S(1)}, u32[]{:S(2)}, u32[]{:S(2)}) %collective-permute-start.47) | collective-permute-done | bytes 196640 | tf_op jit(solution)/shard_map/ppermute | solution.py:56
  (241 shorter events, 52.1 us)
Async XLA Ops:
  0.6 23.1 %collective-permute-start.2 = (bf16[32,3072]{1,0:T(8,128)(2,1)}, bf16[32,3072]{1,0:T(8,128)(2,1)S(1)}, u32[]{:S(2)}, u32[]{:S(2)}) collective-permute-start(bf16[32,3072]{1,0:T(8,128)(2,1)} %refs_0_), channel_id=1, source_target_pairs={{0,6},{1,7},{2,4},{3,5},{4,2},{5,3},{6,0},{7,1},{8,14},{9,15},{10,... | collective-permute-start | bytes 589832 | tf_op jit(solution)/shard_map/ppermute | solution.py:56
  5.8 18.0 %collective-permute-start.1 = (bf16[32,3072]{1,0:T(8,128)(2,1)}, bf16[32,3072]{1,0:T(8,128)(2,1)S(1)}, u32[]{:S(2)}, u32[]{:S(2)}) collective-permute-start(bf16[32,3072]{1,0:T(8,128)(2,1)} %refs_0_), channel_id=1, source_target_pairs={{0,4},{1,5},{2,6},{3,7},{4,0},{5,1},{6,2},{7,3},{8,12},{9,13},{10,... | collective-permute-start | bytes 589832 | tf_op jit(solution)/shard_map/ppermute | solution.py:56
  5.8 13.0 %collective-permute-start = (bf16[32,3072]{1,0:T(8,128)(2,1)}, bf16[32,3072]{1,0:T(8,128)(2,1)S(1)}, u32[]{:S(2)}, u32[]{:S(2)}) collective-permute-start(bf16[32,3072]{1,0:T(8,128)(2,1)} %refs_0_), channel_id=1, source_target_pairs={{0,2},{1,3},{2,0},{3,1},{4,6},{5,7},{6,4},{7,5},{8,10},{9,11},{10,... | collective-permute-start | bytes 589832 | tf_op jit(solution)/shard_map/ppermute | solution.py:56
  18.8 5.5 %collective-permute-start.5 = (bf16[32,128]{1,0:T(8,128)(2,1)S(1)}, bf16[32,128]{1,0:T(8,128)(2,1)S(1)}, u32[]{:S(2)}, u32[]{:S(2)}) collective-permute-start(bf16[32,128]{1,0:T(8,128)(2,1)S(1)} %select_select_fusion.refs_4_), channel_id=1, source_target_pairs={{0,6},{1,7},{2,4},{3,5},{4,2},{5,3},{6,0},{7,1},{8,14},{9,15},{10,... | collective-permute-start | bytes 24584 | tf_op jit(solution)/shard_map/ppermute | solution.py:56
  19.0 5.3 %collective-permute-start.4 = (bf16[32,128]{1,0:T(8,128)(2,1)S(1)}, bf16[32,128]{1,0:T(8,128)(2,1)S(1)}, u32[]{:S(2)}, u32[]{:S(2)}) collective-permute-start(bf16[32,128]{1,0:T(8,128)(2,1)S(1)} %select_select_fusion.refs_4_), channel_id=1, source_target_pairs={{0,4},{1,5},{2,6},{3,7},{4,0},{5,1},{6,2},{7,3},{8,12},{9,13},{10,... | collective-permute-start | bytes 24584 | tf_op jit(solution)/shard_map/ppermute | solution.py:56
  22.6 3.7 collective-permute-start.3
  29.7 21.4 %collective-permute-start.8 = (bf16[4,32,3200]{2,1,0:T(8,128)(2,1)}, bf16[4,32,3200]{2,1,0:T(8,128)(2,1)}, u32[]{:S(2)}, u32[]{:S(2)}) collective-permute-start(bf16[4,32,3200]{2,1,0:T(8,128)(2,1)} %place_group.1.rest_0_.rest_4_), channel_id=1, source_target_pairs={{0,8},{1,17},{2,10},{3,19},{4,12},{5,21},{6,14},{7,23},{8,0},{9,25... | collective-permute-start | bytes 2457608 | tf_op jit(solution)/shard_map/ppermute | solution.py:56
  31.4 21.5 %collective-permute-start.6 = (bf16[32,5120]{1,0:T(8,128)(2,1)S(1)}, bf16[32,5120]{1,0:T(8,128)(2,1)S(1)}, u32[]{:S(2)}, u32[]{:S(2)}) collective-permute-start(bf16[32,5120]{1,0:T(8,128)(2,1)S(1)} %pad_maximum_fusion), channel_id=1, source_target_pairs={{0,4},{1,5},{2,6},{3,7},{4,0},{5,1},{6,2},{7,3},{8,12},{9,13},{10,... | collective-permute-start | bytes 983048 | tf_op jit(solution)/shard_map/ppermute | solution.py:56
  33.5 21.6 %collective-permute-start.9 = (bf16[4,32,3200]{2,1,0:T(8,128)(2,1)}, bf16[4,32,3200]{2,1,0:T(8,128)(2,1)}, u32[]{:S(2)}, u32[]{:S(2)}) collective-permute-start(bf16[4,32,3200]{2,1,0:T(8,128)(2,1)} %place_group.1.rest_0_.rest_4_), channel_id=1, source_target_pairs={{0,16},{1,9},{2,18},{3,11},{4,20},{5,13},{6,22},{7,15},{8,24},{9,1... | collective-permute-start | bytes 2457608 | tf_op jit(solution)/shard_map/ppermute | solution.py:56
  51.2 12.7 %collective-permute-start.10 = (bf16[4,32,3200]{2,1,0:T(8,128)(2,1)}, bf16[4,32,3200]{2,1,0:T(8,128)(2,1)}, u32[]{:S(2)}, u32[]{:S(2)}) collective-permute-start(bf16[4,32,3200]{2,1,0:T(8,128)(2,1)} %collective-permute-done.8.rest_1_.rest_5_), channel_id=1, source_target_pairs={{0,16},{1,9},{2,18},{3,11},{4,20},{5,13},{6,22},{7,15},{8,24},{9,1... | collective-permute-start | bytes 2457608 | tf_op jit(solution)/shard_map/ppermute | solution.py:56
  53.0 10.9 %collective-permute-start.7 = (bf16[2,32,5120]{2,1,0:T(8,128)(2,1)S(1)}, bf16[2,32,5120]{2,1,0:T(8,128)(2,1)S(1)}, u32[]{:S(2)}, u32[]{:S(2)}) collective-permute-start(bf16[2,32,5120]{2,1,0:T(8,128)(2,1)S(1)} %maximum_select_fusion.2), channel_id=1, source_target_pairs={{0,2},{1,3},{2,0},{3,1},{4,6},{5,7},{6,4},{7,5},{8,10},{9,11},{10,... | collective-permute-start | bytes 1966088 | tf_op jit(solution)/shard_map/ppermute | solution.py:56
  54.6 10.6 %collective-permute-start.11 = (bf16[4,32,3200]{2,1,0:T(8,128)(2,1)}, bf16[4,32,3200]{2,1,0:T(8,128)(2,1)S(1)}, u32[]{:S(2)}, u32[]{:S(2)}) collective-permute-start(bf16[4,32,3200]{2,1,0:T(8,128)(2,1)} %place_group.1.rest_0_.rest_4_), channel_id=1, source_target_pairs={{0,1},{1,0},{2,3},{3,2},{4,5},{5,4},{6,7},{7,6},{8,9},{9,8},{10,11... | collective-permute-start | bytes 2457608 | tf_op jit(solution)/shard_map/ppermute | solution.py:56
  54.6 13.7 %collective-permute-start.13 = (bf16[4,32,3200]{2,1,0:T(8,128)(2,1)}, bf16[4,32,3200]{2,1,0:T(8,128)(2,1)}, u32[]{:S(2)}, u32[]{:S(2)}) collective-permute-start(bf16[4,32,3200]{2,1,0:T(8,128)(2,1)} %collective-permute-done.8.rest_1_.rest_5_), channel_id=1, source_target_pairs={{0,1},{1,0},{2,3},{3,2},{4,5},{5,4},{6,7},{7,6},{8,9},{9,8},{10,11... | collective-permute-start | bytes 2457608 | tf_op jit(solution)/shard_map/ppermute | solution.py:56
  55.1 11.7 %collective-permute-start.12 = (bf16[4,32,3200]{2,1,0:T(8,128)(2,1)}, bf16[4,32,3200]{2,1,0:T(8,128)(2,1)S(1)}, u32[]{:S(2)}, u32[]{:S(2)}) collective-permute-start(bf16[4,32,3200]{2,1,0:T(8,128)(2,1)} %collective-permute-done.9.rest_2_.rest_6_), channel_id=1, source_target_pairs={{0,1},{1,0},{2,3},{3,2},{4,5},{5,4},{6,7},{7,6},{8,9},{9,8},{10,11... | collective-permute-start | bytes 2457608 | tf_op jit(solution)/shard_map/ppermute | solution.py:56
  63.8 6.0 %collective-permute-start.14 = (bf16[4,32,3200]{2,1,0:T(8,128)(2,1)}, bf16[4,32,3200]{2,1,0:T(8,128)(2,1)}, u32[]{:S(2)}, u32[]{:S(2)}) collective-permute-start(bf16[4,32,3200]{2,1,0:T(8,128)(2,1)} %collective-permute-done.10.rest_3_.rest_7_), channel_id=1, source_target_pairs={{0,1},{1,0},{2,3},{3,2},{4,5},{5,4},{6,7},{7,6},{8,9},{9,8},{10,11... | collective-permute-start | bytes 2457608 | tf_op jit(solution)/shard_map/ppermute | solution.py:56
  64.2 51.5 %collective-permute-start.20 = (bf16[4,32,5120]{2,1,0:T(8,128)(2,1)S(1)}, bf16[4,32,5120]{2,1,0:T(8,128)(2,1)S(1)}, u32[]{:S(2)}, u32[]{:S(2)}) collective-permute-start(bf16[4,32,5120]{2,1,0:T(8,128)(2,1)S(1)} %bitcast.41), channel_id=1, source_target_pairs={{0,1},{1,0},{2,3},{3,2},{4,5},{5,4},{6,7},{7,6},{8,9},{9,8},{10,11... | collective-permute-start | bytes 3932168 | tf_op jit(solution)/shard_map/ppermute | solution.py:56
  65.2 33.3 %collective-permute-start.17 = (bf16[4,32,5120]{2,1,0:T(8,128)(2,1)S(1)}, bf16[4,32,5120]{2,1,0:T(8,128)(2,1)}, u32[]{:S(2)}, u32[]{:S(2)}) collective-permute-start(bf16[4,32,5120]{2,1,0:T(8,128)(2,1)S(1)} %bitcast.42), channel_id=1, source_target_pairs={{0,16},{1,9},{2,18},{3,11},{4,20},{5,13},{6,22},{7,15},{8,24},{9,1... | collective-permute-start | bytes 3932168 | tf_op jit(solution)/shard_map/ppermute | solution.py:56
  66.8 29.3 %collective-permute-start.16 = (bf16[4,32,5120]{2,1,0:T(8,128)(2,1)S(1)}, bf16[4,32,5120]{2,1,0:T(8,128)(2,1)}, u32[]{:S(2)}, u32[]{:S(2)}) collective-permute-start(bf16[4,32,5120]{2,1,0:T(8,128)(2,1)S(1)} %bitcast.43), channel_id=1, source_target_pairs={{0,8},{1,17},{2,10},{3,19},{4,12},{5,21},{6,14},{7,23},{8,0},{9,25... | collective-permute-start | bytes 3932168 | tf_op jit(solution)/shard_map/ppermute | solution.py:56
  68.3 15.8 %collective-permute-start.15 = (bf16[128,1024]{1,0:T(8,128)(2,1)S(1)}, bf16[128,1024]{1,0:T(8,128)(2,1)S(1)}, u32[]{:S(2)}, u32[]{:S(2)}) collective-permute-start(bf16[128,1024]{1,0:T(8,128)(2,1)S(1)} %copy-done.19), channel_id=1, source_target_pairs={{0,4},{1,5},{2,6},{3,7},{4,0},{5,1},{6,2},{7,3},{8,12},{9,13},{10,... | collective-permute-start | bytes 786440 | tf_op jit(solution)/shard_map/ppermute | solution.py:56
  84.2 14.3 %collective-permute-start.18 = (bf16[2,128,1024]{2,1,0:T(8,128)(2,1)S(1)}, bf16[2,128,1024]{2,1,0:T(8,128)(2,1)S(1)}, u32[]{:S(2)}, u32[]{:S(2)}) collective-permute-start(bf16[2,128,1024]{2,1,0:T(8,128)(2,1)S(1)} %maximum_select_fusion.4), channel_id=1, source_target_pairs={{0,2},{1,3},{2,0},{3,1},{4,6},{5,7},{6,4},{7,5},{8,10},{9,11},{10,... | collective-permute-start | bytes 1572872 | tf_op jit(solution)/shard_map/ppermute | solution.py:56
  96.1 21.1 %collective-permute-start.22 = (bf16[4,32,5120]{2,1,0:T(8,128)(2,1)}, bf16[4,32,5120]{2,1,0:T(8,128)(2,1)}, u32[]{:S(2)}, u32[]{:S(2)}) collective-permute-start(bf16[4,32,5120]{2,1,0:T(8,128)(2,1)} %collective-permute-done.16.rest_1_.rest_9_), channel_id=1, source_target_pairs={{0,1},{1,0},{2,3},{3,2},{4,5},{5,4},{6,7},{7,6},{8,9},{9,8},{10,11... | collective-permute-start | bytes 3932168 | tf_op jit(solution)/shard_map/ppermute | solution.py:56
  97.0 17.8 %collective-permute-start.19 = (bf16[4,32,5120]{2,1,0:T(8,128)(2,1)}, bf16[4,32,5120]{2,1,0:T(8,128)(2,1)S(1)}, u32[]{:S(2)}, u32[]{:S(2)}) collective-permute-start(bf16[4,32,5120]{2,1,0:T(8,128)(2,1)} %collective-permute-done.16.rest_1_.rest_9_), channel_id=1, source_target_pairs={{0,16},{1,9},{2,18},{3,11},{4,20},{5,13},{6,22},{7,15},{8,24},{9,1... | collective-permute-start | bytes 3932168 | tf_op jit(solution)/shard_map/ppermute | solution.py:56
  98.5 19.3 %collective-permute-start.21 = (bf16[4,32,5120]{2,1,0:T(8,128)(2,1)}, bf16[4,32,5120]{2,1,0:T(8,128)(2,1)S(1)}, u32[]{:S(2)}, u32[]{:S(2)}) collective-permute-start(bf16[4,32,5120]{2,1,0:T(8,128)(2,1)} %collective-permute-done.17.rest_2_.rest_10_), channel_id=1, source_target_pairs={{0,1},{1,0},{2,3},{3,2},{4,5},{5,4},{6,7},{7,6},{8,9},{9,8},{10,11... | collective-permute-start | bytes 3932168 | tf_op jit(solution)/shard_map/ppermute | solution.py:56
  115.1 51.1 %collective-permute-start.28 = (bf16[4,128,1024]{2,1,0:T(8,128)(2,1)S(1)}, bf16[4,128,1024]{2,1,0:T(8,128)(2,1)S(1)}, u32[]{:S(2)}, u32[]{:S(2)}) collective-permute-start(bf16[4,128,1024]{2,1,0:T(8,128)(2,1)S(1)} %bitcast.49), channel_id=1, source_target_pairs={{0,1},{1,0},{2,3},{3,2},{4,5},{5,4},{6,7},{7,6},{8,9},{9,8},{10,11... | collective-permute-start | bytes 3145736 | tf_op jit(solution)/shard_map/ppermute | solution.py:56
  115.7 34.1 %collective-permute-start.25 = (bf16[4,128,1024]{2,1,0:T(8,128)(2,1)S(1)}, bf16[4,128,1024]{2,1,0:T(8,128)(2,1)S(1)}, u32[]{:S(2)}, u32[]{:S(2)}) collective-permute-start(bf16[4,128,1024]{2,1,0:T(8,128)(2,1)S(1)} %bitcast.50), channel_id=1, source_target_pairs={{0,16},{1,9},{2,18},{3,11},{4,20},{5,13},{6,22},{7,15},{8,24},{9,1... | collective-permute-start | bytes 3145736 | tf_op jit(solution)/shard_map/ppermute | solution.py:56
  117.2 31.9 %collective-permute-start.24 = (bf16[4,128,1024]{2,1,0:T(8,128)(2,1)S(1)}, bf16[4,128,1024]{2,1,0:T(8,128)(2,1)}, u32[]{:S(2)}, u32[]{:S(2)}) collective-permute-start(bf16[4,128,1024]{2,1,0:T(8,128)(2,1)S(1)} %bitcast.51), channel_id=1, source_target_pairs={{0,8},{1,17},{2,10},{3,19},{4,12},{5,21},{6,14},{7,23},{8,0},{9,25... | collective-permute-start | bytes 3145736 | tf_op jit(solution)/shard_map/ppermute | solution.py:56
  149.1 17.2 %collective-permute-start.30 = (bf16[4,128,1024]{2,1,0:T(8,128)(2,1)}, bf16[4,128,1024]{2,1,0:T(8,128)(2,1)S(1)}, u32[]{:S(2)}, u32[]{:S(2)}) collective-permute-start(bf16[4,128,1024]{2,1,0:T(8,128)(2,1)} %collective-permute-done.24.rest_1_), channel_id=1, source_target_pairs={{0,1},{1,0},{2,3},{3,2},{4,5},{5,4},{6,7},{7,6},{8,9},{9,8},{10,11... | collective-permute-start | bytes 3145736 | tf_op jit(solution)/shard_map/ppermute | solution.py:56
  149.1 16.5 %collective-permute-start.27 = (bf16[4,128,1024]{2,1,0:T(8,128)(2,1)}, bf16[4,128,1024]{2,1,0:T(8,128)(2,1)S(1)}, u32[]{:S(2)}, u32[]{:S(2)}) collective-permute-start(bf16[4,128,1024]{2,1,0:T(8,128)(2,1)} %collective-permute-done.24.rest_1_), channel_id=1, source_target_pairs={{0,16},{1,9},{2,18},{3,11},{4,20},{5,13},{6,22},{7,15},{8,24},{9,1... | collective-permute-start | bytes 3145736 | tf_op jit(solution)/shard_map/ppermute | solution.py:56
  149.8 16.5 %collective-permute-start.29 = (bf16[4,128,1024]{2,1,0:T(8,128)(2,1)S(1)}, bf16[4,128,1024]{2,1,0:T(8,128)(2,1)S(1)}, u32[]{:S(2)}, u32[]{:S(2)}) collective-permute-start(bf16[4,128,1024]{2,1,0:T(8,128)(2,1)S(1)} %collective-permute-done.25.rest_2_), channel_id=1, source_target_pairs={{0,1},{1,0},{2,3},{3,2},{4,5},{5,4},{6,7},{7,6},{8,9},{9,8},{10,11... | collective-permute-start | bytes 3145736 | tf_op jit(solution)/shard_map/ppermute | solution.py:56
  165.7 28.2 %collective-permute-start.26 = (bf16[4,4,128,1024]{3,2,1,0:T(8,128)(2,1)}, bf16[4,4,128,1024]{3,2,1,0:T(8,128)(2,1)}, u32[]{:S(2)}, u32[]{:S(2)}) collective-permute-start(bf16[4,4,128,1024]{3,2,1,0:T(8,128)(2,1)} %get-tuple-element.132), channel_id=1, source_target_pairs={{0,1},{1,0},{2,3},{3,2},{4,5},{5,4},{6,7},{7,6},{8,9},{9,8},{10,11... | collective-permute-start | bytes 12582920 | tf_op jit(solution)/shard_map/ppermute | solution.py:56
  197.1 31.4 %collective-permute-start.32 = (bf16[2,4,128,1024]{3,2,1,0:T(8,128)(2,1)S(1)}, bf16[2,4,128,1024]{3,2,1,0:T(8,128)(2,1)S(1)}, u32[]{:S(2)}, u32[]{:S(2)}) collective-permute-start(bf16[2,4,128,1024]{3,2,1,0:T(8,128)(2,1)S(1)} %add_convert_fusion.1), channel_id=1, source_target_pairs={{0,16},{1,9},{2,18},{3,11},{4,20},{5,13},{6,22},{7,15},{8,24},{9,1... | collective-permute-start | bytes 6291464 | tf_op jit(solution)/shard_map/ppermute | solution.py:56
  228.4 29.0 %collective-permute-start.34 = (bf16[4,4,32,5120]{3,2,1,0:T(8,128)(2,1)}, bf16[4,4,32,5120]{3,2,1,0:T(8,128)(2,1)}, u32[]{:S(2)}, u32[]{:S(2)}) collective-permute-start(bf16[4,4,32,5120]{3,2,1,0:T(8,128)(2,1)} %get-tuple-element.155), channel_id=1, source_target_pairs={{0,1},{1,0},{2,3},{3,2},{4,5},{5,4},{6,7},{7,6},{8,9},{9,8},{10,11... | collective-permute-start | bytes 15728648 | tf_op jit(solution)/shard_map/ppermute | solution.py:56
  231.6 16.1 %collective-permute-start.33 = (bf16[4,128,1024]{2,1,0:T(8,128)(2,1)S(1)}, bf16[4,128,1024]{2,1,0:T(8,128)(2,1)S(1)}, u32[]{:S(2)}, u32[]{:S(2)}) collective-permute-start(bf16[4,128,1024]{2,1,0:T(8,128)(2,1)S(1)} %fusion.1), channel_id=1, source_target_pairs={{0,8},{1,17},{2,10},{3,19},{4,12},{5,21},{6,14},{7,23},{8,0},{9,25... | collective-permute-start | bytes 3145736 | tf_op jit(solution)/shard_map/ppermute | solution.py:56
  252.6 26.4 %collective-permute-start.35 = (bf16[128,1024]{1,0:T(8,128)(2,1)}, bf16[128,1024]{1,0:T(8,128)(2,1)S(1)}, u32[]{:S(2)}, u32[]{:S(2)}) collective-permute-start(bf16[128,1024]{1,0:T(8,128)(2,1)} %get-tuple-element.151), channel_id=1, source_target_pairs={{0,2},{1,3},{2,0},{3,1},{4,6},{5,7},{6,4},{7,5},{8,10},{9,11},{10,... | collective-permute-start | bytes 786440 | tf_op jit(solution)/shard_map/ppermute | solution.py:56
  255.0 24.0 %collective-permute-start.36 = (bf16[128,1024]{1,0:T(8,128)(2,1)}, bf16[128,1024]{1,0:T(8,128)(2,1)S(1)}, u32[]{:S(2)}, u32[]{:S(2)}) collective-permute-start(bf16[128,1024]{1,0:T(8,128)(2,1)} %get-tuple-element.152), channel_id=1, source_target_pairs={{0,4},{1,5},{2,6},{3,7},{4,0},{5,1},{6,2},{7,3},{8,12},{9,13},{10,... | collective-permute-start | bytes 786440 | tf_op jit(solution)/shard_map/ppermute | solution.py:56
  255.7 23.3 %collective-permute-start.37 = (bf16[128,1024]{1,0:T(8,128)(2,1)}, bf16[128,1024]{1,0:T(8,128)(2,1)S(1)}, u32[]{:S(2)}, u32[]{:S(2)}) collective-permute-start(bf16[128,1024]{1,0:T(8,128)(2,1)} %get-tuple-element.153), channel_id=1, source_target_pairs={{0,6},{1,7},{2,4},{3,5},{4,2},{5,3},{6,0},{7,1},{8,14},{9,15},{10,... | collective-permute-start | bytes 786440 | tf_op jit(solution)/shard_map/ppermute | solution.py:56
  262.6 33.6 %collective-permute-start.38 = (bf16[2,4,32,5120]{3,2,1,0:T(8,128)(2,1)}, bf16[2,4,32,5120]{3,2,1,0:T(8,128)(2,1)}, u32[]{:S(2)}, u32[]{:S(2)}) collective-permute-start(bf16[2,4,32,5120]{3,2,1,0:T(8,128)(2,1)} %add_convert_fusion), channel_id=1, source_target_pairs={{0,16},{1,9},{2,18},{3,11},{4,20},{5,13},{6,22},{7,15},{8,24},{9,1... | collective-permute-start | bytes 7864328 | tf_op jit(solution)/shard_map/ppermute | solution.py:56
  292.3 20.6 %collective-permute-start.39 = (bf16[4,4,32,3072]{3,2,1,0:T(8,128)(2,1)}, bf16[4,4,32,3072]{3,2,1,0:T(8,128)(2,1)}, u32[]{:S(2)}, u32[]{:S(2)}) collective-permute-start(bf16[4,4,32,3072]{3,2,1,0:T(8,128)(2,1)} %get-tuple-element.166), channel_id=1, source_target_pairs={{0,1},{1,0},{2,3},{3,2},{4,5},{5,4},{6,7},{7,6},{8,9},{9,8},{10,11... | collective-permute-start | bytes 9437192 | tf_op jit(solution)/shard_map/ppermute | solution.py:56
  298.9 18.5 %collective-permute-start.41 = (bf16[4,32,5120]{2,1,0:T(8,128)(2,1)S(1)}, bf16[4,32,5120]{2,1,0:T(8,128)(2,1)}, u32[]{:S(2)}, u32[]{:S(2)}) collective-permute-start(bf16[4,32,5120]{2,1,0:T(8,128)(2,1)S(1)} %fusion), channel_id=1, source_target_pairs={{0,8},{1,17},{2,10},{3,19},{4,12},{5,21},{6,14},{7,23},{8,0},{9,25... | collective-permute-start | bytes 3932168 | tf_op jit(solution)/shard_map/ppermute | solution.py:56
  316.1 30.1 %collective-permute-start.40 = (bf16[2,4,32,3072]{3,2,1,0:T(8,128)(2,1)}, bf16[2,4,32,3072]{3,2,1,0:T(8,128)(2,1)}, u32[]{:S(2)}, u32[]{:S(2)}) collective-permute-start(bf16[2,4,32,3072]{3,2,1,0:T(8,128)(2,1)} %add_convert_fusion.2), channel_id=1, source_target_pairs={{0,16},{1,9},{2,18},{3,11},{4,20},{5,13},{6,22},{7,15},{8,24},{9,1... | collective-permute-start | bytes 4718600 | tf_op jit(solution)/shard_map/ppermute | solution.py:56
  321.9 40.8 %collective-permute-start.43 = (bf16[32,5120]{1,0:T(8,128)(2,1)}, bf16[32,5120]{1,0:T(8,128)(2,1)S(1)}, u32[]{:S(2)}, u32[]{:S(2)}) collective-permute-start(bf16[32,5120]{1,0:T(8,128)(2,1)} %get-tuple-element.172), channel_id=1, source_target_pairs={{0,2},{1,3},{2,0},{3,1},{4,6},{5,7},{6,4},{7,5},{8,10},{9,11},{10,... | collective-permute-start | bytes 983048 | tf_op jit(solution)/shard_map/ppermute | solution.py:56
  323.5 39.3 %collective-permute-start.44 = (bf16[32,5120]{1,0:T(8,128)(2,1)}, bf16[32,5120]{1,0:T(8,128)(2,1)}, u32[]{:S(2)}, u32[]{:S(2)}) collective-permute-start(bf16[32,5120]{1,0:T(8,128)(2,1)} %get-tuple-element.173), channel_id=1, source_target_pairs={{0,4},{1,5},{2,6},{3,7},{4,0},{5,1},{6,2},{7,3},{8,12},{9,13},{10,... | collective-permute-start | bytes 983048 | tf_op jit(solution)/shard_map/ppermute | solution.py:56
  324.9 37.9 %collective-permute-start.45 = (bf16[32,5120]{1,0:T(8,128)(2,1)}, bf16[32,5120]{1,0:T(8,128)(2,1)}, u32[]{:S(2)}, u32[]{:S(2)}) collective-permute-start(bf16[32,5120]{1,0:T(8,128)(2,1)} %get-tuple-element.174), channel_id=1, source_target_pairs={{0,6},{1,7},{2,4},{3,5},{4,2},{5,3},{6,0},{7,1},{8,14},{9,15},{10,... | collective-permute-start | bytes 983048 | tf_op jit(solution)/shard_map/ppermute | solution.py:56
  348.9 17.0 %collective-permute-start.42 = (bf16[4,32,3072]{2,1,0:T(8,128)(2,1)}, bf16[4,32,3072]{2,1,0:T(8,128)(2,1)S(1)}, u32[]{:S(2)}, u32[]{:S(2)}) collective-permute-start(bf16[4,32,3072]{2,1,0:T(8,128)(2,1)} %fusion.2), channel_id=1, source_target_pairs={{0,8},{1,17},{2,10},{3,19},{4,12},{5,21},{6,14},{7,23},{8,0},{9,25... | collective-permute-start | bytes 2359304 | tf_op jit(solution)/shard_map/ppermute | solution.py:56
  371.1 10.7 %all-to-all-start = ((f32[32,1,384]{2,1,0:T(1,128)}), f32[32,1,384]{2,1,0:T(1,128)S(1)}, u32[]{:S(2)}, u32[]{:S(2)}) async-start(f32[32,1,384]{2,1,0:T(1,128)} %all_to_all.6), calls=%async_computation | async-start | bytes 98304 | tf_op jit(solution)/shard_map/all_to_all | solution.py:65
  376.1 11.2 %collective-permute-start.46 = (bf16[32,3072]{1,0:T(8,128)(2,1)}, bf16[32,3072]{1,0:T(8,128)(2,1)S(1)}, u32[]{:S(2)}, u32[]{:S(2)}) collective-permute-start(bf16[32,3072]{1,0:T(8,128)(2,1)} %get-tuple-element.183), channel_id=1, source_target_pairs={{0,2},{1,3},{2,0},{3,1},{4,6},{5,7},{6,4},{7,5},{8,10},{9,11},{10,... | collective-permute-start | bytes 589832 | tf_op jit(solution)/shard_map/ppermute | solution.py:56
  377.8 17.1 %collective-permute-start.47 = (bf16[32,3072]{1,0:T(8,128)(2,1)S(1)}, bf16[32,3072]{1,0:T(8,128)(2,1)S(1)}, u32[]{:S(2)}, u32[]{:S(2)}) collective-permute-start(bf16[32,3072]{1,0:T(8,128)(2,1)S(1)} %copy-done.51), channel_id=1, source_target_pairs={{0,4},{1,5},{2,6},{3,7},{4,0},{5,1},{6,2},{7,3},{8,12},{9,13},{10,... | collective-permute-start | bytes 589832 | tf_op jit(solution)/shard_map/ppermute | solution.py:56
  380.3 14.7 %collective-permute-start.48 = (bf16[32,3072]{1,0:T(8,128)(2,1)S(1)}, bf16[32,3072]{1,0:T(8,128)(2,1)S(1)}, u32[]{:S(2)}, u32[]{:S(2)}) collective-permute-start(bf16[32,3072]{1,0:T(8,128)(2,1)S(1)} %copy-done.50), channel_id=1, source_target_pairs={{0,6},{1,7},{2,4},{3,5},{4,2},{5,3},{6,0},{7,1},{8,14},{9,15},{10,... | collective-permute-start | bytes 589832 | tf_op jit(solution)/shard_map/ppermute | solution.py:56
  (57 other events, 854.4 us)

commit v6 on v5

--- a/solution.py
+++ b/solution.py
@@ -1125,9 +1125,7 @@
     grad_tokens, sum_in = input_grad(ladder, [grad_projected], tail, grad_middle, lines, qkv_groups)
     flow_qkv.plane(grad_tokens)
     outputs.append(finish_rows(1, *sent(flow_qkv)))
-    own_rest = flow_rest.finish(outputs[1])
     flow_qkv.spread(outputs[1], *([] if ladder.native else flow_rest.last))
-    output = jnp.concatenate(outputs, 0)
 
     sq_final = finals[0] + finals[1]
     members = [sq_frames, sq_middle[1:2], sq_final[1:2], sq_middle[:1], sq_final[:1], valid.reshape(1, -1)]
@@ -1137,6 +1135,8 @@
     table = jnp.pad(table, ((0, 0), (0, -table.shape[1] % 128)))
     own_small = ladder.scatter_small(tie(table, *sent(flow_qkv)))
     own_qkv = flow_qkv.finish(own_small)
+    own_rest = flow_rest.finish(own_small)
+    output = jnp.concatenate([tie(outputs[0], own_small), outputs[1]], 0)
 
     owned = [own_small[ends[i] : ends[i + 1]] for i in range(6)]
     totals = own_small[total : total + 6]

time: 401 us -> 398 us (level)
  Pallas kernels: 231 us -> 238 us
  waiting for transfers between devices: 57 us -> 52 us
  starting transfers between devices: 56.2 us -> 52.1 us
    ppermute x49, waiting for transfers between devices: 55.6 us -> 49 us  [flip(): lax.ppermute(value, self.axes, [(i, i ^ bits[i & CORE]) for i in range(se...]
    pallas_call x4, Pallas kernels: 48.7 us -> 54.6 us  [attn_call(): pl.pallas_call(body, grid_spec=pltpu.PrefetchScalarGridSpec(num_scalar_pr...]
    ppermute x49, starting transfers between devices: 52.9 us -> 48.7 us  [flip(): lax.ppermute(value, self.axes, [(i, i ^ bits[i & CORE]) for i in range(se...]
  transfers between devices with their start and end apart: 50 -> 50, of which waited for: 13 -> 13; matrix products, arithmetic and copies ran while one was open for 10% -> 10% of each run, Pallas kernels for 57% -> 59%
where the time goes in v6:
time: 398 us; the launch traced here: 393 us
  Pallas kernels  238 us (60%)
  starting transfers between devices  52.1 us (13%)
  waiting for transfers between devices  52 us (13%)
  other arithmetic  29.4 us (7%)
  local copies, waits for them, and re-layouts  19.3 us (5%)
    pallas_call x2, Pallas kernels, back(): pl.pallas_call(functools.partial(back_kernel, ladder.native, last, counts...  54.9 us
    pallas_call x4, Pallas kernels, attn_call(): pl.pallas_call(body, grid_spec=pltpu.PrefetchScalarGridSpec(num_scalar_pr...  54.6 us
    ppermute x49, waiting for transfers between devices, flip(): lax.ppermute(value, self.axes, [(i, i ^ bits[i & CORE]) for i in range(se...  49 us
    ppermute x49, starting transfers between devices, flip(): lax.ppermute(value, self.axes, [(i, i ^ bits[i & CORE]) for i in range(se...  48.7 us
    pallas_call x1, Pallas kernels, expand(): pl.pallas_call(functools.partial(expand_kernel, ladder.native, tile, len(...  29.1 us
    pallas_call x2, Pallas kernels, contract(): pl.pallas_call(functools.partial(contract_kernel, ladder.native, part * l...  24.6 us
    pallas_call x1, Pallas kernels, input_grad(): pl.pallas_call(functools.partial(input_grad_kernel, ladder.native, calls)...  17.8 us
    pallas_call x1, Pallas kernels, down_grad(): pl.pallas_call(functools.partial(down_grad_kernel, ladder.native, len(out...  14.8 us
  transfers between devices with their start and end apart: 50, of which 13 were waited for; matrix products, arithmetic and copies ran while one was open for 10% of the time, Pallas kernels for 59%

profile of v6, /device:TPU:0, one launch (start us, length us, event | category | flops | bytes accessed | tf_op | source)
XLA Modules:
  0.0 392.7 jit_solution(4708230082319748571)
XLA Ops:
  0.6 5.1 %collective-permute-start.2 = (bf16[32,3072]{1,0:T(8,128)(2,1)}, bf16[32,3072]{1,0:T(8,128)(2,1)S(1)}, u32[]{:S(2)}, u32[]{:S(2)}) collective-permute-start(bf16[32,3072]{1,0:T(8,128)(2,1)} %refs_0_), channel_id=1, source_target_pairs={{0,6},{1,7},{2,4},{3,5},{4,2},{5,3},{6,0},{7,1},{8,14},{9,15},{10,... | collective-permute-start | bytes 589832 | tf_op jit(solution)/shard_map/ppermute | solution.py:56
  10.5 8.2 %collective-permute-done.refs_1_ = bf16[32,3072]{1,0:T(8,128)(2,1)S(1)} collective-permute-done((bf16[32,3072]{1,0:T(8,128)(2,1)}, bf16[32,3072]{1,0:T(8,128)(2,1)S(1)}, u32[]{:S(2)}, u32[]{:S(2)}) %collective-permute-start) | collective-permute-done | bytes 196640 | tf_op jit(solution)/shard_map/ppermute | solution.py:56
  19.0 3.5 collective-permute-start.4
  24.4 1.9 collective-permute-done.3.refs_5_
  26.9 2.9 place_group.1.rest_0_.rest_4_
  31.4 1.5 collective-permute-start.6
  33.5 1.5 collective-permute-start.9
  35.0 16.1 %collective-permute-done.8.rest_1_.rest_5_ = bf16[4,32,3200]{2,1,0:T(8,128)(2,1)} collective-permute-done((bf16[4,32,3200]{2,1,0:T(8,128)(2,1)}, bf16[4,32,3200]{2,1,0:T(8,128)(2,1)}, u32[]{:S(2)}, u32[]{:S(2)}) %collective-permute-start.8) | collective-permute-done | bytes 819232 | tf_op jit(solution)/shard_map/ppermute | solution.py:56
  51.2 1.5 collective-permute-start.10
  55.1 8.7 %collective-permute-done.10.rest_3_.rest_7_ = bf16[4,32,3200]{2,1,0:T(8,128)(2,1)} collective-permute-done((bf16[4,32,3200]{2,1,0:T(8,128)(2,1)}, bf16[4,32,3200]{2,1,0:T(8,128)(2,1)}, u32[]{:S(2)}, u32[]{:S(2)}) %collective-permute-start.10) | collective-permute-done | bytes 819232 | tf_op jit(solution)/shard_map/ppermute | solution.py:56
  65.2 1.6 collective-permute-start.17
  68.3 1.5 collective-permute-start.15
  69.8 14.3 %project.1 = (bf16[1024,3072]{1,0:T(8,128)(2,1)}, bf16[1024,1024]{1,0:T(8,128)(2,1)}, f32[1,1024]{1,0:T(1,128)}, f32[1,4096]{1,0:T(1,128)}, f32[4,1024]{1,0:T(4,128)}) custom-call(s32[6]{0:T(128)} %pad_add_fusion.meta, bf16[1024,1024]{1,0:T(8,128)(2,1)} %bitcast.67, f32[1024,1]{1,0:T(8,128)} %copy.45.valid_ref, ...), custom_call_target="tpu_custom_call" | custom-call | flops 32199999488 | tf_op jit(solution)/shard_map/project/pallas_call | solution.py:569
  84.9 11.1 %attn_forward.2 = (bf16[1024,1024]{1,0:T(8,128)(2,1)S(1)}, f32[8,8,256]{2,1,0:T(8,128)S(1)}) custom-call(s32[8]{0:T(128)S(1)} %and_select_fusion.refs_0_, s32[1024,128]{1,0:T(8,128)S(1)} %broadcast_in_dim.72.refs_1_, s32[1024,128]{1,0:T(8,128)S(1)} %broadcast_in_dim.74.refs_2_, s32[8,128]{1,0:T(8,128)S(1)} %bitcast.35, ...), custom_call_target="tpu_custom_call" | custom-call | flops 24839999488 | tf_op jit(solution)/shard_map/attn_forward/pallas_call | solution.py:357
  97.0 1.5 collective-permute-start.19
  98.6 11.1 %attn_forward.3 = (bf16[1024,1024]{1,0:T(8,128)(2,1)S(1)}, f32[8,8,256]{2,1,0:T(8,128)S(1)}) custom-call(s32[8]{0:T(128)S(1)} %and_select_fusion.refs_0_, s32[1024,128]{1,0:T(8,128)S(1)} %broadcast_in_dim.72.refs_1_, s32[1024,128]{1,0:T(8,128)S(1)} %broadcast_in_dim.74.refs_2_, s32[8,128]{1,0:T(8,128)S(1)} %bitcast.36, ...), custom_call_target="tpu_custom_call", output_to_operand_aliasing={{0}: (7, {}), {1}: (8, {})} | custom-call | flops 24839999488 | tf_op jit(solution)/shard_map/attn_forward/pallas_call | solution.py:357
  109.7 5.2 %collective-permute-done.19.rest_3_.rest_11_ = bf16[4,32,5120]{2,1,0:T(8,128)(2,1)S(1)} collective-permute-done((bf16[4,32,5120]{2,1,0:T(8,128)(2,1)}, bf16[4,32,5120]{2,1,0:T(8,128)(2,1)S(1)}, u32[]{:S(2)}, u32[]{:S(2)}) %collective-permute-start.19) | collective-permute-done | bytes 1310752 | tf_op jit(solution)/shard_map/ppermute | solution.py:56
  115.7 1.5 collective-permute-start.25
  119.9 29.1 %expand.1 = (f32[1024,1024]{1,0:T(8,128)}, bf16[1024,1024]{1,0:T(8,128)(2,1)}, f32[8,1024]{1,0:T(8,128)}, bf16[1024,4096]{1,0:T(8,128)(2,1)}, bf16[1024,4096]{1,0:T(8,128)(2,1)}) custom-call(s32[6]{0:T(128)} %pad_add_fusion.meta, bf16[1024,1024]{1,0:T(8,128)(2,1)} %copy-done.7, bf16[1024,1024]{1,0:T(8,128)(2,1)} %bitcast.68, ...), custom_call_target="tpu_custom_call" | custom-call | flops 66700001280 | tf_op jit(solution)/shard_map/expand/pallas_call | solution.py:642
  150.8 14.8 %down_grad.1 = (bf16[4,4,128,1024]{3,2,1,0:T(8,128)(2,1)}, bf16[4,4,128,1024]{3,2,1,0:T(8,128)(2,1)}, f32[1,1024]{1,0:T(1,128)}) custom-call(s32[6]{0:T(128)} %pad_add_fusion.meta, bf16[1024,4096]{1,0:T(8,128)(2,1)} %get-tuple-element.187.act_ref, bf16[1024,1024]{1,0:T(8,128)(2,1)} %bitcast.64), custom_call_target="tpu_custom_call" | custom-call | flops 32199999488 | tf_op jit(solution)/shard_map/down_grad/pallas_call | solution.py:709
  166.3 2.8 collective-permute-done.31.rest_7_
  170.1 23.9 %back.2 = (bf16[4,4,32,5120]{3,2,1,0:T(8,128)(2,1)}, bf16[4,4,32,5120]{3,2,1,0:T(8,128)(2,1)}, f32[1024,1024]{1,0:T(8,128)}, f32[1,4096]{1,0:T(1,128)}) custom-call(s32[6]{0:T(128)} %pad_add_fusion.meta, bf16[1024,1024]{1,0:T(8,128)(2,1)} %bitcast.65, bf16[1024,4096]{1,0:T(8,128)(2,1)} %get-tuple-element.136.slope_ref, ...), custom_call_target="tpu_custom_call" | custom-call | flops 46000001024 | tf_op jit(solution)/shard_map/back/pallas_call | solution.py:899
  194.0 3.2 add_convert_fusion.1
  197.4 31.0 %back.3 = (bf16[4,4,32,5120]{3,2,1,0:T(8,128)(2,1)}, bf16[4,4,32,5120]{3,2,1,0:T(8,128)(2,1)}, f32[1024,1024]{1,0:T(8,128)}, bf16[1024,1024]{1,0:T(8,128)(2,1)},...) custom-call(s32[6]{0:T(128)} %pad_add_fusion.meta, ...), custom_call_target="tpu_custom_call", output_to_operand_aliasing={{0}: (24, {}), {1}: (25, {}), {6}: (26, {})} | custom-call | flops 69000003584 | tf_op jit(solution)/shard_map/back/pallas_call | solution.py:899
  228.6 3.0 fusion.1
  231.6 1.9 collective-permute-start.33
  233.5 16.0 %attn_backward.2 = (bf16[3,1024,1024]{2,1,0:T(8,128)(2,1)}, f32[8,1024]{1,0:T(8,128)S(1)}) custom-call(s32[8]{0:T(128)S(1)} %copy-done.6, s32[1024,128]{1,0:T(8,128)S(1)} %broadcast_in_dim.72.refs_1_, s32[1024,128]{1,0:T(8,128)S(1)} %broadcast_in_dim.74.refs_2_, s32[8,128]{1,0:T(8,128)S(1)} %bitcast.37, ...), custom_call_target="tpu_custom_call" | custom-call | flops 31280001024 | tf_op jit(solution)/shard_map/attn_backward/pallas_call | solution.py:357
  249.5 4.0 %spread_sums.3 = (f32[128,1024]{1,0:T(8,128)}, bf16[128,1024]{1,0:T(8,128)(2,1)}, bf16[128,1024]{1,0:T(8,128)(2,1)}, bf16[128,1024]{1,0:T(8,128)(2,1)}) custom-call(s32[6]{0:T(128)} %pad_add_fusion.meta, bf16[4,4,128,1024]{3,2,1,0:T(8,128)(2,1)} %get-tuple-element.132.refs_0_.refs_4_.refs_8_.refs_12_, ...), custom_call_target="tpu_custom_call" | custom-call | flops 6899999744 | tf_op jit(solution)/shard_map/spread_sums/pallas_call | solution.py:110
  253.5 1.5 collective-permute-start.36
  255.1 2.8 collective-permute-start.37
  257.9 5.1 %add_convert_fusion = bf16[2,4,32,5120]{3,2,1,0:T(8,128)(2,1)} fusion(bf16[4,4,32,5120]{3,2,1,0:T(8,128)(2,1)} %collective-permute-done.34.refs_1_.refs_5_.refs_9_.refs_13_, bf16[4,4,32,5120]{3,2,1,0:T(8,128)(2,1)} %get-tuple-element.155.refs_0_.refs_4_.refs_8_.refs_12_), kind=kLoop, calls=%fused_computation | loop fusion | flops 5242880 | bytes 7864320 | tf_op jit(solution)/shard_map/convert_element_type | solution.py:188
  263.1 16.4 %attn_backward.3 = (bf16[3,1024,1024]{2,1,0:T(8,128)(2,1)}, f32[8,1024]{1,0:T(8,128)S(1)}) custom-call(s32[8]{0:T(128)S(1)} %copy-done.6, s32[1024,128]{1,0:T(8,128)S(1)} %copy-done.3, s32[1024,128]{1,0:T(8,128)S(1)} %copy-done.1, s32[8,128]{1,0:T(8,128)S(1)} %bitcast.38, ...), custom_call_target="tpu_custom_call", output_to_operand_aliasing={{0}: (9, {}), {1}: (10, {})} | custom-call | flops 31280001024 | tf_op jit(solution)/shard_map/attn_backward/pallas_call | solution.py:357
  280.4 12.4 %qkv_grad.1 = (bf16[4,4,32,3072]{3,2,1,0:T(8,128)(2,1)}, bf16[4,4,32,3072]{3,2,1,0:T(8,128)(2,1)}) custom-call(s32[6]{0:T(128)} %pad_add_fusion.meta, bf16[1024,1024]{1,0:T(8,128)(2,1)} %get-tuple-element.128.left_ref, bf16[3,1024,1024]{2,1,0:T(8,128)(2,1)} %get-tuple-element.165.right_ref.rest_0_), custom_call_target="tpu_custom_call" | custom-call | flops 18400000000 | tf_op jit(solution)/shard_map/qkv_grad/pallas_call | solution.py:747
  296.7 2.7 fusion
  300.0 12.4 %contract.2 = (bf16[512,1024]{1,0:T(8,128)(2,1)}, f32[8,1024]{1,0:T(8,128)}) custom-call(s32[6]{0:T(128)} %pad_add_fusion.meta, bf16[1024,4096]{1,0:T(8,128)(2,1)} %get-tuple-element.187.act_ref, f32[4,1024]{1,0:T(4,128)} %get-tuple-element.125.lines_ref.rest_3_, f32[1024,1]{1,0:T(8,128)} %copy.45.valid_ref, f32[1024,1024]{1,0:T(8,128)} %get-tuple-element.138.middle_ref, ...), custom_call_target="tpu_custom_call" | custom-call | flops 18400000000 | tf_op jit(solution)/shard_map/contract/pallas_call | solution.py:955
  312.4 2.2 add_convert_fusion.2
  317.1 4.5 %spread_sums.4 = (f32[32,5120]{1,0:T(8,128)}, bf16[32,5120]{1,0:T(8,128)(2,1)}, bf16[32,5120]{1,0:T(8,128)(2,1)}, bf16[32,5120]{1,0:T(8,128)(2,1)}) custom-call(s32[6]{0:T(128)} %pad_add_fusion.meta, bf16[4,4,32,5120]{3,2,1,0:T(8,128)(2,1)} %get-tuple-element.155.refs_0_.refs_4_.refs_8_.refs_12_, ...), custom_call_target="tpu_custom_call" | custom-call | flops 6899999744 | tf_op jit(solution)/shard_map/spread_sums/pallas_call | solution.py:110
  322.8 3.3 collective-permute-start.45
  326.0 17.8 %input_grad.1 = (bf16[1024,1024]{1,0:T(8,128)(2,1)}, f32[8,1024]{1,0:T(8,128)}) custom-call(s32[6]{0:T(128)} %pad_add_fusion.meta, bf16[3,1024,1024]{2,1,0:T(8,128)(2,1)} %get-tuple-element.165.right_ref.rest_0_, bf16[1024,1024]{1,0:T(8,128)(2,1)} %bitcast.69, f32[1024,1024]{1,0:T(8,128)} %get-tuple-element.179.rest_2_, ...), custom_call_target="tpu_custom_call" | custom-call | flops 41400000512 | tf_op jit(solution)/shard_map/input_grad/pallas_call | solution.py:1014
  345.9 2.6 fusion.2
  349.2 12.3 %contract.3 = (bf16[512,1024]{1,0:T(8,128)(2,1)}, f32[8,1024]{1,0:T(8,128)}) custom-call(s32[6]{0:T(128)} %pad_add_fusion.meta, bf16[1024,4096]{1,0:T(8,128)(2,1)} %get-tuple-element.187.act_ref, f32[4,1024]{1,0:T(4,128)} %get-tuple-element.125.lines_ref.rest_3_, f32[1024,1]{1,0:T(8,128)} %copy.45.valid_ref, f32[1024,1024]{1,0:T(8,128)} %get-tuple-element.138.middle_ref, ...), custom_call_target="tpu_custom_call" | custom-call | flops 18400000000 | tf_op jit(solution)/shard_map/contract/pallas_call | solution.py:955
  363.5 3.8 spread_sums.5
  368.0 3.3 all-to-all-start
  371.3 1.8 collective-permute-start.46
  373.2 2.4 collective-permute-start.47
  375.8 3.1 all-to-all-done
  386.6 4.0 %collective-permute-done.47 = bf16[32,3072]{1,0:T(8,128)(2,1)} collective-permute-done((bf16[32,3072]{1,0:T(8,128)(2,1)}, bf16[32,3072]{1,0:T(8,128)(2,1)}, u32[]{:S(2)}, u32[]{:S(2)}) %collective-permute-start.47) | collective-permute-done | bytes 196640 | tf_op jit(solution)/shard_map/ppermute | solution.py:56
  390.6 1.9 convert_add_fusion.2
  (235 shorter events, 45.7 us)
Async XLA Ops:
  0.6 23.1 %collective-permute-start.2 = (bf16[32,3072]{1,0:T(8,128)(2,1)}, bf16[32,3072]{1,0:T(8,128)(2,1)S(1)}, u32[]{:S(2)}, u32[]{:S(2)}) collective-permute-start(bf16[32,3072]{1,0:T(8,128)(2,1)} %refs_0_), channel_id=1, source_target_pairs={{0,6},{1,7},{2,4},{3,5},{4,2},{5,3},{6,0},{7,1},{8,14},{9,15},{10,... | collective-permute-start | bytes 589832 | tf_op jit(solution)/shard_map/ppermute | solution.py:56
  5.8 18.0 %collective-permute-start.1 = (bf16[32,3072]{1,0:T(8,128)(2,1)}, bf16[32,3072]{1,0:T(8,128)(2,1)S(1)}, u32[]{:S(2)}, u32[]{:S(2)}) collective-permute-start(bf16[32,3072]{1,0:T(8,128)(2,1)} %refs_0_), channel_id=1, source_target_pairs={{0,4},{1,5},{2,6},{3,7},{4,0},{5,1},{6,2},{7,3},{8,12},{9,13},{10,... | collective-permute-start | bytes 589832 | tf_op jit(solution)/shard_map/ppermute | solution.py:56
  5.8 13.0 %collective-permute-start = (bf16[32,3072]{1,0:T(8,128)(2,1)}, bf16[32,3072]{1,0:T(8,128)(2,1)S(1)}, u32[]{:S(2)}, u32[]{:S(2)}) collective-permute-start(bf16[32,3072]{1,0:T(8,128)(2,1)} %refs_0_), channel_id=1, source_target_pairs={{0,2},{1,3},{2,0},{3,1},{4,6},{5,7},{6,4},{7,5},{8,10},{9,11},{10,... | collective-permute-start | bytes 589832 | tf_op jit(solution)/shard_map/ppermute | solution.py:56
  18.8 5.5 %collective-permute-start.5 = (bf16[32,128]{1,0:T(8,128)(2,1)S(1)}, bf16[32,128]{1,0:T(8,128)(2,1)S(1)}, u32[]{:S(2)}, u32[]{:S(2)}) collective-permute-start(bf16[32,128]{1,0:T(8,128)(2,1)S(1)} %select_select_fusion.refs_4_), channel_id=1, source_target_pairs={{0,6},{1,7},{2,4},{3,5},{4,2},{5,3},{6,0},{7,1},{8,14},{9,15},{10,... | collective-permute-start | bytes 24584 | tf_op jit(solution)/shard_map/ppermute | solution.py:56
  19.0 5.3 %collective-permute-start.4 = (bf16[32,128]{1,0:T(8,128)(2,1)S(1)}, bf16[32,128]{1,0:T(8,128)(2,1)S(1)}, u32[]{:S(2)}, u32[]{:S(2)}) collective-permute-start(bf16[32,128]{1,0:T(8,128)(2,1)S(1)} %select_select_fusion.refs_4_), channel_id=1, source_target_pairs={{0,4},{1,5},{2,6},{3,7},{4,0},{5,1},{6,2},{7,3},{8,12},{9,13},{10,... | collective-permute-start | bytes 24584 | tf_op jit(solution)/shard_map/ppermute | solution.py:56
  22.6 3.7 collective-permute-start.3
  29.8 21.4 %collective-permute-start.8 = (bf16[4,32,3200]{2,1,0:T(8,128)(2,1)}, bf16[4,32,3200]{2,1,0:T(8,128)(2,1)}, u32[]{:S(2)}, u32[]{:S(2)}) collective-permute-start(bf16[4,32,3200]{2,1,0:T(8,128)(2,1)} %place_group.1.rest_0_.rest_4_), channel_id=1, source_target_pairs={{0,8},{1,17},{2,10},{3,19},{4,12},{5,21},{6,14},{7,23},{8,0},{9,25... | collective-permute-start | bytes 2457608 | tf_op jit(solution)/shard_map/ppermute | solution.py:56
  31.4 21.5 %collective-permute-start.6 = (bf16[32,5120]{1,0:T(8,128)(2,1)S(1)}, bf16[32,5120]{1,0:T(8,128)(2,1)S(1)}, u32[]{:S(2)}, u32[]{:S(2)}) collective-permute-start(bf16[32,5120]{1,0:T(8,128)(2,1)S(1)} %pad_maximum_fusion), channel_id=1, source_target_pairs={{0,4},{1,5},{2,6},{3,7},{4,0},{5,1},{6,2},{7,3},{8,12},{9,13},{10,... | collective-permute-start | bytes 983048 | tf_op jit(solution)/shard_map/ppermute | solution.py:56
  33.5 21.6 %collective-permute-start.9 = (bf16[4,32,3200]{2,1,0:T(8,128)(2,1)}, bf16[4,32,3200]{2,1,0:T(8,128)(2,1)}, u32[]{:S(2)}, u32[]{:S(2)}) collective-permute-start(bf16[4,32,3200]{2,1,0:T(8,128)(2,1)} %place_group.1.rest_0_.rest_4_), channel_id=1, source_target_pairs={{0,16},{1,9},{2,18},{3,11},{4,20},{5,13},{6,22},{7,15},{8,24},{9,1... | collective-permute-start | bytes 2457608 | tf_op jit(solution)/shard_map/ppermute | solution.py:56
  51.2 12.7 %collective-permute-start.10 = (bf16[4,32,3200]{2,1,0:T(8,128)(2,1)}, bf16[4,32,3200]{2,1,0:T(8,128)(2,1)}, u32[]{:S(2)}, u32[]{:S(2)}) collective-permute-start(bf16[4,32,3200]{2,1,0:T(8,128)(2,1)} %collective-permute-done.8.rest_1_.rest_5_), channel_id=1, source_target_pairs={{0,16},{1,9},{2,18},{3,11},{4,20},{5,13},{6,22},{7,15},{8,24},{9,1... | collective-permute-start | bytes 2457608 | tf_op jit(solution)/shard_map/ppermute | solution.py:56
  53.0 10.9 %collective-permute-start.7 = (bf16[2,32,5120]{2,1,0:T(8,128)(2,1)S(1)}, bf16[2,32,5120]{2,1,0:T(8,128)(2,1)S(1)}, u32[]{:S(2)}, u32[]{:S(2)}) collective-permute-start(bf16[2,32,5120]{2,1,0:T(8,128)(2,1)S(1)} %maximum_select_fusion.2), channel_id=1, source_target_pairs={{0,2},{1,3},{2,0},{3,1},{4,6},{5,7},{6,4},{7,5},{8,10},{9,11},{10,... | collective-permute-start | bytes 1966088 | tf_op jit(solution)/shard_map/ppermute | solution.py:56
  54.6 10.6 %collective-permute-start.11 = (bf16[4,32,3200]{2,1,0:T(8,128)(2,1)}, bf16[4,32,3200]{2,1,0:T(8,128)(2,1)S(1)}, u32[]{:S(2)}, u32[]{:S(2)}) collective-permute-start(bf16[4,32,3200]{2,1,0:T(8,128)(2,1)} %place_group.1.rest_0_.rest_4_), channel_id=1, source_target_pairs={{0,1},{1,0},{2,3},{3,2},{4,5},{5,4},{6,7},{7,6},{8,9},{9,8},{10,11... | collective-permute-start | bytes 2457608 | tf_op jit(solution)/shard_map/ppermute | solution.py:56
  54.6 13.7 %collective-permute-start.13 = (bf16[4,32,3200]{2,1,0:T(8,128)(2,1)}, bf16[4,32,3200]{2,1,0:T(8,128)(2,1)}, u32[]{:S(2)}, u32[]{:S(2)}) collective-permute-start(bf16[4,32,3200]{2,1,0:T(8,128)(2,1)} %collective-permute-done.8.rest_1_.rest_5_), channel_id=1, source_target_pairs={{0,1},{1,0},{2,3},{3,2},{4,5},{5,4},{6,7},{7,6},{8,9},{9,8},{10,11... | collective-permute-start | bytes 2457608 | tf_op jit(solution)/shard_map/ppermute | solution.py:56
  55.1 11.7 %collective-permute-start.12 = (bf16[4,32,3200]{2,1,0:T(8,128)(2,1)}, bf16[4,32,3200]{2,1,0:T(8,128)(2,1)S(1)}, u32[]{:S(2)}, u32[]{:S(2)}) collective-permute-start(bf16[4,32,3200]{2,1,0:T(8,128)(2,1)} %collective-permute-done.9.rest_2_.rest_6_), channel_id=1, source_target_pairs={{0,1},{1,0},{2,3},{3,2},{4,5},{5,4},{6,7},{7,6},{8,9},{9,8},{10,11... | collective-permute-start | bytes 2457608 | tf_op jit(solution)/shard_map/ppermute | solution.py:56
  63.8 6.0 %collective-permute-start.14 = (bf16[4,32,3200]{2,1,0:T(8,128)(2,1)}, bf16[4,32,3200]{2,1,0:T(8,128)(2,1)}, u32[]{:S(2)}, u32[]{:S(2)}) collective-permute-start(bf16[4,32,3200]{2,1,0:T(8,128)(2,1)} %collective-permute-done.10.rest_3_.rest_7_), channel_id=1, source_target_pairs={{0,1},{1,0},{2,3},{3,2},{4,5},{5,4},{6,7},{7,6},{8,9},{9,8},{10,11... | collective-permute-start | bytes 2457608 | tf_op jit(solution)/shard_map/ppermute | solution.py:56
  64.2 51.5 %collective-permute-start.20 = (bf16[4,32,5120]{2,1,0:T(8,128)(2,1)S(1)}, bf16[4,32,5120]{2,1,0:T(8,128)(2,1)S(1)}, u32[]{:S(2)}, u32[]{:S(2)}) collective-permute-start(bf16[4,32,5120]{2,1,0:T(8,128)(2,1)S(1)} %bitcast.41), channel_id=1, source_target_pairs={{0,1},{1,0},{2,3},{3,2},{4,5},{5,4},{6,7},{7,6},{8,9},{9,8},{10,11... | collective-permute-start | bytes 3932168 | tf_op jit(solution)/shard_map/ppermute | solution.py:56
  65.2 33.3 %collective-permute-start.17 = (bf16[4,32,5120]{2,1,0:T(8,128)(2,1)S(1)}, bf16[4,32,5120]{2,1,0:T(8,128)(2,1)}, u32[]{:S(2)}, u32[]{:S(2)}) collective-permute-start(bf16[4,32,5120]{2,1,0:T(8,128)(2,1)S(1)} %bitcast.42), channel_id=1, source_target_pairs={{0,16},{1,9},{2,18},{3,11},{4,20},{5,13},{6,22},{7,15},{8,24},{9,1... | collective-permute-start | bytes 3932168 | tf_op jit(solution)/shard_map/ppermute | solution.py:56
  66.8 29.3 %collective-permute-start.16 = (bf16[4,32,5120]{2,1,0:T(8,128)(2,1)S(1)}, bf16[4,32,5120]{2,1,0:T(8,128)(2,1)}, u32[]{:S(2)}, u32[]{:S(2)}) collective-permute-start(bf16[4,32,5120]{2,1,0:T(8,128)(2,1)S(1)} %bitcast.43), channel_id=1, source_target_pairs={{0,8},{1,17},{2,10},{3,19},{4,12},{5,21},{6,14},{7,23},{8,0},{9,25... | collective-permute-start | bytes 3932168 | tf_op jit(solution)/shard_map/ppermute | solution.py:56
  68.3 15.8 %collective-permute-start.15 = (bf16[128,1024]{1,0:T(8,128)(2,1)S(1)}, bf16[128,1024]{1,0:T(8,128)(2,1)S(1)}, u32[]{:S(2)}, u32[]{:S(2)}) collective-permute-start(bf16[128,1024]{1,0:T(8,128)(2,1)S(1)} %copy-done.19), channel_id=1, source_target_pairs={{0,4},{1,5},{2,6},{3,7},{4,0},{5,1},{6,2},{7,3},{8,12},{9,13},{10,... | collective-permute-start | bytes 786440 | tf_op jit(solution)/shard_map/ppermute | solution.py:56
  84.2 14.3 %collective-permute-start.18 = (bf16[2,128,1024]{2,1,0:T(8,128)(2,1)S(1)}, bf16[2,128,1024]{2,1,0:T(8,128)(2,1)S(1)}, u32[]{:S(2)}, u32[]{:S(2)}) collective-permute-start(bf16[2,128,1024]{2,1,0:T(8,128)(2,1)S(1)} %maximum_select_fusion.4), channel_id=1, source_target_pairs={{0,2},{1,3},{2,0},{3,1},{4,6},{5,7},{6,4},{7,5},{8,10},{9,11},{10,... | collective-permute-start | bytes 1572872 | tf_op jit(solution)/shard_map/ppermute | solution.py:56
  96.1 21.2 %collective-permute-start.22 = (bf16[4,32,5120]{2,1,0:T(8,128)(2,1)}, bf16[4,32,5120]{2,1,0:T(8,128)(2,1)}, u32[]{:S(2)}, u32[]{:S(2)}) collective-permute-start(bf16[4,32,5120]{2,1,0:T(8,128)(2,1)} %collective-permute-done.16.rest_1_.rest_9_), channel_id=1, source_target_pairs={{0,1},{1,0},{2,3},{3,2},{4,5},{5,4},{6,7},{7,6},{8,9},{9,8},{10,11... | collective-permute-start | bytes 3932168 | tf_op jit(solution)/shard_map/ppermute | solution.py:56
  97.0 17.8 %collective-permute-start.19 = (bf16[4,32,5120]{2,1,0:T(8,128)(2,1)}, bf16[4,32,5120]{2,1,0:T(8,128)(2,1)S(1)}, u32[]{:S(2)}, u32[]{:S(2)}) collective-permute-start(bf16[4,32,5120]{2,1,0:T(8,128)(2,1)} %collective-permute-done.16.rest_1_.rest_9_), channel_id=1, source_target_pairs={{0,16},{1,9},{2,18},{3,11},{4,20},{5,13},{6,22},{7,15},{8,24},{9,1... | collective-permute-start | bytes 3932168 | tf_op jit(solution)/shard_map/ppermute | solution.py:56
  98.5 19.2 %collective-permute-start.21 = (bf16[4,32,5120]{2,1,0:T(8,128)(2,1)}, bf16[4,32,5120]{2,1,0:T(8,128)(2,1)S(1)}, u32[]{:S(2)}, u32[]{:S(2)}) collective-permute-start(bf16[4,32,5120]{2,1,0:T(8,128)(2,1)} %collective-permute-done.17.rest_2_.rest_10_), channel_id=1, source_target_pairs={{0,1},{1,0},{2,3},{3,2},{4,5},{5,4},{6,7},{7,6},{8,9},{9,8},{10,11... | collective-permute-start | bytes 3932168 | tf_op jit(solution)/shard_map/ppermute | solution.py:56
  115.1 51.1 %collective-permute-start.28 = (bf16[4,128,1024]{2,1,0:T(8,128)(2,1)S(1)}, bf16[4,128,1024]{2,1,0:T(8,128)(2,1)S(1)}, u32[]{:S(2)}, u32[]{:S(2)}) collective-permute-start(bf16[4,128,1024]{2,1,0:T(8,128)(2,1)S(1)} %bitcast.49), channel_id=1, source_target_pairs={{0,1},{1,0},{2,3},{3,2},{4,5},{5,4},{6,7},{7,6},{8,9},{9,8},{10,11... | collective-permute-start | bytes 3145736 | tf_op jit(solution)/shard_map/ppermute | solution.py:56
  115.7 34.1 %collective-permute-start.25 = (bf16[4,128,1024]{2,1,0:T(8,128)(2,1)S(1)}, bf16[4,128,1024]{2,1,0:T(8,128)(2,1)S(1)}, u32[]{:S(2)}, u32[]{:S(2)}) collective-permute-start(bf16[4,128,1024]{2,1,0:T(8,128)(2,1)S(1)} %bitcast.50), channel_id=1, source_target_pairs={{0,16},{1,9},{2,18},{3,11},{4,20},{5,13},{6,22},{7,15},{8,24},{9,1... | collective-permute-start | bytes 3145736 | tf_op jit(solution)/shard_map/ppermute | solution.py:56
  117.2 31.8 %collective-permute-start.24 = (bf16[4,128,1024]{2,1,0:T(8,128)(2,1)S(1)}, bf16[4,128,1024]{2,1,0:T(8,128)(2,1)}, u32[]{:S(2)}, u32[]{:S(2)}) collective-permute-start(bf16[4,128,1024]{2,1,0:T(8,128)(2,1)S(1)} %bitcast.51), channel_id=1, source_target_pairs={{0,8},{1,17},{2,10},{3,19},{4,12},{5,21},{6,14},{7,23},{8,0},{9,25... | collective-permute-start | bytes 3145736 | tf_op jit(solution)/shard_map/ppermute | solution.py:56
  149.1 17.2 %collective-permute-start.30 = (bf16[4,128,1024]{2,1,0:T(8,128)(2,1)}, bf16[4,128,1024]{2,1,0:T(8,128)(2,1)S(1)}, u32[]{:S(2)}, u32[]{:S(2)}) collective-permute-start(bf16[4,128,1024]{2,1,0:T(8,128)(2,1)} %collective-permute-done.24.rest_1_), channel_id=1, source_target_pairs={{0,1},{1,0},{2,3},{3,2},{4,5},{5,4},{6,7},{7,6},{8,9},{9,8},{10,11... | collective-permute-start | bytes 3145736 | tf_op jit(solution)/shard_map/ppermute | solution.py:56
  149.1 16.5 %collective-permute-start.27 = (bf16[4,128,1024]{2,1,0:T(8,128)(2,1)}, bf16[4,128,1024]{2,1,0:T(8,128)(2,1)S(1)}, u32[]{:S(2)}, u32[]{:S(2)}) collective-permute-start(bf16[4,128,1024]{2,1,0:T(8,128)(2,1)} %collective-permute-done.24.rest_1_), channel_id=1, source_target_pairs={{0,16},{1,9},{2,18},{3,11},{4,20},{5,13},{6,22},{7,15},{8,24},{9,1... | collective-permute-start | bytes 3145736 | tf_op jit(solution)/shard_map/ppermute | solution.py:56
  149.8 16.5 %collective-permute-start.29 = (bf16[4,128,1024]{2,1,0:T(8,128)(2,1)S(1)}, bf16[4,128,1024]{2,1,0:T(8,128)(2,1)S(1)}, u32[]{:S(2)}, u32[]{:S(2)}) collective-permute-start(bf16[4,128,1024]{2,1,0:T(8,128)(2,1)S(1)} %collective-permute-done.25.rest_2_), channel_id=1, source_target_pairs={{0,1},{1,0},{2,3},{3,2},{4,5},{5,4},{6,7},{7,6},{8,9},{9,8},{10,11... | collective-permute-start | bytes 3145736 | tf_op jit(solution)/shard_map/ppermute | solution.py:56
  165.8 28.2 %collective-permute-start.26 = (bf16[4,4,128,1024]{3,2,1,0:T(8,128)(2,1)}, bf16[4,4,128,1024]{3,2,1,0:T(8,128)(2,1)}, u32[]{:S(2)}, u32[]{:S(2)}) collective-permute-start(bf16[4,4,128,1024]{3,2,1,0:T(8,128)(2,1)} %get-tuple-element.133), channel_id=1, source_target_pairs={{0,1},{1,0},{2,3},{3,2},{4,5},{5,4},{6,7},{7,6},{8,9},{9,8},{10,11... | collective-permute-start | bytes 12582920 | tf_op jit(solution)/shard_map/ppermute | solution.py:56
  197.2 31.3 %collective-permute-start.32 = (bf16[2,4,128,1024]{3,2,1,0:T(8,128)(2,1)S(1)}, bf16[2,4,128,1024]{3,2,1,0:T(8,128)(2,1)S(1)}, u32[]{:S(2)}, u32[]{:S(2)}) collective-permute-start(bf16[2,4,128,1024]{3,2,1,0:T(8,128)(2,1)S(1)} %add_convert_fusion.1), channel_id=1, source_target_pairs={{0,16},{1,9},{2,18},{3,11},{4,20},{5,13},{6,22},{7,15},{8,24},{9,1... | collective-permute-start | bytes 6291464 | tf_op jit(solution)/shard_map/ppermute | solution.py:56
  228.4 29.5 %collective-permute-start.34 = (bf16[4,4,32,5120]{3,2,1,0:T(8,128)(2,1)}, bf16[4,4,32,5120]{3,2,1,0:T(8,128)(2,1)}, u32[]{:S(2)}, u32[]{:S(2)}) collective-permute-start(bf16[4,4,32,5120]{3,2,1,0:T(8,128)(2,1)} %get-tuple-element.156), channel_id=1, source_target_pairs={{0,1},{1,0},{2,3},{3,2},{4,5},{5,4},{6,7},{7,6},{8,9},{9,8},{10,11... | collective-permute-start | bytes 15728648 | tf_op jit(solution)/shard_map/ppermute | solution.py:56
  231.6 18.0 %collective-permute-start.33 = (bf16[4,128,1024]{2,1,0:T(8,128)(2,1)S(1)}, bf16[4,128,1024]{2,1,0:T(8,128)(2,1)}, u32[]{:S(2)}, u32[]{:S(2)}) collective-permute-start(bf16[4,128,1024]{2,1,0:T(8,128)(2,1)S(1)} %fusion.1), channel_id=1, source_target_pairs={{0,8},{1,17},{2,10},{3,19},{4,12},{5,21},{6,14},{7,23},{8,0},{9,25... | collective-permute-start | bytes 3145736 | tf_op jit(solution)/shard_map/ppermute | solution.py:56
  253.5 26.0 %collective-permute-start.35 = (bf16[128,1024]{1,0:T(8,128)(2,1)}, bf16[128,1024]{1,0:T(8,128)(2,1)S(1)}, u32[]{:S(2)}, u32[]{:S(2)}) collective-permute-start(bf16[128,1024]{1,0:T(8,128)(2,1)} %get-tuple-element.152), channel_id=1, source_target_pairs={{0,2},{1,3},{2,0},{3,1},{4,6},{5,7},{6,4},{7,5},{8,10},{9,11},{10,... | collective-permute-start | bytes 786440 | tf_op jit(solution)/shard_map/ppermute | solution.py:56
  253.5 26.0 %collective-permute-start.36 = (bf16[128,1024]{1,0:T(8,128)(2,1)}, bf16[128,1024]{1,0:T(8,128)(2,1)S(1)}, u32[]{:S(2)}, u32[]{:S(2)}) collective-permute-start(bf16[128,1024]{1,0:T(8,128)(2,1)} %get-tuple-element.153), channel_id=1, source_target_pairs={{0,4},{1,5},{2,6},{3,7},{4,0},{5,1},{6,2},{7,3},{8,12},{9,13},{10,... | collective-permute-start | bytes 786440 | tf_op jit(solution)/shard_map/ppermute | solution.py:56
  255.1 24.4 %collective-permute-start.37 = (bf16[128,1024]{1,0:T(8,128)(2,1)}, bf16[128,1024]{1,0:T(8,128)(2,1)S(1)}, u32[]{:S(2)}, u32[]{:S(2)}) collective-permute-start(bf16[128,1024]{1,0:T(8,128)(2,1)} %get-tuple-element.154), channel_id=1, source_target_pairs={{0,6},{1,7},{2,4},{3,5},{4,2},{5,3},{6,0},{7,1},{8,14},{9,15},{10,... | collective-permute-start | bytes 786440 | tf_op jit(solution)/shard_map/ppermute | solution.py:56
  263.0 33.6 %collective-permute-start.38 = (bf16[2,4,32,5120]{3,2,1,0:T(8,128)(2,1)}, bf16[2,4,32,5120]{3,2,1,0:T(8,128)(2,1)}, u32[]{:S(2)}, u32[]{:S(2)}) collective-permute-start(bf16[2,4,32,5120]{3,2,1,0:T(8,128)(2,1)} %add_convert_fusion), channel_id=1, source_target_pairs={{0,16},{1,9},{2,18},{3,11},{4,20},{5,13},{6,22},{7,15},{8,24},{9,1... | collective-permute-start | bytes 7864328 | tf_op jit(solution)/shard_map/ppermute | solution.py:56
  292.8 19.6 %collective-permute-start.40 = (bf16[4,4,32,3072]{3,2,1,0:T(8,128)(2,1)}, bf16[4,4,32,3072]{3,2,1,0:T(8,128)(2,1)S(1)}, u32[]{:S(2)}, u32[]{:S(2)}) collective-permute-start(bf16[4,4,32,3072]{3,2,1,0:T(8,128)(2,1)} %get-tuple-element.167), channel_id=1, source_target_pairs={{0,1},{1,0},{2,3},{3,2},{4,5},{5,4},{6,7},{7,6},{8,9},{9,8},{10,11... | collective-permute-start | bytes 9437192 | tf_op jit(solution)/shard_map/ppermute | solution.py:56
  299.4 17.8 %collective-permute-start.39 = (bf16[4,32,5120]{2,1,0:T(8,128)(2,1)S(1)}, bf16[4,32,5120]{2,1,0:T(8,128)(2,1)}, u32[]{:S(2)}, u32[]{:S(2)}) collective-permute-start(bf16[4,32,5120]{2,1,0:T(8,128)(2,1)S(1)} %fusion), channel_id=1, source_target_pairs={{0,8},{1,17},{2,10},{3,19},{4,12},{5,21},{6,14},{7,23},{8,0},{9,25... | collective-permute-start | bytes 3932168 | tf_op jit(solution)/shard_map/ppermute | solution.py:56
  314.6 31.4 %collective-permute-start.41 = (bf16[2,4,32,3072]{3,2,1,0:T(8,128)(2,1)}, bf16[2,4,32,3072]{3,2,1,0:T(8,128)(2,1)}, u32[]{:S(2)}, u32[]{:S(2)}) collective-permute-start(bf16[2,4,32,3072]{3,2,1,0:T(8,128)(2,1)} %add_convert_fusion.2), channel_id=1, source_target_pairs={{0,16},{1,9},{2,18},{3,11},{4,20},{5,13},{6,22},{7,15},{8,24},{9,1... | collective-permute-start | bytes 4718600 | tf_op jit(solution)/shard_map/ppermute | solution.py:56
  321.6 41.0 %collective-permute-start.43 = (bf16[32,5120]{1,0:T(8,128)(2,1)}, bf16[32,5120]{1,0:T(8,128)(2,1)S(1)}, u32[]{:S(2)}, u32[]{:S(2)}) collective-permute-start(bf16[32,5120]{1,0:T(8,128)(2,1)} %get-tuple-element.174), channel_id=1, source_target_pairs={{0,2},{1,3},{2,0},{3,1},{4,6},{5,7},{6,4},{7,5},{8,10},{9,11},{10,... | collective-permute-start | bytes 983048 | tf_op jit(solution)/shard_map/ppermute | solution.py:56
  322.8 39.8 %collective-permute-start.44 = (bf16[32,5120]{1,0:T(8,128)(2,1)}, bf16[32,5120]{1,0:T(8,128)(2,1)}, u32[]{:S(2)}, u32[]{:S(2)}) collective-permute-start(bf16[32,5120]{1,0:T(8,128)(2,1)} %get-tuple-element.175), channel_id=1, source_target_pairs={{0,4},{1,5},{2,6},{3,7},{4,0},{5,1},{6,2},{7,3},{8,12},{9,13},{10,... | collective-permute-start | bytes 983048 | tf_op jit(solution)/shard_map/ppermute | solution.py:56
  322.8 39.9 %collective-permute-start.45 = (bf16[32,5120]{1,0:T(8,128)(2,1)}, bf16[32,5120]{1,0:T(8,128)(2,1)}, u32[]{:S(2)}, u32[]{:S(2)}) collective-permute-start(bf16[32,5120]{1,0:T(8,128)(2,1)} %get-tuple-element.176), channel_id=1, source_target_pairs={{0,6},{1,7},{2,4},{3,5},{4,2},{5,3},{6,0},{7,1},{8,14},{9,15},{10,... | collective-permute-start | bytes 983048 | tf_op jit(solution)/shard_map/ppermute | solution.py:56
  348.6 14.0 %collective-permute-start.42 = (bf16[4,32,3072]{2,1,0:T(8,128)(2,1)}, bf16[4,32,3072]{2,1,0:T(8,128)(2,1)S(1)}, u32[]{:S(2)}, u32[]{:S(2)}) collective-permute-start(bf16[4,32,3072]{2,1,0:T(8,128)(2,1)} %fusion.2), channel_id=1, source_target_pairs={{0,8},{1,17},{2,10},{3,19},{4,12},{5,21},{6,14},{7,23},{8,0},{9,25... | collective-permute-start | bytes 2359304 | tf_op jit(solution)/shard_map/ppermute | solution.py:56
  368.0 10.9 %all-to-all-start = ((f32[32,1,384]{2,1,0:T(1,128)}), f32[32,1,384]{2,1,0:T(1,128)S(1)}, u32[]{:S(2)}, u32[]{:S(2)}) async-start(f32[32,1,384]{2,1,0:T(1,128)} %all_to_all.6), calls=%async_computation | async-start | bytes 98304 | tf_op jit(solution)/shard_map/all_to_all | solution.py:65
  371.3 15.3 %collective-permute-start.46 = (bf16[32,3072]{1,0:T(8,128)(2,1)}, bf16[32,3072]{1,0:T(8,128)(2,1)S(1)}, u32[]{:S(2)}, u32[]{:S(2)}) collective-permute-start(bf16[32,3072]{1,0:T(8,128)(2,1)} %get-tuple-element.191), channel_id=1, source_target_pairs={{0,2},{1,3},{2,0},{3,1},{4,6},{5,7},{6,4},{7,5},{8,10},{9,11},{10,... | collective-permute-start | bytes 589832 | tf_op jit(solution)/shard_map/ppermute | solution.py:56
  373.2 17.4 %collective-permute-start.47 = (bf16[32,3072]{1,0:T(8,128)(2,1)}, bf16[32,3072]{1,0:T(8,128)(2,1)}, u32[]{:S(2)}, u32[]{:S(2)}) collective-permute-start(bf16[32,3072]{1,0:T(8,128)(2,1)} %get-tuple-element.192), channel_id=1, source_target_pairs={{0,4},{1,5},{2,6},{3,7},{4,0},{5,1},{6,2},{7,3},{8,12},{9,13},{10,... | collective-permute-start | bytes 589832 | tf_op jit(solution)/shard_map/ppermute | solution.py:56
  375.6 15.0 %collective-permute-start.48 = (bf16[32,3072]{1,0:T(8,128)(2,1)}, bf16[32,3072]{1,0:T(8,128)(2,1)}, u32[]{:S(2)}, u32[]{:S(2)}) collective-permute-start(bf16[32,3072]{1,0:T(8,128)(2,1)} %get-tuple-element.193), channel_id=1, source_target_pairs={{0,6},{1,7},{2,4},{3,5},{4,2},{5,3},{6,0},{7,1},{8,14},{9,15},{10,... | collective-permute-start | bytes 589832 | tf_op jit(solution)/shard_map/ppermute | solution.py:56
  (54 other events, 938.7 us)

commit v7 on v6

--- a/solution.py
+++ b/solution.py
@@ -1133,7 +1133,7 @@
     small_grads = [sum_qv[:2], sum_middle[1:2], sum_in[:1], sum_middle[:1], sum_up, sum_down]
     table = jnp.concatenate([g.reshape(count, -1) for g in small_grads] + [jnp.broadcast_to(members, (count, 6))], 1)
     table = jnp.pad(table, ((0, 0), (0, -table.shape[1] % 128)))
-    own_small = ladder.scatter_small(tie(table, *sent(flow_qkv)))
+    own_small = ladder.scatter_small(tie(table, *sent(flow_qkv), *([] if ladder.native else flow_qkv.last[2:])))
     own_qkv = flow_qkv.finish(own_small)
     own_rest = flow_rest.finish(own_small)
     output = jnp.concatenate([tie(outputs[0], own_small), outputs[1]], 0)

time: 398 us -> 400 us (level)
  starting transfers between devices: 52.1 us -> 59.8 us
  Pallas kernels: 238 us -> 233 us
    ppermute x49, starting transfers between devices: 48.7 us -> 55.1 us  [flip(): lax.ppermute(value, self.axes, [(i, i ^ bits[i & CORE]) for i in range(se...]
    pallas_call x4, Pallas kernels: 54.6 us -> 49.9 us  [attn_call(): pl.pallas_call(body, grid_spec=pltpu.PrefetchScalarGridSpec(num_scalar_pr...]
  transfers between devices with their start and end apart: 50 -> 50, of which waited for: 13 -> 13; matrix products, arithmetic and copies ran while one was open for 10% -> 9% of each run, Pallas kernels for 59% -> 57%
where the time goes in v7:
time: 400 us; the launch traced here: 396 us
  Pallas kernels  233 us (58%)
  starting transfers between devices  59.8 us (15%)
  waiting for transfers between devices  53.6 us (13%)
  other arithmetic  28.4 us (7%)
  local copies, waits for them, and re-layouts  19.3 us (5%)
    ppermute x49, starting transfers between devices, flip(): lax.ppermute(value, self.axes, [(i, i ^ bits[i & CORE]) for i in range(se...  55.1 us
    pallas_call x2, Pallas kernels, back(): pl.pallas_call(functools.partial(back_kernel, ladder.native, last, counts...  54.9 us
    ppermute x49, waiting for transfers between devices, flip(): lax.ppermute(value, self.axes, [(i, i ^ bits[i & CORE]) for i in range(se...  50.4 us
    pallas_call x4, Pallas kernels, attn_call(): pl.pallas_call(body, grid_spec=pltpu.PrefetchScalarGridSpec(num_scalar_pr...  49.9 us
    pallas_call x1, Pallas kernels, expand(): pl.pallas_call(functools.partial(expand_kernel, ladder.native, tile, len(...  29.1 us
    pallas_call x2, Pallas kernels, contract(): pl.pallas_call(functools.partial(contract_kernel, ladder.native, part * l...  24.5 us
    pallas_call x1, Pallas kernels, input_grad(): pl.pallas_call(functools.partial(input_grad_kernel, ladder.native, calls)...  17.8 us
    pallas_call x1, Pallas kernels, down_grad(): pl.pallas_call(functools.partial(down_grad_kernel, ladder.native, len(out...  14.8 us
  transfers between devices with their start and end apart: 50, of which 13 were waited for; matrix products, arithmetic and copies ran while one was open for 9% of the time, Pallas kernels for 57%

profile of v7, /device:TPU:0, one launch (start us, length us, event | category | flops | bytes accessed | tf_op | source)
XLA Modules:
  0.0 396.2 jit_solution(2155583053514891807)
XLA Ops:
  0.6 5.1 %collective-permute-start.2 = (bf16[32,3072]{1,0:T(8,128)(2,1)}, bf16[32,3072]{1,0:T(8,128)(2,1)S(1)}, u32[]{:S(2)}, u32[]{:S(2)}) collective-permute-start(bf16[32,3072]{1,0:T(8,128)(2,1)} %refs_0_), channel_id=1, source_target_pairs={{0,6},{1,7},{2,4},{3,5},{4,2},{5,3},{6,0},{7,1},{8,14},{9,15},{10,... | collective-permute-start | bytes 589832 | tf_op jit(solution)/shard_map/ppermute | solution.py:56
  10.5 8.2 %collective-permute-done.refs_1_ = bf16[32,3072]{1,0:T(8,128)(2,1)S(1)} collective-permute-done((bf16[32,3072]{1,0:T(8,128)(2,1)}, bf16[32,3072]{1,0:T(8,128)(2,1)S(1)}, u32[]{:S(2)}, u32[]{:S(2)}) %collective-permute-start) | collective-permute-done | bytes 196640 | tf_op jit(solution)/shard_map/ppermute | solution.py:56
  19.0 3.5 collective-permute-start.4
  24.4 1.9 collective-permute-done.3.refs_5_
  26.9 2.9 place_group.1.rest_0_.rest_4_
  35.0 16.1 %collective-permute-done.8.rest_1_.rest_5_ = bf16[4,32,3200]{2,1,0:T(8,128)(2,1)} collective-permute-done((bf16[4,32,3200]{2,1,0:T(8,128)(2,1)}, bf16[4,32,3200]{2,1,0:T(8,128)(2,1)}, u32[]{:S(2)}, u32[]{:S(2)}) %collective-permute-start.8) | collective-permute-done | bytes 819232 | tf_op jit(solution)/shard_map/ppermute | solution.py:56
  51.2 1.5 collective-permute-start.10
  55.1 8.7 %collective-permute-done.10.rest_3_.rest_7_ = bf16[4,32,3200]{2,1,0:T(8,128)(2,1)} collective-permute-done((bf16[4,32,3200]{2,1,0:T(8,128)(2,1)}, bf16[4,32,3200]{2,1,0:T(8,128)(2,1)}, u32[]{:S(2)}, u32[]{:S(2)}) %collective-permute-start.10) | collective-permute-done | bytes 819232 | tf_op jit(solution)/shard_map/ppermute | solution.py:56
  65.2 1.6 collective-permute-start.17
  69.8 14.3 %project.1 = (bf16[1024,3072]{1,0:T(8,128)(2,1)}, bf16[1024,1024]{1,0:T(8,128)(2,1)}, f32[1,1024]{1,0:T(1,128)}, f32[1,4096]{1,0:T(1,128)}, f32[4,1024]{1,0:T(4,128)}) custom-call(s32[6]{0:T(128)} %pad_add_fusion.meta, bf16[1024,1024]{1,0:T(8,128)(2,1)} %bitcast.67, f32[1024,1]{1,0:T(8,128)} %copy.45.valid_ref, ...), custom_call_target="tpu_custom_call" | custom-call | flops 32199999488 | tf_op jit(solution)/shard_map/project/pallas_call | solution.py:569
  84.9 10.2 %attn_forward.2 = (bf16[1024,1024]{1,0:T(8,128)(2,1)S(1)}, f32[8,8,256]{2,1,0:T(8,128)S(1)}) custom-call(s32[8]{0:T(128)S(1)} %and_select_fusion.refs_0_, s32[1024,128]{1,0:T(8,128)S(1)} %broadcast_in_dim.72.refs_1_, s32[1024,128]{1,0:T(8,128)S(1)} %broadcast_in_dim.74.refs_2_, s32[8,128]{1,0:T(8,128)S(1)} %bitcast.35, ...), custom_call_target="tpu_custom_call" | custom-call | flops 24839999488 | tf_op jit(solution)/shard_map/attn_forward/pallas_call | solution.py:357
  98.6 10.2 %attn_forward.3 = (bf16[1024,1024]{1,0:T(8,128)(2,1)S(1)}, f32[8,8,256]{2,1,0:T(8,128)S(1)}) custom-call(s32[8]{0:T(128)S(1)} %and_select_fusion.refs_0_, s32[1024,128]{1,0:T(8,128)S(1)} %broadcast_in_dim.72.refs_1_, s32[1024,128]{1,0:T(8,128)S(1)} %broadcast_in_dim.74.refs_2_, s32[8,128]{1,0:T(8,128)S(1)} %bitcast.36, ...), custom_call_target="tpu_custom_call", output_to_operand_aliasing={{0}: (7, {}), {1}: (8, {})} | custom-call | flops 24839999488 | tf_op jit(solution)/shard_map/attn_forward/pallas_call | solution.py:357
  108.8 6.1 %collective-permute-done.19.rest_3_.rest_11_ = bf16[4,32,5120]{2,1,0:T(8,128)(2,1)S(1)} collective-permute-done((bf16[4,32,5120]{2,1,0:T(8,128)(2,1)}, bf16[4,32,5120]{2,1,0:T(8,128)(2,1)S(1)}, u32[]{:S(2)}, u32[]{:S(2)}) %collective-permute-start.19) | collective-permute-done | bytes 1310752 | tf_op jit(solution)/shard_map/ppermute | solution.py:56
  115.7 1.5 collective-permute-start.25
  119.9 29.1 %expand.1 = (f32[1024,1024]{1,0:T(8,128)}, bf16[1024,1024]{1,0:T(8,128)(2,1)}, f32[8,1024]{1,0:T(8,128)}, bf16[1024,4096]{1,0:T(8,128)(2,1)}, bf16[1024,4096]{1,0:T(8,128)(2,1)}) custom-call(s32[6]{0:T(128)} %pad_add_fusion.meta, bf16[1024,1024]{1,0:T(8,128)(2,1)} %copy-done.7, bf16[1024,1024]{1,0:T(8,128)(2,1)} %bitcast.68, ...), custom_call_target="tpu_custom_call" | custom-call | flops 66700001280 | tf_op jit(solution)/shard_map/expand/pallas_call | solution.py:642
  150.8 14.8 %down_grad.1 = (bf16[4,4,128,1024]{3,2,1,0:T(8,128)(2,1)}, bf16[4,4,128,1024]{3,2,1,0:T(8,128)(2,1)}, f32[1,1024]{1,0:T(1,128)}) custom-call(s32[6]{0:T(128)} %pad_add_fusion.meta, bf16[1024,4096]{1,0:T(8,128)(2,1)} %get-tuple-element.187.act_ref, bf16[1024,1024]{1,0:T(8,128)(2,1)} %bitcast.64), custom_call_target="tpu_custom_call" | custom-call | flops 32199999488 | tf_op jit(solution)/shard_map/down_grad/pallas_call | solution.py:709
  166.3 2.8 collective-permute-done.31.rest_7_
  170.1 23.9 %back.2 = (bf16[4,4,32,5120]{3,2,1,0:T(8,128)(2,1)}, bf16[4,4,32,5120]{3,2,1,0:T(8,128)(2,1)}, f32[1024,1024]{1,0:T(8,128)}, f32[1,4096]{1,0:T(1,128)}) custom-call(s32[6]{0:T(128)} %pad_add_fusion.meta, bf16[1024,1024]{1,0:T(8,128)(2,1)} %bitcast.65, bf16[1024,4096]{1,0:T(8,128)(2,1)} %get-tuple-element.136.slope_ref, ...), custom_call_target="tpu_custom_call" | custom-call | flops 46000001024 | tf_op jit(solution)/shard_map/back/pallas_call | solution.py:899
  194.0 3.2 add_convert_fusion.1
  197.4 31.0 %back.3 = (bf16[4,4,32,5120]{3,2,1,0:T(8,128)(2,1)}, bf16[4,4,32,5120]{3,2,1,0:T(8,128)(2,1)}, f32[1024,1024]{1,0:T(8,128)}, bf16[1024,1024]{1,0:T(8,128)(2,1)},...) custom-call(s32[6]{0:T(128)} %pad_add_fusion.meta, ...), custom_call_target="tpu_custom_call", output_to_operand_aliasing={{0}: (24, {}), {1}: (25, {}), {6}: (26, {})} | custom-call | flops 69000003584 | tf_op jit(solution)/shard_map/back/pallas_call | solution.py:899
  228.6 3.0 fusion.1
  231.6 1.9 collective-permute-start.33
  233.5 14.5 %attn_backward.2 = (bf16[3,1024,1024]{2,1,0:T(8,128)(2,1)}, f32[8,1024]{1,0:T(8,128)S(1)}) custom-call(s32[8]{0:T(128)S(1)} %copy-done.6, s32[1024,128]{1,0:T(8,128)S(1)} %broadcast_in_dim.72.refs_1_, s32[1024,128]{1,0:T(8,128)S(1)} %broadcast_in_dim.74.refs_2_, s32[8,128]{1,0:T(8,128)S(1)} %bitcast.37, ...), custom_call_target="tpu_custom_call" | custom-call | flops 31280001024 | tf_op jit(solution)/shard_map/attn_backward/pallas_call | solution.py:357
  248.0 4.0 %spread_sums.3 = (f32[128,1024]{1,0:T(8,128)}, bf16[128,1024]{1,0:T(8,128)(2,1)}, bf16[128,1024]{1,0:T(8,128)(2,1)}, bf16[128,1024]{1,0:T(8,128)(2,1)}) custom-call(s32[6]{0:T(128)} %pad_add_fusion.meta, bf16[4,4,128,1024]{3,2,1,0:T(8,128)(2,1)} %get-tuple-element.132.refs_0_.refs_4_.refs_8_.refs_12_, ...), custom_call_target="tpu_custom_call" | custom-call | flops 6899999744 | tf_op jit(solution)/shard_map/spread_sums/pallas_call | solution.py:110
  252.0 1.9 collective-permute-start.35
  254.7 1.7 collective-permute-start.37
  256.4 5.1 %add_convert_fusion = bf16[2,4,32,5120]{3,2,1,0:T(8,128)(2,1)} fusion(bf16[4,4,32,5120]{3,2,1,0:T(8,128)(2,1)} %collective-permute-done.34.refs_1_.refs_5_.refs_9_.refs_13_, bf16[4,4,32,5120]{3,2,1,0:T(8,128)(2,1)} %get-tuple-element.155.refs_0_.refs_4_.refs_8_.refs_12_), kind=kLoop, calls=%fused_computation | loop fusion | flops 5242880 | bytes 7864320 | tf_op jit(solution)/shard_map/convert_element_type | solution.py:188
  261.5 1.5 collective-permute-start.38
  263.1 14.9 %attn_backward.3 = (bf16[3,1024,1024]{2,1,0:T(8,128)(2,1)}, f32[8,1024]{1,0:T(8,128)S(1)}) custom-call(s32[8]{0:T(128)S(1)} %copy-done.6, s32[1024,128]{1,0:T(8,128)S(1)} %copy-done.3, s32[1024,128]{1,0:T(8,128)S(1)} %copy-done.1, s32[8,128]{1,0:T(8,128)S(1)} %bitcast.38, ...), custom_call_target="tpu_custom_call", output_to_operand_aliasing={{0}: (9, {}), {1}: (10, {})} | custom-call | flops 31280001024 | tf_op jit(solution)/shard_map/attn_backward/pallas_call | solution.py:357
  279.0 12.4 %qkv_grad.1 = (bf16[4,4,32,3072]{3,2,1,0:T(8,128)(2,1)}, bf16[4,4,32,3072]{3,2,1,0:T(8,128)(2,1)}) custom-call(s32[6]{0:T(128)} %pad_add_fusion.meta, bf16[1024,1024]{1,0:T(8,128)(2,1)} %get-tuple-element.128.left_ref, bf16[3,1024,1024]{2,1,0:T(8,128)(2,1)} %get-tuple-element.165.right_ref.rest_0_), custom_call_target="tpu_custom_call" | custom-call | flops 18400000000 | tf_op jit(solution)/shard_map/qkv_grad/pallas_call | solution.py:747
  295.2 2.7 fusion
  297.9 1.7 collective-permute-start.39
  299.6 12.3 %contract.2 = (bf16[512,1024]{1,0:T(8,128)(2,1)}, f32[8,1024]{1,0:T(8,128)}) custom-call(s32[6]{0:T(128)} %pad_add_fusion.meta, bf16[1024,4096]{1,0:T(8,128)(2,1)} %get-tuple-element.187.act_ref, f32[4,1024]{1,0:T(4,128)} %get-tuple-element.125.lines_ref.rest_3_, f32[1024,1]{1,0:T(8,128)} %copy.45.valid_ref, f32[1024,1024]{1,0:T(8,128)} %get-tuple-element.138.middle_ref, ...), custom_call_target="tpu_custom_call" | custom-call | flops 18400000000 | tf_op jit(solution)/shard_map/contract/pallas_call | solution.py:955
  312.0 2.2 add_convert_fusion.2
  315.7 4.5 %spread_sums.4 = (f32[32,5120]{1,0:T(8,128)}, bf16[32,5120]{1,0:T(8,128)(2,1)}, bf16[32,5120]{1,0:T(8,128)(2,1)}, bf16[32,5120]{1,0:T(8,128)(2,1)}) custom-call(s32[6]{0:T(128)} %pad_add_fusion.meta, bf16[4,4,32,5120]{3,2,1,0:T(8,128)(2,1)} %get-tuple-element.155.refs_0_.refs_4_.refs_8_.refs_12_, ...), custom_call_target="tpu_custom_call" | custom-call | flops 6899999744 | tf_op jit(solution)/shard_map/spread_sums/pallas_call | solution.py:110
  320.2 2.8 collective-permute-start.43
  323.3 2.0 collective-permute-start.45
  325.3 17.8 %input_grad.1 = (bf16[1024,1024]{1,0:T(8,128)(2,1)}, f32[8,1024]{1,0:T(8,128)}) custom-call(s32[6]{0:T(128)} %pad_add_fusion.meta, bf16[3,1024,1024]{2,1,0:T(8,128)(2,1)} %get-tuple-element.165.right_ref.rest_0_, bf16[1024,1024]{1,0:T(8,128)(2,1)} %bitcast.69, f32[1024,1024]{1,0:T(8,128)} %get-tuple-element.179.rest_2_, ...), custom_call_target="tpu_custom_call" | custom-call | flops 41400000512 | tf_op jit(solution)/shard_map/input_grad/pallas_call | solution.py:1014
  345.3 1.7 fusion.2
  347.9 12.3 %contract.3 = (bf16[512,1024]{1,0:T(8,128)(2,1)}, f32[8,1024]{1,0:T(8,128)}) custom-call(s32[6]{0:T(128)} %pad_add_fusion.meta, bf16[1024,4096]{1,0:T(8,128)(2,1)} %get-tuple-element.187.act_ref, f32[4,1024]{1,0:T(4,128)} %get-tuple-element.125.lines_ref.rest_3_, f32[1024,1]{1,0:T(8,128)} %copy.45.valid_ref, f32[1024,1024]{1,0:T(8,128)} %get-tuple-element.138.middle_ref, ...), custom_call_target="tpu_custom_call" | custom-call | flops 18400000000 | tf_op jit(solution)/shard_map/contract/pallas_call | solution.py:955
  361.9 3.8 spread_sums.5
  365.7 2.9 collective-permute-start.46
  369.0 4.5 %collective-permute-done.46 = bf16[32,3072]{1,0:T(8,128)(2,1)S(1)} collective-permute-done((bf16[32,3072]{1,0:T(8,128)(2,1)}, bf16[32,3072]{1,0:T(8,128)(2,1)S(1)}, u32[]{:S(2)}, u32[]{:S(2)}) %collective-permute-start.46) | collective-permute-done | bytes 196640 | tf_op jit(solution)/shard_map/ppermute | solution.py:56
  374.1 4.7 %all-to-all-start = ((f32[32,1,384]{2,1,0:T(1,128)}), f32[32,1,384]{2,1,0:T(1,128)S(1)}, u32[]{:S(2)}, u32[]{:S(2)}) async-start(f32[32,1,384]{2,1,0:T(1,128)} %all_to_all.6), calls=%async_computation | async-start | bytes 98304 | tf_op jit(solution)/shard_map/all_to_all | solution.py:65
  378.9 1.8 collective-permute-start.47
  380.7 2.4 collective-permute-start.48
  383.1 3.3 all-to-all-done
  394.2 1.8 convert_add_fusion.2
  (235 shorter events, 51.1 us)
Async XLA Ops:
  0.6 23.1 %collective-permute-start.2 = (bf16[32,3072]{1,0:T(8,128)(2,1)}, bf16[32,3072]{1,0:T(8,128)(2,1)S(1)}, u32[]{:S(2)}, u32[]{:S(2)}) collective-permute-start(bf16[32,3072]{1,0:T(8,128)(2,1)} %refs_0_), channel_id=1, source_target_pairs={{0,6},{1,7},{2,4},{3,5},{4,2},{5,3},{6,0},{7,1},{8,14},{9,15},{10,... | collective-permute-start | bytes 589832 | tf_op jit(solution)/shard_map/ppermute | solution.py:56
  5.8 18.0 %collective-permute-start.1 = (bf16[32,3072]{1,0:T(8,128)(2,1)}, bf16[32,3072]{1,0:T(8,128)(2,1)S(1)}, u32[]{:S(2)}, u32[]{:S(2)}) collective-permute-start(bf16[32,3072]{1,0:T(8,128)(2,1)} %refs_0_), channel_id=1, source_target_pairs={{0,4},{1,5},{2,6},{3,7},{4,0},{5,1},{6,2},{7,3},{8,12},{9,13},{10,... | collective-permute-start | bytes 589832 | tf_op jit(solution)/shard_map/ppermute | solution.py:56
  5.8 13.0 %collective-permute-start = (bf16[32,3072]{1,0:T(8,128)(2,1)}, bf16[32,3072]{1,0:T(8,128)(2,1)S(1)}, u32[]{:S(2)}, u32[]{:S(2)}) collective-permute-start(bf16[32,3072]{1,0:T(8,128)(2,1)} %refs_0_), channel_id=1, source_target_pairs={{0,2},{1,3},{2,0},{3,1},{4,6},{5,7},{6,4},{7,5},{8,10},{9,11},{10,... | collective-permute-start | bytes 589832 | tf_op jit(solution)/shard_map/ppermute | solution.py:56
  18.8 5.5 %collective-permute-start.5 = (bf16[32,128]{1,0:T(8,128)(2,1)S(1)}, bf16[32,128]{1,0:T(8,128)(2,1)S(1)}, u32[]{:S(2)}, u32[]{:S(2)}) collective-permute-start(bf16[32,128]{1,0:T(8,128)(2,1)S(1)} %select_select_fusion.refs_4_), channel_id=1, source_target_pairs={{0,6},{1,7},{2,4},{3,5},{4,2},{5,3},{6,0},{7,1},{8,14},{9,15},{10,... | collective-permute-start | bytes 24584 | tf_op jit(solution)/shard_map/ppermute | solution.py:56
  19.0 5.3 %collective-permute-start.4 = (bf16[32,128]{1,0:T(8,128)(2,1)S(1)}, bf16[32,128]{1,0:T(8,128)(2,1)S(1)}, u32[]{:S(2)}, u32[]{:S(2)}) collective-permute-start(bf16[32,128]{1,0:T(8,128)(2,1)S(1)} %select_select_fusion.refs_4_), channel_id=1, source_target_pairs={{0,4},{1,5},{2,6},{3,7},{4,0},{5,1},{6,2},{7,3},{8,12},{9,13},{10,... | collective-permute-start | bytes 24584 | tf_op jit(solution)/shard_map/ppermute | solution.py:56
  22.6 3.7 collective-permute-start.3
  29.8 21.4 %collective-permute-start.8 = (bf16[4,32,3200]{2,1,0:T(8,128)(2,1)}, bf16[4,32,3200]{2,1,0:T(8,128)(2,1)}, u32[]{:S(2)}, u32[]{:S(2)}) collective-permute-start(bf16[4,32,3200]{2,1,0:T(8,128)(2,1)} %place_group.1.rest_0_.rest_4_), channel_id=1, source_target_pairs={{0,8},{1,17},{2,10},{3,19},{4,12},{5,21},{6,14},{7,23},{8,0},{9,25... | collective-permute-start | bytes 2457608 | tf_op jit(solution)/shard_map/ppermute | solution.py:56
  31.4 21.5 %collective-permute-start.6 = (bf16[32,5120]{1,0:T(8,128)(2,1)S(1)}, bf16[32,5120]{1,0:T(8,128)(2,1)S(1)}, u32[]{:S(2)}, u32[]{:S(2)}) collective-permute-start(bf16[32,5120]{1,0:T(8,128)(2,1)S(1)} %pad_maximum_fusion), channel_id=1, source_target_pairs={{0,4},{1,5},{2,6},{3,7},{4,0},{5,1},{6,2},{7,3},{8,12},{9,13},{10,... | collective-permute-start | bytes 983048 | tf_op jit(solution)/shard_map/ppermute | solution.py:56
  33.5 21.6 %collective-permute-start.9 = (bf16[4,32,3200]{2,1,0:T(8,128)(2,1)}, bf16[4,32,3200]{2,1,0:T(8,128)(2,1)}, u32[]{:S(2)}, u32[]{:S(2)}) collective-permute-start(bf16[4,32,3200]{2,1,0:T(8,128)(2,1)} %place_group.1.rest_0_.rest_4_), channel_id=1, source_target_pairs={{0,16},{1,9},{2,18},{3,11},{4,20},{5,13},{6,22},{7,15},{8,24},{9,1... | collective-permute-start | bytes 2457608 | tf_op jit(solution)/shard_map/ppermute | solution.py:56
  51.2 12.7 %collective-permute-start.10 = (bf16[4,32,3200]{2,1,0:T(8,128)(2,1)}, bf16[4,32,3200]{2,1,0:T(8,128)(2,1)}, u32[]{:S(2)}, u32[]{:S(2)}) collective-permute-start(bf16[4,32,3200]{2,1,0:T(8,128)(2,1)} %collective-permute-done.8.rest_1_.rest_5_), channel_id=1, source_target_pairs={{0,16},{1,9},{2,18},{3,11},{4,20},{5,13},{6,22},{7,15},{8,24},{9,1... | collective-permute-start | bytes 2457608 | tf_op jit(solution)/shard_map/ppermute | solution.py:56
  53.0 10.9 %collective-permute-start.7 = (bf16[2,32,5120]{2,1,0:T(8,128)(2,1)S(1)}, bf16[2,32,5120]{2,1,0:T(8,128)(2,1)S(1)}, u32[]{:S(2)}, u32[]{:S(2)}) collective-permute-start(bf16[2,32,5120]{2,1,0:T(8,128)(2,1)S(1)} %maximum_select_fusion.2), channel_id=1, source_target_pairs={{0,2},{1,3},{2,0},{3,1},{4,6},{5,7},{6,4},{7,5},{8,10},{9,11},{10,... | collective-permute-start | bytes 1966088 | tf_op jit(solution)/shard_map/ppermute | solution.py:56
  54.6 10.6 %collective-permute-start.11 = (bf16[4,32,3200]{2,1,0:T(8,128)(2,1)}, bf16[4,32,3200]{2,1,0:T(8,128)(2,1)S(1)}, u32[]{:S(2)}, u32[]{:S(2)}) collective-permute-start(bf16[4,32,3200]{2,1,0:T(8,128)(2,1)} %place_group.1.rest_0_.rest_4_), channel_id=1, source_target_pairs={{0,1},{1,0},{2,3},{3,2},{4,5},{5,4},{6,7},{7,6},{8,9},{9,8},{10,11... | collective-permute-start | bytes 2457608 | tf_op jit(solution)/shard_map/ppermute | solution.py:56
  54.6 13.7 %collective-permute-start.13 = (bf16[4,32,3200]{2,1,0:T(8,128)(2,1)}, bf16[4,32,3200]{2,1,0:T(8,128)(2,1)}, u32[]{:S(2)}, u32[]{:S(2)}) collective-permute-start(bf16[4,32,3200]{2,1,0:T(8,128)(2,1)} %collective-permute-done.8.rest_1_.rest_5_), channel_id=1, source_target_pairs={{0,1},{1,0},{2,3},{3,2},{4,5},{5,4},{6,7},{7,6},{8,9},{9,8},{10,11... | collective-permute-start | bytes 2457608 | tf_op jit(solution)/shard_map/ppermute | solution.py:56
  55.1 11.7 %collective-permute-start.12 = (bf16[4,32,3200]{2,1,0:T(8,128)(2,1)}, bf16[4,32,3200]{2,1,0:T(8,128)(2,1)S(1)}, u32[]{:S(2)}, u32[]{:S(2)}) collective-permute-start(bf16[4,32,3200]{2,1,0:T(8,128)(2,1)} %collective-permute-done.9.rest_2_.rest_6_), channel_id=1, source_target_pairs={{0,1},{1,0},{2,3},{3,2},{4,5},{5,4},{6,7},{7,6},{8,9},{9,8},{10,11... | collective-permute-start | bytes 2457608 | tf_op jit(solution)/shard_map/ppermute | solution.py:56
  63.8 6.0 %collective-permute-start.14 = (bf16[4,32,3200]{2,1,0:T(8,128)(2,1)}, bf16[4,32,3200]{2,1,0:T(8,128)(2,1)}, u32[]{:S(2)}, u32[]{:S(2)}) collective-permute-start(bf16[4,32,3200]{2,1,0:T(8,128)(2,1)} %collective-permute-done.10.rest_3_.rest_7_), channel_id=1, source_target_pairs={{0,1},{1,0},{2,3},{3,2},{4,5},{5,4},{6,7},{7,6},{8,9},{9,8},{10,11... | collective-permute-start | bytes 2457608 | tf_op jit(solution)/shard_map/ppermute | solution.py:56
  64.2 51.5 %collective-permute-start.20 = (bf16[4,32,5120]{2,1,0:T(8,128)(2,1)S(1)}, bf16[4,32,5120]{2,1,0:T(8,128)(2,1)S(1)}, u32[]{:S(2)}, u32[]{:S(2)}) collective-permute-start(bf16[4,32,5120]{2,1,0:T(8,128)(2,1)S(1)} %bitcast.41), channel_id=1, source_target_pairs={{0,1},{1,0},{2,3},{3,2},{4,5},{5,4},{6,7},{7,6},{8,9},{9,8},{10,11... | collective-permute-start | bytes 3932168 | tf_op jit(solution)/shard_map/ppermute | solution.py:56
  65.2 33.3 %collective-permute-start.17 = (bf16[4,32,5120]{2,1,0:T(8,128)(2,1)S(1)}, bf16[4,32,5120]{2,1,0:T(8,128)(2,1)}, u32[]{:S(2)}, u32[]{:S(2)}) collective-permute-start(bf16[4,32,5120]{2,1,0:T(8,128)(2,1)S(1)} %bitcast.42), channel_id=1, source_target_pairs={{0,16},{1,9},{2,18},{3,11},{4,20},{5,13},{6,22},{7,15},{8,24},{9,1... | collective-permute-start | bytes 3932168 | tf_op jit(solution)/shard_map/ppermute | solution.py:56
  66.8 29.3 %collective-permute-start.16 = (bf16[4,32,5120]{2,1,0:T(8,128)(2,1)S(1)}, bf16[4,32,5120]{2,1,0:T(8,128)(2,1)}, u32[]{:S(2)}, u32[]{:S(2)}) collective-permute-start(bf16[4,32,5120]{2,1,0:T(8,128)(2,1)S(1)} %bitcast.43), channel_id=1, source_target_pairs={{0,8},{1,17},{2,10},{3,19},{4,12},{5,21},{6,14},{7,23},{8,0},{9,25... | collective-permute-start | bytes 3932168 | tf_op jit(solution)/shard_map/ppermute | solution.py:56
  68.3 15.8 %collective-permute-start.15 = (bf16[128,1024]{1,0:T(8,128)(2,1)S(1)}, bf16[128,1024]{1,0:T(8,128)(2,1)S(1)}, u32[]{:S(2)}, u32[]{:S(2)}) collective-permute-start(bf16[128,1024]{1,0:T(8,128)(2,1)S(1)} %copy-done.19), channel_id=1, source_target_pairs={{0,4},{1,5},{2,6},{3,7},{4,0},{5,1},{6,2},{7,3},{8,12},{9,13},{10,... | collective-permute-start | bytes 786440 | tf_op jit(solution)/shard_map/ppermute | solution.py:56
  84.2 14.3 %collective-permute-start.18 = (bf16[2,128,1024]{2,1,0:T(8,128)(2,1)S(1)}, bf16[2,128,1024]{2,1,0:T(8,128)(2,1)S(1)}, u32[]{:S(2)}, u32[]{:S(2)}) collective-permute-start(bf16[2,128,1024]{2,1,0:T(8,128)(2,1)S(1)} %maximum_select_fusion.4), channel_id=1, source_target_pairs={{0,2},{1,3},{2,0},{3,1},{4,6},{5,7},{6,4},{7,5},{8,10},{9,11},{10,... | collective-permute-start | bytes 1572872 | tf_op jit(solution)/shard_map/ppermute | solution.py:56
  96.1 21.2 %collective-permute-start.22 = (bf16[4,32,5120]{2,1,0:T(8,128)(2,1)}, bf16[4,32,5120]{2,1,0:T(8,128)(2,1)}, u32[]{:S(2)}, u32[]{:S(2)}) collective-permute-start(bf16[4,32,5120]{2,1,0:T(8,128)(2,1)} %collective-permute-done.16.rest_1_.rest_9_), channel_id=1, source_target_pairs={{0,1},{1,0},{2,3},{3,2},{4,5},{5,4},{6,7},{7,6},{8,9},{9,8},{10,11... | collective-permute-start | bytes 3932168 | tf_op jit(solution)/shard_map/ppermute | solution.py:56
  97.0 17.8 %collective-permute-start.19 = (bf16[4,32,5120]{2,1,0:T(8,128)(2,1)}, bf16[4,32,5120]{2,1,0:T(8,128)(2,1)S(1)}, u32[]{:S(2)}, u32[]{:S(2)}) collective-permute-start(bf16[4,32,5120]{2,1,0:T(8,128)(2,1)} %collective-permute-done.16.rest_1_.rest_9_), channel_id=1, source_target_pairs={{0,16},{1,9},{2,18},{3,11},{4,20},{5,13},{6,22},{7,15},{8,24},{9,1... | collective-permute-start | bytes 3932168 | tf_op jit(solution)/shard_map/ppermute | solution.py:56
  98.5 19.2 %collective-permute-start.21 = (bf16[4,32,5120]{2,1,0:T(8,128)(2,1)}, bf16[4,32,5120]{2,1,0:T(8,128)(2,1)S(1)}, u32[]{:S(2)}, u32[]{:S(2)}) collective-permute-start(bf16[4,32,5120]{2,1,0:T(8,128)(2,1)} %collective-permute-done.17.rest_2_.rest_10_), channel_id=1, source_target_pairs={{0,1},{1,0},{2,3},{3,2},{4,5},{5,4},{6,7},{7,6},{8,9},{9,8},{10,11... | collective-permute-start | bytes 3932168 | tf_op jit(solution)/shard_map/ppermute | solution.py:56
  115.1 51.1 %collective-permute-start.28 = (bf16[4,128,1024]{2,1,0:T(8,128)(2,1)S(1)}, bf16[4,128,1024]{2,1,0:T(8,128)(2,1)S(1)}, u32[]{:S(2)}, u32[]{:S(2)}) collective-permute-start(bf16[4,128,1024]{2,1,0:T(8,128)(2,1)S(1)} %bitcast.49), channel_id=1, source_target_pairs={{0,1},{1,0},{2,3},{3,2},{4,5},{5,4},{6,7},{7,6},{8,9},{9,8},{10,11... | collective-permute-start | bytes 3145736 | tf_op jit(solution)/shard_map/ppermute | solution.py:56
  115.7 34.1 %collective-permute-start.25 = (bf16[4,128,1024]{2,1,0:T(8,128)(2,1)S(1)}, bf16[4,128,1024]{2,1,0:T(8,128)(2,1)S(1)}, u32[]{:S(2)}, u32[]{:S(2)}) collective-permute-start(bf16[4,128,1024]{2,1,0:T(8,128)(2,1)S(1)} %bitcast.50), channel_id=1, source_target_pairs={{0,16},{1,9},{2,18},{3,11},{4,20},{5,13},{6,22},{7,15},{8,24},{9,1... | collective-permute-start | bytes 3145736 | tf_op jit(solution)/shard_map/ppermute | solution.py:56
  117.2 31.8 %collective-permute-start.24 = (bf16[4,128,1024]{2,1,0:T(8,128)(2,1)S(1)}, bf16[4,128,1024]{2,1,0:T(8,128)(2,1)}, u32[]{:S(2)}, u32[]{:S(2)}) collective-permute-start(bf16[4,128,1024]{2,1,0:T(8,128)(2,1)S(1)} %bitcast.51), channel_id=1, source_target_pairs={{0,8},{1,17},{2,10},{3,19},{4,12},{5,21},{6,14},{7,23},{8,0},{9,25... | collective-permute-start | bytes 3145736 | tf_op jit(solution)/shard_map/ppermute | solution.py:56
  149.1 17.2 %collective-permute-start.30 = (bf16[4,128,1024]{2,1,0:T(8,128)(2,1)}, bf16[4,128,1024]{2,1,0:T(8,128)(2,1)S(1)}, u32[]{:S(2)}, u32[]{:S(2)}) collective-permute-start(bf16[4,128,1024]{2,1,0:T(8,128)(2,1)} %collective-permute-done.24.rest_1_), channel_id=1, source_target_pairs={{0,1},{1,0},{2,3},{3,2},{4,5},{5,4},{6,7},{7,6},{8,9},{9,8},{10,11... | collective-permute-start | bytes 3145736 | tf_op jit(solution)/shard_map/ppermute | solution.py:56
  149.1 16.5 %collective-permute-start.27 = (bf16[4,128,1024]{2,1,0:T(8,128)(2,1)}, bf16[4,128,1024]{2,1,0:T(8,128)(2,1)S(1)}, u32[]{:S(2)}, u32[]{:S(2)}) collective-permute-start(bf16[4,128,1024]{2,1,0:T(8,128)(2,1)} %collective-permute-done.24.rest_1_), channel_id=1, source_target_pairs={{0,16},{1,9},{2,18},{3,11},{4,20},{5,13},{6,22},{7,15},{8,24},{9,1... | collective-permute-start | bytes 3145736 | tf_op jit(solution)/shard_map/ppermute | solution.py:56
  149.8 16.5 %collective-permute-start.29 = (bf16[4,128,1024]{2,1,0:T(8,128)(2,1)S(1)}, bf16[4,128,1024]{2,1,0:T(8,128)(2,1)S(1)}, u32[]{:S(2)}, u32[]{:S(2)}) collective-permute-start(bf16[4,128,1024]{2,1,0:T(8,128)(2,1)S(1)} %collective-permute-done.25.rest_2_), channel_id=1, source_target_pairs={{0,1},{1,0},{2,3},{3,2},{4,5},{5,4},{6,7},{7,6},{8,9},{9,8},{10,11... | collective-permute-start | bytes 3145736 | tf_op jit(solution)/shard_map/ppermute | solution.py:56
  165.8 28.2 %collective-permute-start.26 = (bf16[4,4,128,1024]{3,2,1,0:T(8,128)(2,1)}, bf16[4,4,128,1024]{3,2,1,0:T(8,128)(2,1)}, u32[]{:S(2)}, u32[]{:S(2)}) collective-permute-start(bf16[4,4,128,1024]{3,2,1,0:T(8,128)(2,1)} %get-tuple-element.133), channel_id=1, source_target_pairs={{0,1},{1,0},{2,3},{3,2},{4,5},{5,4},{6,7},{7,6},{8,9},{9,8},{10,11... | collective-permute-start | bytes 12582920 | tf_op jit(solution)/shard_map/ppermute | solution.py:56
  197.2 31.3 %collective-permute-start.32 = (bf16[2,4,128,1024]{3,2,1,0:T(8,128)(2,1)S(1)}, bf16[2,4,128,1024]{3,2,1,0:T(8,128)(2,1)S(1)}, u32[]{:S(2)}, u32[]{:S(2)}) collective-permute-start(bf16[2,4,128,1024]{3,2,1,0:T(8,128)(2,1)S(1)} %add_convert_fusion.1), channel_id=1, source_target_pairs={{0,16},{1,9},{2,18},{3,11},{4,20},{5,13},{6,22},{7,15},{8,24},{9,1... | collective-permute-start | bytes 6291464 | tf_op jit(solution)/shard_map/ppermute | solution.py:56
  228.4 28.0 %collective-permute-start.34 = (bf16[4,4,32,5120]{3,2,1,0:T(8,128)(2,1)}, bf16[4,4,32,5120]{3,2,1,0:T(8,128)(2,1)}, u32[]{:S(2)}, u32[]{:S(2)}) collective-permute-start(bf16[4,4,32,5120]{3,2,1,0:T(8,128)(2,1)} %get-tuple-element.156), channel_id=1, source_target_pairs={{0,1},{1,0},{2,3},{3,2},{4,5},{5,4},{6,7},{7,6},{8,9},{9,8},{10,11... | collective-permute-start | bytes 15728648 | tf_op jit(solution)/shard_map/ppermute | solution.py:56
  231.6 16.5 %collective-permute-start.33 = (bf16[4,128,1024]{2,1,0:T(8,128)(2,1)S(1)}, bf16[4,128,1024]{2,1,0:T(8,128)(2,1)}, u32[]{:S(2)}, u32[]{:S(2)}) collective-permute-start(bf16[4,128,1024]{2,1,0:T(8,128)(2,1)S(1)} %fusion.1), channel_id=1, source_target_pairs={{0,8},{1,17},{2,10},{3,19},{4,12},{5,21},{6,14},{7,23},{8,0},{9,25... | collective-permute-start | bytes 3145736 | tf_op jit(solution)/shard_map/ppermute | solution.py:56
  252.0 26.0 %collective-permute-start.35 = (bf16[128,1024]{1,0:T(8,128)(2,1)}, bf16[128,1024]{1,0:T(8,128)(2,1)S(1)}, u32[]{:S(2)}, u32[]{:S(2)}) collective-permute-start(bf16[128,1024]{1,0:T(8,128)(2,1)} %get-tuple-element.152), channel_id=1, source_target_pairs={{0,2},{1,3},{2,0},{3,1},{4,6},{5,7},{6,4},{7,5},{8,10},{9,11},{10,... | collective-permute-start | bytes 786440 | tf_op jit(solution)/shard_map/ppermute | solution.py:56
  254.0 24.0 %collective-permute-start.36 = (bf16[128,1024]{1,0:T(8,128)(2,1)}, bf16[128,1024]{1,0:T(8,128)(2,1)S(1)}, u32[]{:S(2)}, u32[]{:S(2)}) collective-permute-start(bf16[128,1024]{1,0:T(8,128)(2,1)} %get-tuple-element.153), channel_id=1, source_target_pairs={{0,4},{1,5},{2,6},{3,7},{4,0},{5,1},{6,2},{7,3},{8,12},{9,13},{10,... | collective-permute-start | bytes 786440 | tf_op jit(solution)/shard_map/ppermute | solution.py:56
  254.7 23.3 %collective-permute-start.37 = (bf16[128,1024]{1,0:T(8,128)(2,1)}, bf16[128,1024]{1,0:T(8,128)(2,1)S(1)}, u32[]{:S(2)}, u32[]{:S(2)}) collective-permute-start(bf16[128,1024]{1,0:T(8,128)(2,1)} %get-tuple-element.154), channel_id=1, source_target_pairs={{0,6},{1,7},{2,4},{3,5},{4,2},{5,3},{6,0},{7,1},{8,14},{9,15},{10,... | collective-permute-start | bytes 786440 | tf_op jit(solution)/shard_map/ppermute | solution.py:56
  261.5 33.7 %collective-permute-start.38 = (bf16[2,4,32,5120]{3,2,1,0:T(8,128)(2,1)}, bf16[2,4,32,5120]{3,2,1,0:T(8,128)(2,1)}, u32[]{:S(2)}, u32[]{:S(2)}) collective-permute-start(bf16[2,4,32,5120]{3,2,1,0:T(8,128)(2,1)} %add_convert_fusion), channel_id=1, source_target_pairs={{0,16},{1,9},{2,18},{3,11},{4,20},{5,13},{6,22},{7,15},{8,24},{9,1... | collective-permute-start | bytes 7864328 | tf_op jit(solution)/shard_map/ppermute | solution.py:56
  291.3 20.6 %collective-permute-start.40 = (bf16[4,4,32,3072]{3,2,1,0:T(8,128)(2,1)}, bf16[4,4,32,3072]{3,2,1,0:T(8,128)(2,1)S(1)}, u32[]{:S(2)}, u32[]{:S(2)}) collective-permute-start(bf16[4,4,32,3072]{3,2,1,0:T(8,128)(2,1)} %get-tuple-element.167), channel_id=1, source_target_pairs={{0,1},{1,0},{2,3},{3,2},{4,5},{5,4},{6,7},{7,6},{8,9},{9,8},{10,11... | collective-permute-start | bytes 9437192 | tf_op jit(solution)/shard_map/ppermute | solution.py:56
  297.9 17.8 %collective-permute-start.39 = (bf16[4,32,5120]{2,1,0:T(8,128)(2,1)S(1)}, bf16[4,32,5120]{2,1,0:T(8,128)(2,1)}, u32[]{:S(2)}, u32[]{:S(2)}) collective-permute-start(bf16[4,32,5120]{2,1,0:T(8,128)(2,1)S(1)} %fusion), channel_id=1, source_target_pairs={{0,8},{1,17},{2,10},{3,19},{4,12},{5,21},{6,14},{7,23},{8,0},{9,25... | collective-permute-start | bytes 3932168 | tf_op jit(solution)/shard_map/ppermute | solution.py:56
  314.1 31.1 %collective-permute-start.41 = (bf16[2,4,32,3072]{3,2,1,0:T(8,128)(2,1)}, bf16[2,4,32,3072]{3,2,1,0:T(8,128)(2,1)}, u32[]{:S(2)}, u32[]{:S(2)}) collective-permute-start(bf16[2,4,32,3072]{3,2,1,0:T(8,128)(2,1)} %add_convert_fusion.2), channel_id=1, source_target_pairs={{0,16},{1,9},{2,18},{3,11},{4,20},{5,13},{6,22},{7,15},{8,24},{9,1... | collective-permute-start | bytes 4718600 | tf_op jit(solution)/shard_map/ppermute | solution.py:56
  320.2 40.8 %collective-permute-start.43 = (bf16[32,5120]{1,0:T(8,128)(2,1)}, bf16[32,5120]{1,0:T(8,128)(2,1)S(1)}, u32[]{:S(2)}, u32[]{:S(2)}) collective-permute-start(bf16[32,5120]{1,0:T(8,128)(2,1)} %get-tuple-element.174), channel_id=1, source_target_pairs={{0,2},{1,3},{2,0},{3,1},{4,6},{5,7},{6,4},{7,5},{8,10},{9,11},{10,... | collective-permute-start | bytes 983048 | tf_op jit(solution)/shard_map/ppermute | solution.py:56
  322.9 38.1 %collective-permute-start.44 = (bf16[32,5120]{1,0:T(8,128)(2,1)}, bf16[32,5120]{1,0:T(8,128)(2,1)}, u32[]{:S(2)}, u32[]{:S(2)}) collective-permute-start(bf16[32,5120]{1,0:T(8,128)(2,1)} %get-tuple-element.175), channel_id=1, source_target_pairs={{0,4},{1,5},{2,6},{3,7},{4,0},{5,1},{6,2},{7,3},{8,12},{9,13},{10,... | collective-permute-start | bytes 983048 | tf_op jit(solution)/shard_map/ppermute | solution.py:56
  323.3 37.7 %collective-permute-start.45 = (bf16[32,5120]{1,0:T(8,128)(2,1)}, bf16[32,5120]{1,0:T(8,128)(2,1)}, u32[]{:S(2)}, u32[]{:S(2)}) collective-permute-start(bf16[32,5120]{1,0:T(8,128)(2,1)} %get-tuple-element.176), channel_id=1, source_target_pairs={{0,6},{1,7},{2,4},{3,5},{4,2},{5,3},{6,0},{7,1},{8,14},{9,15},{10,... | collective-permute-start | bytes 983048 | tf_op jit(solution)/shard_map/ppermute | solution.py:56
  347.0 14.0 %collective-permute-start.42 = (bf16[4,32,3072]{2,1,0:T(8,128)(2,1)S(1)}, bf16[4,32,3072]{2,1,0:T(8,128)(2,1)S(1)}, u32[]{:S(2)}, u32[]{:S(2)}) collective-permute-start(bf16[4,32,3072]{2,1,0:T(8,128)(2,1)S(1)} %fusion.2), channel_id=1, source_target_pairs={{0,8},{1,17},{2,10},{3,19},{4,12},{5,21},{6,14},{7,23},{8,0},{9,25... | collective-permute-start | bytes 2359304 | tf_op jit(solution)/shard_map/ppermute | solution.py:56
  365.7 7.7 %collective-permute-start.46 = (bf16[32,3072]{1,0:T(8,128)(2,1)}, bf16[32,3072]{1,0:T(8,128)(2,1)S(1)}, u32[]{:S(2)}, u32[]{:S(2)}) collective-permute-start(bf16[32,3072]{1,0:T(8,128)(2,1)} %get-tuple-element.193), channel_id=1, source_target_pairs={{0,6},{1,7},{2,4},{3,5},{4,2},{5,3},{6,0},{7,1},{8,14},{9,15},{10,... | collective-permute-start | bytes 589832 | tf_op jit(solution)/shard_map/ppermute | solution.py:56
  374.1 12.3 %all-to-all-start = ((f32[32,1,384]{2,1,0:T(1,128)}), f32[32,1,384]{2,1,0:T(1,128)S(1)}, u32[]{:S(2)}, u32[]{:S(2)}) async-start(f32[32,1,384]{2,1,0:T(1,128)} %all_to_all.6), calls=%async_computation | async-start | bytes 98304 | tf_op jit(solution)/shard_map/all_to_all | solution.py:65
  378.9 13.8 %collective-permute-start.47 = (bf16[32,3072]{1,0:T(8,128)(2,1)}, bf16[32,3072]{1,0:T(8,128)(2,1)}, u32[]{:S(2)}, u32[]{:S(2)}) collective-permute-start(bf16[32,3072]{1,0:T(8,128)(2,1)} %get-tuple-element.191), channel_id=1, source_target_pairs={{0,2},{1,3},{2,0},{3,1},{4,6},{5,7},{6,4},{7,5},{8,10},{9,11},{10,... | collective-permute-start | bytes 589832 | tf_op jit(solution)/shard_map/ppermute | solution.py:56
  380.7 10.7 %collective-permute-start.48 = (bf16[32,3072]{1,0:T(8,128)(2,1)}, bf16[32,3072]{1,0:T(8,128)(2,1)}, u32[]{:S(2)}, u32[]{:S(2)}) collective-permute-start(bf16[32,3072]{1,0:T(8,128)(2,1)} %get-tuple-element.192), channel_id=1, source_target_pairs={{0,4},{1,5},{2,6},{3,7},{4,0},{5,1},{6,2},{7,3},{8,12},{9,13},{10,... | collective-permute-start | bytes 589832 | tf_op jit(solution)/shard_map/ppermute | solution.py:56
  (54 other events, 928.1 us)
